TPU v7x, 512 devices: a whole 4x8x8 slice. The times are simulated.
512 devices in a mesh: patch: 2 (over core), lat: 8 (over y), lon: 32 (over z, x).
Axes of the slice: x: 4, y: 8, z: 8, core: 2. Of those that a mesh axis runs over, the one named last changes fastest.
Arguments:
- velocity: float32 [2, 3, 128, 256, 128], P('patch', None, 'lat', 'lon'), may hold values from -6 to 6
- forcing: float32 [2, 3, 128, 256, 128], P('patch', None, 'lat', 'lon'), may hold values from -3 to 3
- viscosity: float32 [2, 128, 256, 128], P('patch', 'lat', 'lon'), may hold values from 1 to 10
- ghost_slots: int32 [2, 768], P('patch'), may hold values from 0 to 767, each once within a row
- corner_rows: int32 [2, 8, 96], P('patch', 'lat', 'lon'), may hold values from 0 to 15
- corner_cols: int32 [2, 8, 96], P('patch', 'lat', 'lon'), may hold values from 0 to 7
- corner_weights: float32 [2, 8, 4, 96], P('patch', 'lat', None, 'lon'), may hold values from 0 to 1, as said below
Outputs:
- new_velocity: float32 [2, 3, 128, 256, 128], P('patch', None, 'lat', 'lon')
- residual: float32 [2, 3, 128, 256, 128], P('patch', None, 'lat', 'lon')
Inputs may be any that keep to these rules, and one draw needn't show every extreme that they name: `ghost_slots`: each row names every slot of the other patch exactly once. `corner_rows`: the row below the corner is read too, from the next device or as zero beyond the patch. `corner_cols`: the column after the corner is read too, from the next device or as zero beyond the patch. `corner_weights`: the four weights of a slot are (1 - s)(1 - t), s(1 - t), (1 - s)t and st for some s and t in [0, 1).
All inputs are finite; a program needn't handle non-finite values.
Results may differ from a plain program's by a relative error of at most 0.0001.
Values sent between devices are 32-bit elements; how exact they have to be, the bound alone decides.
No kernel may reach another device: no remote copies, remote signals or barrier semaphores. Data moves between devices by JAX's collectives and lax.ppermute only.
A program may use at most 64 MiB of HBM per device.

v0:
```python
import jax
import jax.numpy as jnp
from jax import lax
from jax.sharding import PartitionSpec as P

SWEEPS = 2
COARSE = 8


RELAX = 0.8


def with_halo(shard, sides, width):
    for axis, dim in sides:
        devices, length = (lax.axis_size(axis), shard.shape[dim])
        up = [(i, (i + 1) % devices) for i in range(devices - 1)]
        down = [(j, i) for i, j in up]
        last = lax.slice_in_dim(shard, length - width, length, axis=dim)
        first = lax.slice_in_dim(shard, 0, width, axis=dim)
        before = lax.ppermute(last, axis, up)
        after = lax.ppermute(first, axis, down)
        shard = jnp.concatenate([before, shard, after], axis=dim)
    return shard


def swapped(value, axis, apart):
    mask = 2**apart
    pairs = [(source, source ^ mask) for source in range(lax.axis_size(axis))]
    return lax.ppermute(value, axis, pairs)


def face_terms(padded_visc, weight_scale):
    centre = padded_visc[1:-1, 1:-1, 1:-1]
    return (
        weight_scale * (centre + padded_visc[:-2, 1:-1, 1:-1]),
        weight_scale * (centre + padded_visc[2:, 1:-1, 1:-1]),
        weight_scale * (centre + padded_visc[1:-1, :-2, 1:-1]),
        weight_scale * (centre + padded_visc[1:-1, 2:, 1:-1]),
        weight_scale * (centre + padded_visc[1:-1, 1:-1, :-2]),
        weight_scale * (centre + padded_visc[1:-1, 1:-1, 2:]),
    )


def diagonal_of(face_coefs):
    return (
        face_coefs[0]
        + face_coefs[1]
        + face_coefs[2]
        + face_coefs[3]
        + face_coefs[4]
        + face_coefs[5]
    )


def neighbour_sum(padded, face_coefs):
    summed = face_coefs[0] * padded[:, :-2, 1:-1, 1:-1]
    summed = summed + face_coefs[1] * padded[:, 2:, 1:-1, 1:-1]
    summed = summed + face_coefs[2] * padded[:, 1:-1, :-2, 1:-1]
    summed = summed + face_coefs[3] * padded[:, 1:-1, 2:, 1:-1]
    summed = summed + face_coefs[4] * padded[:, 1:-1, 1:-1, :-2]
    summed = summed + face_coefs[5] * padded[:, 1:-1, 1:-1, 2:]
    return summed


def bilinear(weight_rows, corner_list):
    summed = weight_rows[0][None, :, None] * corner_list[0]
    summed = summed + weight_rows[1][None, :, None] * corner_list[1]
    summed = summed + weight_rows[2][None, :, None] * corner_list[2]
    summed = summed + weight_rows[3][None, :, None] * corner_list[3]
    return summed


def clamp_take(source_array, along_dim, offset, block_size, whole_size, margin):
    position = offset + jnp.arange(-margin, block_size + margin, dtype=jnp.int32)
    picked = jnp.clip(position, 0, whole_size - 1) - offset + margin
    return jnp.take(source_array, picked, axis=along_dim)


def per_device(velocity, forcing, viscosity, ghost_slots, corner_rows, corner_cols, corner_weights):
    start_field = velocity[0]
    force_block = forcing[0]
    viscous = viscosity[0]
    row_block, col_block, levels = viscous.shape
    lat_count = lax.axis_size("lat")
    lon_count = lax.axis_size("lon")
    lat_index = lax.axis_index("lat")
    lon_index = lax.axis_index("lon")
    lat_cells = row_block * lat_count
    lon_cells = col_block * lon_count
    row_offset = lat_index * row_block
    col_offset = lon_index * col_block
    ghost_count = ghost_slots.shape[1]
    order_row = ghost_slots[0]
    rim_width = 1
    visc_rim = with_halo(viscous, (("lat", 0), ("lon", 1)), 2)
    visc_ext = clamp_take(visc_rim, 0, row_offset, row_block, lat_cells, 2)
    visc_ext = clamp_take(visc_ext, 1, col_offset, col_block, lon_cells, 2)
    visc_ext = jnp.pad(visc_ext, ((0, 0), (0, 0), (2, 2)), mode="edge")
    loop_coefs = face_terms(visc_ext[:, :, 1:-1], 0.5)
    loop_diag = diagonal_of(loop_coefs)
    loop_rows = row_offset + jnp.arange(-1, row_block + 1, dtype=jnp.int32)
    loop_cols = col_offset + jnp.arange(-1, col_block + 1, dtype=jnp.int32)
    loop_parity = (
        loop_rows[:, None, None]
        + loop_cols[None, :, None]
        + jnp.arange(levels, dtype=jnp.int32)[None, None, :]
    ) % 2
    loop_inside = (
        ((loop_rows >= 0) & (loop_rows < lat_cells))[:, None]
        & ((loop_cols >= 0) & (loop_cols < lon_cells))[None, :]
    )[:, :, None]
    ext_rows = row_offset + jnp.arange(-rim_width, row_block + rim_width, dtype=jnp.int32)
    ext_cols = col_offset + jnp.arange(-rim_width, col_block + rim_width, dtype=jnp.int32)
    rows_inside = (ext_rows >= 0) & (ext_rows < lat_cells)
    cols_inside = (ext_cols >= 0) & (ext_cols < lon_cells)

    def slot_lookup(ghost_ids):
        return jnp.take(order_row, jnp.clip(ghost_ids, 0, ghost_count - 1))

    rim_slots = (
        slot_lookup(ext_cols),
        slot_lookup(lon_cells + ext_cols),
        slot_lookup(2 * lon_cells + ext_rows),
        slot_lookup(2 * lon_cells + lat_cells + ext_rows),
    )

    def extend(block_field):
        return with_halo(block_field, (("lat", 1), ("lon", 2)), rim_width)

    grown_field = extend(start_field)
    source_view = grown_field[
        :, rim_width : rim_width + row_block + 1, rim_width : rim_width + col_block + 1
    ]
    rows_given = corner_rows[0, 0]
    cols_given = corner_cols[0, 0]
    weights = corner_weights[0, 0]
    corners = (
        source_view[:, rows_given, cols_given],
        source_view[:, rows_given + 1, cols_given],
        source_view[:, rows_given, cols_given + 1],
        source_view[:, rows_given + 1, cols_given + 1],
    )
    corner_slots = jnp.transpose(jnp.stack(corners, axis=0), (2, 0, 1, 3))
    weight_slots = jnp.transpose(weights)
    partner_corners, partner_weights = swapped((corner_slots, weight_slots), "patch", 0)
    blank_rims = tuple(
        (jnp.zeros((3, rim_slot.shape[0], levels), jnp.float32) for rim_slot in rim_slots)
    )
    piece_corners = lax.all_gather(partner_corners, ("lat", "lon"), axis=0, tiled=True)
    piece_weights = lax.all_gather(partner_weights, ("lat", "lon"), axis=0, tiled=True)
    count_here = piece_corners.shape[0]
    outcome = []
    for rim_index in range(4):
        local_ids = rim_slots[rim_index]
        inside = (local_ids >= 0) & (local_ids < count_here)
        safe_ids = jnp.clip(local_ids, 0, count_here - 1)
        got_corners = jnp.transpose(jnp.take(piece_corners, safe_ids, axis=0), (1, 2, 0, 3))
        got_weights = jnp.transpose(jnp.take(piece_weights, safe_ids, axis=0))
        ghost_value = bilinear(
            got_weights, (got_corners[0], got_corners[1], got_corners[2], got_corners[3])
        )
        outcome.append(jnp.where(inside[None, :, None], ghost_value, blank_rims[rim_index]))
    rim_values = tuple(outcome)
    top_valid = cols_inside & (lat_index == 0)
    bottom_valid = cols_inside & (lat_index == lat_count - 1)
    left_valid = rows_inside & (lon_index == 0)
    right_valid = rows_inside & (lon_index == lon_count - 1)
    lower_row = rim_width + row_block
    right_col = rim_width + col_block

    def with_ghosts(grown):
        grown = grown.at[:, rim_width - 1].set(
            jnp.where(top_valid[None, :, None], rim_values[0], grown[:, rim_width - 1])
        )
        grown = grown.at[:, lower_row].set(
            jnp.where(bottom_valid[None, :, None], rim_values[1], grown[:, lower_row])
        )
        grown = grown.at[:, :, rim_width - 1].set(
            jnp.where(left_valid[None, :, None], rim_values[2], grown[:, :, rim_width - 1])
        )
        grown = grown.at[:, :, right_col].set(
            jnp.where(right_valid[None, :, None], rim_values[3], grown[:, :, right_col])
        )
        return grown

    def relax_colour(grown, colour, margin):
        first_cell = rim_width - margin
        row_end = rim_width + row_block + margin
        col_end = rim_width + col_block + margin
        loop_shift = 1 - margin
        region_rows = row_block + 2 * margin
        region_cols = col_block + 2 * margin
        padded = jnp.pad(grown, ((0, 0), (0, 0), (0, 0), (1, 1)))
        region_coefs = tuple(
            (
                face_coef[
                    loop_shift : loop_shift + region_rows, loop_shift : loop_shift + region_cols
                ]
                for face_coef in loop_coefs
            )
        )
        region_diag = loop_diag[
            loop_shift : loop_shift + region_rows, loop_shift : loop_shift + region_cols
        ]
        relaxed = (force_block + neighbour_sum(padded, region_coefs)) / region_diag
        chosen = (
            loop_parity[
                loop_shift : loop_shift + region_rows, loop_shift : loop_shift + region_cols
            ]
            == colour
        ) & loop_inside[
            loop_shift : loop_shift + region_rows, loop_shift : loop_shift + region_cols
        ]
        updated = jnp.where(chosen[None], relaxed, grown[:, first_cell:row_end, first_cell:col_end])
        return grown.at[:, first_cell:row_end, first_cell:col_end].set(updated)

    def interior(grown):
        return grown[:, rim_width : rim_width + row_block, rim_width : rim_width + col_block]

    current = with_ghosts(grown_field)
    for sweep_index in range(SWEEPS):
        if sweep_index > 0:
            current = with_ghosts(extend(interior(current)))
        current = relax_colour(current, 0, 0)
        current = with_ghosts(extend(interior(current)))
        current = relax_colour(current, 1, 0)
    smoothed = interior(current)
    grown_last = with_ghosts(extend(smoothed))
    padded_last = jnp.pad(grown_last, ((0, 0), (0, 0), (0, 0), (1, 1)))
    inner_coefs = tuple((face_coef[1:-1, 1:-1] for face_coef in loop_coefs))
    inner_diag = loop_diag[1:-1, 1:-1]
    residual_field = force_block - (inner_diag * smoothed - neighbour_sum(padded_last, inner_coefs))
    half_rows = row_block // 2
    half_cols = col_block // 2
    half_levels = levels // 2
    coarse_rhs = residual_field.reshape(3, half_rows, 2, half_cols, 2, half_levels, 2).mean(
        axis=(2, 4, 6)
    )
    coarse_visc = visc_ext.reshape(half_rows + 2, 2, half_cols + 2, 2, half_levels + 2, 2).mean(
        axis=(1, 3, 5)
    )
    coarse_coefs = face_terms(coarse_visc, 0.125)
    coarse_diag = diagonal_of(coarse_coefs)
    coarse_error = RELAX * coarse_rhs / coarse_diag
    for turn_index in range(COARSE - 1):
        coarse_grown = with_halo(coarse_error, (("lat", 1), ("lon", 2)), 1)
        coarse_pad = jnp.pad(coarse_grown, ((0, 0), (0, 0), (0, 0), (1, 1)))
        coarse_error = (
            coarse_error
            + RELAX
            * (coarse_rhs - (coarse_diag * coarse_error - neighbour_sum(coarse_pad, coarse_coefs)))
            / coarse_diag
        )
    correction = jnp.repeat(jnp.repeat(jnp.repeat(coarse_error, 2, axis=1), 2, axis=2), 2, axis=3)
    new_field = smoothed + correction
    return (new_field[None], residual_field[None])


def solution(mesh):
    placed = (
        P("patch", None, "lat", "lon", None),
        P("patch", None, "lat", "lon", None),
        P("patch", "lat", "lon", None),
        P("patch", None),
        P("patch", "lat", "lon"),
        P("patch", "lat", "lon"),
        P("patch", "lat", None, "lon"),
    )
    return jax.shard_map(
        per_device,
        mesh=mesh,
        in_specs=placed,
        out_specs=(P("patch", None, "lat", "lon", None), P("patch", None, "lat", "lon", None)),
        check_vma=False,
    )
```

profile of v0, /device:TPU:6, one launch (start us, length us, event | category | flops | bytes accessed | tf_op | source)
XLA Modules:
  0.0 1015.0 jit_solution(3838266500594718935)
XLA Ops:
  8.3 3.5 collective-permute-start.4
  13.2 4.2 collective-permute-done.5
  17.5 2.7 collective-permute-start.7
  20.9 4.5 collective-permute-done.7
  32.3 2.1 collective-permute-start.8
  35.1 3.5 collective-permute-start
  43.9 677.3 %all-gather = f32[256,3,4]{2,1,0:T(4,128)S(1)} all-gather(f32[1,3,4]{2,1,0:T(4,128)S(1)} %bitcast.274), channel_id=1, replica_groups=mesh['patch'=2,'lat'=8,'lon'=32] {'lat','lon'}, dimensions={0}, use_global_device_ids=true | all-gather | bytes 12336 | tf_op jit(solution)/shard_map/all_gather | solution.py:150
  724.7 3.6 collective-permute-start.2
  728.2 5.2 collective-permute-start.3
  733.7 2.7 collective-permute-start.6
  740.1 8.1 copy.123
  748.2 2.9 gather_fusion.11
  751.2 2.9 gather_fusion.8
  754.1 3.0 gather_fusion.17
  757.1 3.0 gather_fusion.14
  764.4 4.2 collective-permute-done.11
  768.7 4.4 collective-permute-start.12
  773.0 3.8 collective-permute-start.13
  776.9 4.1 collective-permute-done.13
  785.1 9.4 collective-permute-done.15
  794.6 1.9 collective-permute-start.16
  796.5 3.9 collective-permute-start.17
  800.5 4.0 collective-permute-done.17
  805.6 5.1 collective-permute-start.18
  812.1 4.2 collective-permute-done.19
  816.3 1.9 collective-permute-start.20
  818.3 4.1 collective-permute-start.21
  822.6 4.8 reshape.1395
  827.3 4.6 reduce_sum.19
  833.0 3.9 collective-permute-start.22
  838.4 4.2 collective-permute-done.23
  842.6 4.0 collective-permute-start.24
  848.7 5.9 collective-permute-done.25
  855.6 14.0 %reshape.1394 = f32[3,8,2,4,2,64,2]{6,5,4,3,2,1,0:T(8,128)} reshape(f32[3,16,8,128]{3,2,1,0:T(8,128)S(1)} %copy.142) | data formatting | bytes 393216 | tf_op jit(solution)/shard_map/reshape | solution.py:236
  869.6 5.5 reduce_sum.18
  875.2 3.1 collective-permute-start.26
  879.7 4.2 collective-permute-done.27
  883.9 1.9 collective-permute-start.28
  885.8 3.9 collective-permute-start.29
  889.8 3.7 collective-permute-done.29
  893.9 3.1 collective-permute-start.30
  898.3 4.2 collective-permute-done.31
  904.5 3.9 collective-permute-start.33
  908.4 3.8 collective-permute-done.33
  912.6 3.1 collective-permute-start.34
  917.0 4.2 collective-permute-done.35
  923.2 3.9 collective-permute-start.37
  927.1 3.8 collective-permute-done.37
  931.2 3.1 collective-permute-start.38
  935.7 4.2 collective-permute-done.39
  941.9 3.9 collective-permute-start.41
  945.8 3.8 collective-permute-done.41
  949.9 3.1 collective-permute-start.42
  954.4 4.2 collective-permute-done.43
  960.6 3.9 collective-permute-start.45
  964.5 3.8 collective-permute-done.45
  968.6 3.1 collective-permute-start.46
  973.1 4.2 collective-permute-done.47
  979.2 3.9 collective-permute-start.49
  983.2 3.8 collective-permute-done.49
  987.3 3.1 collective-permute-start.50
  991.8 4.2 collective-permute-done.51
  997.9 3.9 collective-permute-start.53
  1002.5 3.1 collective-permute-done.53
  (244 shorter events, 65.7 us)
Async XLA Ops:
  7.2 33.1 %copy-start = (s32[1,768]{1,0:T(1,128)S(1)}, s32[1,768]{1,0:T(1,128)}, u32[]{:S(2)}) copy-start(s32[1,768]{1,0:T(1,128)} %param.70) | copy-start | bytes 9220
  7.2 717.5 %copy-start.2 = (f32[1,16,8,128]{3,2,1,0:T(8,128)S(1)}, f32[1,16,8,128]{3,2,1,0:T(8,128)}, u32[]{:S(2)}) copy-start(f32[1,16,8,128]{3,2,1,0:T(8,128)} %param.69) | copy-start | bytes 196612
  7.2 732.9 %all-gather.3.cloned.1.call-start = ((), (), s32[]{:S(2)}) async-start(), calls=%async_computation | async-start | bytes 6316032 | tf_op jit(solution)/shard_map/all_gather | solution.py:149
  8.3 4.9 collective-permute-start.4
  11.8 5.6 collective-permute-start.5
  17.5 8.0 collective-permute-start.7
  27.9 3.1 collective-permute-start.9
  30.9 0.6 copy-start.3
  32.3 11.4 %collective-permute-start.8 = (f32[3,4]{0,1:T(4,128)S(1)}, f32[3,4]{0,1:T(4,128)S(1)}, u32[]{:S(2)}, u32[]{:S(2)}) collective-permute-start(f32[3,4]{0,1:T(4,128)S(1)} %bitcast.275), channel_id=1, source_target_pairs={{0,256},{256,0},{1,257},{257,1},{2,258},{258,2},{3,259},{259,3},{4... | collective-permute-start | bytes 152 | tf_op jit(solution)/shard_map/ppermute | solution.py:29
  35.1 689.5 %collective-permute-start = (f32[2,8,128]{2,1,0:T(8,128)S(1)}, f32[2,8,128]{2,1,0:T(8,128)S(1)}, u32[]{:S(2)}, u32[]{:S(2)}) collective-permute-start(f32[2,8,128]{2,1,0:T(8,128)S(1)} %get-tuple-element.390), channel_id=1, source_target_pairs={{0,32},{32,64},{64,96},{96,128},{128,160},{160,192},{192,224},{1,3... | collective-permute-start | bytes 24584 | tf_op jit(solution)/shard_map/ppermute | solution.py:20
  38.6 686.0 %collective-permute-start.1 = (f32[2,8,128]{2,1,0:T(8,128)S(1)}, f32[2,8,128]{2,1,0:T(8,128)S(1)}, u32[]{:S(2)}, u32[]{:S(2)}) collective-permute-start(f32[2,8,128]{2,1,0:T(8,128)S(1)} %get-tuple-element.391), channel_id=1, source_target_pairs={{32,0},{64,32},{96,64},{128,96},{160,128},{192,160},{224,192},{33,... | collective-permute-start | bytes 24584 | tf_op jit(solution)/shard_map/ppermute | solution.py:21
  724.7 11.8 %collective-permute-start.2 = (f32[20,2,128]{2,1,0:T(2,128)S(1)}, f32[20,2,128]{2,1,0:T(2,128)S(1)}, u32[]{:S(2)}, u32[]{:S(2)}) collective-permute-start(f32[20,2,128]{2,1,0:T(2,128)S(1)} %get-tuple-element.388), channel_id=1, source_target_pairs={{0,1},{1,2},{2,3},{3,4},{4,5},{5,6},{6,7},{7,8},{8,9},{9,10},{10,1... | collective-permute-start | bytes 61448 | tf_op jit(solution)/shard_map/ppermute | solution.py:20
  728.2 8.2 collective-permute-start.3
  733.7 6.3 collective-permute-start.6
  740.1 21.0 %copy-start.1 = (f32[1,3,16,8,128]{4,3,2,1,0:T(8,128)S(1)}, f32[1,3,16,8,128]{4,3,2,1,0:T(8,128)}, u32[]{:S(2)}) copy-start(f32[1,3,16,8,128]{4,3,2,1,0:T(8,128)} %param.68) | copy-start | bytes 589828
  761.7 2.7 collective-permute-start.10
  763.0 5.6 collective-permute-start.11
  768.7 8.2 collective-permute-start.12
  773.0 8.0 collective-permute-start.13
  782.1 3.1 collective-permute-start.14
  783.7 10.9 %collective-permute-start.15 = (f32[3,1,8,128]{3,0,2,1:T(4,128)S(1)}, f32[3,1,8,128]{3,0,2,1:T(4,128)S(1)}, u32[]{:S(2)}, u32[]{:S(2)}) collective-permute-start(f32[3,1,8,128]{3,0,2,1:T(4,128)S(1)} %get-tuple-element.368), channel_id=1, source_target_pairs={{32,0},{64,32},{96,64},{128,96},{160,128},{192,160},{224,192},{33,... | collective-permute-start | bytes 36872 | tf_op jit(solution)/shard_map/ppermute | solution.py:21
  794.6 5.9 collective-permute-start.16
  796.5 8.0 collective-permute-start.17
  805.6 6.6 collective-permute-start.18
  810.7 5.6 collective-permute-start.19
  816.3 15.6 %collective-permute-start.20 = (f32[3,18,1,128]{3,0,2,1:T(4,128)S(1)}, f32[3,18,1,128]{3,0,2,1:T(4,128)S(1)}, u32[]{:S(2)}, u32[]{:S(2)}) collective-permute-start(f32[3,18,1,128]{3,0,2,1:T(4,128)S(1)} %get-tuple-element.355), channel_id=1, source_target_pairs={{0,1},{1,2},{2,3},{3,4},{4,5},{5,6},{6,7},{7,8},{8,9},{9,10},{10,1... | collective-permute-start | bytes 82952 | tf_op jit(solution)/shard_map/ppermute | solution.py:20
  818.3 13.7 %collective-permute-start.21 = (f32[3,18,1,128]{3,0,2,1:T(4,128)S(1)}, f32[3,18,1,128]{3,0,2,1:T(4,128)S(1)}, u32[]{:S(2)}, u32[]{:S(2)}) collective-permute-start(f32[3,18,1,128]{3,0,2,1:T(4,128)S(1)} %get-tuple-element.356), channel_id=1, source_target_pairs={{1,0},{2,1},{3,2},{4,3},{5,4},{6,5},{7,6},{8,7},{9,8},{10,9},{11,1... | collective-permute-start | bytes 82952 | tf_op jit(solution)/shard_map/ppermute | solution.py:21
  833.0 5.4 collective-permute-start.22
  837.0 5.6 collective-permute-start.23
  842.6 6.1 collective-permute-start.24
  846.7 8.0 collective-permute-start.25
  875.2 4.5 collective-permute-start.26
  878.3 5.5 collective-permute-start.27
  883.9 5.9 collective-permute-start.28
  885.8 7.7 collective-permute-start.29
  893.9 4.5 collective-permute-start.30
  897.0 5.5 collective-permute-start.31
  902.6 5.9 collective-permute-start.32
  904.5 7.7 collective-permute-start.33
  912.6 4.5 collective-permute-start.34
  915.7 5.5 collective-permute-start.35
  921.3 5.9 collective-permute-start.36
  923.2 7.7 collective-permute-start.37
  931.2 4.5 collective-permute-start.38
  934.4 5.5 collective-permute-start.39
  939.9 5.9 collective-permute-start.40
  941.9 7.7 collective-permute-start.41
  949.9 4.5 collective-permute-start.42
  953.1 5.5 collective-permute-start.43
  958.6 5.9 collective-permute-start.44
  960.6 7.7 collective-permute-start.45
  968.6 4.5 collective-permute-start.46
  971.8 5.5 collective-permute-start.47
  977.3 5.9 collective-permute-start.48
  979.2 7.7 collective-permute-start.49
  987.3 4.5 collective-permute-start.50
  990.4 5.5 collective-permute-start.51
  996.0 6.6 collective-permute-start.52
  997.9 7.7 collective-permute-start.53
Sparse Core Ops, SparseCore 0:
  31.7 133.1 all-gather.2
where the time goes:
time: 1020 us
  blocking collectives  677 us (66%)
  starting transfers between devices  143 us (14%)
  waiting for transfers between devices  103 us (10%)
  local copies, waits for them, and re-layouts  55 us (5%)
  other arithmetic  21 us (2%)
  between operations  15.5 us (2%)
    all_gather x1, blocking collectives, per_device(): lax.all_gather(partner_weights, ('lat', 'lon'), axis=0, tiled=True)  677 us
    ppermute x26, waiting for transfers between devices, with_halo(): after = lax.ppermute(first, axis, down)  100 us
    ppermute x26, starting transfers between devices, with_halo(): before = lax.ppermute(last, axis, up)  72.8 us
    ppermute x26, starting transfers between devices, with_halo(): after = lax.ppermute(first, axis, down)  66 us
  transfers between devices with their start and end apart: 55, of which 30 were waited for; matrix products, arithmetic and copies ran while one was open for 2% of the time, Pallas kernels for 0%

commit v1 on v0

v1 whole, which is shorter than its diff:
```python
import jax
import jax.numpy as jnp
from jax import lax
from jax.experimental import pallas as pl
from jax.experimental.pallas import tpu as pltpu
from jax.sharding import PartitionSpec as P

AXES = ("patch", "lat", "lon")
RELAX = 0.8
COARSE = 8
PAD = 6
VMEM = pl.BlockSpec(memory_space=pltpu.VMEM)
SMEM = pl.BlockSpec(memory_space=pltpu.SMEM)


def shifted(value, by_lat, by_lon):
    patches, lats, lons = (lax.axis_size(axis) for axis in AXES)
    pairs = []
    for p in range(patches):
        for a in range(lats):
            for b in range(lons):
                a2, b2 = a + by_lat, b + by_lon
                if 0 <= a2 < lats and 0 <= b2 < lons:
                    pairs.append(((p * lats + a) * lons + b, (p * lats + a2) * lons + b2))
    return lax.ppermute(value, AXES, pairs)


def lanes_of(shape):
    return lax.broadcasted_iota(jnp.int32, shape, len(shape) - 1)


def rows_of(shape):
    return lax.broadcasted_iota(jnp.int32, shape, len(shape) - 2)


def roll(value, by, axis):
    return pltpu.roll(value, by % value.shape[axis], axis)


def lane_partner(value, odd_lane):
    return jnp.where(odd_lane, roll(value, 1, 1), roll(value, -1, 1))


def row_partner(value, odd_row):
    return jnp.where(odd_row, roll(value, 1, 0), roll(value, -1, 0))


def interp_kernel(rows_ref, cols_ref, weights_ref, v_ref, right_ref, below_ref, out_ref, pad_ref):
    rows = v_ref.shape[1]
    pad_ref[:, :rows, 0:8] = v_ref[...]
    pad_ref[:, :rows, 8:16] = right_ref[...]
    pad_ref[:, rows] = below_ref[:, 0, 8:24]
    for slot in range(3):
        row, col = rows_ref[slot], cols_ref[slot]
        for comp in range(3):
            total = weights_ref[0, slot] * pad_ref[comp, row, pl.ds(col, 1), :]
            total = total + weights_ref[1, slot] * pad_ref[comp, row + 1, pl.ds(col, 1), :]
            total = total + weights_ref[2, slot] * pad_ref[comp, row, pl.ds(col + 1, 1), :]
            total = total + weights_ref[3, slot] * pad_ref[comp, row + 1, pl.ds(col + 1, 1), :]
            out_ref[pl.ds(slot * 3 + comp, 1), :] = total


def smooth_kernel(
    place_ref, ghost_ref, v_ref, f_ref, mu_ref, left_ref, right_ref, above_ref, below_ref, slot_ref,
    res_ref, smooth_ref, message_ref,
    V, F, MU, CN, CW, CE, CD, CU, DG, INV,
):
    lat, lon = place_ref[0], place_ref[1]
    last_lat, last_lon = place_ref[2], place_ref[3]
    wide = (24, 128)
    lane, row = lanes_of(wide), rows_of(wide)
    odd_lane, odd_row = (lane & 1) == 1, (row & 1) == 1
    own = slice(PAD, PAD + 16)

    for comp in range(3):
        V[comp, own, 0:8] = left_ref[comp]
        V[comp, own, 8:16] = v_ref[comp]
        V[comp, own, 16:24] = right_ref[comp]
        V[comp, 1:6] = above_ref[comp]
        V[comp, 22:27] = below_ref[comp]
        F[comp, own, 0:8] = left_ref[3 + comp]
        F[comp, own, 8:16] = f_ref[comp]
        F[comp, own, 16:24] = right_ref[3 + comp]
        F[comp, 1:6] = above_ref[3 + comp]
        F[comp, 22:27] = below_ref[3 + comp]
    MU[own, 0:8] = left_ref[6]
    MU[own, 8:16] = mu_ref[...]
    MU[own, 16:24] = right_ref[6]
    MU[1:6] = above_ref[6]
    MU[22:27] = below_ref[6]

    @pl.when(lat == 0)
    def _():
        MU[4] = MU[6]
        MU[5] = MU[6]
        for col in range(-4, 12):
            base = ghost_ref[jnp.clip(lon * 8 + col, 0, (last_lon + 1) * 8 - 1)]
            for comp in range(3):
                V[comp, 5, 8 + col : 9 + col] = slot_ref[base + comp]

    @pl.when(lat == last_lat)
    def _():
        MU[22] = MU[21]
        MU[23] = MU[21]
        for col in range(-4, 12):
            base = ghost_ref[(last_lon + 1) * 8 + jnp.clip(lon * 8 + col, 0, (last_lon + 1) * 8 - 1)]
            for comp in range(3):
                V[comp, 22, 8 + col : 9 + col] = slot_ref[base + comp]

    side_start = 2 * (last_lon + 1) * 8
    side_rows = (last_lat + 1) * 16

    @pl.when(lon == 0)
    def _():
        for i in range(1, 27):
            MU[i, 0:8] = jnp.broadcast_to(MU[i, 8:9], (8, 128))
        for r in range(-4, 20):
            base = ghost_ref[side_start + jnp.clip(lat * 16 + r, 0, side_rows - 1)]
            for comp in range(3):
                V[comp, r + PAD, 7:8] = slot_ref[base + comp]

    @pl.when(lon == last_lon)
    def _():
        for i in range(1, 27):
            MU[i, 16:24] = jnp.broadcast_to(MU[i, 15:16], (8, 128))
        for r in range(-4, 20):
            base = ghost_ref[side_start + side_rows + jnp.clip(lat * 16 + r, 0, side_rows - 1)]
            for comp in range(3):
                V[comp, r + PAD, 16:17] = slot_ref[base + comp]

    def coefficients(i, carry):
        mid = MU[i]
        north = 0.5 * (mid + MU[i - 1])
        south = 0.5 * (mid + MU[i + 1])
        west = 0.5 * (mid + roll(mid, 1, 0))
        east = 0.5 * (mid + roll(mid, -1, 0))
        down = 0.5 * (mid + jnp.where(lane == 0, mid, roll(mid, 1, 1)))
        up = 0.5 * (mid + jnp.where(lane == 127, mid, roll(mid, -1, 1)))
        total = north + south + west + east + down + up
        CN[i] = north
        CN[i + 1] = south
        CW[i] = west
        CE[i] = east
        CD[i] = jnp.where(lane == 0, 0.0, down)
        CU[i] = jnp.where(lane == 127, 0.0, up)
        DG[i] = total
        INV[i] = 1.0 / total
        return carry

    lax.fori_loop(2, 26, coefficients, 0)

    inside = ((row >= 8) | (lon > 0)) & ((row < 16) | (lon < last_lon))
    parity = (row + lane) & 1
    masks = ((parity == 0) & inside, (parity == 1) & inside)

    def weighted(comp, i, here):
        total = F[comp, i] + CN[i] * V[comp, i - 1]
        total = total + CN[i + 1] * V[comp, i + 1]
        total = total + CW[i] * roll(here, 1, 0)
        total = total + CE[i] * roll(here, -1, 0)
        total = total + CD[i] * roll(here, 1, 1)
        return total + CU[i] * roll(here, -1, 1)

    def relax(colour, pairs):
        def step(pair, carry):
            for k in range(2):
                i = 2 * pair + PAD + k
                for comp in range(3):
                    here = V[comp, i]
                    fresh = weighted(comp, i, here) * INV[i]
                    V[comp, i] = jnp.where(masks[(colour + k) % 2], fresh, here)
            return carry

        first = jnp.where(lat == 0, 0, -pairs)
        last = jnp.where(lat == last_lat, 8, 8 + pairs)
        lax.fori_loop(first, last, step, 0)

    relax(0, 2)
    relax(1, 2)
    relax(0, 1)
    relax(1, 1)

    def coarse_visc(i):
        both = MU[i] + MU[i + 1]
        flat = 0.25 * (both + row_partner(both, odd_row))
        return flat, 0.5 * (flat + lane_partner(flat, odd_lane))

    tile = (8, 128)
    lane8, row8 = lanes_of(tile), rows_of(tile)
    odd_lane8, odd_row8 = (lane8 & 1) == 1, (row8 & 1) == 1

    def packed(parts):
        low = jnp.where(odd_lane8, parts[1], parts[0])
        high = jnp.where(odd_lane8, parts[3], parts[2])
        return jnp.where(odd_row8, high, low)

    layers = [coarse_visc(PAD + 2 * k) for k in (-1, 0)]
    inverse = []
    for k in range(8):
        layers.append(coarse_visc(PAD + 2 * k + 2))
        before, (flat, visc), after = layers[k][1], layers[k + 1], layers[k + 2][1]
        edge_down = jnp.where(lane == 0, flat, roll(flat, 1, 1))
        edge_up = jnp.where(lane == 127, flat, roll(flat, -1, 1))
        total = 6.0 * visc + before + after + roll(visc, 2, 0) + roll(visc, -2, 0)
        total = total + jnp.where(lane < 2, edge_down, roll(visc, 2, 1))
        total = total + jnp.where(lane >= 126, edge_up, roll(visc, -2, 1))
        over = RELAX / (0.125 * total[8:16])
        inverse.append(over)
        parts = []
        for comp in range(3):
            rhs = jnp.zeros(tile, jnp.float32)
            for r in (2 * k, 2 * k + 1):
                i = r + PAD
                here = V[comp, i]
                left = (weighted(comp, i, here) - DG[i] * here)[8:16]
                res_ref[comp, r] = left
                rhs = rhs + left
            rhs = rhs + lane_partner(rhs, odd_lane8)
            rhs = rhs + row_partner(rhs, odd_row8)
            parts.append(0.125 * rhs * over)
        message_ref[k] = packed(parts + [visc[8:16]])
        if k % 4 == 3:
            message_ref[8 + k // 4] = packed(inverse[k - 3 : k + 1])
    for comp in range(3):
        smooth_ref[comp] = V[comp, own, 8:16]


def coarse_kernel(
    mid_ref, above_ref, below_ref, smooth_ref, out_ref, Q, CV, DV, E, AN, AS, AW, AE, AD, AU
):
    wide = (40, 128)
    lane, row = lanes_of(wide), rows_of(wide)
    odd_lane, odd_row = (lane & 1) == 1, (row & 1) == 1

    def spread(value, part, odd_l, odd_r):
        keep = odd_l if part % 2 else ~odd_l
        value = jnp.where(keep, value, roll(value, -1 if part % 2 else 1, 1))
        keep = odd_r if part // 2 else ~odd_r
        return jnp.where(keep, value, roll(value, -1 if part // 2 else 1, 0))

    for n in range(22):
        ref, t = (above_ref, n + 1) if n < 7 else (mid_ref, n - 7) if n < 15 else (below_ref, n - 15)
        value = ref[t]
        Q[n] = value
        CV[n] = spread(value, 3, odd_lane, odd_row)
        if 1 <= n <= 20:
            DV[n] = 0.125 * spread(ref[8 + t // 4], t % 4, odd_lane, odd_row)

    def coefficients(n, carry):
        visc, over = CV[n], DV[n]
        AN[n] = over * (visc + CV[n - 1])
        AS[n] = over * (visc + CV[n + 1])
        AW[n] = over * (visc + roll(visc, 2, 0))
        AE[n] = over * (visc + roll(visc, -2, 0))
        AD[n] = jnp.where(lane < 2, 0.0, over * (visc + roll(visc, 2, 1)))
        AU[n] = jnp.where(lane >= 126, 0.0, over * (visc + roll(visc, -2, 1)))
        return carry

    lax.fori_loop(1, 21, coefficients, 0)

    for turn in range(1, COARSE):
        old = Q if turn == 1 else E.at[turn % 2]
        new = E.at[(turn + 1) % 2]

        def step(n, carry, old=old, new=new):
            here = old[n]
            total = Q[n] + (1.0 - RELAX) * here
            total = total + AN[n] * old[n - 1]
            total = total + AS[n] * old[n + 1]
            total = total + AW[n] * roll(here, 2, 0)
            total = total + AE[n] * roll(here, -2, 0)
            total = total + AD[n] * roll(here, 2, 1)
            new[n] = total + AU[n] * roll(here, -2, 1)
            return carry

        lax.fori_loop(turn, 22 - turn, step, 0)

    final = E.at[COARSE % 2]
    tile = (8, 128)
    lane8, row8 = lanes_of(tile), rows_of(tile)
    odd_lane8, odd_row8 = (lane8 & 1) == 1, (row8 & 1) == 1
    for k in range(8):
        value = final[7 + k, 16:24]
        for comp in range(3):
            error = spread(value, comp, odd_lane8, odd_row8)
            for r in (2 * k, 2 * k + 1):
                out_ref[comp, r] = smooth_ref[comp, r] + error


def whole(shape):
    return pl.BlockSpec(shape, lambda step: (0,) * len(shape))


def per_device(velocity, forcing, viscosity, ghost_slots, corner_rows, corner_cols, corner_weights):
    v, f, mu = velocity[0], forcing[0], viscosity[0]
    lats, lons = lax.axis_size("lat"), lax.axis_size("lon")
    params = pltpu.CompilerParams(vmem_limit_bytes=32 * 2**20)
    f32 = jnp.float32
    place = jnp.stack(
        [lax.axis_index("lat"), lax.axis_index("lon"), jnp.int32(lats - 1), jnp.int32(lons - 1)]
    ).astype(jnp.int32)
    slots = ghost_slots[0]
    ghost_base = ((slots // 3) % lons) * (9 * lats) + ((slots // (3 * lons)) * 3 + slots % 3) * 3

    own = jnp.concatenate([v, f, mu[None]], axis=0)
    left = shifted(own, 0, 1)
    right = shifted(own, 0, -1)
    ext_top = jnp.concatenate([left[:, :5], own[:, :5], right[:, :5]], axis=2)
    ext_low = jnp.concatenate([left[:, 11:], own[:, 11:], right[:, 11:]], axis=2)
    below = shifted(ext_top, -1, 0)
    above = shifted(ext_low, 1, 0)

    values = pl.pallas_call(
        interp_kernel,
        grid=(1,),
        out_shape=jax.ShapeDtypeStruct((9, 128), f32),
        in_specs=[SMEM, SMEM, SMEM, VMEM, whole((3, 16, 8, 128)), whole((3, 1, 24, 128))],
        out_specs=VMEM,
        scratch_shapes=[pltpu.VMEM((3, 17, 16, 128), f32)],
        compiler_params=params,
        name="interp",
    )(corner_rows[0, 0], corner_cols[0, 0], corner_weights[0, 0], v, right, below)

    spread = jnp.broadcast_to(values[None], (2 * lats, 9, 128))
    column = lax.all_to_all(spread, ("patch", "lat"), 0, 0, tiled=True)
    column = column.reshape(2, lats * 9, 128)
    column = jnp.where(lax.axis_index("patch") == 0, column[1], column[0])
    everything = lax.all_to_all(
        jnp.broadcast_to(column[None], (lons, lats * 9, 128)), "lon", 0, 0, tiled=True
    )
    everything = everything.reshape(lons * lats * 9, 1, 128)

    block = jax.ShapeDtypeStruct((3, 16, 8, 128), f32)
    field = pltpu.VMEM((3, 28, 24, 128), f32)
    plane = pltpu.VMEM((28, 24, 128), f32)
    residual, smoothed, message = pl.pallas_call(
        smooth_kernel,
        out_shape=(block, block, jax.ShapeDtypeStruct((10, 8, 128), f32)),
        in_specs=[SMEM, SMEM] + [VMEM] * 8,
        out_specs=(VMEM, VMEM, VMEM),
        scratch_shapes=[field, field] + [plane] * 8,
        compiler_params=params,
        name="smooth",
    )(place, ghost_base, v, f, mu, left, right, above, below, everything)

    tiles = [
        shifted(message, 0, 2),
        shifted(message, 0, 1),
        message,
        shifted(message, 0, -1),
        shifted(message, 0, -2),
    ]
    band = jnp.concatenate(tiles, axis=1)
    band_below = shifted(band, -1, 0)
    band_above = shifted(band, 1, 0)
    coarse = pltpu.VMEM((22, 40, 128), f32)
    new = pl.pallas_call(
        coarse_kernel,
        out_shape=block,
        in_specs=[VMEM] * 4,
        out_specs=VMEM,
        scratch_shapes=[coarse, coarse, coarse, pltpu.VMEM((2, 22, 40, 128), f32)] + [coarse] * 6,
        compiler_params=params,
        name="coarse",
    )(band, band_above, band_below, smoothed)
    return new[None], residual[None]


def solution(mesh):
    placed = (
        P("patch", None, "lat", "lon", None),
        P("patch", None, "lat", "lon", None),
        P("patch", "lat", "lon", None),
        P("patch", None),
        P("patch", "lat", "lon"),
        P("patch", "lat", "lon"),
        P("patch", "lat", None, "lon"),
    )
    return jax.shard_map(
        per_device,
        mesh=mesh,
        in_specs=placed,
        out_specs=(P("patch", None, "lat", "lon", None), P("patch", None, "lat", "lon", None)),
        check_vma=False,
    )
```

time: 1020 us -> 145 us (0.14)
  blocking collectives: 677 us -> 0 us
  starting transfers between devices: 143 us -> 53.3 us
  local copies, waits for them, and re-layouts: 55 us -> 1.99 us
  waiting for transfers between devices: 103 us -> 66.2 us
  Pallas kernels: 0 us -> 19.8 us
  other arithmetic: 21 us -> 1.35 us
  between operations: 15.5 us -> 0.89 us
    all_gather x1 -> x0, blocking collectives: 677 us -> none  [per_device(): lax.all_gather(partner_weights, ('lat', 'lon'), axis=0, tiled=True)]
    ppermute x54 -> x10, starting transfers between devices: 143 us -> 31.5 us  [shifted(): return lax.ppermute(value, AXES, pairs)]
    ppermute x54 -> x10, waiting for transfers between devices: 103 us -> 39 us  [shifted(): return lax.ppermute(value, AXES, pairs)]
    all_to_all x0 -> x2, waiting for transfers between devices: none -> 27.1 us  [the longest x1 18.6 us: per_device(): lax.all_to_all(jnp.broadcast_to(column[None], (lons, lats * 9, 128)), 'lo...]
    all_to_all x0 -> x2, starting transfers between devices: none -> 21.8 us  [the longest x1 14.6 us: per_device(): lax.all_to_all(jnp.broadcast_to(column[None], (lons, lats * 9, 128)), 'lo...]
    gather x18 -> x0, local copies, waits for them, and re-layouts: 20.1 us -> none  [the longest x4 11.8 us: per_device(): jnp.take(piece_corners, safe_ids, axis=0)]
    reshape x6 -> x0, local copies, waits for them, and re-layouts: 19.9 us -> none  [the longest x1 14 us: per_device(): residual_field.reshape(3, half_rows, 2, half_cols, 2, half_levels, 2)]
    pallas_call x0 -> x3, Pallas kernels: none -> 19.8 us  [the longest x1 10.7 us: per_device(): pl.pallas_call(coarse_kernel, out_shape=block, in_specs=[VMEM] * 4, out_s...]
  transfers between devices with their start and end apart: 55 -> 12, of which waited for: 30 -> 10; matrix products, arithmetic and copies ran while one was open for 2% -> 0% of each run, Pallas kernels for 0% -> 0%
where the time goes in v1:
time: 145 us; the launch traced here: 144 us
  waiting for transfers between devices  66.2 us (46%)
  starting transfers between devices  53.3 us (37%)
  Pallas kernels  19.8 us (14%)
  local copies, waits for them, and re-layouts  1.99 us (1%)
    ppermute x10, waiting for transfers between devices, shifted(): return lax.ppermute(value, AXES, pairs)  39 us
    ppermute x10, starting transfers between devices, shifted(): return lax.ppermute(value, AXES, pairs)  31.5 us
    all_to_all x1, waiting for transfers between devices, per_device(): lax.all_to_all(jnp.broadcast_to(column[None], (lons, lats * 9, 128)), 'lo...  18.6 us
    all_to_all x1, starting transfers between devices, per_device(): lax.all_to_all(jnp.broadcast_to(column[None], (lons, lats * 9, 128)), 'lo...  14.6 us
    pallas_call x1, Pallas kernels, per_device(): pl.pallas_call(coarse_kernel, out_shape=block, in_specs=[VMEM] * 4, out_s...  10.7 us
    all_to_all x1, waiting for transfers between devices, per_device(): column = lax.all_to_all(spread, ('patch', 'lat'), 0, 0, tiled=True)  8.54 us
    pallas_call x1, Pallas kernels, per_device(): pl.pallas_call(smooth_kernel, out_shape=(block, block, jax.ShapeDtypeStru...  8.45 us
    all_to_all x1, starting transfers between devices, per_device(): column = lax.all_to_all(spread, ('patch', 'lat'), 0, 0, tiled=True)  7.21 us
  transfers between devices with their start and end apart: 12, of which 10 were waited for; matrix products, arithmetic and copies ran while one was open for 0% of the time, Pallas kernels for 0%

profile of v1, /device:TPU:6, one launch (start us, length us, event | category | flops | bytes accessed | tf_op | source)
XLA Modules:
  0.0 143.5 jit_solution(15193652927695116963)
XLA Ops:
  0.6 1.1 pad_maximum_fusion
  1.7 0.0 copy-start.6
  1.7 0.0 copy-start
  1.7 0.0 copy-start.3
  1.8 0.0 copy-start.4
  1.8 2.9 %collective-permute-start.1 = (f32[7,16,8,128]{3,2,1,0:T(8,128)S(1)}, f32[7,16,8,128]{3,2,1,0:T(8,128)S(1)}, u32[]{:S(2)}, u32[]{:S(2)}) collective-permute-start(f32[7,16,8,128]{3,2,1,0:T(8,128)S(1)} %pad_maximum_fusion), channel_id=1, source_target_pairs={{1,0},{2,1},{3,2},{4,3},{5,4},{6,5},{7,6},{8,7},{9,8},{10,9},{11,1... | collective-permute-start | bytes 1376264 | tf_op jit(solution)/shard_map/ppermute | solution.py:25
  4.6 5.2 %collective-permute-start = (f32[7,16,8,128]{3,2,1,0:T(8,128)S(1)}, f32[7,16,8,128]{3,2,1,0:T(8,128)S(1)}, u32[]{:S(2)}, u32[]{:S(2)}) collective-permute-start(f32[7,16,8,128]{3,2,1,0:T(8,128)S(1)} %pad_maximum_fusion), channel_id=1, source_target_pairs={{0,1},{1,2},{2,3},{3,4},{4,5},{5,6},{6,7},{7,8},{8,9},{9,10},{10,1... | collective-permute-start | bytes 1376264 | tf_op jit(solution)/shard_map/ppermute | solution.py:25
  9.9 8.3 %collective-permute-done.1.right_ref = f32[7,16,8,128]{3,2,1,0:T(8,128)S(1)} collective-permute-done((f32[7,16,8,128]{3,2,1,0:T(8,128)S(1)}, f32[7,16,8,128]{3,2,1,0:T(8,128)S(1)}, u32[]{:S(2)}, u32[]{:S(2)}) %collective-permute-start.1) | collective-permute-done | bytes 458784 | tf_op jit(solution)/shard_map/ppermute | solution.py:25
  18.2 1.2 collective-permute-done.left_ref
  19.4 1.3 collective-permute-start.3
  20.7 0.0 copy-done.6
  20.7 0.1 copy.10
  20.8 11.0 %collective-permute-done.3.below_ref = f32[7,5,24,128]{3,2,1,0:T(8,128)S(1)} collective-permute-done((f32[7,5,24,128]{3,2,1,0:T(8,128)S(1)}, f32[7,5,24,128]{3,2,1,0:T(8,128)S(1)}, u32[]{:S(2)}, u32[]{:S(2)}) %collective-permute-start.3) | collective-permute-done | bytes 430112 | tf_op jit(solution)/shard_map/ppermute | solution.py:25
  31.8 0.0 copy-done
  31.8 0.0 copy-done.3
  31.8 0.0 copy-done.4
  31.8 0.6 interp.1
  32.5 0.7 broadcast_in_dim.8
  33.1 7.2 %all-to-all-start = ((f32[16,9,128]{2,1,0:T(8,128)}), f32[16,9,128]{2,1,0:T(8,128)S(1)}, u32[]{:S(2)}, u32[]{:S(2)}) async-start(f32[16,9,128]{2,1,0:T(8,128)} %broadcast_in_dim.8), calls=%async_computation | async-start | bytes 262144 | tf_op jit(solution)/shard_map/all_to_all | solution.py:325
  40.3 8.5 %all-to-all-done = f32[16,9,128]{2,1,0:T(8,128)S(1)} async-done(((f32[16,9,128]{2,1,0:T(8,128)}), f32[16,9,128]{2,1,0:T(8,128)S(1)}, u32[]{:S(2)}, u32[]{:S(2)}) %all-to-all-start) | async-done | bytes 73760 | tf_op jit(solution)/shard_map/all_to_all | solution.py:325
  48.9 1.1 broadcast_in_dim.9
  50.0 0.0 copy-start.5
  50.0 0.0 copy-start.1
  50.0 0.0 copy-start.2
  50.0 14.6 %all-to-all-start.1 = ((f32[32,72,128]{2,1,0:T(8,128)}), f32[32,72,128]{2,1,0:T(8,128)S(1)}, u32[]{:S(2)}, u32[]{:S(2)}) async-start(f32[32,72,128]{2,1,0:T(8,128)} %broadcast_in_dim.9), calls=%async_computation.1 | async-start | bytes 2359296 | tf_op jit(solution)/shard_map/all_to_all | solution.py:328
  64.6 0.0 copy-done.5
  64.7 3.5 %collective-permute-start.2 = (f32[7,5,24,128]{3,2,1,0:T(8,128)S(1)}, f32[7,5,24,128]{3,2,1,0:T(8,128)S(1)}, u32[]{:S(2)}, u32[]{:S(2)}) collective-permute-start(f32[7,5,24,128]{3,2,1,0:T(8,128)S(1)} %pad_maximum_fusion.1), channel_id=1, source_target_pairs={{0,32},{1,33},{2,34},{3,35},{4,36},{5,37},{6,38},{7,39},{8,40},{9,... | collective-permute-start | bytes 1290248 | tf_op jit(solution)/shard_map/ppermute | solution.py:25
  68.2 0.1 pad_add_fusion.place_ref
  68.3 7.9 %collective-permute-done.2.above_ref = f32[7,5,24,128]{3,2,1,0:T(8,128)S(1)} collective-permute-done((f32[7,5,24,128]{3,2,1,0:T(8,128)S(1)}, f32[7,5,24,128]{3,2,1,0:T(8,128)S(1)}, u32[]{:S(2)}, u32[]{:S(2)}) %collective-permute-start.2) | collective-permute-done | bytes 430112 | tf_op jit(solution)/shard_map/ppermute | solution.py:25
  76.3 18.6 %all-to-all-done.1 = f32[32,72,128]{2,1,0:T(8,128)S(1)} async-done(((f32[32,72,128]{2,1,0:T(8,128)}), f32[32,72,128]{2,1,0:T(8,128)S(1)}, u32[]{:S(2)}, u32[]{:S(2)}) %all-to-all-start.1) | async-done | bytes 1179680 | tf_op jit(solution)/shard_map/all_to_all | solution.py:328
  94.9 0.0 copy-done.1
  94.9 0.0 copy-done.2
  94.9 8.5 %smooth.1 = (f32[3,16,8,128]{3,2,1,0:T(8,128)}, f32[3,16,8,128]{3,2,1,0:T(8,128)S(1)}, f32[10,8,128]{2,1,0:T(8,128)S(1)}) custom-call(s32[4]{0:T(128)S(1)} %pad_add_fusion.place_ref, s32[768]{0:T(1024)S(1)} %fusion.2.ghost_ref, f32[3,16,8,128]{3,2,1,0:T(8,128)S(1)} %bitcast.14, f32[3,16,8,128]{3,2,1,0:T(8,128)S(1)} %bitcast.16, f32[16,8,128]{2,1,0:T(8,128)S(1)} %bitcast.17, ...), custom_call_target="tpu_custom_call" | custom-call | tf_op jit(solution)/shard_map/smooth/pallas_call | solution.py:336
  103.3 3.4 %collective-permute-start.4 = (f32[10,8,128]{2,1,0:T(8,128)S(1)}, f32[10,8,128]{2,1,0:T(8,128)S(1)}, u32[]{:S(2)}, u32[]{:S(2)}) collective-permute-start(f32[10,8,128]{2,1,0:T(8,128)S(1)} %get-tuple-element.5), channel_id=1, source_target_pairs={{0,2},{1,3},{2,4},{3,5},{4,6},{5,7},{6,8},{7,9},{8,10},{9,11},{10,... | collective-permute-start | bytes 122888 | tf_op jit(solution)/shard_map/ppermute | solution.py:25
  106.7 4.0 %collective-permute-start.5 = (f32[10,8,128]{2,1,0:T(8,128)S(1)}, f32[10,8,128]{2,1,0:T(8,128)S(1)}, u32[]{:S(2)}, u32[]{:S(2)}) collective-permute-start(f32[10,8,128]{2,1,0:T(8,128)S(1)} %get-tuple-element.5), channel_id=1, source_target_pairs={{0,1},{1,2},{2,3},{3,4},{4,5},{5,6},{6,7},{7,8},{8,9},{9,10},{10,1... | collective-permute-start | bytes 122888 | tf_op jit(solution)/shard_map/ppermute | solution.py:25
  110.7 1.9 %collective-permute-start.6 = (f32[10,8,128]{2,1,0:T(8,128)S(1)}, f32[10,8,128]{2,1,0:T(8,128)S(1)}, u32[]{:S(2)}, u32[]{:S(2)}) collective-permute-start(f32[10,8,128]{2,1,0:T(8,128)S(1)} %get-tuple-element.5), channel_id=1, source_target_pairs={{1,0},{2,1},{3,2},{4,3},{5,4},{6,5},{7,6},{8,7},{9,8},{10,9},{11,1... | collective-permute-start | bytes 122888 | tf_op jit(solution)/shard_map/ppermute | solution.py:25
  112.6 3.9 %collective-permute-start.7 = (f32[10,8,128]{2,1,0:T(8,128)S(1)}, f32[10,8,128]{2,1,0:T(8,128)S(1)}, u32[]{:S(2)}, u32[]{:S(2)}) collective-permute-start(f32[10,8,128]{2,1,0:T(8,128)S(1)} %get-tuple-element.5), channel_id=1, source_target_pairs={{2,0},{3,1},{4,2},{5,3},{6,4},{7,5},{8,6},{9,7},{10,8},{11,9},{12,... | collective-permute-start | bytes 122888 | tf_op jit(solution)/shard_map/ppermute | solution.py:25
  116.5 0.0 collective-permute-done.4
  116.6 0.0 collective-permute-done.5
  116.6 2.1 %collective-permute-done.6 = f32[10,8,128]{2,1,0:T(8,128)S(1)} collective-permute-done((f32[10,8,128]{2,1,0:T(8,128)S(1)}, f32[10,8,128]{2,1,0:T(8,128)S(1)}, u32[]{:S(2)}, u32[]{:S(2)}) %collective-permute-start.6) | collective-permute-done | bytes 40992 | tf_op jit(solution)/shard_map/ppermute | solution.py:25
  118.7 2.2 %collective-permute-done.7 = f32[10,8,128]{2,1,0:T(8,128)S(1)} collective-permute-done((f32[10,8,128]{2,1,0:T(8,128)S(1)}, f32[10,8,128]{2,1,0:T(8,128)S(1)}, u32[]{:S(2)}, u32[]{:S(2)}) %collective-permute-start.7) | collective-permute-done | bytes 40992 | tf_op jit(solution)/shard_map/ppermute | solution.py:25
  120.9 4.2 %collective-permute-start.8 = (f32[10,40,128]{2,1,0:T(8,128)S(1)}, f32[10,40,128]{2,1,0:T(8,128)S(1)}, u32[]{:S(2)}, u32[]{:S(2)}) collective-permute-start(f32[10,40,128]{2,1,0:T(8,128)S(1)} %constant_dynamic-update-slice_fusion.mid_ref), channel_id=1, source_target_pairs={{0,32},{1,33},{2,34},{3,35},{4,36},{5,37},{6,38},{7,39},{8,40},{9,... | collective-permute-start | bytes 614408 | tf_op jit(solution)/shard_map/ppermute | solution.py:25
  125.1 1.3 collective-permute-start.9
  126.4 1.9 %collective-permute-done.8.above_ref = f32[10,40,128]{2,1,0:T(8,128)S(1)} collective-permute-done((f32[10,40,128]{2,1,0:T(8,128)S(1)}, f32[10,40,128]{2,1,0:T(8,128)S(1)}, u32[]{:S(2)}, u32[]{:S(2)}) %collective-permute-start.8) | collective-permute-done | bytes 204832 | tf_op jit(solution)/shard_map/ppermute | solution.py:25
  128.4 4.4 %collective-permute-done.9.below_ref = f32[10,40,128]{2,1,0:T(8,128)S(1)} collective-permute-done((f32[10,40,128]{2,1,0:T(8,128)S(1)}, f32[10,40,128]{2,1,0:T(8,128)S(1)}, u32[]{:S(2)}, u32[]{:S(2)}) %collective-permute-start.9) | collective-permute-done | bytes 204832 | tf_op jit(solution)/shard_map/ppermute | solution.py:25
  132.8 10.7 %coarse.1 = f32[3,16,8,128]{3,2,1,0:T(8,128)} custom-call(f32[10,40,128]{2,1,0:T(8,128)S(1)} %constant_dynamic-update-slice_fusion.mid_ref, f32[10,40,128]{2,1,0:T(8,128)S(1)} %collective-permute-done.8.above_ref, f32[10,40,128]{2,1,0:T(8,128)S(1)} %collective-permute-done.9.below_ref, f32[3,16,8,128]{3,2,1,0:T(8,128)S(1)} %get-tuple-element.6.smooth_ref), custom_call_target="tpu_custom_call" | custom-call | tf_op jit(solution)/shard_map/coarse/pallas_call | solution.py:357
  (15 shorter events, 0.3 us)
Async XLA Ops:
  1.7 19.0 %copy-start.6 = (f32[1,1,4,3]{2,1,3,0:T(1,128)S(1)}, f32[1,1,4,3]{2,1,3,0:T(1,128)}, u32[]{:S(2)}) copy-start(f32[1,1,4,3]{2,1,3,0:T(1,128)} %param.13) | copy-start | bytes 148
  1.7 30.1 %copy-start = (f32[1,3,16,8,128]{4,3,2,1,0:T(8,128)S(1)}, f32[1,3,16,8,128]{4,3,2,1,0:T(8,128)}, u32[]{:S(2)}) copy-start(f32[1,3,16,8,128]{4,3,2,1,0:T(8,128)} %param.7) | copy-start | bytes 589828
  1.7 30.1 %copy-start.3 = (s32[1,1,3]{2,1,0:T(1,128)S(1)}, s32[1,1,3]{2,1,0:T(1,128)}, u32[]{:S(2)}) copy-start(s32[1,1,3]{2,1,0:T(1,128)} %param.11) | copy-start | bytes 40
  1.8 30.1 %copy-start.4 = (s32[1,1,3]{2,1,0:T(1,128)S(1)}, s32[1,1,3]{2,1,0:T(1,128)}, u32[]{:S(2)}) copy-start(s32[1,1,3]{2,1,0:T(1,128)} %param.12) | copy-start | bytes 40
  1.8 16.4 %collective-permute-start.1 = (f32[7,16,8,128]{3,2,1,0:T(8,128)S(1)}, f32[7,16,8,128]{3,2,1,0:T(8,128)S(1)}, u32[]{:S(2)}, u32[]{:S(2)}) collective-permute-start(f32[7,16,8,128]{3,2,1,0:T(8,128)S(1)} %pad_maximum_fusion), channel_id=1, source_target_pairs={{1,0},{2,1},{3,2},{4,3},{5,4},{6,5},{7,6},{8,7},{9,8},{10,9},{11,1... | collective-permute-start | bytes 1376264 | tf_op jit(solution)/shard_map/ppermute | solution.py:25
  4.6 14.7 %collective-permute-start = (f32[7,16,8,128]{3,2,1,0:T(8,128)S(1)}, f32[7,16,8,128]{3,2,1,0:T(8,128)S(1)}, u32[]{:S(2)}, u32[]{:S(2)}) collective-permute-start(f32[7,16,8,128]{3,2,1,0:T(8,128)S(1)} %pad_maximum_fusion), channel_id=1, source_target_pairs={{0,1},{1,2},{2,3},{3,4},{4,5},{5,6},{6,7},{7,8},{8,9},{9,10},{10,1... | collective-permute-start | bytes 1376264 | tf_op jit(solution)/shard_map/ppermute | solution.py:25
  19.4 12.4 %collective-permute-start.3 = (f32[7,5,24,128]{3,2,1,0:T(8,128)S(1)}, f32[7,5,24,128]{3,2,1,0:T(8,128)S(1)}, u32[]{:S(2)}, u32[]{:S(2)}) collective-permute-start(f32[7,5,24,128]{3,2,1,0:T(8,128)S(1)} %pad_maximum_fusion.2), channel_id=1, source_target_pairs={{32,0},{33,1},{34,2},{35,3},{36,4},{37,5},{38,6},{39,7},{40,8},{41... | collective-permute-start | bytes 1290248 | tf_op jit(solution)/shard_map/ppermute | solution.py:25
  33.1 15.8 %all-to-all-start = ((f32[16,9,128]{2,1,0:T(8,128)}), f32[16,9,128]{2,1,0:T(8,128)S(1)}, u32[]{:S(2)}, u32[]{:S(2)}) async-start(f32[16,9,128]{2,1,0:T(8,128)} %broadcast_in_dim.8), calls=%async_computation | async-start | bytes 262144 | tf_op jit(solution)/shard_map/all_to_all | solution.py:325
  50.0 14.6 %copy-start.5 = (s32[1,768]{1,0:T(1,128)S(1)}, s32[1,768]{1,0:T(1,128)}, u32[]{:S(2)}) copy-start(s32[1,768]{1,0:T(1,128)} %param.10) | copy-start | bytes 9220
  50.0 44.9 %copy-start.1 = (f32[1,3,16,8,128]{4,3,2,1,0:T(8,128)S(1)}, f32[1,3,16,8,128]{4,3,2,1,0:T(8,128)}, u32[]{:S(2)}) copy-start(f32[1,3,16,8,128]{4,3,2,1,0:T(8,128)} %param.8) | copy-start | bytes 589828
  50.0 44.9 %copy-start.2 = (f32[1,16,8,128]{3,2,1,0:T(8,128)S(1)}, f32[1,16,8,128]{3,2,1,0:T(8,128)}, u32[]{:S(2)}) copy-start(f32[1,16,8,128]{3,2,1,0:T(8,128)} %param.9) | copy-start | bytes 196612
  50.0 44.9 %all-to-all-start.1 = ((f32[32,72,128]{2,1,0:T(8,128)}), f32[32,72,128]{2,1,0:T(8,128)S(1)}, u32[]{:S(2)}, u32[]{:S(2)}) async-start(f32[32,72,128]{2,1,0:T(8,128)} %broadcast_in_dim.9), calls=%async_computation.1 | async-start | bytes 2359296 | tf_op jit(solution)/shard_map/all_to_all | solution.py:328
  64.7 11.6 %collective-permute-start.2 = (f32[7,5,24,128]{3,2,1,0:T(8,128)S(1)}, f32[7,5,24,128]{3,2,1,0:T(8,128)S(1)}, u32[]{:S(2)}, u32[]{:S(2)}) collective-permute-start(f32[7,5,24,128]{3,2,1,0:T(8,128)S(1)} %pad_maximum_fusion.1), channel_id=1, source_target_pairs={{0,32},{1,33},{2,34},{3,35},{4,36},{5,37},{6,38},{7,39},{8,40},{9,... | collective-permute-start | bytes 1290248 | tf_op jit(solution)/shard_map/ppermute | solution.py:25
  103.3 13.2 %collective-permute-start.4 = (f32[10,8,128]{2,1,0:T(8,128)S(1)}, f32[10,8,128]{2,1,0:T(8,128)S(1)}, u32[]{:S(2)}, u32[]{:S(2)}) collective-permute-start(f32[10,8,128]{2,1,0:T(8,128)S(1)} %get-tuple-element.5), channel_id=1, source_target_pairs={{0,2},{1,3},{2,4},{3,5},{4,6},{5,7},{6,8},{7,9},{8,10},{9,11},{10,... | collective-permute-start | bytes 122888 | tf_op jit(solution)/shard_map/ppermute | solution.py:25
  106.7 9.8 %collective-permute-start.5 = (f32[10,8,128]{2,1,0:T(8,128)S(1)}, f32[10,8,128]{2,1,0:T(8,128)S(1)}, u32[]{:S(2)}, u32[]{:S(2)}) collective-permute-start(f32[10,8,128]{2,1,0:T(8,128)S(1)} %get-tuple-element.5), channel_id=1, source_target_pairs={{0,1},{1,2},{2,3},{3,4},{4,5},{5,6},{6,7},{7,8},{8,9},{9,10},{10,1... | collective-permute-start | bytes 122888 | tf_op jit(solution)/shard_map/ppermute | solution.py:25
  110.7 8.0 %collective-permute-start.6 = (f32[10,8,128]{2,1,0:T(8,128)S(1)}, f32[10,8,128]{2,1,0:T(8,128)S(1)}, u32[]{:S(2)}, u32[]{:S(2)}) collective-permute-start(f32[10,8,128]{2,1,0:T(8,128)S(1)} %get-tuple-element.5), channel_id=1, source_target_pairs={{1,0},{2,1},{3,2},{4,3},{5,4},{6,5},{7,6},{8,7},{9,8},{10,9},{11,1... | collective-permute-start | bytes 122888 | tf_op jit(solution)/shard_map/ppermute | solution.py:25
  112.6 8.3 %collective-permute-start.7 = (f32[10,8,128]{2,1,0:T(8,128)S(1)}, f32[10,8,128]{2,1,0:T(8,128)S(1)}, u32[]{:S(2)}, u32[]{:S(2)}) collective-permute-start(f32[10,8,128]{2,1,0:T(8,128)S(1)} %get-tuple-element.5), channel_id=1, source_target_pairs={{2,0},{3,1},{4,2},{5,3},{6,4},{7,5},{8,6},{9,7},{10,8},{11,9},{12,... | collective-permute-start | bytes 122888 | tf_op jit(solution)/shard_map/ppermute | solution.py:25
  120.9 7.4 %collective-permute-start.8 = (f32[10,40,128]{2,1,0:T(8,128)S(1)}, f32[10,40,128]{2,1,0:T(8,128)S(1)}, u32[]{:S(2)}, u32[]{:S(2)}) collective-permute-start(f32[10,40,128]{2,1,0:T(8,128)S(1)} %constant_dynamic-update-slice_fusion.mid_ref), channel_id=1, source_target_pairs={{0,32},{1,33},{2,34},{3,35},{4,36},{5,37},{6,38},{7,39},{8,40},{9,... | collective-permute-start | bytes 614408 | tf_op jit(solution)/shard_map/ppermute | solution.py:25
  125.1 7.7 %collective-permute-start.9 = (f32[10,40,128]{2,1,0:T(8,128)S(1)}, f32[10,40,128]{2,1,0:T(8,128)S(1)}, u32[]{:S(2)}, u32[]{:S(2)}) collective-permute-start(f32[10,40,128]{2,1,0:T(8,128)S(1)} %constant_dynamic-update-slice_fusion.mid_ref), channel_id=1, source_target_pairs={{32,0},{33,1},{34,2},{35,3},{36,4},{37,5},{38,6},{39,7},{40,8},{41... | collective-permute-start | bytes 614408 | tf_op jit(solution)/shard_map/ppermute | solution.py:25

commit v2 on v1

v2 whole, which is shorter than its diff:
```python
import jax
import jax.numpy as jnp
from jax import lax
from jax.experimental import pallas as pl
from jax.experimental.pallas import tpu as pltpu
from jax.sharding import PartitionSpec as P

AXES = ("patch", "lat", "lon")
RELAX = 0.8
COARSE = 8
PAD = 6
CELLS = 32
VMEM = pl.BlockSpec(memory_space=pltpu.VMEM)
SMEM = pl.BlockSpec(memory_space=pltpu.SMEM)


def shifted(value, by_lat, by_lon):
    patches, lats, lons = (lax.axis_size(axis) for axis in AXES)
    pairs = []
    for p in range(patches):
        for a in range(lats):
            for b in range(lons):
                a2, b2 = a + by_lat, b + by_lon
                if 0 <= a2 < lats and 0 <= b2 < lons:
                    pairs.append(((p * lats + a) * lons + b, (p * lats + a2) * lons + b2))
    return lax.ppermute(value, AXES, pairs)


def lanes_of(shape):
    return lax.broadcasted_iota(jnp.int32, shape, len(shape) - 1)


def rows_of(shape):
    return lax.broadcasted_iota(jnp.int32, shape, len(shape) - 2)


def roll(value, by, axis):
    return pltpu.roll(value, by % value.shape[axis], axis)


def lane_partner(value, odd_lane):
    return jnp.where(odd_lane, roll(value, 1, 1), roll(value, -1, 1))


def row_partner(value, odd_row):
    return jnp.where(odd_row, roll(value, 1, 0), roll(value, -1, 0))


def interp_kernel(
    rows_ref, cols_ref, weights_ref, v_ref, right_ref, below_ref, corner_ref, out_ref, pad_ref
):
    rows = v_ref.shape[1]
    for comp in range(3):
        pad_ref[comp, :rows, 0:8] = v_ref[comp]
        pad_ref[comp, rows, 0:8] = below_ref[comp]
        for row in range(rows):
            pad_ref[comp, row, 8:9] = right_ref[comp, row : row + 1]
        pad_ref[comp, rows, 8:9] = corner_ref[comp : comp + 1]
    for slot in range(3):
        row, col = rows_ref[slot], cols_ref[slot]
        for comp in range(3):
            total = weights_ref[0, slot] * pad_ref[comp, row, pl.ds(col, 1), :]
            total = total + weights_ref[1, slot] * pad_ref[comp, row + 1, pl.ds(col, 1), :]
            total = total + weights_ref[2, slot] * pad_ref[comp, row, pl.ds(col + 1, 1), :]
            total = total + weights_ref[3, slot] * pad_ref[comp, row + 1, pl.ds(col + 1, 1), :]
            out_ref[slot * 3 + comp : slot * 3 + comp + 1] = total


def pick_kernel(place_ref, cells_ref, source_ref, row_ref, out_ref):
    lon, last_lat, last_lon = place_ref[1], place_ref[2], place_ref[3]
    edge = (lon == 0) | (lon == last_lon)

    def copy(dest, position):
        base = source_ref[cells_ref[dest * CELLS + position]]
        for comp in range(3):
            out_ref[dest * 3 * CELLS + position * 3 + comp] = row_ref[base + comp]

    @pl.when(edge)
    def _():
        def step(dest, carry):
            for position in range(CELLS):
                copy(dest, position)
            return carry

        lax.fori_loop(0, last_lat + 1, step, 0)

    @pl.when(~edge)
    def _():
        for position in range(16):
            copy(0, position)
            copy(last_lat, position)


def prepare_kernel(
    place_ref, f_ref, mu_ref, left_ref, right_ref, above_ref, below_ref,
    F, CN, CS, CW, CE, CD, CU, DG, over_ref, visc_ref, MU,
):
    lat, lon = place_ref[0], place_ref[1]
    last_lat, last_lon = place_ref[2], place_ref[3]
    wide = (24, 128)
    lane, row = lanes_of(wide), rows_of(wide)
    odd_lane, odd_row = (lane & 1) == 1, (row & 1) == 1
    own = slice(PAD, PAD + 16)
    MU[own, 0:8] = left_ref[6]
    MU[own, 8:16] = mu_ref[...]
    MU[own, 16:24] = right_ref[6]
    MU[1:6] = above_ref[6]
    MU[22:27] = below_ref[6]

    @pl.when(lat == 0)
    def _():
        MU[4] = MU[6]
        MU[5] = MU[6]

    @pl.when(lat == last_lat)
    def _():
        MU[22] = MU[21]
        MU[23] = MU[21]

    @pl.when(lon == 0)
    def _():
        for i in range(1, 27):
            MU[i, 0:8] = jnp.broadcast_to(MU[i, 8:9], (8, 128))

    @pl.when(lon == last_lon)
    def _():
        for i in range(1, 27):
            MU[i, 16:24] = jnp.broadcast_to(MU[i, 15:16], (8, 128))

    for i in range(2, 26):
        mid = MU[i]
        north = 0.5 * (mid + MU[i - 1])
        south = 0.5 * (mid + MU[i + 1])
        west = 0.5 * (mid + roll(mid, 1, 0))
        east = 0.5 * (mid + roll(mid, -1, 0))
        down = 0.5 * (mid + jnp.where(lane == 0, mid, roll(mid, 1, 1)))
        up = 0.5 * (mid + jnp.where(lane == 127, mid, roll(mid, -1, 1)))
        total = north + south + west + east + down + up
        inverse = 1.0 / total
        CN[i] = north * inverse
        CS[i] = south * inverse
        CW[i] = west * inverse
        CE[i] = east * inverse
        CD[i] = jnp.where(lane == 0, 0.0, down * inverse)
        CU[i] = jnp.where(lane == 127, 0.0, up * inverse)
        if PAD <= i < PAD + 16:
            DG[i - PAD] = total[8:16]
        for comp in range(3):
            if i < PAD:
                force = above_ref[3 + comp, i - 1]
                F[comp, i] = force * inverse
            elif i >= PAD + 16:
                force = below_ref[3 + comp, i - PAD - 16]
                F[comp, i] = force * inverse
            else:
                F[comp, i, 0:8] = left_ref[3 + comp, i - PAD] * inverse[0:8]
                F[comp, i, 8:16] = f_ref[comp, i - PAD] * inverse[8:16]
                F[comp, i, 16:24] = right_ref[3 + comp, i - PAD] * inverse[16:24]

    def coarse_visc(i):
        both = MU[i] + MU[i + 1]
        flat = 0.25 * (both + row_partner(both, odd_row))
        return flat, 0.5 * (flat + lane_partner(flat, odd_lane))

    layers = [coarse_visc(PAD + 2 * k) for k in (-1, 0)]
    for k in range(8):
        layers.append(coarse_visc(PAD + 2 * k + 2))
        before, (flat, visc), after = layers[k][1], layers[k + 1], layers[k + 2][1]
        edge_down = jnp.where(lane == 0, flat, roll(flat, 1, 1))
        edge_up = jnp.where(lane == 127, flat, roll(flat, -1, 1))
        total = 6.0 * visc + before + after + roll(visc, 2, 0) + roll(visc, -2, 0)
        total = total + jnp.where(lane < 2, edge_down, roll(visc, 2, 1))
        total = total + jnp.where(lane >= 126, edge_up, roll(visc, -2, 1))
        over_ref[k] = RELAX / (0.125 * total[8:16])
        visc_ref[k] = visc[8:16]


def smooth_kernel(
    place_ref, ghost_ref, v_ref, left_ref, right_ref, above_ref, below_ref, slot_ref,
    F, CN, CS, CW, CE, CD, CU, DG, over_ref, visc_ref,
    res_ref, smooth_ref, message_ref, A, B,
):
    lat, lon = place_ref[0], place_ref[1]
    last_lat, last_lon = place_ref[2], place_ref[3]
    wide = (24, 128)
    lane, row = lanes_of(wide), rows_of(wide)
    own = slice(PAD, PAD + 16)

    for comp in range(3):
        A[comp, own, 0:8] = left_ref[comp]
        A[comp, own, 8:16] = v_ref[comp]
        A[comp, own, 16:24] = right_ref[comp]
        A[comp, 1:6] = above_ref[comp]
        A[comp, 22:27] = below_ref[comp]

    edge = (lon == 0) | (lon == last_lon)
    all_cols, all_rows = (last_lon + 1) * 8, (last_lat + 1) * 16

    def fill_row(i, start):
        for col in range(-4, 12):
            along = jnp.where(lon == 0, col, col + 4)
            packed_at = jnp.where((lat == 0) & (along < 4), along, along + 20)
            position = jnp.clip(jnp.where(edge, packed_at, col + 4), 0, CELLS - 1)
            cell = start + jnp.clip(lon * 8 + col, 0, all_cols - 1)
            base = ghost_ref[cell] + 3 * position
            for comp in range(3):
                A[comp, i, 8 + col : 9 + col] = slot_ref[base + comp]

    def fill_side(col, start):
        for r in range(-4, 20):
            base = ghost_ref[start + jnp.clip(lat * 16 + r, 0, all_rows - 1)] + 3 * (r + 4)
            for comp in range(3):
                A[comp, r + PAD, 8 + col : 9 + col] = slot_ref[base + comp]

    pl.when(lat == 0)(lambda: fill_row(5, 0))
    pl.when(lat == last_lat)(lambda: fill_row(22, all_cols))
    pl.when(lon == 0)(lambda: fill_side(-1, 2 * all_cols))
    pl.when(lon == last_lon)(lambda: fill_side(8, 2 * all_cols + all_rows))

    inside = ((row >= 8) | (lon > 0)) & ((row < 16) | (lon < last_lon))
    parity = jnp.where(inside, (row + lane) & 1, 2)

    def weighted(source, comp, i, here):
        total = F[comp, i] + CN[i] * source[comp, i - 1]
        total = total + CS[i] * source[comp, i + 1]
        total = total + CW[i] * roll(here, 1, 0)
        total = total + CE[i] * roll(here, -1, 0)
        total = total + CD[i] * roll(here, 1, 1)
        return total + CU[i] * roll(here, -1, 1)

    wanted = {}
    for colour in range(2):
        wanted[colour, "mid"] = jnp.int32(colour)
        wanted[colour, "top"] = jnp.where(lat == 0, 3, colour)
        wanted[colour, "low"] = jnp.where(lat == last_lat, 3, colour)

    def relax(colour, reach, source, target):
        for r in range(-reach, 16 + reach):
            i = r + PAD
            zone = "top" if r < 0 else "low" if r > 15 else "mid"
            mask = parity == wanted[(colour + r) % 2, zone]
            for comp in range(3):
                here = source[comp, i]
                target[comp, i] = jnp.where(mask, weighted(source, comp, i, here), here)

    relax(0, 4, A, B)
    relax(1, 3, B, A)
    relax(0, 2, A, B)
    relax(1, 1, B, A)

    tile = (8, 128)
    lane8, row8 = lanes_of(tile), rows_of(tile)
    odd_lane8, odd_row8 = (lane8 & 1) == 1, (row8 & 1) == 1

    def packed(parts):
        low = jnp.where(odd_lane8, parts[1], parts[0])
        high = jnp.where(odd_lane8, parts[3], parts[2])
        return jnp.where(odd_row8, high, low)

    for k in range(8):
        parts = []
        for comp in range(3):
            rhs = jnp.zeros(tile, jnp.float32)
            for r in (2 * k, 2 * k + 1):
                here = A[comp, r + PAD]
                smooth_ref[comp, r] = here[8:16]
                left = DG[r] * (weighted(A, comp, r + PAD, here) - here)[8:16]
                res_ref[comp, r] = left
                rhs = rhs + left
            rhs = rhs + lane_partner(rhs, odd_lane8)
            rhs = rhs + row_partner(rhs, odd_row8)
            parts.append(0.125 * rhs * over_ref[k])
        message_ref[k] = packed(parts + [visc_ref[k]])
        if k % 4 == 3:
            message_ref[8 + k // 4] = packed([over_ref[j] for j in range(k - 3, k + 1)])


def coarse_kernel(
    mid_ref, above_ref, below_ref, smooth_ref, out_ref, Q, CV, DV, E, AN, AS, AW, AE, AD, AU
):
    wide = (40, 128)
    lane, row = lanes_of(wide), rows_of(wide)
    odd_lane, odd_row = (lane & 1) == 1, (row & 1) == 1

    def spread(value, part, odd_l, odd_r):
        keep = odd_l if part % 2 else ~odd_l
        value = jnp.where(keep, value, roll(value, -1 if part % 2 else 1, 1))
        keep = odd_r if part // 2 else ~odd_r
        return jnp.where(keep, value, roll(value, -1 if part // 2 else 1, 0))

    for n in range(22):
        ref, t = (above_ref, n + 1) if n < 7 else (mid_ref, n - 7) if n < 15 else (below_ref, n - 15)
        value = ref[t]
        Q[n] = value
        CV[n] = spread(value, 3, odd_lane, odd_row)
        if 1 <= n <= 20:
            DV[n] = 0.125 * spread(ref[8 + t // 4], t % 4, odd_lane, odd_row)

    def far(n):
        return max(0, 7 - n, n - 14)

    def span(reach):
        return slice(0, 40) if reach > 3 else slice(8, 32)

    for n in range(1, 21):
        cols = span(6 - far(n))
        edge = lane[cols]
        visc, over = CV[n, cols], DV[n, cols]
        AN[n, cols] = over * (visc + CV[n - 1, cols])
        AS[n, cols] = over * (visc + CV[n + 1, cols])
        AW[n, cols] = over * (visc + roll(visc, 2, 0))
        AE[n, cols] = over * (visc + roll(visc, -2, 0))
        AD[n, cols] = jnp.where(edge < 2, 0.0, over * (visc + roll(visc, 2, 1)))
        AU[n, cols] = jnp.where(edge >= 126, 0.0, over * (visc + roll(visc, -2, 1)))

    for turn in range(1, COARSE):
        old = Q if turn == 1 else E.at[turn % 2]
        new = E.at[(turn + 1) % 2]
        for n in range(turn, 22 - turn):
            cols = span(7 - turn - far(n))
            here = old[n, cols]
            total = Q[n, cols] + (1.0 - RELAX) * here
            total = total + AN[n, cols] * old[n - 1, cols]
            total = total + AS[n, cols] * old[n + 1, cols]
            total = total + AW[n, cols] * roll(here, 2, 0)
            total = total + AE[n, cols] * roll(here, -2, 0)
            total = total + AD[n, cols] * roll(here, 2, 1)
            new[n, cols] = total + AU[n, cols] * roll(here, -2, 1)

    final = E.at[COARSE % 2]
    tile = (8, 128)
    lane8, row8 = lanes_of(tile), rows_of(tile)
    odd_lane8, odd_row8 = (lane8 & 1) == 1, (row8 & 1) == 1
    for k in range(8):
        value = final[7 + k, 16:24]
        for comp in range(3):
            error = spread(value, comp, odd_lane8, odd_row8)
            for r in (2 * k, 2 * k + 1):
                out_ref[comp, r] = smooth_ref[comp, r] + error


def wanted_cells(lats, lons, lon):
    dest = jnp.arange(lats, dtype=jnp.int32)[:, None]
    position = jnp.arange(CELLS, dtype=jnp.int32)[None, :]
    rows, cols = lats * 16, lons * 8
    edge = (lon == 0) | (lon == lons - 1)
    side_row = dest * 16 + position - 4
    on_side = edge & (position < 24) & (side_row >= 0) & (side_row < rows)
    side = 2 * cols + jnp.where(lon == 0, 0, rows) + jnp.clip(side_row, 0, rows - 1)
    along = jnp.where((dest == 0) & (position < 4), position, position - 20)
    corner_col = jnp.where(lon == 0, along, lon * 8 + along - 4)
    col = jnp.where(edge, corner_col, lon * 8 + position - 4)
    row_cell = jnp.where(dest == 0, 0, cols) + jnp.clip(col, 0, cols - 1)
    return jnp.where(on_side, side, row_cell)


def per_device(velocity, forcing, viscosity, ghost_slots, corner_rows, corner_cols, corner_weights):
    v, f, mu = velocity[0], forcing[0], viscosity[0]
    lats, lons = lax.axis_size("lat"), lax.axis_size("lon")
    params = pltpu.CompilerParams(vmem_limit_bytes=32 * 2**20)
    f32 = jnp.float32
    place = jnp.stack(
        [lax.axis_index("lat"), lax.axis_index("lon"), jnp.int32(lats - 1), jnp.int32(lons - 1)]
    ).astype(jnp.int32)
    slots = ghost_slots[0]
    source_rows = ((slots // 3) % lons) * 9 + (slots % 3) * 3
    ghost_rows = (slots // (3 * lons)) * (3 * CELLS)
    cells = wanted_cells(lats, lons, lax.axis_index("lon")).reshape(-1)

    corner_right = shifted(v[:, :, 0], 0, -1)
    corner_below = shifted(v[:, 0], -1, 0)
    corner_both = shifted(v[:, 0, 0], -1, -1)
    values = pl.pallas_call(
        interp_kernel,
        out_shape=jax.ShapeDtypeStruct((9, 128), f32),
        in_specs=[SMEM] * 3 + [VMEM] * 4,
        out_specs=VMEM,
        scratch_shapes=[pltpu.VMEM((3, 17, 16, 128), f32)],
        compiler_params=params,
        name="interp",
    )(
        corner_rows[0, 0], corner_cols[0, 0], corner_weights[0, 0],
        v, corner_right, corner_below, corner_both,
    )
    values = lax.ppermute(values, "patch", [(0, 1), (1, 0)])

    own = jnp.concatenate([v, f, mu[None]], axis=0)
    left = shifted(own, 0, 1)
    right = shifted(own, 0, -1)
    ext_top = jnp.concatenate([left[:, :5], own[:, :5], right[:, :5]], axis=2)
    ext_low = jnp.concatenate([left[:, 11:], own[:, 11:], right[:, 11:]], axis=2)
    below = shifted(ext_top, -1, 0)
    above = shifted(ext_low, 1, 0)

    around = lax.all_to_all(
        jnp.broadcast_to(values[None], (lons, 9, 128)), "lon", 0, 0, tiled=True
    )
    chosen = pl.pallas_call(
        pick_kernel,
        out_shape=jax.ShapeDtypeStruct((lats * 3 * CELLS, 1, 128), f32),
        in_specs=[SMEM, SMEM, SMEM, VMEM],
        out_specs=VMEM,
        compiler_params=params,
        name="pick",
    )(place, cells, source_rows, around.reshape(lons * 9, 1, 128))
    everything = lax.all_to_all(chosen.reshape(lats, 3 * CELLS, 128), "lat", 0, 0, tiled=True)
    everything = everything.reshape(lats * 3 * CELLS, 1, 128)

    block = jax.ShapeDtypeStruct((3, 16, 8, 128), f32)
    field = (3, 28, 24, 128)
    plane = jax.ShapeDtypeStruct((28, 24, 128), f32)
    half = jax.ShapeDtypeStruct((8, 8, 128), f32)
    prepared = pl.pallas_call(
        prepare_kernel,
        out_shape=[jax.ShapeDtypeStruct(field, f32)] + [plane] * 6
        + [jax.ShapeDtypeStruct((16, 8, 128), f32), half, half],
        in_specs=[SMEM] + [VMEM] * 6,
        out_specs=[VMEM] * 10,
        scratch_shapes=[pltpu.VMEM((28, 24, 128), f32)],
        compiler_params=params,
        name="prepare",
    )(place, f, mu, left, right, above, below)
    residual, smoothed, message = pl.pallas_call(
        smooth_kernel,
        out_shape=(block, block, jax.ShapeDtypeStruct((10, 8, 128), f32)),
        in_specs=[SMEM, SMEM] + [VMEM] * 16,
        out_specs=(VMEM, VMEM, VMEM),
        scratch_shapes=[pltpu.VMEM(field, f32)] * 2,
        compiler_params=params,
        name="smooth",
    )(place, ghost_rows, v, left, right, above, below, everything, *prepared)

    tiles = [
        shifted(message, 0, 2),
        shifted(message, 0, 1),
        message,
        shifted(message, 0, -1),
        shifted(message, 0, -2),
    ]
    band = jnp.concatenate(tiles, axis=1)
    band_below = shifted(band, -1, 0)
    band_above = shifted(band, 1, 0)
    coarse = pltpu.VMEM((22, 40, 128), f32)
    new = pl.pallas_call(
        coarse_kernel,
        out_shape=block,
        in_specs=[VMEM] * 4,
        out_specs=VMEM,
        scratch_shapes=[coarse, coarse, coarse, pltpu.VMEM((2, 22, 40, 128), f32)] + [coarse] * 6,
        compiler_params=params,
        name="coarse",
    )(band, band_above, band_below, smoothed)
    return new[None], residual[None]


def solution(mesh):
    placed = (
        P("patch", None, "lat", "lon", None),
        P("patch", None, "lat", "lon", None),
        P("patch", "lat", "lon", None),
        P("patch", None),
        P("patch", "lat", "lon"),
        P("patch", "lat", "lon"),
        P("patch", "lat", None, "lon"),
    )
    return jax.shard_map(
        per_device,
        mesh=mesh,
        in_specs=placed,
        out_specs=(P("patch", None, "lat", "lon", None), P("patch", None, "lat", "lon", None)),
        check_vma=False,
    )
```

time: 145 us -> 129 us (0.89)
  the two profiles are of different devices: /device:TPU:6 before, /device:TPU:96 now
where the time goes in v2:
time: 129 us; the launch traced here: 128 us
  starting transfers between devices  65.7 us (51%)
  waiting for transfers between devices  36.6 us (28%)
  local copies, waits for them, and re-layouts  13.7 us (11%)
  Pallas kernels  9.47 us (7%)
  other arithmetic  1.65 us (1%)
    ppermute x13, starting transfers between devices, shifted(): return lax.ppermute(value, AXES, pairs)  43.7 us
    ppermute x13, waiting for transfers between devices, shifted(): return lax.ppermute(value, AXES, pairs)  23.6 us
    all_to_all x1, starting transfers between devices, per_device(): lax.all_to_all(jnp.broadcast_to(values[None], (lons, 9, 128)), 'lon', 0,...  12.7 us
    all_to_all x1, waiting for transfers between devices, per_device(): lax.all_to_all(jnp.broadcast_to(values[None], (lons, 9, 128)), 'lon', 0,...  12.4 us
    unnamed x44, local copies, waits for them, and re-layouts  12.4 us
    all_to_all x1, starting transfers between devices, per_device(): lax.all_to_all(chosen.reshape(lats, 3 * CELLS, 128), 'lat', 0, 0, tiled=T...  7.32 us
    pallas_call x1, Pallas kernels, per_device(): pl.pallas_call(smooth_kernel, out_shape=(block, block, jax.ShapeDtypeStru...  4.34 us
  transfers between devices with their start and end apart: 16, of which 7 were waited for; matrix products, arithmetic and copies ran while one was open for 2% of the time, Pallas kernels for 2%

profile of v2, /device:TPU:96, one launch (start us, length us, event | category | flops | bytes accessed | tf_op | source)
XLA Modules:
  0.0 128.1 jit_solution(14960209417343231417)
XLA Ops:
  0.6 1.1 pad_maximum_fusion
  1.8 3.8 %collective-permute-start.1 = (f32[7,16,8,128]{3,2,1,0:T(8,128)S(1)}, f32[7,16,8,128]{3,2,1,0:T(8,128)S(1)}, u32[]{:S(2)}, u32[]{:S(2)}) collective-permute-start(f32[7,16,8,128]{3,2,1,0:T(8,128)S(1)} %pad_maximum_fusion), channel_id=1, source_target_pairs={{1,0},{2,1},{3,2},{4,3},{5,4},{6,5},{7,6},{8,7},{9,8},{10,9},{11,1... | collective-permute-start | bytes 1376264 | tf_op jit(solution)/shard_map/ppermute | solution.py:26
  5.5 2.1 %collective-permute-start = (f32[7,16,8,128]{3,2,1,0:T(8,128)S(1)}, f32[7,16,8,128]{3,2,1,0:T(8,128)S(1)}, u32[]{:S(2)}, u32[]{:S(2)}) collective-permute-start(f32[7,16,8,128]{3,2,1,0:T(8,128)S(1)} %pad_maximum_fusion), channel_id=1, source_target_pairs={{0,1},{1,2},{2,3},{3,4},{4,5},{5,6},{6,7},{7,8},{8,9},{9,10},{10,1... | collective-permute-start | bytes 1376264 | tf_op jit(solution)/shard_map/ppermute | solution.py:26
  7.7 5.8 %collective-permute-start.6 = (f32[3,128]{1,0:T(4,128)S(1)}, f32[3,128]{1,0:T(4,128)S(1)}, u32[]{:S(2)}, u32[]{:S(2)}) collective-permute-start(f32[3,128]{1,0:T(4,128)S(1)} %bitcast.35), channel_id=1, source_target_pairs={{33,0},{34,1},{35,2},{36,3},{37,4},{38,5},{39,6},{40,7},{41,8},{42... | collective-permute-start | bytes 4616 | tf_op jit(solution)/shard_map/ppermute | solution.py:26
  13.4 2.4 %collective-permute-start.5 = (f32[3,8,128]{2,1,0:T(8,128)S(1)}, f32[3,8,128]{2,1,0:T(8,128)S(1)}, u32[]{:S(2)}, u32[]{:S(2)}) collective-permute-start(f32[3,8,128]{2,1,0:T(8,128)S(1)} %slice_bitcast_fusion), channel_id=1, source_target_pairs={{32,0},{33,1},{34,2},{35,3},{36,4},{37,5},{38,6},{39,7},{40,8},{41... | collective-permute-start | bytes 36872 | tf_op jit(solution)/shard_map/ppermute | solution.py:26
  15.8 2.0 %collective-permute-start.4 = (f32[3,16,128]{2,1,0:T(8,128)S(1)}, f32[3,16,128]{2,1,0:T(8,128)S(1)}, u32[]{:S(2)}, u32[]{:S(2)}) collective-permute-start(f32[3,16,128]{2,1,0:T(8,128)S(1)} %bitcast.34), channel_id=1, source_target_pairs={{1,0},{2,1},{3,2},{4,3},{5,4},{6,5},{7,6},{8,7},{9,8},{10,9},{11,1... | collective-permute-start | bytes 73736 | tf_op jit(solution)/shard_map/ppermute | solution.py:26
  17.9 0.0 copy-start.17
  17.9 0.6 copy-done.17
  18.7 0.1 fusion.8
  18.8 0.1 clamp_add_fusion
  18.9 0.1 iota_select_fusion
  18.9 0.0 copy-start.18
  19.0 0.7 copy-done.18
  19.6 0.1 copy.10
  19.7 1.8 %collective-permute-done.4.right_ref = f32[3,16,128]{2,1,0:T(8,128)S(1)} collective-permute-done((f32[3,16,128]{2,1,0:T(8,128)S(1)}, f32[3,16,128]{2,1,0:T(8,128)S(1)}, u32[]{:S(2)}, u32[]{:S(2)}) %collective-permute-start.4) | collective-permute-done | bytes 24608 | tf_op jit(solution)/shard_map/ppermute | solution.py:26
  21.5 0.7 copy-done.15
  22.2 0.0 copy-done.16
  22.2 0.6 interp.1
  22.8 1.9 %collective-permute-start.7 = (f32[9,128]{1,0:T(8,128)S(1)}, f32[9,128]{1,0:T(8,128)S(1)}, u32[]{:S(2)}, u32[]{:S(2)}) collective-permute-start(f32[9,128]{1,0:T(8,128)S(1)} %interp.1), channel_id=1, source_target_pairs={{0,256},{256,0},{1,257},{257,1},{2,258},{258,2},{3,259},{259,3},{4... | collective-permute-start | bytes 13832 | tf_op jit(solution)/shard_map/ppermute | solution.py:385
  24.8 0.1 reshape.92
  24.9 0.1 select_n.73
  24.9 0.1 reshape.91
  25.0 0.1 add.104
  25.1 0.1 add.105
  25.2 0.1 broadcast_in_dim.49
  25.3 0.6 collective-permute-done.7
  25.9 0.7 broadcast_in_dim.50
  26.6 12.7 %all-to-all-start = ((f32[32,9,128]{2,1,0:T(8,128)}), f32[32,9,128]{2,1,0:T(8,128)S(1)}, u32[]{:S(2)}, u32[]{:S(2)}) async-start(f32[32,9,128]{2,1,0:T(8,128)} %broadcast_in_dim.50), calls=%async_computation | async-start | bytes 524288 | tf_op jit(solution)/shard_map/all_to_all | solution.py:395
  39.3 0.1 pad_add_fusion.place_ref
  39.4 12.4 %all-to-all-done = f32[32,9,128]{2,1,0:T(8,128)S(1)} async-done(((f32[32,9,128]{2,1,0:T(8,128)}), f32[32,9,128]{2,1,0:T(8,128)S(1)}, u32[]{:S(2)}, u32[]{:S(2)}) %all-to-all-start) | async-done | bytes 147488 | tf_op jit(solution)/shard_map/all_to_all | solution.py:395
  51.8 1.4 %pick.1 = f32[768,1,128]{2,1,0:T(1,128)} custom-call(s32[4]{0:T(128)S(1)} %pad_add_fusion.place_ref, s32[256]{0:T(256)S(1)} %add_select_fusion.4.cells_ref, s32[768]{0:T(1024)S(1)} %get-tuple-element.39.source_ref, f32[288,1,128]{2,1,0:T(1,128)S(1)} %bitcast.28), custom_call_target="tpu_custom_call" | custom-call | tf_op jit(solution)/shard_map/pick/pallas_call | solution.py:398
  53.3 7.3 %all-to-all-start.1 = ((f32[8,96,128]{2,1,0:T(8,128)}), f32[8,96,128]{2,1,0:T(8,128)S(1)}, u32[]{:S(2)}, u32[]{:S(2)}) async-start(f32[8,96,128]{2,1,0:T(8,128)} %bitcast.10), calls=%async_computation.1 | async-start | bytes 786432 | tf_op jit(solution)/shard_map/all_to_all | solution.py:406
  60.6 0.0 collective-permute-done.1.right_ref
  60.7 2.5 %collective-permute-start.2 = (f32[7,5,24,128]{3,2,1,0:T(8,128)S(1)}, f32[7,5,24,128]{3,2,1,0:T(8,128)S(1)}, u32[]{:S(2)}, u32[]{:S(2)}) collective-permute-start(f32[7,5,24,128]{3,2,1,0:T(8,128)S(1)} %pad_maximum_fusion.1), channel_id=1, source_target_pairs={{0,32},{1,33},{2,34},{3,35},{4,36},{5,37},{6,38},{7,39},{8,40},{9,... | collective-permute-start | bytes 1290248 | tf_op jit(solution)/shard_map/ppermute | solution.py:26
  63.2 0.0 copy-start.1
  63.2 0.0 copy-start.14
  63.2 4.7 %collective-permute-start.3 = (f32[7,5,24,128]{3,2,1,0:T(8,128)S(1)}, f32[7,5,24,128]{3,2,1,0:T(8,128)S(1)}, u32[]{:S(2)}, u32[]{:S(2)}) collective-permute-start(f32[7,5,24,128]{3,2,1,0:T(8,128)S(1)} %pad_maximum_fusion.2), channel_id=1, source_target_pairs={{32,0},{33,1},{34,2},{35,3},{36,4},{37,5},{38,6},{39,7},{40,8},{41... | collective-permute-start | bytes 1290248 | tf_op jit(solution)/shard_map/ppermute | solution.py:26
  68.0 9.3 %collective-permute-done.2.above_ref = f32[7,5,24,128]{3,2,1,0:T(8,128)S(1)} collective-permute-done((f32[7,5,24,128]{3,2,1,0:T(8,128)S(1)}, f32[7,5,24,128]{3,2,1,0:T(8,128)S(1)}, u32[]{:S(2)}, u32[]{:S(2)}) %collective-permute-start.2) | collective-permute-done | bytes 430112 | tf_op jit(solution)/shard_map/ppermute | solution.py:26
  77.2 0.0 collective-permute-done.3.below_ref
  77.2 1.1 prepare.1
  78.4 0.7 copy-done.2
  79.1 0.7 copy-done.4
  79.8 0.7 copy-done.6
  80.6 0.7 copy-done.8
  81.3 0.7 copy-done.10
  82.0 0.7 copy-done.12
  82.8 0.0 all-to-all-done.1
  82.8 1.0 copy-done.3
  83.7 1.0 copy-done.5
  84.7 1.0 copy-done.7
  85.7 1.0 copy-done.9
  86.7 1.0 copy-done.11
  87.7 1.0 copy-done.13
  88.6 4.3 %smooth.1 = (f32[3,16,8,128]{3,2,1,0:T(8,128)}, f32[3,16,8,128]{3,2,1,0:T(8,128)S(1)}, f32[10,8,128]{2,1,0:T(8,128)S(1)}) custom-call(s32[4]{0:T(128)S(1)} %pad_add_fusion.place_ref, s32[768]{0:T(1024)S(1)} %get-tuple-element.40.ghost_ref, f32[3,16,8,128]{3,2,1,0:T(8,128)S(1)} %bitcast.24, f32[7,16,8,128]{3,2,1,0:T(8,128)S(1)} %collective-permute-done.left_ref, ...), custom_call_target="tpu_custom_call" | custom-call | tf_op jit(solution)/shard_map/smooth/pallas_call | solution.py:423
  93.0 3.8 %collective-permute-start.8 = (f32[10,8,128]{2,1,0:T(8,128)S(1)}, f32[10,8,128]{2,1,0:T(8,128)S(1)}, u32[]{:S(2)}, u32[]{:S(2)}) collective-permute-start(f32[10,8,128]{2,1,0:T(8,128)S(1)} %get-tuple-element.25), channel_id=1, source_target_pairs={{0,2},{1,3},{2,4},{3,5},{4,6},{5,7},{6,8},{7,9},{8,10},{9,11},{10,... | collective-permute-start | bytes 122888 | tf_op jit(solution)/shard_map/ppermute | solution.py:26
  96.7 4.5 %collective-permute-start.11 = (f32[10,8,128]{2,1,0:T(8,128)S(1)}, f32[10,8,128]{2,1,0:T(8,128)S(1)}, u32[]{:S(2)}, u32[]{:S(2)}) collective-permute-start(f32[10,8,128]{2,1,0:T(8,128)S(1)} %get-tuple-element.25), channel_id=1, source_target_pairs={{2,0},{3,1},{4,2},{5,3},{6,4},{7,5},{8,6},{9,7},{10,8},{11,9},{12,... | collective-permute-start | bytes 122888 | tf_op jit(solution)/shard_map/ppermute | solution.py:26
  101.2 3.4 %collective-permute-start.10 = (f32[10,8,128]{2,1,0:T(8,128)S(1)}, f32[10,8,128]{2,1,0:T(8,128)S(1)}, u32[]{:S(2)}, u32[]{:S(2)}) collective-permute-start(f32[10,8,128]{2,1,0:T(8,128)S(1)} %get-tuple-element.25), channel_id=1, source_target_pairs={{1,0},{2,1},{3,2},{4,3},{5,4},{6,5},{7,6},{8,7},{9,8},{10,9},{11,1... | collective-permute-start | bytes 122888 | tf_op jit(solution)/shard_map/ppermute | solution.py:26
  104.6 2.4 %collective-permute-start.9 = (f32[10,8,128]{2,1,0:T(8,128)S(1)}, f32[10,8,128]{2,1,0:T(8,128)S(1)}, u32[]{:S(2)}, u32[]{:S(2)}) collective-permute-start(f32[10,8,128]{2,1,0:T(8,128)S(1)} %get-tuple-element.25), channel_id=1, source_target_pairs={{0,1},{1,2},{2,3},{3,4},{4,5},{5,6},{6,7},{7,8},{8,9},{9,10},{10,1... | collective-permute-start | bytes 122888 | tf_op jit(solution)/shard_map/ppermute | solution.py:26
  107.1 5.5 %collective-permute-done.9 = f32[10,8,128]{2,1,0:T(8,128)S(1)} collective-permute-done((f32[10,8,128]{2,1,0:T(8,128)S(1)}, f32[10,8,128]{2,1,0:T(8,128)S(1)}, u32[]{:S(2)}, u32[]{:S(2)}) %collective-permute-start.9) | collective-permute-done | bytes 40992 | tf_op jit(solution)/shard_map/ppermute | solution.py:26
  112.7 4.6 %collective-permute-start.13 = (f32[10,40,128]{2,1,0:T(8,128)S(1)}, f32[10,40,128]{2,1,0:T(8,128)S(1)}, u32[]{:S(2)}, u32[]{:S(2)}) collective-permute-start(f32[10,40,128]{2,1,0:T(8,128)S(1)} %constant_dynamic-update-slice_fusion.mid_ref), channel_id=1, source_target_pairs={{32,0},{33,1},{34,2},{35,3},{36,4},{37,5},{38,6},{39,7},{40,8},{41... | collective-permute-start | bytes 614408 | tf_op jit(solution)/shard_map/ppermute | solution.py:26
  117.3 1.9 %collective-permute-start.12 = (f32[10,40,128]{2,1,0:T(8,128)S(1)}, f32[10,40,128]{2,1,0:T(8,128)S(1)}, u32[]{:S(2)}, u32[]{:S(2)}) collective-permute-start(f32[10,40,128]{2,1,0:T(8,128)S(1)} %constant_dynamic-update-slice_fusion.mid_ref), channel_id=1, source_target_pairs={{0,32},{1,33},{2,34},{3,35},{4,36},{5,37},{6,38},{7,39},{8,40},{9,... | collective-permute-start | bytes 614408 | tf_op jit(solution)/shard_map/ppermute | solution.py:26
  119.2 1.3 %collective-permute-done.13.below_ref = f32[10,40,128]{2,1,0:T(8,128)S(1)} collective-permute-done((f32[10,40,128]{2,1,0:T(8,128)S(1)}, f32[10,40,128]{2,1,0:T(8,128)S(1)}, u32[]{:S(2)}, u32[]{:S(2)}) %collective-permute-start.13) | collective-permute-done | bytes 204832 | tf_op jit(solution)/shard_map/ppermute | solution.py:26
  120.5 5.6 %collective-permute-done.12.above_ref = f32[10,40,128]{2,1,0:T(8,128)S(1)} collective-permute-done((f32[10,40,128]{2,1,0:T(8,128)S(1)}, f32[10,40,128]{2,1,0:T(8,128)S(1)}, u32[]{:S(2)}, u32[]{:S(2)}) %collective-permute-start.12) | collective-permute-done | bytes 204832 | tf_op jit(solution)/shard_map/ppermute | solution.py:26
  126.2 2.0 %coarse.1 = f32[3,16,8,128]{3,2,1,0:T(8,128)} custom-call(f32[10,40,128]{2,1,0:T(8,128)S(1)} %constant_dynamic-update-slice_fusion.mid_ref, f32[10,40,128]{2,1,0:T(8,128)S(1)} %collective-permute-done.12.above_ref, f32[10,40,128]{2,1,0:T(8,128)S(1)} %collective-permute-done.13.below_ref, f32[3,16,8,128]{3,2,1,0:T(8,128)S(1)} %get-tuple-element.26.smooth_ref), custom_call_target="tpu_custom_call" | custom-call | tf_op jit(solution)/shard_map/coarse/pallas_call | solution.py:444
  (51 shorter events, 0.4 us)
Async XLA Ops:
  0.6 7.0 %copy-start = (f32[1,3,16,8,128]{4,3,2,1,0:T(8,128)S(1)}, f32[1,3,16,8,128]{4,3,2,1,0:T(8,128)}, u32[]{:S(2)}) copy-start(f32[1,3,16,8,128]{4,3,2,1,0:T(8,128)} %param.7) | copy-start | bytes 589828
  1.8 58.8 %collective-permute-start.1 = (f32[7,16,8,128]{3,2,1,0:T(8,128)S(1)}, f32[7,16,8,128]{3,2,1,0:T(8,128)S(1)}, u32[]{:S(2)}, u32[]{:S(2)}) collective-permute-start(f32[7,16,8,128]{3,2,1,0:T(8,128)S(1)} %pad_maximum_fusion), channel_id=1, source_target_pairs={{1,0},{2,1},{3,2},{4,3},{5,4},{6,5},{7,6},{8,7},{9,8},{10,9},{11,1... | collective-permute-start | bytes 1376264 | tf_op jit(solution)/shard_map/ppermute | solution.py:26
  5.5 55.1 %collective-permute-start = (f32[7,16,8,128]{3,2,1,0:T(8,128)S(1)}, f32[7,16,8,128]{3,2,1,0:T(8,128)S(1)}, u32[]{:S(2)}, u32[]{:S(2)}) collective-permute-start(f32[7,16,8,128]{3,2,1,0:T(8,128)S(1)} %pad_maximum_fusion), channel_id=1, source_target_pairs={{0,1},{1,2},{2,3},{3,4},{4,5},{5,6},{6,7},{7,8},{8,9},{9,10},{10,1... | collective-permute-start | bytes 1376264 | tf_op jit(solution)/shard_map/ppermute | solution.py:26
  7.7 12.1 %collective-permute-start.6 = (f32[3,128]{1,0:T(4,128)S(1)}, f32[3,128]{1,0:T(4,128)S(1)}, u32[]{:S(2)}, u32[]{:S(2)}) collective-permute-start(f32[3,128]{1,0:T(4,128)S(1)} %bitcast.35), channel_id=1, source_target_pairs={{33,0},{34,1},{35,2},{36,3},{37,4},{38,5},{39,6},{40,7},{41,8},{42... | collective-permute-start | bytes 4616 | tf_op jit(solution)/shard_map/ppermute | solution.py:26
  13.4 6.3 %collective-permute-start.5 = (f32[3,8,128]{2,1,0:T(8,128)S(1)}, f32[3,8,128]{2,1,0:T(8,128)S(1)}, u32[]{:S(2)}, u32[]{:S(2)}) collective-permute-start(f32[3,8,128]{2,1,0:T(8,128)S(1)} %slice_bitcast_fusion), channel_id=1, source_target_pairs={{32,0},{33,1},{34,2},{35,3},{36,4},{37,5},{38,6},{39,7},{40,8},{41... | collective-permute-start | bytes 36872 | tf_op jit(solution)/shard_map/ppermute | solution.py:26
  15.8 5.7 %collective-permute-start.4 = (f32[3,16,128]{2,1,0:T(8,128)S(1)}, f32[3,16,128]{2,1,0:T(8,128)S(1)}, u32[]{:S(2)}, u32[]{:S(2)}) collective-permute-start(f32[3,16,128]{2,1,0:T(8,128)S(1)} %bitcast.34), channel_id=1, source_target_pairs={{1,0},{2,1},{3,2},{4,3},{5,4},{6,5},{7,6},{8,7},{9,8},{10,9},{11,1... | collective-permute-start | bytes 73736 | tf_op jit(solution)/shard_map/ppermute | solution.py:26
  17.9 0.7 copy-start.17
  18.9 0.7 copy-start.18
  21.5 0.7 copy-start.15
  21.5 0.7 copy-start.16
  22.8 3.1 %collective-permute-start.7 = (f32[9,128]{1,0:T(8,128)S(1)}, f32[9,128]{1,0:T(8,128)S(1)}, u32[]{:S(2)}, u32[]{:S(2)}) collective-permute-start(f32[9,128]{1,0:T(8,128)S(1)} %interp.1), channel_id=1, source_target_pairs={{0,256},{256,0},{1,257},{257,1},{2,258},{258,2},{3,259},{259,3},{4... | collective-permute-start | bytes 13832 | tf_op jit(solution)/shard_map/ppermute | solution.py:385
  26.6 25.2 %all-to-all-start = ((f32[32,9,128]{2,1,0:T(8,128)}), f32[32,9,128]{2,1,0:T(8,128)S(1)}, u32[]{:S(2)}, u32[]{:S(2)}) async-start(f32[32,9,128]{2,1,0:T(8,128)} %broadcast_in_dim.50), calls=%async_computation | async-start | bytes 524288 | tf_op jit(solution)/shard_map/all_to_all | solution.py:395
  53.3 29.5 %all-to-all-start.1 = ((f32[8,96,128]{2,1,0:T(8,128)}), f32[8,96,128]{2,1,0:T(8,128)S(1)}, u32[]{:S(2)}, u32[]{:S(2)}) async-start(f32[8,96,128]{2,1,0:T(8,128)} %bitcast.10), calls=%async_computation.1 | async-start | bytes 786432 | tf_op jit(solution)/shard_map/all_to_all | solution.py:406
  60.7 16.5 %collective-permute-start.2 = (f32[7,5,24,128]{3,2,1,0:T(8,128)S(1)}, f32[7,5,24,128]{3,2,1,0:T(8,128)S(1)}, u32[]{:S(2)}, u32[]{:S(2)}) collective-permute-start(f32[7,5,24,128]{3,2,1,0:T(8,128)S(1)} %pad_maximum_fusion.1), channel_id=1, source_target_pairs={{0,32},{1,33},{2,34},{3,35},{4,36},{5,37},{6,38},{7,39},{8,40},{9,... | collective-permute-start | bytes 1290248 | tf_op jit(solution)/shard_map/ppermute | solution.py:26
  63.2 14.1 %copy-start.1 = (f32[1,3,16,8,128]{4,3,2,1,0:T(8,128)S(1)}, f32[1,3,16,8,128]{4,3,2,1,0:T(8,128)}, u32[]{:S(2)}) copy-start(f32[1,3,16,8,128]{4,3,2,1,0:T(8,128)} %param.8) | copy-start | bytes 589828
  63.2 14.1 %copy-start.14 = (f32[1,16,8,128]{3,2,1,0:T(8,128)S(1)}, f32[1,16,8,128]{3,2,1,0:T(8,128)}, u32[]{:S(2)}) copy-start(f32[1,16,8,128]{3,2,1,0:T(8,128)} %param.9) | copy-start | bytes 196612
  63.2 14.0 %collective-permute-start.3 = (f32[7,5,24,128]{3,2,1,0:T(8,128)S(1)}, f32[7,5,24,128]{3,2,1,0:T(8,128)S(1)}, u32[]{:S(2)}, u32[]{:S(2)}) collective-permute-start(f32[7,5,24,128]{3,2,1,0:T(8,128)S(1)} %pad_maximum_fusion.2), channel_id=1, source_target_pairs={{32,0},{33,1},{34,2},{35,3},{36,4},{37,5},{38,6},{39,7},{40,8},{41... | collective-permute-start | bytes 1290248 | tf_op jit(solution)/shard_map/ppermute | solution.py:26
  78.4 0.7 copy-start.2
  79.1 0.8 copy-start.4
  79.8 0.7 copy-start.6
  80.6 0.7 copy-start.8
  81.3 0.7 copy-start.10
  82.0 0.7 copy-start.12
  82.8 1.0 copy-start.3
  83.7 1.0 copy-start.5
  84.7 1.0 copy-start.7
  85.7 1.0 copy-start.9
  86.7 1.0 copy-start.11
  87.7 1.0 copy-start.13
  93.0 14.1 %collective-permute-start.8 = (f32[10,8,128]{2,1,0:T(8,128)S(1)}, f32[10,8,128]{2,1,0:T(8,128)S(1)}, u32[]{:S(2)}, u32[]{:S(2)}) collective-permute-start(f32[10,8,128]{2,1,0:T(8,128)S(1)} %get-tuple-element.25), channel_id=1, source_target_pairs={{0,2},{1,3},{2,4},{3,5},{4,6},{5,7},{6,8},{7,9},{8,10},{9,11},{10,... | collective-permute-start | bytes 122888 | tf_op jit(solution)/shard_map/ppermute | solution.py:26
  96.7 15.9 %collective-permute-start.11 = (f32[10,8,128]{2,1,0:T(8,128)S(1)}, f32[10,8,128]{2,1,0:T(8,128)S(1)}, u32[]{:S(2)}, u32[]{:S(2)}) collective-permute-start(f32[10,8,128]{2,1,0:T(8,128)S(1)} %get-tuple-element.25), channel_id=1, source_target_pairs={{2,0},{3,1},{4,2},{5,3},{6,4},{7,5},{8,6},{9,7},{10,8},{11,9},{12,... | collective-permute-start | bytes 122888 | tf_op jit(solution)/shard_map/ppermute | solution.py:26
  101.2 11.4 %collective-permute-start.10 = (f32[10,8,128]{2,1,0:T(8,128)S(1)}, f32[10,8,128]{2,1,0:T(8,128)S(1)}, u32[]{:S(2)}, u32[]{:S(2)}) collective-permute-start(f32[10,8,128]{2,1,0:T(8,128)S(1)} %get-tuple-element.25), channel_id=1, source_target_pairs={{1,0},{2,1},{3,2},{4,3},{5,4},{6,5},{7,6},{8,7},{9,8},{10,9},{11,1... | collective-permute-start | bytes 122888 | tf_op jit(solution)/shard_map/ppermute | solution.py:26
  104.6 8.0 %collective-permute-start.9 = (f32[10,8,128]{2,1,0:T(8,128)S(1)}, f32[10,8,128]{2,1,0:T(8,128)S(1)}, u32[]{:S(2)}, u32[]{:S(2)}) collective-permute-start(f32[10,8,128]{2,1,0:T(8,128)S(1)} %get-tuple-element.25), channel_id=1, source_target_pairs={{0,1},{1,2},{2,3},{3,4},{4,5},{5,6},{6,7},{7,8},{8,9},{9,10},{10,1... | collective-permute-start | bytes 122888 | tf_op jit(solution)/shard_map/ppermute | solution.py:26
  112.7 7.8 %collective-permute-start.13 = (f32[10,40,128]{2,1,0:T(8,128)S(1)}, f32[10,40,128]{2,1,0:T(8,128)S(1)}, u32[]{:S(2)}, u32[]{:S(2)}) collective-permute-start(f32[10,40,128]{2,1,0:T(8,128)S(1)} %constant_dynamic-update-slice_fusion.mid_ref), channel_id=1, source_target_pairs={{32,0},{33,1},{34,2},{35,3},{36,4},{37,5},{38,6},{39,7},{40,8},{41... | collective-permute-start | bytes 614408 | tf_op jit(solution)/shard_map/ppermute | solution.py:26
  117.3 8.9 %collective-permute-start.12 = (f32[10,40,128]{2,1,0:T(8,128)S(1)}, f32[10,40,128]{2,1,0:T(8,128)S(1)}, u32[]{:S(2)}, u32[]{:S(2)}) collective-permute-start(f32[10,40,128]{2,1,0:T(8,128)S(1)} %constant_dynamic-update-slice_fusion.mid_ref), channel_id=1, source_target_pairs={{0,32},{1,33},{2,34},{3,35},{4,36},{5,37},{6,38},{7,39},{8,40},{9,... | collective-permute-start | bytes 614408 | tf_op jit(solution)/shard_map/ppermute | solution.py:26

commit v3 on v2

--- a/solution.py
+++ b/solution.py
@@ -4,6 +4,7 @@
 from jax.experimental import pallas as pl
 from jax.experimental.pallas import tpu as pltpu
 from jax.sharding import PartitionSpec as P
+
 
 AXES = ("patch", "lat", "lon")
 RELAX = 0.8
@@ -52,7 +53,7 @@
     rows = v_ref.shape[1]
     for comp in range(3):
         pad_ref[comp, :rows, 0:8] = v_ref[comp]
-        pad_ref[comp, rows, 0:8] = below_ref[comp]
+        pad_ref[comp, rows, 0:8] = below_ref[comp, 0]
         for row in range(rows):
             pad_ref[comp, row, 8:9] = right_ref[comp, row : row + 1]
         pad_ref[comp, rows, 8:9] = corner_ref[comp : comp + 1]
@@ -91,9 +92,48 @@
             copy(last_lat, position)
 
 
-def prepare_kernel(
+def pack_kernel(v_ref, f_ref, mu_ref, above_ref, below_ref, right_ref, left_ref):
+    sub = rows_of((8, 128))
+
+    def row(field, r):
+        if r < 0:
+            return above_ref[field, r + 5]
+        if r > 15:
+            return below_ref[field, r - 16]
+        if field == 6:
+            return mu_ref[r]
+        return v_ref[field, r] if field < 3 else f_ref[field - 3, r]
+
+    for field in range(7):
+        for t in range(12):
+            even, odd = row(field, 2 * t - 4), roll(row(field, 2 * t - 3), 4, 0)
+            right_ref[12 * field + t] = jnp.where(sub < 4, odd, even)
+            left_ref[12 * field + t] = jnp.where(sub < 4, even, odd)
+    for n, field in enumerate((0, 1, 2, 6)):
+        for j in range(2):
+            third = fourth = row(field, 8 * j)
+            for s in range(8):
+                value = row(field, 8 * j + s)
+                third = jnp.where(sub == s, roll(value, s - 3, 0), third)
+                fourth = jnp.where(sub == s, roll(value, s - 4, 0), fourth)
+            right_ref[84 + 2 * n + j] = third
+            left_ref[84 + 2 * n + j] = fourth
+
+
+def side_tile(ref, field, r, col, sub):
+    value = ref[12 * field + (r + 4) // 2]
+    if r % 2:
+        value = roll(value, 4, 0)
+    extra = {0: 0, 1: 1, 2: 2, 6: 3}.get(field)
+    if extra is None or not 0 <= r < 16:
+        return value
+    fifth = roll(ref[84 + 2 * extra + r // 8], col - r % 8, 0)
+    return jnp.where(sub == col, fifth, value)
+
+
+def prepare(
     place_ref, f_ref, mu_ref, left_ref, right_ref, above_ref, below_ref,
-    F, CN, CS, CW, CE, CD, CU, DG, over_ref, visc_ref, MU,
+    F, C, DG, over_ref, visc_ref, MU,
 ):
     lat, lon = place_ref[0], place_ref[1]
     last_lat, last_lon = place_ref[2], place_ref[3]
@@ -101,11 +141,16 @@
     lane, row = lanes_of(wide), rows_of(wide)
     odd_lane, odd_row = (lane & 1) == 1, (row & 1) == 1
     own = slice(PAD, PAD + 16)
-    MU[own, 0:8] = left_ref[6]
+    sub = rows_of((8, 128))
     MU[own, 8:16] = mu_ref[...]
-    MU[own, 16:24] = right_ref[6]
-    MU[1:6] = above_ref[6]
-    MU[22:27] = below_ref[6]
+    MU[1:6, 8:16] = above_ref[6]
+    MU[22:27, 8:16] = below_ref[6]
+    for r in range(-4, 20):
+        MU[r + PAD, 0:8] = side_tile(left_ref, 6, r, 3, sub)
+        MU[r + PAD, 16:24] = side_tile(right_ref, 6, r, 4, sub)
+    for i in (1, 26):
+        MU[i, 0:8] = MU[i, 8:16]
+        MU[i, 16:24] = MU[i, 8:16]
 
     @pl.when(lat == 0)
     def _():
@@ -137,25 +182,23 @@
         up = 0.5 * (mid + jnp.where(lane == 127, mid, roll(mid, -1, 1)))
         total = north + south + west + east + down + up
         inverse = 1.0 / total
-        CN[i] = north * inverse
-        CS[i] = south * inverse
-        CW[i] = west * inverse
-        CE[i] = east * inverse
-        CD[i] = jnp.where(lane == 0, 0.0, down * inverse)
-        CU[i] = jnp.where(lane == 127, 0.0, up * inverse)
-        if PAD <= i < PAD + 16:
-            DG[i - PAD] = total[8:16]
+        C[0, i] = north * inverse
+        C[1, i] = south * inverse
+        C[2, i] = west * inverse
+        C[3, i] = east * inverse
+        C[4, i] = jnp.where(lane == 0, 0.0, down * inverse)
+        C[5, i] = jnp.where(lane == 127, 0.0, up * inverse)
+        r = i - PAD
+        if 0 <= r < 16:
+            DG[r] = total[8:16]
         for comp in range(3):
-            if i < PAD:
-                force = above_ref[3 + comp, i - 1]
-                F[comp, i] = force * inverse
-            elif i >= PAD + 16:
-                force = below_ref[3 + comp, i - PAD - 16]
-                F[comp, i] = force * inverse
+            if r < 0:
+                force = above_ref[3 + comp, r + 5]
             else:
-                F[comp, i, 0:8] = left_ref[3 + comp, i - PAD] * inverse[0:8]
-                F[comp, i, 8:16] = f_ref[comp, i - PAD] * inverse[8:16]
-                F[comp, i, 16:24] = right_ref[3 + comp, i - PAD] * inverse[16:24]
+                force = f_ref[comp, r] if r < 16 else below_ref[3 + comp, r - 16]
+            F[comp, i, 8:16] = force * inverse[8:16]
+            F[comp, i, 0:8] = side_tile(left_ref, 3 + comp, r, 3, sub) * inverse[0:8]
+            F[comp, i, 16:24] = side_tile(right_ref, 3 + comp, r, 4, sub) * inverse[16:24]
 
     def coarse_visc(i):
         both = MU[i] + MU[i + 1]
@@ -176,22 +219,26 @@
 
 
 def smooth_kernel(
-    place_ref, ghost_ref, v_ref, left_ref, right_ref, above_ref, below_ref, slot_ref,
-    F, CN, CS, CW, CE, CD, CU, DG, over_ref, visc_ref,
-    res_ref, smooth_ref, message_ref, A, B,
+    place_ref, ghost_ref, v_ref, f_ref, mu_ref, left_ref, right_ref, above_ref, below_ref, slot_ref,
+    res_ref, smooth_ref, message_ref, A, B, F, C, DG, over_ref, visc_ref, MU,
 ):
     lat, lon = place_ref[0], place_ref[1]
     last_lat, last_lon = place_ref[2], place_ref[3]
     wide = (24, 128)
     lane, row = lanes_of(wide), rows_of(wide)
+    sub = rows_of((8, 128))
     own = slice(PAD, PAD + 16)
 
     for comp in range(3):
-        A[comp, own, 0:8] = left_ref[comp]
         A[comp, own, 8:16] = v_ref[comp]
-        A[comp, own, 16:24] = right_ref[comp]
-        A[comp, 1:6] = above_ref[comp]
-        A[comp, 22:27] = below_ref[comp]
+        A[comp, 1:6, 8:16] = above_ref[comp]
+        A[comp, 22:27, 8:16] = below_ref[comp]
+        for r in range(-4, 20):
+            A[comp, r + PAD, 0:8] = side_tile(left_ref, comp, r, 3, sub)
+            A[comp, r + PAD, 16:24] = side_tile(right_ref, comp, r, 4, sub)
+        for i in (1, 26):
+            A[comp, i, 0:8] = A[comp, i, 8:16]
+            A[comp, i, 16:24] = A[comp, i, 8:16]
 
     edge = (lon == 0) | (lon == last_lon)
     all_cols, all_rows = (last_lon + 1) * 8, (last_lat + 1) * 16
@@ -212,6 +259,10 @@
             for comp in range(3):
                 A[comp, r + PAD, 8 + col : 9 + col] = slot_ref[base + comp]
 
+    prepare(
+        place_ref, f_ref, mu_ref, left_ref, right_ref, above_ref, below_ref,
+        F, C, DG, over_ref, visc_ref, MU,
+    )
     pl.when(lat == 0)(lambda: fill_row(5, 0))
     pl.when(lat == last_lat)(lambda: fill_row(22, all_cols))
     pl.when(lon == 0)(lambda: fill_side(-1, 2 * all_cols))
@@ -221,12 +272,12 @@
     parity = jnp.where(inside, (row + lane) & 1, 2)
 
     def weighted(source, comp, i, here):
-        total = F[comp, i] + CN[i] * source[comp, i - 1]
-        total = total + CS[i] * source[comp, i + 1]
-        total = total + CW[i] * roll(here, 1, 0)
-        total = total + CE[i] * roll(here, -1, 0)
-        total = total + CD[i] * roll(here, 1, 1)
-        return total + CU[i] * roll(here, -1, 1)
+        total = F[comp, i] + C[0, i] * source[comp, i - 1]
+        total = total + C[1, i] * source[comp, i + 1]
+        total = total + C[2, i] * roll(here, 1, 0)
+        total = total + C[3, i] * roll(here, -1, 0)
+        total = total + C[4, i] * roll(here, 1, 1)
+        return total + C[5, i] * roll(here, -1, 1)
 
     wanted = {}
     for colour in range(2):
@@ -288,16 +339,26 @@
         keep = odd_r if part // 2 else ~odd_r
         return jnp.where(keep, value, roll(value, -1 if part // 2 else 1, 0))
 
-    for n in range(22):
-        ref, t = (above_ref, n + 1) if n < 7 else (mid_ref, n - 7) if n < 15 else (below_ref, n - 15)
-        value = ref[t]
-        Q[n] = value
-        CV[n] = spread(value, 3, odd_lane, odd_row)
-        if 1 <= n <= 20:
-            DV[n] = 0.125 * spread(ref[8 + t // 4], t % 4, odd_lane, odd_row)
-
     def far(n):
         return max(0, 7 - n, n - 14)
+
+    for n in range(22):
+        away = far(n)
+        if away == 0:
+            t = n - 7
+            Q[n] = mid_ref[t]
+            cols, over = slice(0, 40), mid_ref[8 + t // 4]
+        else:
+            ref, t = (above_ref, n + 1) if n < 7 else (below_ref, n - 15)
+            tiles = range(5) if away < 3 else range(1, 4)
+            first = 5 * (away - 1) if away < 3 else 10 + 3 * (away - 3) - 1
+            for j in tiles:
+                Q[n, 8 * j : 8 * j + 8] = ref[first + j]
+            cols = slice(8 * tiles[0], 8 * tiles[-1] + 8)
+            over = [ref[25 + 5 * (t // 4) + j] for j in tiles]
+            over = jnp.concatenate(over, axis=0)
+        CV[n, cols] = spread(Q[n, cols], 3, odd_lane[cols], odd_row[cols])
+        DV[n, cols] = 0.125 * spread(over, t % 4, odd_lane[cols], odd_row[cols])
 
     def span(reach):
         return slice(0, 40) if reach > 3 else slice(8, 32)
@@ -368,8 +429,11 @@
     cells = wanted_cells(lats, lons, lax.axis_index("lon")).reshape(-1)
 
     corner_right = shifted(v[:, :, 0], 0, -1)
-    corner_below = shifted(v[:, 0], -1, 0)
     corner_both = shifted(v[:, 0, 0], -1, -1)
+    top = jnp.concatenate([v[:, :5], f[:, :5], mu[None, :5]], axis=0)
+    low = jnp.concatenate([v[:, 11:], f[:, 11:], mu[None, 11:]], axis=0)
+    below = shifted(top, -1, 0)
+    above = shifted(low, 1, 0)
     values = pl.pallas_call(
         interp_kernel,
         out_shape=jax.ShapeDtypeStruct((9, 128), f32),
@@ -380,21 +444,24 @@
         name="interp",
     )(
         corner_rows[0, 0], corner_cols[0, 0], corner_weights[0, 0],
-        v, corner_right, corner_below, corner_both,
+        v, corner_right, below, corner_both,
     )
     values = lax.ppermute(values, "patch", [(0, 1), (1, 0)])
-
-    own = jnp.concatenate([v, f, mu[None]], axis=0)
-    left = shifted(own, 0, 1)
-    right = shifted(own, 0, -1)
-    ext_top = jnp.concatenate([left[:, :5], own[:, :5], right[:, :5]], axis=2)
-    ext_low = jnp.concatenate([left[:, 11:], own[:, 11:], right[:, 11:]], axis=2)
-    below = shifted(ext_top, -1, 0)
-    above = shifted(ext_low, 1, 0)
-
-    around = lax.all_to_all(
-        jnp.broadcast_to(values[None], (lons, 9, 128)), "lon", 0, 0, tiled=True
-    )
+    spread = jnp.broadcast_to(values.reshape(1, 1, 1152), (lons, 1, 1152))
+    around = lax.all_to_all(spread, "lon", 0, 0, tiled=True)
+
+    message_tiles = jax.ShapeDtypeStruct((92, 8, 128), f32)
+    to_right, to_left = pl.pallas_call(
+        pack_kernel,
+        out_shape=(message_tiles, message_tiles),
+        in_specs=[VMEM] * 5,
+        out_specs=(VMEM, VMEM),
+        compiler_params=params,
+        name="pack",
+    )(v, f, mu, above, below)
+    left = shifted(to_right, 0, 1)
+    right = shifted(to_left, 0, -1)
+
     chosen = pl.pallas_call(
         pick_kernel,
         out_shape=jax.ShapeDtypeStruct((lats * 3 * CELLS, 1, 128), f32),
@@ -408,27 +475,19 @@
 
     block = jax.ShapeDtypeStruct((3, 16, 8, 128), f32)
     field = (3, 28, 24, 128)
-    plane = jax.ShapeDtypeStruct((28, 24, 128), f32)
-    half = jax.ShapeDtypeStruct((8, 8, 128), f32)
-    prepared = pl.pallas_call(
-        prepare_kernel,
-        out_shape=[jax.ShapeDtypeStruct(field, f32)] + [plane] * 6
-        + [jax.ShapeDtypeStruct((16, 8, 128), f32), half, half],
-        in_specs=[SMEM] + [VMEM] * 6,
-        out_specs=[VMEM] * 10,
-        scratch_shapes=[pltpu.VMEM((28, 24, 128), f32)],
-        compiler_params=params,
-        name="prepare",
-    )(place, f, mu, left, right, above, below)
     residual, smoothed, message = pl.pallas_call(
         smooth_kernel,
         out_shape=(block, block, jax.ShapeDtypeStruct((10, 8, 128), f32)),
-        in_specs=[SMEM, SMEM] + [VMEM] * 16,
+        in_specs=[SMEM, SMEM] + [VMEM] * 8,
         out_specs=(VMEM, VMEM, VMEM),
-        scratch_shapes=[pltpu.VMEM(field, f32)] * 2,
+        scratch_shapes=[pltpu.VMEM(field, f32)] * 3
+        + [
+            pltpu.VMEM(shape, f32)
+            for shape in ((6, 28, 24, 128), (16, 8, 128), (8, 8, 128), (8, 8, 128), (28, 24, 128))
+        ],
         compiler_params=params,
         name="smooth",
-    )(place, ghost_rows, v, left, right, above, below, everything, *prepared)
+    )(place, ghost_rows, v, f, mu, left, right, above, below, everything)
 
     tiles = [
         shifted(message, 0, 2),
@@ -438,8 +497,13 @@
         shifted(message, 0, -2),
     ]
     band = jnp.concatenate(tiles, axis=1)
-    band_below = shifted(band, -1, 0)
-    band_above = shifted(band, 1, 0)
+    tile_list = (-1, 8, 128)
+    inverse = band[8:10].reshape(tile_list)
+    to_above = [band[0:2].reshape(tile_list), band[2:7, 8:32].reshape(tile_list), inverse]
+    to_below = [band[7:8], band[6:7]] + [band[r : r + 1, 8:32] for r in (5, 4, 3, 2, 1)]
+    to_below = [part.reshape(tile_list) for part in to_below] + [inverse]
+    band_below = shifted(jnp.concatenate(to_above, axis=0), -1, 0)
+    band_above = shifted(jnp.concatenate(to_below, axis=0), 1, 0)
     coarse = pltpu.VMEM((22, 40, 128), f32)
     new = pl.pallas_call(
         coarse_kernel,

time: 129 us -> 121 us (0.938)
  the two profiles are of different devices: /device:TPU:96 before, /device:TPU:88 now
where the time goes in v3:
time: 121 us; the launch traced here: 120 us
  starting transfers between devices  64.1 us (53%)
  waiting for transfers between devices  40.1 us (33%)
  Pallas kernels  8.77 us (7%)
  local copies, waits for them, and re-layouts  5.97 us (5%)
    ppermute x12, starting transfers between devices, shifted(): return lax.ppermute(value, AXES, pairs)  44.3 us
    ppermute x12, waiting for transfers between devices, shifted(): return lax.ppermute(value, AXES, pairs)  28.9 us
    all_to_all x1, starting transfers between devices, per_device(): around = lax.all_to_all(spread, 'lon', 0, 0, tiled=True)  11.7 us
    all_to_all x1, waiting for transfers between devices, per_device(): around = lax.all_to_all(spread, 'lon', 0, 0, tiled=True)  10.2 us
    all_to_all x1, starting transfers between devices, per_device(): lax.all_to_all(chosen.reshape(lats, 3 * CELLS, 128), 'lat', 0, 0, tiled=T...  6.22 us
    pallas_call x1, Pallas kernels, per_device(): pl.pallas_call(smooth_kernel, out_shape=(block, block, jax.ShapeDtypeStru...  4.72 us
  transfers between devices with their start and end apart: 15, of which 9 were waited for; matrix products, arithmetic and copies ran while one was open for 2% of the time, Pallas kernels for 0%

profile of v3, /device:TPU:88, one launch (start us, length us, event | category | flops | bytes accessed | tf_op | source)
XLA Modules:
  0.0 120.5 jit_solution(2221562240552404490)
XLA Ops:
  0.6 0.0 copy-start.1
  0.6 0.7 slice.85
  1.4 3.6 %collective-permute-start.5 = (f32[3,128]{1,0:T(4,128)S(1)}, f32[3,128]{1,0:T(4,128)S(1)}, u32[]{:S(2)}, u32[]{:S(2)}) collective-permute-start(f32[3,128]{1,0:T(4,128)S(1)} %bitcast.72), channel_id=1, source_target_pairs={{33,0},{34,1},{35,2},{36,3},{37,4},{38,5},{39,6},{40,7},{41,8},{42... | collective-permute-start | bytes 4616 | tf_op jit(solution)/shard_map/ppermute | solution.py:27
  5.0 0.9 slice.84
  6.0 0.0 copy-start.2
  6.0 2.9 %collective-permute-start.4 = (f32[3,16,128]{2,1,0:T(8,128)S(1)}, f32[3,16,128]{2,1,0:T(8,128)S(1)}, u32[]{:S(2)}, u32[]{:S(2)}) collective-permute-start(f32[3,16,128]{2,1,0:T(8,128)S(1)} %bitcast.70), channel_id=1, source_target_pairs={{1,0},{2,1},{3,2},{4,3},{5,4},{6,5},{7,6},{8,7},{9,8},{10,9},{11,1... | collective-permute-start | bytes 73736 | tf_op jit(solution)/shard_map/ppermute | solution.py:27
  8.9 0.9 fusion.10
  9.7 0.0 copy-done.2
  9.8 0.0 copy-done.1
  9.8 0.0 copy-start
  9.8 2.5 %collective-permute-start.1 = (f32[7,5,8,128]{3,2,1,0:T(8,128)S(1)}, f32[7,5,8,128]{3,2,1,0:T(8,128)S(1)}, u32[]{:S(2)}, u32[]{:S(2)}) collective-permute-start(f32[7,5,8,128]{3,2,1,0:T(8,128)S(1)} %pad_maximum_fusion.1), channel_id=1, source_target_pairs={{32,0},{33,1},{34,2},{35,3},{36,4},{37,5},{38,6},{39,7},{40,8},{41... | collective-permute-start | bytes 430088 | tf_op jit(solution)/shard_map/ppermute | solution.py:27
  12.4 0.1 fusion.8
  12.5 0.1 reshape.139
  12.6 0.1 iota_select_fusion
  12.7 0.1 select_n.73
  12.7 0.1 clamp_add_fusion
  12.8 0.1 reshape.138
  12.9 0.1 add.104
  13.0 0.1 add.105
  13.0 0.1 broadcast_in_dim.52
  13.1 0.0 copy-start.5
  13.1 0.7 copy-done.5
  13.8 0.0 copy-start.6
  13.9 0.6 copy-done.6
  14.5 0.1 copy.10
  14.6 0.0 collective-permute-done.5.corner_ref
  14.6 0.0 collective-permute-done.4.right_ref
  14.6 3.6 %collective-permute-done.1.below_ref = f32[7,5,8,128]{3,2,1,0:T(8,128)S(1)} collective-permute-done((f32[7,5,8,128]{3,2,1,0:T(8,128)S(1)}, f32[7,5,8,128]{3,2,1,0:T(8,128)S(1)}, u32[]{:S(2)}, u32[]{:S(2)}) %collective-permute-start.1) | collective-permute-done | bytes 143392 | tf_op jit(solution)/shard_map/ppermute | solution.py:27
  18.2 0.0 copy-start.3
  18.2 0.0 copy-start.4
  18.2 0.0 copy-done
  18.2 0.6 copy-done.3
  18.8 0.0 copy-done.4
  18.8 0.6 interp.1
  19.5 1.9 %collective-permute-start.6 = (f32[9,128]{1,0:T(8,128)S(1)}, f32[9,128]{1,0:T(8,128)S(1)}, u32[]{:S(2)}, u32[]{:S(2)}) collective-permute-start(f32[9,128]{1,0:T(8,128)S(1)} %interp.1), channel_id=1, source_target_pairs={{0,256},{256,0},{1,257},{257,1},{2,258},{258,2},{3,259},{259,3},{4... | collective-permute-start | bytes 13832 | tf_op jit(solution)/shard_map/ppermute | solution.py:449
  21.4 1.1 collective-permute-done.6
  22.5 0.7 broadcast_in_dim.54
  23.3 11.7 %all-to-all-start = ((f32[32,1,1152]{2,1,0:T(1,128)}), f32[32,1,1152]{2,1,0:T(1,128)S(1)}, u32[]{:S(2)}, u32[]{:S(2)}) async-start(f32[32,1,1152]{2,1,0:T(1,128)} %broadcast_in_dim.54), calls=%async_computation | async-start | bytes 294912 | tf_op jit(solution)/shard_map/all_to_all | solution.py:451
  34.9 0.1 pad_add_fusion.place_ref
  35.0 10.2 %all-to-all-done = f32[32,1,1152]{2,1,0:T(1,128)S(1)} async-done(((f32[32,1,1152]{2,1,0:T(1,128)}), f32[32,1,1152]{2,1,0:T(1,128)S(1)}, u32[]{:S(2)}, u32[]{:S(2)}) %all-to-all-start) | async-done | bytes 147488 | tf_op jit(solution)/shard_map/all_to_all | solution.py:451
  45.2 1.4 %pick.1 = f32[768,1,128]{2,1,0:T(1,128)} custom-call(s32[4]{0:T(128)S(1)} %pad_add_fusion.place_ref, s32[256]{0:T(256)S(1)} %add_select_fusion.4.cells_ref, s32[768]{0:T(1024)S(1)} %get-tuple-element.31.source_ref, f32[288,1,128]{2,1,0:T(1,128)S(1)} %bitcast.59), custom_call_target="tpu_custom_call" | custom-call | tf_op jit(solution)/shard_map/pick/pallas_call | solution.py:465
  46.6 6.2 %all-to-all-start.1 = ((f32[8,96,128]{2,1,0:T(8,128)}), f32[8,96,128]{2,1,0:T(8,128)S(1)}, u32[]{:S(2)}, u32[]{:S(2)}) async-start(f32[8,96,128]{2,1,0:T(8,128)} %bitcast.11), calls=%async_computation.1 | async-start | bytes 786432 | tf_op jit(solution)/shard_map/all_to_all | solution.py:473
  52.8 4.6 %collective-permute-start = (f32[7,5,8,128]{3,2,1,0:T(8,128)S(1)}, f32[7,5,8,128]{3,2,1,0:T(8,128)S(1)}, u32[]{:S(2)}, u32[]{:S(2)}) collective-permute-start(f32[7,5,8,128]{3,2,1,0:T(8,128)S(1)} %pad_maximum_fusion), channel_id=1, source_target_pairs={{0,32},{1,33},{2,34},{3,35},{4,36},{5,37},{6,38},{7,39},{8,40},{9,... | collective-permute-start | bytes 430088 | tf_op jit(solution)/shard_map/ppermute | solution.py:27
  57.4 6.0 %collective-permute-done.above_ref = f32[7,5,8,128]{3,2,1,0:T(8,128)S(1)} collective-permute-done((f32[7,5,8,128]{3,2,1,0:T(8,128)S(1)}, f32[7,5,8,128]{3,2,1,0:T(8,128)S(1)}, u32[]{:S(2)}, u32[]{:S(2)}) %collective-permute-start) | collective-permute-done | bytes 143392 | tf_op jit(solution)/shard_map/ppermute | solution.py:27
  63.4 0.1 pack.1
  63.5 2.7 %collective-permute-start.2 = (f32[92,8,128]{2,1,0:T(8,128)S(1)}, f32[92,8,128]{2,1,0:T(8,128)S(1)}, u32[]{:S(2)}, u32[]{:S(2)}) collective-permute-start(f32[92,8,128]{2,1,0:T(8,128)S(1)} %get-tuple-element.7), channel_id=1, source_target_pairs={{0,1},{1,2},{2,3},{3,4},{4,5},{5,6},{6,7},{7,8},{8,9},{9,10},{10,1... | collective-permute-start | bytes 1130504 | tf_op jit(solution)/shard_map/ppermute | solution.py:27
  66.2 5.2 %collective-permute-start.3 = (f32[92,8,128]{2,1,0:T(8,128)S(1)}, f32[92,8,128]{2,1,0:T(8,128)S(1)}, u32[]{:S(2)}, u32[]{:S(2)}) collective-permute-start(f32[92,8,128]{2,1,0:T(8,128)S(1)} %get-tuple-element.8), channel_id=1, source_target_pairs={{1,0},{2,1},{3,2},{4,3},{5,4},{6,5},{7,6},{8,7},{9,8},{10,9},{11,1... | collective-permute-start | bytes 1130504 | tf_op jit(solution)/shard_map/ppermute | solution.py:27
  71.5 5.8 %collective-permute-done.2.left_ref = f32[92,8,128]{2,1,0:T(8,128)S(1)} collective-permute-done((f32[92,8,128]{2,1,0:T(8,128)S(1)}, f32[92,8,128]{2,1,0:T(8,128)S(1)}, u32[]{:S(2)}, u32[]{:S(2)}) %collective-permute-start.2) | collective-permute-done | bytes 376864 | tf_op jit(solution)/shard_map/ppermute | solution.py:27
  77.2 1.2 collective-permute-done.3.right_ref
  78.4 0.0 all-to-all-done.1
  78.4 4.7 %smooth.1 = (f32[3,16,8,128]{3,2,1,0:T(8,128)}, f32[3,16,8,128]{3,2,1,0:T(8,128)S(1)}, f32[10,8,128]{2,1,0:T(8,128)S(1)}) custom-call(s32[4]{0:T(128)S(1)} %pad_add_fusion.place_ref, s32[768]{0:T(1024)S(1)} %get-tuple-element.32.ghost_ref, f32[3,16,8,128]{3,2,1,0:T(8,128)S(1)} %bitcast.54, f32[3,16,8,128]{3,2,1,0:T(8,128)S(1)} %bitcast.58, ...), custom_call_target="tpu_custom_call" | custom-call | tf_op jit(solution)/shard_map/smooth/pallas_call | solution.py:478
  83.1 4.0 %collective-permute-start.7 = (f32[10,8,128]{2,1,0:T(8,128)S(1)}, f32[10,8,128]{2,1,0:T(8,128)S(1)}, u32[]{:S(2)}, u32[]{:S(2)}) collective-permute-start(f32[10,8,128]{2,1,0:T(8,128)S(1)} %get-tuple-element.9), channel_id=1, source_target_pairs={{0,2},{1,3},{2,4},{3,5},{4,6},{5,7},{6,8},{7,9},{8,10},{9,11},{10,... | collective-permute-start | bytes 122888 | tf_op jit(solution)/shard_map/ppermute | solution.py:27
  87.1 4.2 %collective-permute-start.10 = (f32[10,8,128]{2,1,0:T(8,128)S(1)}, f32[10,8,128]{2,1,0:T(8,128)S(1)}, u32[]{:S(2)}, u32[]{:S(2)}) collective-permute-start(f32[10,8,128]{2,1,0:T(8,128)S(1)} %get-tuple-element.9), channel_id=1, source_target_pairs={{2,0},{3,1},{4,2},{5,3},{6,4},{7,5},{8,6},{9,7},{10,8},{11,9},{12,... | collective-permute-start | bytes 122888 | tf_op jit(solution)/shard_map/ppermute | solution.py:27
  91.4 5.6 %collective-permute-start.9 = (f32[10,8,128]{2,1,0:T(8,128)S(1)}, f32[10,8,128]{2,1,0:T(8,128)S(1)}, u32[]{:S(2)}, u32[]{:S(2)}) collective-permute-start(f32[10,8,128]{2,1,0:T(8,128)S(1)} %get-tuple-element.9), channel_id=1, source_target_pairs={{1,0},{2,1},{3,2},{4,3},{5,4},{6,5},{7,6},{8,7},{9,8},{10,9},{11,1... | collective-permute-start | bytes 122888 | tf_op jit(solution)/shard_map/ppermute | solution.py:27
  97.0 1.9 %collective-permute-start.8 = (f32[10,8,128]{2,1,0:T(8,128)S(1)}, f32[10,8,128]{2,1,0:T(8,128)S(1)}, u32[]{:S(2)}, u32[]{:S(2)}) collective-permute-start(f32[10,8,128]{2,1,0:T(8,128)S(1)} %get-tuple-element.9), channel_id=1, source_target_pairs={{0,1},{1,2},{2,3},{3,4},{4,5},{5,6},{6,7},{7,8},{8,9},{9,10},{10,1... | collective-permute-start | bytes 122888 | tf_op jit(solution)/shard_map/ppermute | solution.py:27
  98.9 0.0 collective-permute-done.7
  98.9 6.1 %collective-permute-done.8 = f32[10,8,128]{2,1,0:T(8,128)S(1)} collective-permute-done((f32[10,8,128]{2,1,0:T(8,128)S(1)}, f32[10,8,128]{2,1,0:T(8,128)S(1)}, u32[]{:S(2)}, u32[]{:S(2)}) %collective-permute-start.8) | collective-permute-done | bytes 40992 | tf_op jit(solution)/shard_map/ppermute | solution.py:27
  105.0 0.0 collective-permute-done.9
  105.0 0.0 collective-permute-done.10
  105.2 5.1 %collective-permute-start.11 = (f32[35,8,128]{2,1,0:T(8,128)S(1)}, f32[35,8,128]{2,1,0:T(8,128)S(1)}, u32[]{:S(2)}, u32[]{:S(2)}) collective-permute-start(f32[35,8,128]{2,1,0:T(8,128)S(1)} %constant_dynamic-update-slice_fusion.8), channel_id=1, source_target_pairs={{0,32},{1,33},{2,34},{3,35},{4,36},{5,37},{6,38},{7,39},{8,40},{9,... | collective-permute-start | bytes 430088 | tf_op jit(solution)/shard_map/ppermute | solution.py:27
  110.3 1.9 %collective-permute-start.12 = (f32[35,8,128]{2,1,0:T(8,128)S(1)}, f32[35,8,128]{2,1,0:T(8,128)S(1)}, u32[]{:S(2)}, u32[]{:S(2)}) collective-permute-start(f32[35,8,128]{2,1,0:T(8,128)S(1)} %pad_maximum_fusion.2), channel_id=1, source_target_pairs={{32,0},{33,1},{34,2},{35,3},{36,4},{37,5},{38,6},{39,7},{40,8},{41... | collective-permute-start | bytes 430088 | tf_op jit(solution)/shard_map/ppermute | solution.py:27
  112.2 0.7 collective-permute-done.11.above_ref
  112.9 5.6 %collective-permute-done.12.below_ref = f32[35,8,128]{2,1,0:T(8,128)S(1)} collective-permute-done((f32[35,8,128]{2,1,0:T(8,128)S(1)}, f32[35,8,128]{2,1,0:T(8,128)S(1)}, u32[]{:S(2)}, u32[]{:S(2)}) %collective-permute-start.12) | collective-permute-done | bytes 143392 | tf_op jit(solution)/shard_map/ppermute | solution.py:27
  118.5 1.9 %coarse.1 = f32[3,16,8,128]{3,2,1,0:T(8,128)} custom-call(f32[10,40,128]{2,1,0:T(8,128)S(1)} %constant_dynamic-update-slice_fusion.mid_ref, f32[35,8,128]{2,1,0:T(8,128)S(1)} %collective-permute-done.11.above_ref, f32[35,8,128]{2,1,0:T(8,128)S(1)} %collective-permute-done.12.below_ref, f32[3,16,8,128]{3,2,1,0:T(8,128)S(1)} %get-tuple-element.10.smooth_ref), custom_call_target="tpu_custom_call" | custom-call | tf_op jit(solution)/shard_map/coarse/pallas_call | solution.py:508
  (33 shorter events, 0.3 us)
Async XLA Ops:
  0.6 9.1 %copy-start.1 = (f32[1,3,16,8,128]{4,3,2,1,0:T(8,128)S(1)}, f32[1,3,16,8,128]{4,3,2,1,0:T(8,128)}, u32[]{:S(2)}) copy-start(f32[1,3,16,8,128]{4,3,2,1,0:T(8,128)} %param.8) | copy-start | bytes 589828
  1.4 13.2 %collective-permute-start.5 = (f32[3,128]{1,0:T(4,128)S(1)}, f32[3,128]{1,0:T(4,128)S(1)}, u32[]{:S(2)}, u32[]{:S(2)}) collective-permute-start(f32[3,128]{1,0:T(4,128)S(1)} %bitcast.72), channel_id=1, source_target_pairs={{33,0},{34,1},{35,2},{36,3},{37,4},{38,5},{39,6},{40,7},{41,8},{42... | collective-permute-start | bytes 4616 | tf_op jit(solution)/shard_map/ppermute | solution.py:27
  6.0 3.8 %copy-start.2 = (f32[1,16,8,128]{3,2,1,0:T(8,128)S(1)}, f32[1,16,8,128]{3,2,1,0:T(8,128)}, u32[]{:S(2)}) copy-start(f32[1,16,8,128]{3,2,1,0:T(8,128)} %param.9) | copy-start | bytes 196612
  6.0 8.6 %collective-permute-start.4 = (f32[3,16,128]{2,1,0:T(8,128)S(1)}, f32[3,16,128]{2,1,0:T(8,128)S(1)}, u32[]{:S(2)}, u32[]{:S(2)}) collective-permute-start(f32[3,16,128]{2,1,0:T(8,128)S(1)} %bitcast.70), channel_id=1, source_target_pairs={{1,0},{2,1},{3,2},{4,3},{5,4},{6,5},{7,6},{8,7},{9,8},{10,9},{11,1... | collective-permute-start | bytes 73736 | tf_op jit(solution)/shard_map/ppermute | solution.py:27
  9.8 8.4 %copy-start = (f32[1,3,16,8,128]{4,3,2,1,0:T(8,128)S(1)}, f32[1,3,16,8,128]{4,3,2,1,0:T(8,128)}, u32[]{:S(2)}) copy-start(f32[1,3,16,8,128]{4,3,2,1,0:T(8,128)} %param.7) | copy-start | bytes 589828
  9.8 8.3 %collective-permute-start.1 = (f32[7,5,8,128]{3,2,1,0:T(8,128)S(1)}, f32[7,5,8,128]{3,2,1,0:T(8,128)S(1)}, u32[]{:S(2)}, u32[]{:S(2)}) collective-permute-start(f32[7,5,8,128]{3,2,1,0:T(8,128)S(1)} %pad_maximum_fusion.1), channel_id=1, source_target_pairs={{32,0},{33,1},{34,2},{35,3},{36,4},{37,5},{38,6},{39,7},{40,8},{41... | collective-permute-start | bytes 430088 | tf_op jit(solution)/shard_map/ppermute | solution.py:27
  13.1 0.7 copy-start.5
  13.8 0.7 copy-start.6
  18.2 0.7 copy-start.3
  18.2 0.7 copy-start.4
  19.5 3.1 %collective-permute-start.6 = (f32[9,128]{1,0:T(8,128)S(1)}, f32[9,128]{1,0:T(8,128)S(1)}, u32[]{:S(2)}, u32[]{:S(2)}) collective-permute-start(f32[9,128]{1,0:T(8,128)S(1)} %interp.1), channel_id=1, source_target_pairs={{0,256},{256,0},{1,257},{257,1},{2,258},{258,2},{3,259},{259,3},{4... | collective-permute-start | bytes 13832 | tf_op jit(solution)/shard_map/ppermute | solution.py:449
  23.3 21.9 %all-to-all-start = ((f32[32,1,1152]{2,1,0:T(1,128)}), f32[32,1,1152]{2,1,0:T(1,128)S(1)}, u32[]{:S(2)}, u32[]{:S(2)}) async-start(f32[32,1,1152]{2,1,0:T(1,128)} %broadcast_in_dim.54), calls=%async_computation | async-start | bytes 294912 | tf_op jit(solution)/shard_map/all_to_all | solution.py:451
  46.6 31.8 %all-to-all-start.1 = ((f32[8,96,128]{2,1,0:T(8,128)}), f32[8,96,128]{2,1,0:T(8,128)S(1)}, u32[]{:S(2)}, u32[]{:S(2)}) async-start(f32[8,96,128]{2,1,0:T(8,128)} %bitcast.11), calls=%async_computation.1 | async-start | bytes 786432 | tf_op jit(solution)/shard_map/all_to_all | solution.py:473
  52.8 10.6 %collective-permute-start = (f32[7,5,8,128]{3,2,1,0:T(8,128)S(1)}, f32[7,5,8,128]{3,2,1,0:T(8,128)S(1)}, u32[]{:S(2)}, u32[]{:S(2)}) collective-permute-start(f32[7,5,8,128]{3,2,1,0:T(8,128)S(1)} %pad_maximum_fusion), channel_id=1, source_target_pairs={{0,32},{1,33},{2,34},{3,35},{4,36},{5,37},{6,38},{7,39},{8,40},{9,... | collective-permute-start | bytes 430088 | tf_op jit(solution)/shard_map/ppermute | solution.py:27
  63.5 13.7 %collective-permute-start.2 = (f32[92,8,128]{2,1,0:T(8,128)S(1)}, f32[92,8,128]{2,1,0:T(8,128)S(1)}, u32[]{:S(2)}, u32[]{:S(2)}) collective-permute-start(f32[92,8,128]{2,1,0:T(8,128)S(1)} %get-tuple-element.7), channel_id=1, source_target_pairs={{0,1},{1,2},{2,3},{3,4},{4,5},{5,6},{6,7},{7,8},{8,9},{9,10},{10,1... | collective-permute-start | bytes 1130504 | tf_op jit(solution)/shard_map/ppermute | solution.py:27
  66.2 12.2 %collective-permute-start.3 = (f32[92,8,128]{2,1,0:T(8,128)S(1)}, f32[92,8,128]{2,1,0:T(8,128)S(1)}, u32[]{:S(2)}, u32[]{:S(2)}) collective-permute-start(f32[92,8,128]{2,1,0:T(8,128)S(1)} %get-tuple-element.8), channel_id=1, source_target_pairs={{1,0},{2,1},{3,2},{4,3},{5,4},{6,5},{7,6},{8,7},{9,8},{10,9},{11,1... | collective-permute-start | bytes 1130504 | tf_op jit(solution)/shard_map/ppermute | solution.py:27
  83.1 15.8 %collective-permute-start.7 = (f32[10,8,128]{2,1,0:T(8,128)S(1)}, f32[10,8,128]{2,1,0:T(8,128)S(1)}, u32[]{:S(2)}, u32[]{:S(2)}) collective-permute-start(f32[10,8,128]{2,1,0:T(8,128)S(1)} %get-tuple-element.9), channel_id=1, source_target_pairs={{0,2},{1,3},{2,4},{3,5},{4,6},{5,7},{6,8},{7,9},{8,10},{9,11},{10,... | collective-permute-start | bytes 122888 | tf_op jit(solution)/shard_map/ppermute | solution.py:27
  87.1 17.9 %collective-permute-start.10 = (f32[10,8,128]{2,1,0:T(8,128)S(1)}, f32[10,8,128]{2,1,0:T(8,128)S(1)}, u32[]{:S(2)}, u32[]{:S(2)}) collective-permute-start(f32[10,8,128]{2,1,0:T(8,128)S(1)} %get-tuple-element.9), channel_id=1, source_target_pairs={{2,0},{3,1},{4,2},{5,3},{6,4},{7,5},{8,6},{9,7},{10,8},{11,9},{12,... | collective-permute-start | bytes 122888 | tf_op jit(solution)/shard_map/ppermute | solution.py:27
  91.4 13.6 %collective-permute-start.9 = (f32[10,8,128]{2,1,0:T(8,128)S(1)}, f32[10,8,128]{2,1,0:T(8,128)S(1)}, u32[]{:S(2)}, u32[]{:S(2)}) collective-permute-start(f32[10,8,128]{2,1,0:T(8,128)S(1)} %get-tuple-element.9), channel_id=1, source_target_pairs={{1,0},{2,1},{3,2},{4,3},{5,4},{6,5},{7,6},{8,7},{9,8},{10,9},{11,1... | collective-permute-start | bytes 122888 | tf_op jit(solution)/shard_map/ppermute | solution.py:27
  97.0 8.0 %collective-permute-start.8 = (f32[10,8,128]{2,1,0:T(8,128)S(1)}, f32[10,8,128]{2,1,0:T(8,128)S(1)}, u32[]{:S(2)}, u32[]{:S(2)}) collective-permute-start(f32[10,8,128]{2,1,0:T(8,128)S(1)} %get-tuple-element.9), channel_id=1, source_target_pairs={{0,1},{1,2},{2,3},{3,4},{4,5},{5,6},{6,7},{7,8},{8,9},{9,10},{10,1... | collective-permute-start | bytes 122888 | tf_op jit(solution)/shard_map/ppermute | solution.py:27
  105.2 7.7 %collective-permute-start.11 = (f32[35,8,128]{2,1,0:T(8,128)S(1)}, f32[35,8,128]{2,1,0:T(8,128)S(1)}, u32[]{:S(2)}, u32[]{:S(2)}) collective-permute-start(f32[35,8,128]{2,1,0:T(8,128)S(1)} %constant_dynamic-update-slice_fusion.8), channel_id=1, source_target_pairs={{0,32},{1,33},{2,34},{3,35},{4,36},{5,37},{6,38},{7,39},{8,40},{9,... | collective-permute-start | bytes 430088 | tf_op jit(solution)/shard_map/ppermute | solution.py:27
  110.3 8.2 %collective-permute-start.12 = (f32[35,8,128]{2,1,0:T(8,128)S(1)}, f32[35,8,128]{2,1,0:T(8,128)S(1)}, u32[]{:S(2)}, u32[]{:S(2)}) collective-permute-start(f32[35,8,128]{2,1,0:T(8,128)S(1)} %pad_maximum_fusion.2), channel_id=1, source_target_pairs={{32,0},{33,1},{34,2},{35,3},{36,4},{37,5},{38,6},{39,7},{40,8},{41... | collective-permute-start | bytes 430088 | tf_op jit(solution)/shard_map/ppermute | solution.py:27

commit v4 on v3

--- a/solution.py
+++ b/solution.py
@@ -47,24 +47,74 @@
     return jnp.where(odd_row, roll(value, 1, 0), roll(value, -1, 0))
 
 
-def interp_kernel(
-    rows_ref, cols_ref, weights_ref, v_ref, right_ref, below_ref, corner_ref, out_ref, pad_ref
-):
-    rows = v_ref.shape[1]
+def first_kernel(v_ref, edge_ref, below_ref, corner_ref):
+    sub = rows_of((8, 128))
     for comp in range(3):
-        pad_ref[comp, :rows, 0:8] = v_ref[comp]
-        pad_ref[comp, rows, 0:8] = below_ref[comp, 0]
-        for row in range(rows):
-            pad_ref[comp, row, 8:9] = right_ref[comp, row : row + 1]
-        pad_ref[comp, rows, 8:9] = corner_ref[comp : comp + 1]
+        corner_ref[comp : comp + 1] = v_ref[comp, 0, 0:1]
+        below_ref[comp] = v_ref[comp, 0]
+        for j in range(2):
+            first = v_ref[comp, 8 * j]
+            for r in range(1, 8):
+                first = jnp.where(sub == r, roll(v_ref[comp, 8 * j + r], r, 0), first)
+            edge_ref[comp, 8 * j : 8 * j + 8] = first
+
+
+def cut_kernel(v_ref, f_ref, mu_ref, right_ref, left_ref):
+    sub = rows_of((8, 128))
+
+    def row(field, r):
+        if field == 6:
+            return mu_ref[r]
+        return v_ref[field, r] if field < 3 else f_ref[field - 3, r]
+
+    for field in range(7):
+        for t in range(8):
+            even, odd = row(field, 2 * t), roll(row(field, 2 * t + 1), 4, 0)
+            right_ref[8 * field + t] = jnp.where(sub < 4, odd, even)
+            left_ref[8 * field + t] = jnp.where(sub < 4, even, odd)
+    for n, field in enumerate((0, 1, 2, 6)):
+        for j in range(2):
+            third = fourth = row(field, 8 * j)
+            for r in range(8):
+                value = row(field, 8 * j + r)
+                third = jnp.where(sub == r, roll(value, r - 3, 0), third)
+                fourth = jnp.where(sub == r, roll(value, r - 4, 0), fourth)
+            right_ref[56 + 2 * n + j] = third
+            left_ref[56 + 2 * n + j] = fourth
+
+
+def blend_kernel(rows_ref, cols_ref, weights_ref, v_ref, own_ref, edge_ref, below_ref, corner_ref):
+    tall, flat = rows_of((16, 128)), rows_of((8, 128))
     for slot in range(3):
         row, col = rows_ref[slot], cols_ref[slot]
+        w0, w1, w2, w3 = (weights_ref[k, slot] for k in range(4))
+        here, next_one = flat == col, flat == col + 1
+        upper = jnp.where(here, w0, jnp.where(next_one, w2, 0.0))
+        lower = jnp.where(here, w1, jnp.where(next_one, w3, 0.0))
+        within = row < 15
+        next_row = jnp.where(within, row + 1, row)
+        inner = jnp.where(within, lower, 0.0)
         for comp in range(3):
-            total = weights_ref[0, slot] * pad_ref[comp, row, pl.ds(col, 1), :]
-            total = total + weights_ref[1, slot] * pad_ref[comp, row + 1, pl.ds(col, 1), :]
-            total = total + weights_ref[2, slot] * pad_ref[comp, row, pl.ds(col + 1, 1), :]
-            total = total + weights_ref[3, slot] * pad_ref[comp, row + 1, pl.ds(col + 1, 1), :]
-            out_ref[slot * 3 + comp : slot * 3 + comp + 1] = total
+            total = upper * v_ref[comp, row] + inner * v_ref[comp, next_row]
+            own_ref[3 * slot + comp] = jnp.sum(total, axis=0, keepdims=True)
+        beside = jnp.where(tall == row, w2, jnp.where(tall == row + 1, w3, 0.0))
+        edge_ref[slot] = jnp.where(col == 7, beside, 0.0)
+        below_ref[slot] = jnp.where(within, 0.0, lower)
+        both = jnp.where((row == 15) & (col == 7), w3, 0.0)
+        corner_ref[slot] = jnp.full((1, 128), both, jnp.float32)
+
+
+def interp_kernel(
+    own_ref, edge_w, below_w, corner_w, edge_ref, below_ref, corner_ref, out_ref
+):
+    for slot in range(3):
+        for comp in range(3):
+            beside = edge_w[slot] * edge_ref[comp]
+            total = beside[0:8] + beside[8:16] + below_w[slot] * below_ref[comp]
+            total = jnp.sum(total, axis=0, keepdims=True) + own_ref[3 * slot + comp]
+            total = total + corner_w[slot] * corner_ref[comp : comp + 1]
+            for dest in range(out_ref.shape[0] // 9):
+                out_ref[9 * dest + 3 * slot + comp] = total
 
 
 def pick_kernel(place_ref, cells_ref, source_ref, row_ref, out_ref):
@@ -92,43 +142,40 @@
             copy(last_lat, position)
 
 
-def pack_kernel(v_ref, f_ref, mu_ref, above_ref, below_ref, right_ref, left_ref):
-    sub = rows_of((8, 128))
-
-    def row(field, r):
-        if r < 0:
-            return above_ref[field, r + 5]
-        if r > 15:
-            return below_ref[field, r - 16]
-        if field == 6:
-            return mu_ref[r]
-        return v_ref[field, r] if field < 3 else f_ref[field - 3, r]
-
-    for field in range(7):
-        for t in range(12):
-            even, odd = row(field, 2 * t - 4), roll(row(field, 2 * t - 3), 4, 0)
-            right_ref[12 * field + t] = jnp.where(sub < 4, odd, even)
-            left_ref[12 * field + t] = jnp.where(sub < 4, even, odd)
-    for n, field in enumerate((0, 1, 2, 6)):
-        for j in range(2):
-            third = fourth = row(field, 8 * j)
-            for s in range(8):
-                value = row(field, 8 * j + s)
-                third = jnp.where(sub == s, roll(value, s - 3, 0), third)
-                fourth = jnp.where(sub == s, roll(value, s - 4, 0), fourth)
-            right_ref[84 + 2 * n + j] = third
-            left_ref[84 + 2 * n + j] = fourth
+def lat_tile(field, away, side):
+    if field in (0, 1, 2, 6):
+        return 9 * (field if field < 6 else 3) + (5 if side else 0) + away - 1
+    return 36 + 7 * (field - 3) + (4 if side else 0) + away - 1
 
 
 def side_tile(ref, field, r, col, sub):
-    value = ref[12 * field + (r + 4) // 2]
+    value = ref[8 * field + r // 2]
     if r % 2:
         value = roll(value, 4, 0)
     extra = {0: 0, 1: 1, 2: 2, 6: 3}.get(field)
-    if extra is None or not 0 <= r < 16:
+    if extra is None:
         return value
-    fifth = roll(ref[84 + 2 * extra + r // 8], col - r % 8, 0)
+    fifth = roll(ref[56 + 2 * extra + r // 8], col - r % 8, 0)
     return jnp.where(sub == col, fifth, value)
+
+
+def pack_kernel(v_ref, f_ref, mu_ref, left_ref, right_ref, up_ref, down_ref):
+    sub = rows_of((8, 128))
+    for field in range(7):
+        force = 3 <= field < 6
+        for away in range(1, 5 if force else 6):
+            for ref, r in ((up_ref, away - 1), (down_ref, 16 - away)):
+                if field == 6:
+                    value = mu_ref[r]
+                else:
+                    value = f_ref[field - 3, r] if force else v_ref[field, r]
+                ref[lat_tile(field, away, False)] = value
+                if away < (4 if force else 5):
+                    ref[lat_tile(field, away, True)] = jnp.where(
+                        sub < 4,
+                        side_tile(right_ref, field, r, 4, sub),
+                        side_tile(left_ref, field, r, 3, sub),
+                    )
 
 
 def prepare(
@@ -142,15 +189,19 @@
     odd_lane, odd_row = (lane & 1) == 1, (row & 1) == 1
     own = slice(PAD, PAD + 16)
     sub = rows_of((8, 128))
+
+    def outer(ref, field, away, side):
+        return ref[lat_tile(field, away, side)]
+
     MU[own, 8:16] = mu_ref[...]
-    MU[1:6, 8:16] = above_ref[6]
-    MU[22:27, 8:16] = below_ref[6]
-    for r in range(-4, 20):
+    for r in range(16):
         MU[r + PAD, 0:8] = side_tile(left_ref, 6, r, 3, sub)
         MU[r + PAD, 16:24] = side_tile(right_ref, 6, r, 4, sub)
-    for i in (1, 26):
-        MU[i, 0:8] = MU[i, 8:16]
-        MU[i, 16:24] = MU[i, 8:16]
+    for away in range(1, 6):
+        for i, ref in ((PAD - away, above_ref), (PAD + 15 + away, below_ref)):
+            value = outer(ref, 6, away, False)
+            beside = outer(ref, 6, away, True) if away < 5 else value
+            MU[i, 0:8], MU[i, 8:16], MU[i, 16:24] = beside, value, beside
 
     @pl.when(lat == 0)
     def _():
@@ -192,13 +243,18 @@
         if 0 <= r < 16:
             DG[r] = total[8:16]
         for comp in range(3):
-            if r < 0:
-                force = above_ref[3 + comp, r + 5]
+            if 0 <= r < 16:
+                force = f_ref[comp, r]
+                west_force = side_tile(left_ref, 3 + comp, r, 3, sub)
+                east_force = side_tile(right_ref, 3 + comp, r, 4, sub)
             else:
-                force = f_ref[comp, r] if r < 16 else below_ref[3 + comp, r - 16]
+                ref, away = (above_ref, -r) if r < 0 else (below_ref, r - 15)
+                force = outer(ref, 3 + comp, away, False)
+                beside = outer(ref, 3 + comp, away, True) if away < 4 else force
+                west_force = east_force = beside
+            F[comp, i, 0:8] = west_force * inverse[0:8]
             F[comp, i, 8:16] = force * inverse[8:16]
-            F[comp, i, 0:8] = side_tile(left_ref, 3 + comp, r, 3, sub) * inverse[0:8]
-            F[comp, i, 16:24] = side_tile(right_ref, 3 + comp, r, 4, sub) * inverse[16:24]
+            F[comp, i, 16:24] = east_force * inverse[16:24]
 
     def coarse_visc(i):
         both = MU[i] + MU[i + 1]
@@ -231,14 +287,14 @@
 
     for comp in range(3):
         A[comp, own, 8:16] = v_ref[comp]
-        A[comp, 1:6, 8:16] = above_ref[comp]
-        A[comp, 22:27, 8:16] = below_ref[comp]
-        for r in range(-4, 20):
+        for r in range(16):
             A[comp, r + PAD, 0:8] = side_tile(left_ref, comp, r, 3, sub)
             A[comp, r + PAD, 16:24] = side_tile(right_ref, comp, r, 4, sub)
-        for i in (1, 26):
-            A[comp, i, 0:8] = A[comp, i, 8:16]
-            A[comp, i, 16:24] = A[comp, i, 8:16]
+        for away in range(1, 6):
+            for i, ref in ((PAD - away, above_ref), (PAD + 15 + away, below_ref)):
+                value = ref[lat_tile(comp, away, False)]
+                beside = ref[lat_tile(comp, away, True)] if away < 5 else value
+                A[comp, i, 0:8], A[comp, i, 8:16], A[comp, i, 16:24] = beside, value, beside
 
     edge = (lon == 0) | (lon == last_lon)
     all_cols, all_rows = (last_lon + 1) * 8, (last_lat + 1) * 16
@@ -428,39 +484,35 @@
     ghost_rows = (slots // (3 * lons)) * (3 * CELLS)
     cells = wanted_cells(lats, lons, lax.axis_index("lon")).reshape(-1)
 
-    corner_right = shifted(v[:, :, 0], 0, -1)
-    corner_both = shifted(v[:, 0, 0], -1, -1)
-    top = jnp.concatenate([v[:, :5], f[:, :5], mu[None, :5]], axis=0)
-    low = jnp.concatenate([v[:, 11:], f[:, 11:], mu[None, 11:]], axis=0)
-    below = shifted(top, -1, 0)
-    above = shifted(low, 1, 0)
-    values = pl.pallas_call(
-        interp_kernel,
-        out_shape=jax.ShapeDtypeStruct((9, 128), f32),
-        in_specs=[SMEM] * 3 + [VMEM] * 4,
-        out_specs=VMEM,
-        scratch_shapes=[pltpu.VMEM((3, 17, 16, 128), f32)],
-        compiler_params=params,
-        name="interp",
-    )(
-        corner_rows[0, 0], corner_cols[0, 0], corner_weights[0, 0],
-        v, corner_right, below, corner_both,
-    )
-    values = lax.ppermute(values, "patch", [(0, 1), (1, 0)])
-    spread = jnp.broadcast_to(values.reshape(1, 1, 1152), (lons, 1, 1152))
-    around = lax.all_to_all(spread, "lon", 0, 0, tiled=True)
-
-    message_tiles = jax.ShapeDtypeStruct((92, 8, 128), f32)
-    to_right, to_left = pl.pallas_call(
-        pack_kernel,
-        out_shape=(message_tiles, message_tiles),
-        in_specs=[VMEM] * 5,
-        out_specs=(VMEM, VMEM),
-        compiler_params=params,
-        name="pack",
-    )(v, f, mu, above, below)
+    def kernel(body, shapes, specs):
+        return pl.pallas_call(
+            body,
+            out_shape=[jax.ShapeDtypeStruct(shape, f32) for shape in shapes],
+            in_specs=specs,
+            out_specs=[VMEM] * len(shapes),
+            compiler_params=params,
+        )
+
+    edge, first_row, first_cell = kernel(
+        first_kernel, ((3, 16, 128), (3, 8, 128), (3, 128)), [VMEM]
+    )(v)
+    edge = shifted(edge, 0, -1)
+    first_cell = shifted(first_cell, -1, -1)
+    first_row = shifted(first_row, -1, 0)
+    to_right, to_left = kernel(cut_kernel, ((64, 8, 128),) * 2, [VMEM] * 3)(v, f, mu)
     left = shifted(to_right, 0, 1)
     right = shifted(to_left, 0, -1)
+    blended = kernel(
+        blend_kernel, ((9, 1, 128), (3, 16, 128), (3, 8, 128), (3, 1, 128)), [SMEM] * 3 + [VMEM]
+    )(corner_rows[0, 0], corner_cols[0, 0], corner_weights[0, 0], v)
+    (values,) = kernel(interp_kernel, ((9 * lons, 1, 128),), [VMEM] * 7)(
+        *blended, edge, first_row, first_cell
+    )
+    values = lax.ppermute(values.reshape(lons, 1, 1152), "patch", [(0, 1), (1, 0)])
+    around = lax.all_to_all(values, "lon", 0, 0, tiled=True)
+    to_above, to_below = kernel(pack_kernel, ((57, 8, 128),) * 2, [VMEM] * 5)(v, f, mu, left, right)
+    below = shifted(to_above, -1, 0)
+    above = shifted(to_below, 1, 0)
 
     chosen = pl.pallas_call(
         pick_kernel,

time: 121 us -> 115 us (0.950)
  the two profiles are of different devices: /device:TPU:88 before, /device:TPU:80 now
where the time goes in v4:
time: 115 us
  starting transfers between devices  68.6 us (60%)
  waiting for transfers between devices  32.7 us (28%)
  Pallas kernels  8.88 us (8%)
  local copies, waits for them, and re-layouts  2.92 us (3%)
    ppermute x13, starting transfers between devices, shifted(): return lax.ppermute(value, AXES, pairs)  45.5 us
    ppermute x13, waiting for transfers between devices, shifted(): return lax.ppermute(value, AXES, pairs)  21.2 us
    all_to_all x1, starting transfers between devices, per_device(): around = lax.all_to_all(values, 'lon', 0, 0, tiled=True)  13.4 us
    all_to_all x1, waiting for transfers between devices, per_device(): around = lax.all_to_all(values, 'lon', 0, 0, tiled=True)  10.1 us
    all_to_all x1, starting transfers between devices, per_device(): lax.all_to_all(chosen.reshape(lats, 3 * CELLS, 128), 'lat', 0, 0, tiled=T...  7.79 us
    pallas_call x1, Pallas kernels, per_device(): pl.pallas_call(smooth_kernel, out_shape=(block, block, jax.ShapeDtypeStru...  4.71 us
    unnamed x27, local copies, waits for them, and re-layouts  2.41 us
  transfers between devices with their start and end apart: 16, of which 10 were waited for; matrix products, arithmetic and copies ran while one was open for 1% of the time, Pallas kernels for 1%

profile of v4, /device:TPU:80, one launch (start us, length us, event | category | flops | bytes accessed | tf_op | source)
XLA Modules:
  0.0 114.6 jit_solution(15238562508725989138)
XLA Ops:
  0.6 0.0 copy-start
  0.6 0.9 copy-done
  1.6 3.8 %collective-permute-start.6 = (f32[3,128]{1,0:T(4,128)S(1)}, f32[3,128]{1,0:T(4,128)S(1)}, u32[]{:S(2)}, u32[]{:S(2)}) collective-permute-start(f32[3,128]{1,0:T(4,128)S(1)} %get-tuple-element.26), channel_id=1, source_target_pairs={{33,0},{34,1},{35,2},{36,3},{37,4},{38,5},{39,6},{40,7},{41,8},{42... | collective-permute-start | bytes 4616 | tf_op jit(solution)/shard_map/ppermute | solution.py:27
  5.4 2.4 %collective-permute-start.5 = (f32[3,8,128]{2,1,0:T(8,128)S(1)}, f32[3,8,128]{2,1,0:T(8,128)S(1)}, u32[]{:S(2)}, u32[]{:S(2)}) collective-permute-start(f32[3,8,128]{2,1,0:T(8,128)S(1)} %get-tuple-element.25), channel_id=1, source_target_pairs={{32,0},{33,1},{34,2},{35,3},{36,4},{37,5},{38,6},{39,7},{40,8},{41... | collective-permute-start | bytes 36872 | tf_op jit(solution)/shard_map/ppermute | solution.py:27
  7.7 2.7 %collective-permute-start.4 = (f32[3,16,128]{2,1,0:T(8,128)S(1)}, f32[3,16,128]{2,1,0:T(8,128)S(1)}, u32[]{:S(2)}, u32[]{:S(2)}) collective-permute-start(f32[3,16,128]{2,1,0:T(8,128)S(1)} %get-tuple-element.24), channel_id=1, source_target_pairs={{1,0},{2,1},{3,2},{4,3},{5,4},{6,5},{7,6},{8,7},{9,8},{10,9},{11,1... | collective-permute-start | bytes 73736 | tf_op jit(solution)/shard_map/ppermute | solution.py:27
  10.6 0.1 fusion.8
  10.6 0.1 reshape.135
  10.7 0.1 iota_select_fusion
  10.8 0.1 select_n.73
  10.9 0.1 clamp_add_fusion
  11.0 0.1 reshape.134
  11.0 0.1 add.104
  11.1 0.1 add.105
  11.2 0.1 broadcast_in_dim.43
  11.3 0.0 copy-start.7
  11.3 0.7 copy-done.7
  12.0 0.1 copy.10
  12.1 0.0 copy-start.4
  12.1 0.0 copy-start.5
  12.1 0.0 copy-done.1
  12.1 0.6 copy-done.4
  12.7 0.0 copy-done.5
  12.7 0.6 shard_map.88
  13.3 0.0 collective-permute-done.6.corner_ref
  13.3 0.0 collective-permute-done.5.below_ref
  13.4 0.1 collective-permute-done.4.edge_ref
  13.4 0.0 copy-start.6
  13.5 0.1 shard_map.90
  13.5 1.9 %collective-permute-start.7 = (f32[32,1,1152]{2,1,0:T(1,128)S(1)}, f32[32,1,1152]{2,1,0:T(1,128)}, u32[]{:S(2)}, u32[]{:S(2)}) collective-permute-start(f32[32,1,1152]{2,1,0:T(1,128)S(1)} %bitcast.58), channel_id=1, source_target_pairs={{0,256},{256,0},{1,257},{257,1},{2,258},{258,2},{3,259},{259,3},{4... | collective-permute-start | bytes 442376 | tf_op jit(solution)/shard_map/ppermute | solution.py:511
  15.5 0.0 copy-done.6
  15.6 1.4 %collective-permute-done.7 = f32[32,1,1152]{2,1,0:T(1,128)} collective-permute-done((f32[32,1,1152]{2,1,0:T(1,128)S(1)}, f32[32,1,1152]{2,1,0:T(1,128)}, u32[]{:S(2)}, u32[]{:S(2)}) %collective-permute-start.7) | collective-permute-done | bytes 147488 | tf_op jit(solution)/shard_map/ppermute | solution.py:511
  16.9 13.4 %all-to-all-start = ((f32[32,1,1152]{2,1,0:T(1,128)}), f32[32,1,1152]{2,1,0:T(1,128)S(1)}, u32[]{:S(2)}, u32[]{:S(2)}) async-start(f32[32,1,1152]{2,1,0:T(1,128)} %collective-permute-done.7), calls=%async_computation | async-start | bytes 294912 | tf_op jit(solution)/shard_map/all_to_all | solution.py:512
  30.3 0.1 pad_add_fusion.place_ref
  30.4 10.1 %all-to-all-done = f32[32,1,1152]{2,1,0:T(1,128)S(1)} async-done(((f32[32,1,1152]{2,1,0:T(1,128)}), f32[32,1,1152]{2,1,0:T(1,128)S(1)}, u32[]{:S(2)}, u32[]{:S(2)}) %all-to-all-start) | async-done | bytes 147488 | tf_op jit(solution)/shard_map/all_to_all | solution.py:512
  40.6 1.4 %pick.1 = f32[768,1,128]{2,1,0:T(1,128)} custom-call(s32[4]{0:T(128)S(1)} %pad_add_fusion.place_ref, s32[256]{0:T(256)S(1)} %add_select_fusion.4.cells_ref, s32[768]{0:T(1024)S(1)} %get-tuple-element.43.source_ref, f32[288,1,128]{2,1,0:T(1,128)S(1)} %bitcast.54), custom_call_target="tpu_custom_call" | custom-call | tf_op jit(solution)/shard_map/pick/pallas_call | solution.py:517
  42.0 0.0 copy-start.2
  42.0 0.0 copy-start.3
  42.0 7.8 %all-to-all-start.1 = ((f32[8,96,128]{2,1,0:T(8,128)}), f32[8,96,128]{2,1,0:T(8,128)S(1)}, u32[]{:S(2)}, u32[]{:S(2)}) async-start(f32[8,96,128]{2,1,0:T(8,128)} %bitcast.10), calls=%async_computation.1 | async-start | bytes 786432 | tf_op jit(solution)/shard_map/all_to_all | solution.py:525
  49.8 0.0 copy-done.2
  49.8 0.0 copy-done.3
  49.8 0.1 shard_map.86
  49.9 2.4 %collective-permute-start = (f32[64,8,128]{2,1,0:T(8,128)S(1)}, f32[64,8,128]{2,1,0:T(8,128)S(1)}, u32[]{:S(2)}, u32[]{:S(2)}) collective-permute-start(f32[64,8,128]{2,1,0:T(8,128)S(1)} %get-tuple-element.16), channel_id=1, source_target_pairs={{0,1},{1,2},{2,3},{3,4},{4,5},{5,6},{6,7},{7,8},{8,9},{9,10},{10,1... | collective-permute-start | bytes 786440 | tf_op jit(solution)/shard_map/ppermute | solution.py:27
  52.3 5.5 %collective-permute-start.1 = (f32[64,8,128]{2,1,0:T(8,128)S(1)}, f32[64,8,128]{2,1,0:T(8,128)S(1)}, u32[]{:S(2)}, u32[]{:S(2)}) collective-permute-start(f32[64,8,128]{2,1,0:T(8,128)S(1)} %get-tuple-element.17), channel_id=1, source_target_pairs={{1,0},{2,1},{3,2},{4,3},{5,4},{6,5},{7,6},{8,7},{9,8},{10,9},{11,1... | collective-permute-start | bytes 786440 | tf_op jit(solution)/shard_map/ppermute | solution.py:27
  57.8 2.4 %collective-permute-done.left_ref = f32[64,8,128]{2,1,0:T(8,128)S(1)} collective-permute-done((f32[64,8,128]{2,1,0:T(8,128)S(1)}, f32[64,8,128]{2,1,0:T(8,128)S(1)}, u32[]{:S(2)}, u32[]{:S(2)}) %collective-permute-start) | collective-permute-done | bytes 262176 | tf_op jit(solution)/shard_map/ppermute | solution.py:27
  60.2 1.5 %collective-permute-done.1.right_ref = f32[64,8,128]{2,1,0:T(8,128)S(1)} collective-permute-done((f32[64,8,128]{2,1,0:T(8,128)S(1)}, f32[64,8,128]{2,1,0:T(8,128)S(1)}, u32[]{:S(2)}, u32[]{:S(2)}) %collective-permute-start.1) | collective-permute-done | bytes 262176 | tf_op jit(solution)/shard_map/ppermute | solution.py:27
  61.7 3.4 %collective-permute-start.2 = (f32[57,8,128]{2,1,0:T(8,128)S(1)}, f32[57,8,128]{2,1,0:T(8,128)S(1)}, u32[]{:S(2)}, u32[]{:S(2)}) collective-permute-start(f32[57,8,128]{2,1,0:T(8,128)S(1)} %get-tuple-element.18), channel_id=1, source_target_pairs={{0,32},{1,33},{2,34},{3,35},{4,36},{5,37},{6,38},{7,39},{8,40},{9,... | collective-permute-start | bytes 700424 | tf_op jit(solution)/shard_map/ppermute | solution.py:27
  65.1 2.5 %collective-permute-start.3 = (f32[57,8,128]{2,1,0:T(8,128)S(1)}, f32[57,8,128]{2,1,0:T(8,128)S(1)}, u32[]{:S(2)}, u32[]{:S(2)}) collective-permute-start(f32[57,8,128]{2,1,0:T(8,128)S(1)} %get-tuple-element.19), channel_id=1, source_target_pairs={{32,0},{33,1},{34,2},{35,3},{36,4},{37,5},{38,6},{39,7},{40,8},{41... | collective-permute-start | bytes 700424 | tf_op jit(solution)/shard_map/ppermute | solution.py:27
  67.6 2.1 %collective-permute-done.2.above_ref = f32[57,8,128]{2,1,0:T(8,128)S(1)} collective-permute-done((f32[57,8,128]{2,1,0:T(8,128)S(1)}, f32[57,8,128]{2,1,0:T(8,128)S(1)}, u32[]{:S(2)}, u32[]{:S(2)}) %collective-permute-start.2) | collective-permute-done | bytes 233504 | tf_op jit(solution)/shard_map/ppermute | solution.py:27
  69.7 4.0 %collective-permute-done.3.below_ref = f32[57,8,128]{2,1,0:T(8,128)S(1)} collective-permute-done((f32[57,8,128]{2,1,0:T(8,128)S(1)}, f32[57,8,128]{2,1,0:T(8,128)S(1)}, u32[]{:S(2)}, u32[]{:S(2)}) %collective-permute-start.3) | collective-permute-done | bytes 233504 | tf_op jit(solution)/shard_map/ppermute | solution.py:27
  73.7 0.0 all-to-all-done.1
  73.7 4.7 %smooth.1 = (f32[3,16,8,128]{3,2,1,0:T(8,128)}, f32[3,16,8,128]{3,2,1,0:T(8,128)S(1)}, f32[10,8,128]{2,1,0:T(8,128)S(1)}) custom-call(s32[4]{0:T(128)S(1)} %pad_add_fusion.place_ref, s32[768]{0:T(1024)S(1)} %get-tuple-element.44.ghost_ref, f32[3,16,8,128]{3,2,1,0:T(8,128)S(1)} %bitcast.49, f32[3,16,8,128]{3,2,1,0:T(8,128)S(1)} %bitcast.52, ...), custom_call_target="tpu_custom_call" | custom-call | tf_op jit(solution)/shard_map/smooth/pallas_call | solution.py:530
  78.5 3.0 %collective-permute-start.8 = (f32[10,8,128]{2,1,0:T(8,128)S(1)}, f32[10,8,128]{2,1,0:T(8,128)S(1)}, u32[]{:S(2)}, u32[]{:S(2)}) collective-permute-start(f32[10,8,128]{2,1,0:T(8,128)S(1)} %get-tuple-element.27), channel_id=1, source_target_pairs={{0,2},{1,3},{2,4},{3,5},{4,6},{5,7},{6,8},{7,9},{8,10},{9,11},{10,... | collective-permute-start | bytes 122888 | tf_op jit(solution)/shard_map/ppermute | solution.py:27
  81.5 5.2 %collective-permute-start.11 = (f32[10,8,128]{2,1,0:T(8,128)S(1)}, f32[10,8,128]{2,1,0:T(8,128)S(1)}, u32[]{:S(2)}, u32[]{:S(2)}) collective-permute-start(f32[10,8,128]{2,1,0:T(8,128)S(1)} %get-tuple-element.27), channel_id=1, source_target_pairs={{2,0},{3,1},{4,2},{5,3},{6,4},{7,5},{8,6},{9,7},{10,8},{11,9},{12,... | collective-permute-start | bytes 122888 | tf_op jit(solution)/shard_map/ppermute | solution.py:27
  86.7 5.6 %collective-permute-start.10 = (f32[10,8,128]{2,1,0:T(8,128)S(1)}, f32[10,8,128]{2,1,0:T(8,128)S(1)}, u32[]{:S(2)}, u32[]{:S(2)}) collective-permute-start(f32[10,8,128]{2,1,0:T(8,128)S(1)} %get-tuple-element.27), channel_id=1, source_target_pairs={{1,0},{2,1},{3,2},{4,3},{5,4},{6,5},{7,6},{8,7},{9,8},{10,9},{11,1... | collective-permute-start | bytes 122888 | tf_op jit(solution)/shard_map/ppermute | solution.py:27
  92.3 1.9 %collective-permute-start.9 = (f32[10,8,128]{2,1,0:T(8,128)S(1)}, f32[10,8,128]{2,1,0:T(8,128)S(1)}, u32[]{:S(2)}, u32[]{:S(2)}) collective-permute-start(f32[10,8,128]{2,1,0:T(8,128)S(1)} %get-tuple-element.27), channel_id=1, source_target_pairs={{0,1},{1,2},{2,3},{3,4},{4,5},{5,6},{6,7},{7,8},{8,9},{9,10},{10,1... | collective-permute-start | bytes 122888 | tf_op jit(solution)/shard_map/ppermute | solution.py:27
  94.2 0.0 collective-permute-done.8
  94.3 6.1 %collective-permute-done.9 = f32[10,8,128]{2,1,0:T(8,128)S(1)} collective-permute-done((f32[10,8,128]{2,1,0:T(8,128)S(1)}, f32[10,8,128]{2,1,0:T(8,128)S(1)}, u32[]{:S(2)}, u32[]{:S(2)}) %collective-permute-start.9) | collective-permute-done | bytes 40992 | tf_op jit(solution)/shard_map/ppermute | solution.py:27
  100.3 0.0 collective-permute-done.10
  100.4 0.0 collective-permute-done.11
  100.5 5.1 %collective-permute-start.12 = (f32[35,8,128]{2,1,0:T(8,128)S(1)}, f32[35,8,128]{2,1,0:T(8,128)S(1)}, u32[]{:S(2)}, u32[]{:S(2)}) collective-permute-start(f32[35,8,128]{2,1,0:T(8,128)S(1)} %constant_dynamic-update-slice_fusion.8), channel_id=1, source_target_pairs={{0,32},{1,33},{2,34},{3,35},{4,36},{5,37},{6,38},{7,39},{8,40},{9,... | collective-permute-start | bytes 430088 | tf_op jit(solution)/shard_map/ppermute | solution.py:27
  105.7 1.9 %collective-permute-start.13 = (f32[35,8,128]{2,1,0:T(8,128)S(1)}, f32[35,8,128]{2,1,0:T(8,128)S(1)}, u32[]{:S(2)}, u32[]{:S(2)}) collective-permute-start(f32[35,8,128]{2,1,0:T(8,128)S(1)} %pad_maximum_fusion), channel_id=1, source_target_pairs={{32,0},{33,1},{34,2},{35,3},{36,4},{37,5},{38,6},{39,7},{40,8},{41... | collective-permute-start | bytes 430088 | tf_op jit(solution)/shard_map/ppermute | solution.py:27
  107.6 0.7 collective-permute-done.12.above_ref
  108.3 4.4 %collective-permute-done.13.below_ref = f32[35,8,128]{2,1,0:T(8,128)S(1)} collective-permute-done((f32[35,8,128]{2,1,0:T(8,128)S(1)}, f32[35,8,128]{2,1,0:T(8,128)S(1)}, u32[]{:S(2)}, u32[]{:S(2)}) %collective-permute-start.13) | collective-permute-done | bytes 143392 | tf_op jit(solution)/shard_map/ppermute | solution.py:27
  112.7 1.9 %coarse.1 = f32[3,16,8,128]{3,2,1,0:T(8,128)} custom-call(f32[10,40,128]{2,1,0:T(8,128)S(1)} %constant_dynamic-update-slice_fusion.mid_ref, f32[35,8,128]{2,1,0:T(8,128)S(1)} %collective-permute-done.12.above_ref, f32[35,8,128]{2,1,0:T(8,128)S(1)} %collective-permute-done.13.below_ref, f32[3,16,8,128]{3,2,1,0:T(8,128)S(1)} %get-tuple-element.28.smooth_ref), custom_call_target="tpu_custom_call" | custom-call | tf_op jit(solution)/shard_map/coarse/pallas_call | solution.py:560
  (31 shorter events, 0.3 us)
Async XLA Ops:
  0.6 0.9 copy-start
  1.6 10.5 %copy-start.1 = (f32[1,3,16,8,128]{4,3,2,1,0:T(8,128)S(1)}, f32[1,3,16,8,128]{4,3,2,1,0:T(8,128)}, u32[]{:S(2)}) copy-start(f32[1,3,16,8,128]{4,3,2,1,0:T(8,128)} %param.7) | copy-start | bytes 589828
  1.6 11.8 %collective-permute-start.6 = (f32[3,128]{1,0:T(4,128)S(1)}, f32[3,128]{1,0:T(4,128)S(1)}, u32[]{:S(2)}, u32[]{:S(2)}) collective-permute-start(f32[3,128]{1,0:T(4,128)S(1)} %get-tuple-element.26), channel_id=1, source_target_pairs={{33,0},{34,1},{35,2},{36,3},{37,4},{38,5},{39,6},{40,7},{41,8},{42... | collective-permute-start | bytes 4616 | tf_op jit(solution)/shard_map/ppermute | solution.py:27
  5.4 8.0 %collective-permute-start.5 = (f32[3,8,128]{2,1,0:T(8,128)S(1)}, f32[3,8,128]{2,1,0:T(8,128)S(1)}, u32[]{:S(2)}, u32[]{:S(2)}) collective-permute-start(f32[3,8,128]{2,1,0:T(8,128)S(1)} %get-tuple-element.25), channel_id=1, source_target_pairs={{32,0},{33,1},{34,2},{35,3},{36,4},{37,5},{38,6},{39,7},{40,8},{41... | collective-permute-start | bytes 36872 | tf_op jit(solution)/shard_map/ppermute | solution.py:27
  7.7 5.7 %collective-permute-start.4 = (f32[3,16,128]{2,1,0:T(8,128)S(1)}, f32[3,16,128]{2,1,0:T(8,128)S(1)}, u32[]{:S(2)}, u32[]{:S(2)}) collective-permute-start(f32[3,16,128]{2,1,0:T(8,128)S(1)} %get-tuple-element.24), channel_id=1, source_target_pairs={{1,0},{2,1},{3,2},{4,3},{5,4},{6,5},{7,6},{8,7},{9,8},{10,9},{11,1... | collective-permute-start | bytes 73736 | tf_op jit(solution)/shard_map/ppermute | solution.py:27
  11.3 0.7 copy-start.7
  12.1 0.7 copy-start.4
  12.1 0.7 copy-start.5
  13.4 2.0 %copy-start.6 = (s32[1,768]{1,0:T(1,128)S(1)}, s32[1,768]{1,0:T(1,128)}, u32[]{:S(2)}) copy-start(s32[1,768]{1,0:T(1,128)} %param.10) | copy-start | bytes 9220
  13.5 3.4 %collective-permute-start.7 = (f32[32,1,1152]{2,1,0:T(1,128)S(1)}, f32[32,1,1152]{2,1,0:T(1,128)}, u32[]{:S(2)}, u32[]{:S(2)}) collective-permute-start(f32[32,1,1152]{2,1,0:T(1,128)S(1)} %bitcast.58), channel_id=1, source_target_pairs={{0,256},{256,0},{1,257},{257,1},{2,258},{258,2},{3,259},{259,3},{4... | collective-permute-start | bytes 442376 | tf_op jit(solution)/shard_map/ppermute | solution.py:511
  16.9 23.6 %all-to-all-start = ((f32[32,1,1152]{2,1,0:T(1,128)}), f32[32,1,1152]{2,1,0:T(1,128)S(1)}, u32[]{:S(2)}, u32[]{:S(2)}) async-start(f32[32,1,1152]{2,1,0:T(1,128)} %collective-permute-done.7), calls=%async_computation | async-start | bytes 294912 | tf_op jit(solution)/shard_map/all_to_all | solution.py:512
  42.0 7.8 %copy-start.2 = (f32[1,3,16,8,128]{4,3,2,1,0:T(8,128)S(1)}, f32[1,3,16,8,128]{4,3,2,1,0:T(8,128)}, u32[]{:S(2)}) copy-start(f32[1,3,16,8,128]{4,3,2,1,0:T(8,128)} %param.8) | copy-start | bytes 589828
  42.0 7.8 %copy-start.3 = (f32[1,16,8,128]{3,2,1,0:T(8,128)S(1)}, f32[1,16,8,128]{3,2,1,0:T(8,128)}, u32[]{:S(2)}) copy-start(f32[1,16,8,128]{3,2,1,0:T(8,128)} %param.9) | copy-start | bytes 196612
  42.0 31.8 %all-to-all-start.1 = ((f32[8,96,128]{2,1,0:T(8,128)}), f32[8,96,128]{2,1,0:T(8,128)S(1)}, u32[]{:S(2)}, u32[]{:S(2)}) async-start(f32[8,96,128]{2,1,0:T(8,128)} %bitcast.10), calls=%async_computation.1 | async-start | bytes 786432 | tf_op jit(solution)/shard_map/all_to_all | solution.py:525
  49.9 10.4 %collective-permute-start = (f32[64,8,128]{2,1,0:T(8,128)S(1)}, f32[64,8,128]{2,1,0:T(8,128)S(1)}, u32[]{:S(2)}, u32[]{:S(2)}) collective-permute-start(f32[64,8,128]{2,1,0:T(8,128)S(1)} %get-tuple-element.16), channel_id=1, source_target_pairs={{0,1},{1,2},{2,3},{3,4},{4,5},{5,6},{6,7},{7,8},{8,9},{9,10},{10,1... | collective-permute-start | bytes 786440 | tf_op jit(solution)/shard_map/ppermute | solution.py:27
  52.3 9.4 %collective-permute-start.1 = (f32[64,8,128]{2,1,0:T(8,128)S(1)}, f32[64,8,128]{2,1,0:T(8,128)S(1)}, u32[]{:S(2)}, u32[]{:S(2)}) collective-permute-start(f32[64,8,128]{2,1,0:T(8,128)S(1)} %get-tuple-element.17), channel_id=1, source_target_pairs={{1,0},{2,1},{3,2},{4,3},{5,4},{6,5},{7,6},{8,7},{9,8},{10,9},{11,1... | collective-permute-start | bytes 786440 | tf_op jit(solution)/shard_map/ppermute | solution.py:27
  61.7 8.0 %collective-permute-start.2 = (f32[57,8,128]{2,1,0:T(8,128)S(1)}, f32[57,8,128]{2,1,0:T(8,128)S(1)}, u32[]{:S(2)}, u32[]{:S(2)}) collective-permute-start(f32[57,8,128]{2,1,0:T(8,128)S(1)} %get-tuple-element.18), channel_id=1, source_target_pairs={{0,32},{1,33},{2,34},{3,35},{4,36},{5,37},{6,38},{7,39},{8,40},{9,... | collective-permute-start | bytes 700424 | tf_op jit(solution)/shard_map/ppermute | solution.py:27
  65.1 8.6 %collective-permute-start.3 = (f32[57,8,128]{2,1,0:T(8,128)S(1)}, f32[57,8,128]{2,1,0:T(8,128)S(1)}, u32[]{:S(2)}, u32[]{:S(2)}) collective-permute-start(f32[57,8,128]{2,1,0:T(8,128)S(1)} %get-tuple-element.19), channel_id=1, source_target_pairs={{32,0},{33,1},{34,2},{35,3},{36,4},{37,5},{38,6},{39,7},{40,8},{41... | collective-permute-start | bytes 700424 | tf_op jit(solution)/shard_map/ppermute | solution.py:27
  78.5 15.8 %collective-permute-start.8 = (f32[10,8,128]{2,1,0:T(8,128)S(1)}, f32[10,8,128]{2,1,0:T(8,128)S(1)}, u32[]{:S(2)}, u32[]{:S(2)}) collective-permute-start(f32[10,8,128]{2,1,0:T(8,128)S(1)} %get-tuple-element.27), channel_id=1, source_target_pairs={{0,2},{1,3},{2,4},{3,5},{4,6},{5,7},{6,8},{7,9},{8,10},{9,11},{10,... | collective-permute-start | bytes 122888 | tf_op jit(solution)/shard_map/ppermute | solution.py:27
  81.5 18.9 %collective-permute-start.11 = (f32[10,8,128]{2,1,0:T(8,128)S(1)}, f32[10,8,128]{2,1,0:T(8,128)S(1)}, u32[]{:S(2)}, u32[]{:S(2)}) collective-permute-start(f32[10,8,128]{2,1,0:T(8,128)S(1)} %get-tuple-element.27), channel_id=1, source_target_pairs={{2,0},{3,1},{4,2},{5,3},{6,4},{7,5},{8,6},{9,7},{10,8},{11,9},{12,... | collective-permute-start | bytes 122888 | tf_op jit(solution)/shard_map/ppermute | solution.py:27
  86.7 13.6 %collective-permute-start.10 = (f32[10,8,128]{2,1,0:T(8,128)S(1)}, f32[10,8,128]{2,1,0:T(8,128)S(1)}, u32[]{:S(2)}, u32[]{:S(2)}) collective-permute-start(f32[10,8,128]{2,1,0:T(8,128)S(1)} %get-tuple-element.27), channel_id=1, source_target_pairs={{1,0},{2,1},{3,2},{4,3},{5,4},{6,5},{7,6},{8,7},{9,8},{10,9},{11,1... | collective-permute-start | bytes 122888 | tf_op jit(solution)/shard_map/ppermute | solution.py:27
  92.3 8.0 %collective-permute-start.9 = (f32[10,8,128]{2,1,0:T(8,128)S(1)}, f32[10,8,128]{2,1,0:T(8,128)S(1)}, u32[]{:S(2)}, u32[]{:S(2)}) collective-permute-start(f32[10,8,128]{2,1,0:T(8,128)S(1)} %get-tuple-element.27), channel_id=1, source_target_pairs={{0,1},{1,2},{2,3},{3,4},{4,5},{5,6},{6,7},{7,8},{8,9},{9,10},{10,1... | collective-permute-start | bytes 122888 | tf_op jit(solution)/shard_map/ppermute | solution.py:27
  100.5 7.8 %collective-permute-start.12 = (f32[35,8,128]{2,1,0:T(8,128)S(1)}, f32[35,8,128]{2,1,0:T(8,128)S(1)}, u32[]{:S(2)}, u32[]{:S(2)}) collective-permute-start(f32[35,8,128]{2,1,0:T(8,128)S(1)} %constant_dynamic-update-slice_fusion.8), channel_id=1, source_target_pairs={{0,32},{1,33},{2,34},{3,35},{4,36},{5,37},{6,38},{7,39},{8,40},{9,... | collective-permute-start | bytes 430088 | tf_op jit(solution)/shard_map/ppermute | solution.py:27
  105.7 7.0 %collective-permute-start.13 = (f32[35,8,128]{2,1,0:T(8,128)S(1)}, f32[35,8,128]{2,1,0:T(8,128)S(1)}, u32[]{:S(2)}, u32[]{:S(2)}) collective-permute-start(f32[35,8,128]{2,1,0:T(8,128)S(1)} %pad_maximum_fusion), channel_id=1, source_target_pairs={{32,0},{33,1},{34,2},{35,3},{36,4},{37,5},{38,6},{39,7},{40,8},{41... | collective-permute-start | bytes 430088 | tf_op jit(solution)/shard_map/ppermute | solution.py:27

commit v5 on v4

--- a/solution.py
+++ b/solution.py
@@ -59,28 +59,21 @@
             edge_ref[comp, 8 * j : 8 * j + 8] = first
 
 
-def cut_kernel(v_ref, f_ref, mu_ref, right_ref, left_ref):
-    sub = rows_of((8, 128))
-
-    def row(field, r):
-        if field == 6:
-            return mu_ref[r]
-        return v_ref[field, r] if field < 3 else f_ref[field - 3, r]
-
+def lat_tile(field, away):
+    if 3 <= field < 6:
+        return 20 + 4 * (field - 3) + away - 1
+    return 5 * min(field, 3) + away - 1
+
+
+def cut_kernel(v_ref, f_ref, mu_ref, up_ref, down_ref):
     for field in range(7):
-        for t in range(8):
-            even, odd = row(field, 2 * t), roll(row(field, 2 * t + 1), 4, 0)
-            right_ref[8 * field + t] = jnp.where(sub < 4, odd, even)
-            left_ref[8 * field + t] = jnp.where(sub < 4, even, odd)
-    for n, field in enumerate((0, 1, 2, 6)):
-        for j in range(2):
-            third = fourth = row(field, 8 * j)
-            for r in range(8):
-                value = row(field, 8 * j + r)
-                third = jnp.where(sub == r, roll(value, r - 3, 0), third)
-                fourth = jnp.where(sub == r, roll(value, r - 4, 0), fourth)
-            right_ref[56 + 2 * n + j] = third
-            left_ref[56 + 2 * n + j] = fourth
+        for away in range(1, 5 if 3 <= field < 6 else 6):
+            for ref, r in ((up_ref, away - 1), (down_ref, 16 - away)):
+                if field == 6:
+                    value = mu_ref[r]
+                else:
+                    value = v_ref[field, r] if field < 3 else f_ref[field - 3, r]
+                ref[lat_tile(field, away)] = value
 
 
 def blend_kernel(rows_ref, cols_ref, weights_ref, v_ref, own_ref, edge_ref, below_ref, corner_ref):
@@ -142,40 +135,43 @@
             copy(last_lat, position)
 
 
-def lat_tile(field, away, side):
-    if field in (0, 1, 2, 6):
-        return 9 * (field if field < 6 else 3) + (5 if side else 0) + away - 1
-    return 36 + 7 * (field - 3) + (4 if side else 0) + away - 1
-
-
 def side_tile(ref, field, r, col, sub):
-    value = ref[8 * field + r // 2]
+    value = ref[12 * field + (r + 4) // 2]
     if r % 2:
         value = roll(value, 4, 0)
     extra = {0: 0, 1: 1, 2: 2, 6: 3}.get(field)
-    if extra is None:
+    if extra is None or not 0 <= r < 16:
         return value
-    fifth = roll(ref[56 + 2 * extra + r // 8], col - r % 8, 0)
+    fifth = roll(ref[84 + 2 * extra + r // 8], col - r % 8, 0)
     return jnp.where(sub == col, fifth, value)
 
 
-def pack_kernel(v_ref, f_ref, mu_ref, left_ref, right_ref, up_ref, down_ref):
+def pack_kernel(v_ref, f_ref, mu_ref, above_ref, below_ref, right_ref, left_ref):
     sub = rows_of((8, 128))
+
+    def row(field, r):
+        if r < 0:
+            return above_ref[lat_tile(field, -r)]
+        if r > 15:
+            return below_ref[lat_tile(field, r - 15)]
+        if field == 6:
+            return mu_ref[r]
+        return v_ref[field, r] if field < 3 else f_ref[field - 3, r]
+
     for field in range(7):
-        force = 3 <= field < 6
-        for away in range(1, 5 if force else 6):
-            for ref, r in ((up_ref, away - 1), (down_ref, 16 - away)):
-                if field == 6:
-                    value = mu_ref[r]
-                else:
-                    value = f_ref[field - 3, r] if force else v_ref[field, r]
-                ref[lat_tile(field, away, False)] = value
-                if away < (4 if force else 5):
-                    ref[lat_tile(field, away, True)] = jnp.where(
-                        sub < 4,
-                        side_tile(right_ref, field, r, 4, sub),
-                        side_tile(left_ref, field, r, 3, sub),
-                    )
+        for t in range(12):
+            even, odd = row(field, 2 * t - 4), roll(row(field, 2 * t - 3), 4, 0)
+            right_ref[12 * field + t] = jnp.where(sub < 4, odd, even)
+            left_ref[12 * field + t] = jnp.where(sub < 4, even, odd)
+    for n, field in enumerate((0, 1, 2, 6)):
+        for j in range(2):
+            third = fourth = row(field, 8 * j)
+            for r in range(8):
+                value = row(field, 8 * j + r)
+                third = jnp.where(sub == r, roll(value, r - 3, 0), third)
+                fourth = jnp.where(sub == r, roll(value, r - 4, 0), fourth)
+            right_ref[84 + 2 * n + j] = third
+            left_ref[84 + 2 * n + j] = fourth
 
 
 def prepare(
@@ -189,19 +185,16 @@
     odd_lane, odd_row = (lane & 1) == 1, (row & 1) == 1
     own = slice(PAD, PAD + 16)
     sub = rows_of((8, 128))
-
-    def outer(ref, field, away, side):
-        return ref[lat_tile(field, away, side)]
-
     MU[own, 8:16] = mu_ref[...]
-    for r in range(16):
+    for r in range(-4, 20):
         MU[r + PAD, 0:8] = side_tile(left_ref, 6, r, 3, sub)
         MU[r + PAD, 16:24] = side_tile(right_ref, 6, r, 4, sub)
     for away in range(1, 6):
         for i, ref in ((PAD - away, above_ref), (PAD + 15 + away, below_ref)):
-            value = outer(ref, 6, away, False)
-            beside = outer(ref, 6, away, True) if away < 5 else value
-            MU[i, 0:8], MU[i, 8:16], MU[i, 16:24] = beside, value, beside
+            value = ref[lat_tile(6, away)]
+            MU[i, 8:16] = value
+            if away == 5:
+                MU[i, 0:8] = MU[i, 16:24] = value
 
     @pl.when(lat == 0)
     def _():
@@ -245,16 +238,12 @@
         for comp in range(3):
             if 0 <= r < 16:
                 force = f_ref[comp, r]
-                west_force = side_tile(left_ref, 3 + comp, r, 3, sub)
-                east_force = side_tile(right_ref, 3 + comp, r, 4, sub)
             else:
                 ref, away = (above_ref, -r) if r < 0 else (below_ref, r - 15)
-                force = outer(ref, 3 + comp, away, False)
-                beside = outer(ref, 3 + comp, away, True) if away < 4 else force
-                west_force = east_force = beside
-            F[comp, i, 0:8] = west_force * inverse[0:8]
+                force = ref[lat_tile(3 + comp, away)]
+            F[comp, i, 0:8] = side_tile(left_ref, 3 + comp, r, 3, sub) * inverse[0:8]
             F[comp, i, 8:16] = force * inverse[8:16]
-            F[comp, i, 16:24] = east_force * inverse[16:24]
+            F[comp, i, 16:24] = side_tile(right_ref, 3 + comp, r, 4, sub) * inverse[16:24]
 
     def coarse_visc(i):
         both = MU[i] + MU[i + 1]
@@ -287,14 +276,15 @@
 
     for comp in range(3):
         A[comp, own, 8:16] = v_ref[comp]
-        for r in range(16):
+        for r in range(-4, 20):
             A[comp, r + PAD, 0:8] = side_tile(left_ref, comp, r, 3, sub)
             A[comp, r + PAD, 16:24] = side_tile(right_ref, comp, r, 4, sub)
         for away in range(1, 6):
             for i, ref in ((PAD - away, above_ref), (PAD + 15 + away, below_ref)):
-                value = ref[lat_tile(comp, away, False)]
-                beside = ref[lat_tile(comp, away, True)] if away < 5 else value
-                A[comp, i, 0:8], A[comp, i, 8:16], A[comp, i, 16:24] = beside, value, beside
+                value = ref[lat_tile(comp, away)]
+                A[comp, i, 8:16] = value
+                if away == 5:
+                    A[comp, i, 0:8] = A[comp, i, 16:24] = value
 
     edge = (lon == 0) | (lon == last_lon)
     all_cols, all_rows = (last_lon + 1) * 8, (last_lat + 1) * 16
@@ -499,9 +489,6 @@
     edge = shifted(edge, 0, -1)
     first_cell = shifted(first_cell, -1, -1)
     first_row = shifted(first_row, -1, 0)
-    to_right, to_left = kernel(cut_kernel, ((64, 8, 128),) * 2, [VMEM] * 3)(v, f, mu)
-    left = shifted(to_right, 0, 1)
-    right = shifted(to_left, 0, -1)
     blended = kernel(
         blend_kernel, ((9, 1, 128), (3, 16, 128), (3, 8, 128), (3, 1, 128)), [SMEM] * 3 + [VMEM]
     )(corner_rows[0, 0], corner_cols[0, 0], corner_weights[0, 0], v)
@@ -510,7 +497,7 @@
     )
     values = lax.ppermute(values.reshape(lons, 1, 1152), "patch", [(0, 1), (1, 0)])
     around = lax.all_to_all(values, "lon", 0, 0, tiled=True)
-    to_above, to_below = kernel(pack_kernel, ((57, 8, 128),) * 2, [VMEM] * 5)(v, f, mu, left, right)
+    to_above, to_below = kernel(cut_kernel, ((32, 8, 128),) * 2, [VMEM] * 3)(v, f, mu)
     below = shifted(to_above, -1, 0)
     above = shifted(to_below, 1, 0)
 
@@ -524,6 +511,9 @@
     )(place, cells, source_rows, around.reshape(lons * 9, 1, 128))
     everything = lax.all_to_all(chosen.reshape(lats, 3 * CELLS, 128), "lat", 0, 0, tiled=True)
     everything = everything.reshape(lats * 3 * CELLS, 1, 128)
+    to_right, to_left = kernel(pack_kernel, ((92, 8, 128),) * 2, [VMEM] * 5)(v, f, mu, above, below)
+    left = shifted(to_right, 0, 1)
+    right = shifted(to_left, 0, -1)
 
     block = jax.ShapeDtypeStruct((3, 16, 8, 128), f32)
     field = (3, 28, 24, 128)

time: 115 us -> 118 us (1.026)
  the two profiles are of different devices: /device:TPU:80 before, /device:TPU:88 now
where the time goes in v5:
time: 118 us; the launch traced here: 117 us
  starting transfers between devices  67.9 us (58%)
  waiting for transfers between devices  35.8 us (30%)
  Pallas kernels  8.86 us (8%)
  local copies, waits for them, and re-layouts  2.92 us (2%)
    ppermute x13, starting transfers between devices, shifted(): return lax.ppermute(value, AXES, pairs)  44.9 us
    ppermute x13, waiting for transfers between devices, shifted(): return lax.ppermute(value, AXES, pairs)  24.3 us
    all_to_all x1, starting transfers between devices, per_device(): around = lax.all_to_all(values, 'lon', 0, 0, tiled=True)  13.4 us
    all_to_all x1, waiting for transfers between devices, per_device(): around = lax.all_to_all(values, 'lon', 0, 0, tiled=True)  10.1 us
    all_to_all x1, starting transfers between devices, per_device(): lax.all_to_all(chosen.reshape(lats, 3 * CELLS, 128), 'lat', 0, 0, tiled=T...  7.68 us
    pallas_call x1, Pallas kernels, per_device(): pl.pallas_call(smooth_kernel, out_shape=(block, block, jax.ShapeDtypeStru...  4.71 us
    unnamed x27, local copies, waits for them, and re-layouts  2.41 us
  transfers between devices with their start and end apart: 16, of which 10 were waited for; matrix products, arithmetic and copies ran while one was open for 1% of the time, Pallas kernels for 1%

profile of v5, /device:TPU:88, one launch (start us, length us, event | category | flops | bytes accessed | tf_op | source)
XLA Modules:
  0.0 117.0 jit_solution(1130797768087255467)
XLA Ops:
  0.6 0.0 copy-start
  0.6 0.9 copy-done
  1.6 0.0 copy-start.1
  1.6 3.8 %collective-permute-start.6 = (f32[3,128]{1,0:T(4,128)S(1)}, f32[3,128]{1,0:T(4,128)S(1)}, u32[]{:S(2)}, u32[]{:S(2)}) collective-permute-start(f32[3,128]{1,0:T(4,128)S(1)} %get-tuple-element.26), channel_id=1, source_target_pairs={{33,0},{34,1},{35,2},{36,3},{37,4},{38,5},{39,6},{40,7},{41,8},{42... | collective-permute-start | bytes 4616 | tf_op jit(solution)/shard_map/ppermute | solution.py:27
  5.4 2.4 %collective-permute-start.5 = (f32[3,8,128]{2,1,0:T(8,128)S(1)}, f32[3,8,128]{2,1,0:T(8,128)S(1)}, u32[]{:S(2)}, u32[]{:S(2)}) collective-permute-start(f32[3,8,128]{2,1,0:T(8,128)S(1)} %get-tuple-element.25), channel_id=1, source_target_pairs={{32,0},{33,1},{34,2},{35,3},{36,4},{37,5},{38,6},{39,7},{40,8},{41... | collective-permute-start | bytes 36872 | tf_op jit(solution)/shard_map/ppermute | solution.py:27
  7.7 2.7 %collective-permute-start.4 = (f32[3,16,128]{2,1,0:T(8,128)S(1)}, f32[3,16,128]{2,1,0:T(8,128)S(1)}, u32[]{:S(2)}, u32[]{:S(2)}) collective-permute-start(f32[3,16,128]{2,1,0:T(8,128)S(1)} %get-tuple-element.24), channel_id=1, source_target_pairs={{1,0},{2,1},{3,2},{4,3},{5,4},{6,5},{7,6},{8,7},{9,8},{10,9},{11,1... | collective-permute-start | bytes 73736 | tf_op jit(solution)/shard_map/ppermute | solution.py:27
  10.6 0.1 fusion.8
  10.6 0.1 reshape.135
  10.7 0.1 iota_select_fusion
  10.8 0.1 select_n.73
  10.9 0.1 clamp_add_fusion
  11.0 0.1 reshape.134
  11.0 0.1 add.104
  11.1 0.1 add.105
  11.2 0.1 broadcast_in_dim.43
  11.3 0.0 copy-start.7
  11.3 0.7 copy-done.7
  12.0 0.1 copy.10
  12.1 0.0 copy-start.4
  12.1 0.0 copy-done.1
  12.1 0.6 copy-done.4
  12.7 0.0 copy-done.5
  12.7 0.6 shard_map.88
  13.3 0.0 collective-permute-done.6.corner_ref
  13.3 0.0 collective-permute-done.5.below_ref
  13.4 0.1 collective-permute-done.4.edge_ref
  13.4 0.0 copy-start.6
  13.5 0.1 shard_map.90
  13.5 1.9 %collective-permute-start.7 = (f32[32,1,1152]{2,1,0:T(1,128)S(1)}, f32[32,1,1152]{2,1,0:T(1,128)}, u32[]{:S(2)}, u32[]{:S(2)}) collective-permute-start(f32[32,1,1152]{2,1,0:T(1,128)S(1)} %bitcast.58), channel_id=1, source_target_pairs={{0,256},{256,0},{1,257},{257,1},{2,258},{258,2},{3,259},{259,3},{4... | collective-permute-start | bytes 442376 | tf_op jit(solution)/shard_map/ppermute | solution.py:498
  15.5 0.0 copy-done.6
  15.6 1.4 %collective-permute-done.7 = f32[32,1,1152]{2,1,0:T(1,128)} collective-permute-done((f32[32,1,1152]{2,1,0:T(1,128)S(1)}, f32[32,1,1152]{2,1,0:T(1,128)}, u32[]{:S(2)}, u32[]{:S(2)}) %collective-permute-start.7) | collective-permute-done | bytes 147488 | tf_op jit(solution)/shard_map/ppermute | solution.py:498
  16.9 13.4 %all-to-all-start = ((f32[32,1,1152]{2,1,0:T(1,128)}), f32[32,1,1152]{2,1,0:T(1,128)S(1)}, u32[]{:S(2)}, u32[]{:S(2)}) async-start(f32[32,1,1152]{2,1,0:T(1,128)} %collective-permute-done.7), calls=%async_computation | async-start | bytes 294912 | tf_op jit(solution)/shard_map/all_to_all | solution.py:499
  30.3 0.1 pad_add_fusion.place_ref
  30.4 10.1 %all-to-all-done = f32[32,1,1152]{2,1,0:T(1,128)S(1)} async-done(((f32[32,1,1152]{2,1,0:T(1,128)}), f32[32,1,1152]{2,1,0:T(1,128)S(1)}, u32[]{:S(2)}, u32[]{:S(2)}) %all-to-all-start) | async-done | bytes 147488 | tf_op jit(solution)/shard_map/all_to_all | solution.py:499
  40.6 1.4 %pick.1 = f32[768,1,128]{2,1,0:T(1,128)} custom-call(s32[4]{0:T(128)S(1)} %pad_add_fusion.place_ref, s32[256]{0:T(256)S(1)} %add_select_fusion.4.cells_ref, s32[768]{0:T(1024)S(1)} %get-tuple-element.43.source_ref, f32[288,1,128]{2,1,0:T(1,128)S(1)} %bitcast.54), custom_call_target="tpu_custom_call" | custom-call | tf_op jit(solution)/shard_map/pick/pallas_call | solution.py:504
  42.0 0.0 copy-start.2
  42.0 0.0 copy-start.3
  42.0 7.7 %all-to-all-start.1 = ((f32[8,96,128]{2,1,0:T(8,128)}), f32[8,96,128]{2,1,0:T(8,128)S(1)}, u32[]{:S(2)}, u32[]{:S(2)}) async-start(f32[8,96,128]{2,1,0:T(8,128)} %bitcast.10), calls=%async_computation.1 | async-start | bytes 786432 | tf_op jit(solution)/shard_map/all_to_all | solution.py:512
  49.7 0.0 copy-done.2
  49.7 0.0 copy-done.3
  49.7 4.6 %collective-permute-start = (f32[32,8,128]{2,1,0:T(8,128)S(1)}, f32[32,8,128]{2,1,0:T(8,128)S(1)}, u32[]{:S(2)}, u32[]{:S(2)}) collective-permute-start(f32[32,8,128]{2,1,0:T(8,128)S(1)} %get-tuple-element.16), channel_id=1, source_target_pairs={{0,32},{1,33},{2,34},{3,35},{4,36},{5,37},{6,38},{7,39},{8,40},{9,... | collective-permute-start | bytes 393224 | tf_op jit(solution)/shard_map/ppermute | solution.py:27
  54.3 1.9 %collective-permute-start.1 = (f32[32,8,128]{2,1,0:T(8,128)S(1)}, f32[32,8,128]{2,1,0:T(8,128)S(1)}, u32[]{:S(2)}, u32[]{:S(2)}) collective-permute-start(f32[32,8,128]{2,1,0:T(8,128)S(1)} %get-tuple-element.17), channel_id=1, source_target_pairs={{32,0},{33,1},{34,2},{35,3},{36,4},{37,5},{38,6},{39,7},{40,8},{41... | collective-permute-start | bytes 393224 | tf_op jit(solution)/shard_map/ppermute | solution.py:27
  56.2 3.8 %collective-permute-done.above_ref = f32[32,8,128]{2,1,0:T(8,128)S(1)} collective-permute-done((f32[32,8,128]{2,1,0:T(8,128)S(1)}, f32[32,8,128]{2,1,0:T(8,128)S(1)}, u32[]{:S(2)}, u32[]{:S(2)}) %collective-permute-start) | collective-permute-done | bytes 131104 | tf_op jit(solution)/shard_map/ppermute | solution.py:27
  60.0 2.4 %collective-permute-done.1.below_ref = f32[32,8,128]{2,1,0:T(8,128)S(1)} collective-permute-done((f32[32,8,128]{2,1,0:T(8,128)S(1)}, f32[32,8,128]{2,1,0:T(8,128)S(1)}, u32[]{:S(2)}, u32[]{:S(2)}) %collective-permute-start.1) | collective-permute-done | bytes 131104 | tf_op jit(solution)/shard_map/ppermute | solution.py:27
  62.4 0.1 shard_map.87
  62.5 2.7 %collective-permute-start.2 = (f32[92,8,128]{2,1,0:T(8,128)S(1)}, f32[92,8,128]{2,1,0:T(8,128)S(1)}, u32[]{:S(2)}, u32[]{:S(2)}) collective-permute-start(f32[92,8,128]{2,1,0:T(8,128)S(1)} %get-tuple-element.18), channel_id=1, source_target_pairs={{0,1},{1,2},{2,3},{3,4},{4,5},{5,6},{6,7},{7,8},{8,9},{9,10},{10,1... | collective-permute-start | bytes 1130504 | tf_op jit(solution)/shard_map/ppermute | solution.py:27
  65.2 5.3 %collective-permute-start.3 = (f32[92,8,128]{2,1,0:T(8,128)S(1)}, f32[92,8,128]{2,1,0:T(8,128)S(1)}, u32[]{:S(2)}, u32[]{:S(2)}) collective-permute-start(f32[92,8,128]{2,1,0:T(8,128)S(1)} %get-tuple-element.19), channel_id=1, source_target_pairs={{1,0},{2,1},{3,2},{4,3},{5,4},{6,5},{7,6},{8,7},{9,8},{10,9},{11,1... | collective-permute-start | bytes 1130504 | tf_op jit(solution)/shard_map/ppermute | solution.py:27
  70.4 5.0 %collective-permute-done.2.left_ref = f32[92,8,128]{2,1,0:T(8,128)S(1)} collective-permute-done((f32[92,8,128]{2,1,0:T(8,128)S(1)}, f32[92,8,128]{2,1,0:T(8,128)S(1)}, u32[]{:S(2)}, u32[]{:S(2)}) %collective-permute-start.2) | collective-permute-done | bytes 376864 | tf_op jit(solution)/shard_map/ppermute | solution.py:27
  75.4 1.2 %collective-permute-done.3.right_ref = f32[92,8,128]{2,1,0:T(8,128)S(1)} collective-permute-done((f32[92,8,128]{2,1,0:T(8,128)S(1)}, f32[92,8,128]{2,1,0:T(8,128)S(1)}, u32[]{:S(2)}, u32[]{:S(2)}) %collective-permute-start.3) | collective-permute-done | bytes 376864 | tf_op jit(solution)/shard_map/ppermute | solution.py:27
  76.6 0.0 all-to-all-done.1
  76.6 4.7 %smooth.1 = (f32[3,16,8,128]{3,2,1,0:T(8,128)}, f32[3,16,8,128]{3,2,1,0:T(8,128)S(1)}, f32[10,8,128]{2,1,0:T(8,128)S(1)}) custom-call(s32[4]{0:T(128)S(1)} %pad_add_fusion.place_ref, s32[768]{0:T(1024)S(1)} %get-tuple-element.44.ghost_ref, f32[3,16,8,128]{3,2,1,0:T(8,128)S(1)} %bitcast.49, f32[3,16,8,128]{3,2,1,0:T(8,128)S(1)} %bitcast.52, ...), custom_call_target="tpu_custom_call" | custom-call | tf_op jit(solution)/shard_map/smooth/pallas_call | solution.py:520
  81.3 4.4 %collective-permute-start.8 = (f32[10,8,128]{2,1,0:T(8,128)S(1)}, f32[10,8,128]{2,1,0:T(8,128)S(1)}, u32[]{:S(2)}, u32[]{:S(2)}) collective-permute-start(f32[10,8,128]{2,1,0:T(8,128)S(1)} %get-tuple-element.27), channel_id=1, source_target_pairs={{0,2},{1,3},{2,4},{3,5},{4,6},{5,7},{6,8},{7,9},{8,10},{9,11},{10,... | collective-permute-start | bytes 122888 | tf_op jit(solution)/shard_map/ppermute | solution.py:27
  85.7 3.8 %collective-permute-start.11 = (f32[10,8,128]{2,1,0:T(8,128)S(1)}, f32[10,8,128]{2,1,0:T(8,128)S(1)}, u32[]{:S(2)}, u32[]{:S(2)}) collective-permute-start(f32[10,8,128]{2,1,0:T(8,128)S(1)} %get-tuple-element.27), channel_id=1, source_target_pairs={{2,0},{3,1},{4,2},{5,3},{6,4},{7,5},{8,6},{9,7},{10,8},{11,9},{12,... | collective-permute-start | bytes 122888 | tf_op jit(solution)/shard_map/ppermute | solution.py:27
  89.5 5.6 %collective-permute-start.10 = (f32[10,8,128]{2,1,0:T(8,128)S(1)}, f32[10,8,128]{2,1,0:T(8,128)S(1)}, u32[]{:S(2)}, u32[]{:S(2)}) collective-permute-start(f32[10,8,128]{2,1,0:T(8,128)S(1)} %get-tuple-element.27), channel_id=1, source_target_pairs={{1,0},{2,1},{3,2},{4,3},{5,4},{6,5},{7,6},{8,7},{9,8},{10,9},{11,1... | collective-permute-start | bytes 122888 | tf_op jit(solution)/shard_map/ppermute | solution.py:27
  95.1 1.9 %collective-permute-start.9 = (f32[10,8,128]{2,1,0:T(8,128)S(1)}, f32[10,8,128]{2,1,0:T(8,128)S(1)}, u32[]{:S(2)}, u32[]{:S(2)}) collective-permute-start(f32[10,8,128]{2,1,0:T(8,128)S(1)} %get-tuple-element.27), channel_id=1, source_target_pairs={{0,1},{1,2},{2,3},{3,4},{4,5},{5,6},{6,7},{7,8},{8,9},{9,10},{10,1... | collective-permute-start | bytes 122888 | tf_op jit(solution)/shard_map/ppermute | solution.py:27
  97.1 0.0 collective-permute-done.8
  97.1 6.1 %collective-permute-done.9 = f32[10,8,128]{2,1,0:T(8,128)S(1)} collective-permute-done((f32[10,8,128]{2,1,0:T(8,128)S(1)}, f32[10,8,128]{2,1,0:T(8,128)S(1)}, u32[]{:S(2)}, u32[]{:S(2)}) %collective-permute-start.9) | collective-permute-done | bytes 40992 | tf_op jit(solution)/shard_map/ppermute | solution.py:27
  103.2 0.0 collective-permute-done.10
  103.2 0.0 collective-permute-done.11
  103.3 3.5 %collective-permute-start.12 = (f32[35,8,128]{2,1,0:T(8,128)S(1)}, f32[35,8,128]{2,1,0:T(8,128)S(1)}, u32[]{:S(2)}, u32[]{:S(2)}) collective-permute-start(f32[35,8,128]{2,1,0:T(8,128)S(1)} %constant_dynamic-update-slice_fusion.8), channel_id=1, source_target_pairs={{0,32},{1,33},{2,34},{3,35},{4,36},{5,37},{6,38},{7,39},{8,40},{9,... | collective-permute-start | bytes 430088 | tf_op jit(solution)/shard_map/ppermute | solution.py:27
  106.9 2.3 %collective-permute-start.13 = (f32[35,8,128]{2,1,0:T(8,128)S(1)}, f32[35,8,128]{2,1,0:T(8,128)S(1)}, u32[]{:S(2)}, u32[]{:S(2)}) collective-permute-start(f32[35,8,128]{2,1,0:T(8,128)S(1)} %pad_maximum_fusion), channel_id=1, source_target_pairs={{32,0},{33,1},{34,2},{35,3},{36,4},{37,5},{38,6},{39,7},{40,8},{41... | collective-permute-start | bytes 430088 | tf_op jit(solution)/shard_map/ppermute | solution.py:27
  109.2 1.1 collective-permute-done.12.above_ref
  110.3 4.7 %collective-permute-done.13.below_ref = f32[35,8,128]{2,1,0:T(8,128)S(1)} collective-permute-done((f32[35,8,128]{2,1,0:T(8,128)S(1)}, f32[35,8,128]{2,1,0:T(8,128)S(1)}, u32[]{:S(2)}, u32[]{:S(2)}) %collective-permute-start.13) | collective-permute-done | bytes 143392 | tf_op jit(solution)/shard_map/ppermute | solution.py:27
  115.1 1.9 %coarse.1 = f32[3,16,8,128]{3,2,1,0:T(8,128)} custom-call(f32[10,40,128]{2,1,0:T(8,128)S(1)} %constant_dynamic-update-slice_fusion.mid_ref, f32[35,8,128]{2,1,0:T(8,128)S(1)} %collective-permute-done.12.above_ref, f32[35,8,128]{2,1,0:T(8,128)S(1)} %collective-permute-done.13.below_ref, f32[3,16,8,128]{3,2,1,0:T(8,128)S(1)} %get-tuple-element.28.smooth_ref), custom_call_target="tpu_custom_call" | custom-call | tf_op jit(solution)/shard_map/coarse/pallas_call | solution.py:550
  (31 shorter events, 0.3 us)
Async XLA Ops:
  0.6 0.9 copy-start
  1.6 10.5 %copy-start.1 = (f32[1,3,16,8,128]{4,3,2,1,0:T(8,128)S(1)}, f32[1,3,16,8,128]{4,3,2,1,0:T(8,128)}, u32[]{:S(2)}) copy-start(f32[1,3,16,8,128]{4,3,2,1,0:T(8,128)} %param.7) | copy-start | bytes 589828
  1.6 11.8 %collective-permute-start.6 = (f32[3,128]{1,0:T(4,128)S(1)}, f32[3,128]{1,0:T(4,128)S(1)}, u32[]{:S(2)}, u32[]{:S(2)}) collective-permute-start(f32[3,128]{1,0:T(4,128)S(1)} %get-tuple-element.26), channel_id=1, source_target_pairs={{33,0},{34,1},{35,2},{36,3},{37,4},{38,5},{39,6},{40,7},{41,8},{42... | collective-permute-start | bytes 4616 | tf_op jit(solution)/shard_map/ppermute | solution.py:27
  5.4 8.0 %collective-permute-start.5 = (f32[3,8,128]{2,1,0:T(8,128)S(1)}, f32[3,8,128]{2,1,0:T(8,128)S(1)}, u32[]{:S(2)}, u32[]{:S(2)}) collective-permute-start(f32[3,8,128]{2,1,0:T(8,128)S(1)} %get-tuple-element.25), channel_id=1, source_target_pairs={{32,0},{33,1},{34,2},{35,3},{36,4},{37,5},{38,6},{39,7},{40,8},{41... | collective-permute-start | bytes 36872 | tf_op jit(solution)/shard_map/ppermute | solution.py:27
  7.7 5.7 %collective-permute-start.4 = (f32[3,16,128]{2,1,0:T(8,128)S(1)}, f32[3,16,128]{2,1,0:T(8,128)S(1)}, u32[]{:S(2)}, u32[]{:S(2)}) collective-permute-start(f32[3,16,128]{2,1,0:T(8,128)S(1)} %get-tuple-element.24), channel_id=1, source_target_pairs={{1,0},{2,1},{3,2},{4,3},{5,4},{6,5},{7,6},{8,7},{9,8},{10,9},{11,1... | collective-permute-start | bytes 73736 | tf_op jit(solution)/shard_map/ppermute | solution.py:27
  11.3 0.7 copy-start.7
  12.1 0.7 copy-start.4
  12.1 0.7 copy-start.5
  13.4 2.0 %copy-start.6 = (s32[1,768]{1,0:T(1,128)S(1)}, s32[1,768]{1,0:T(1,128)}, u32[]{:S(2)}) copy-start(s32[1,768]{1,0:T(1,128)} %param.10) | copy-start | bytes 9220
  13.5 3.4 %collective-permute-start.7 = (f32[32,1,1152]{2,1,0:T(1,128)S(1)}, f32[32,1,1152]{2,1,0:T(1,128)}, u32[]{:S(2)}, u32[]{:S(2)}) collective-permute-start(f32[32,1,1152]{2,1,0:T(1,128)S(1)} %bitcast.58), channel_id=1, source_target_pairs={{0,256},{256,0},{1,257},{257,1},{2,258},{258,2},{3,259},{259,3},{4... | collective-permute-start | bytes 442376 | tf_op jit(solution)/shard_map/ppermute | solution.py:498
  16.9 23.6 %all-to-all-start = ((f32[32,1,1152]{2,1,0:T(1,128)}), f32[32,1,1152]{2,1,0:T(1,128)S(1)}, u32[]{:S(2)}, u32[]{:S(2)}) async-start(f32[32,1,1152]{2,1,0:T(1,128)} %collective-permute-done.7), calls=%async_computation | async-start | bytes 294912 | tf_op jit(solution)/shard_map/all_to_all | solution.py:499
  42.0 7.7 %copy-start.2 = (f32[1,3,16,8,128]{4,3,2,1,0:T(8,128)S(1)}, f32[1,3,16,8,128]{4,3,2,1,0:T(8,128)}, u32[]{:S(2)}) copy-start(f32[1,3,16,8,128]{4,3,2,1,0:T(8,128)} %param.8) | copy-start | bytes 589828
  42.0 7.7 %copy-start.3 = (f32[1,16,8,128]{3,2,1,0:T(8,128)S(1)}, f32[1,16,8,128]{3,2,1,0:T(8,128)}, u32[]{:S(2)}) copy-start(f32[1,16,8,128]{3,2,1,0:T(8,128)} %param.9) | copy-start | bytes 196612
  42.0 34.6 %all-to-all-start.1 = ((f32[8,96,128]{2,1,0:T(8,128)}), f32[8,96,128]{2,1,0:T(8,128)S(1)}, u32[]{:S(2)}, u32[]{:S(2)}) async-start(f32[8,96,128]{2,1,0:T(8,128)} %bitcast.10), calls=%async_computation.1 | async-start | bytes 786432 | tf_op jit(solution)/shard_map/all_to_all | solution.py:512
  49.7 10.3 %collective-permute-start = (f32[32,8,128]{2,1,0:T(8,128)S(1)}, f32[32,8,128]{2,1,0:T(8,128)S(1)}, u32[]{:S(2)}, u32[]{:S(2)}) collective-permute-start(f32[32,8,128]{2,1,0:T(8,128)S(1)} %get-tuple-element.16), channel_id=1, source_target_pairs={{0,32},{1,33},{2,34},{3,35},{4,36},{5,37},{6,38},{7,39},{8,40},{9,... | collective-permute-start | bytes 393224 | tf_op jit(solution)/shard_map/ppermute | solution.py:27
  54.3 8.1 %collective-permute-start.1 = (f32[32,8,128]{2,1,0:T(8,128)S(1)}, f32[32,8,128]{2,1,0:T(8,128)S(1)}, u32[]{:S(2)}, u32[]{:S(2)}) collective-permute-start(f32[32,8,128]{2,1,0:T(8,128)S(1)} %get-tuple-element.17), channel_id=1, source_target_pairs={{32,0},{33,1},{34,2},{35,3},{36,4},{37,5},{38,6},{39,7},{40,8},{41... | collective-permute-start | bytes 393224 | tf_op jit(solution)/shard_map/ppermute | solution.py:27
  62.5 12.9 %collective-permute-start.2 = (f32[92,8,128]{2,1,0:T(8,128)S(1)}, f32[92,8,128]{2,1,0:T(8,128)S(1)}, u32[]{:S(2)}, u32[]{:S(2)}) collective-permute-start(f32[92,8,128]{2,1,0:T(8,128)S(1)} %get-tuple-element.18), channel_id=1, source_target_pairs={{0,1},{1,2},{2,3},{3,4},{4,5},{5,6},{6,7},{7,8},{8,9},{9,10},{10,1... | collective-permute-start | bytes 1130504 | tf_op jit(solution)/shard_map/ppermute | solution.py:27
  65.2 11.4 %collective-permute-start.3 = (f32[92,8,128]{2,1,0:T(8,128)S(1)}, f32[92,8,128]{2,1,0:T(8,128)S(1)}, u32[]{:S(2)}, u32[]{:S(2)}) collective-permute-start(f32[92,8,128]{2,1,0:T(8,128)S(1)} %get-tuple-element.19), channel_id=1, source_target_pairs={{1,0},{2,1},{3,2},{4,3},{5,4},{6,5},{7,6},{8,7},{9,8},{10,9},{11,1... | collective-permute-start | bytes 1130504 | tf_op jit(solution)/shard_map/ppermute | solution.py:27
  81.3 15.8 %collective-permute-start.8 = (f32[10,8,128]{2,1,0:T(8,128)S(1)}, f32[10,8,128]{2,1,0:T(8,128)S(1)}, u32[]{:S(2)}, u32[]{:S(2)}) collective-permute-start(f32[10,8,128]{2,1,0:T(8,128)S(1)} %get-tuple-element.27), channel_id=1, source_target_pairs={{0,2},{1,3},{2,4},{3,5},{4,6},{5,7},{6,8},{7,9},{8,10},{9,11},{10,... | collective-permute-start | bytes 122888 | tf_op jit(solution)/shard_map/ppermute | solution.py:27
  85.7 17.5 %collective-permute-start.11 = (f32[10,8,128]{2,1,0:T(8,128)S(1)}, f32[10,8,128]{2,1,0:T(8,128)S(1)}, u32[]{:S(2)}, u32[]{:S(2)}) collective-permute-start(f32[10,8,128]{2,1,0:T(8,128)S(1)} %get-tuple-element.27), channel_id=1, source_target_pairs={{2,0},{3,1},{4,2},{5,3},{6,4},{7,5},{8,6},{9,7},{10,8},{11,9},{12,... | collective-permute-start | bytes 122888 | tf_op jit(solution)/shard_map/ppermute | solution.py:27
  89.5 13.6 %collective-permute-start.10 = (f32[10,8,128]{2,1,0:T(8,128)S(1)}, f32[10,8,128]{2,1,0:T(8,128)S(1)}, u32[]{:S(2)}, u32[]{:S(2)}) collective-permute-start(f32[10,8,128]{2,1,0:T(8,128)S(1)} %get-tuple-element.27), channel_id=1, source_target_pairs={{1,0},{2,1},{3,2},{4,3},{5,4},{6,5},{7,6},{8,7},{9,8},{10,9},{11,1... | collective-permute-start | bytes 122888 | tf_op jit(solution)/shard_map/ppermute | solution.py:27
  95.1 8.0 %collective-permute-start.9 = (f32[10,8,128]{2,1,0:T(8,128)S(1)}, f32[10,8,128]{2,1,0:T(8,128)S(1)}, u32[]{:S(2)}, u32[]{:S(2)}) collective-permute-start(f32[10,8,128]{2,1,0:T(8,128)S(1)} %get-tuple-element.27), channel_id=1, source_target_pairs={{0,1},{1,2},{2,3},{3,4},{4,5},{5,6},{6,7},{7,8},{8,9},{9,10},{10,1... | collective-permute-start | bytes 122888 | tf_op jit(solution)/shard_map/ppermute | solution.py:27
  103.3 7.0 %collective-permute-start.12 = (f32[35,8,128]{2,1,0:T(8,128)S(1)}, f32[35,8,128]{2,1,0:T(8,128)S(1)}, u32[]{:S(2)}, u32[]{:S(2)}) collective-permute-start(f32[35,8,128]{2,1,0:T(8,128)S(1)} %constant_dynamic-update-slice_fusion.8), channel_id=1, source_target_pairs={{0,32},{1,33},{2,34},{3,35},{4,36},{5,37},{6,38},{7,39},{8,40},{9,... | collective-permute-start | bytes 430088 | tf_op jit(solution)/shard_map/ppermute | solution.py:27
  106.9 8.2 %collective-permute-start.13 = (f32[35,8,128]{2,1,0:T(8,128)S(1)}, f32[35,8,128]{2,1,0:T(8,128)S(1)}, u32[]{:S(2)}, u32[]{:S(2)}) collective-permute-start(f32[35,8,128]{2,1,0:T(8,128)S(1)} %pad_maximum_fusion), channel_id=1, source_target_pairs={{32,0},{33,1},{34,2},{35,3},{36,4},{37,5},{38,6},{39,7},{40,8},{41... | collective-permute-start | bytes 430088 | tf_op jit(solution)/shard_map/ppermute | solution.py:27

commit v6 on v5

--- a/solution.py
+++ b/solution.py
@@ -25,6 +25,32 @@
                 if 0 <= a2 < lats and 0 <= b2 < lons:
                     pairs.append(((p * lats + a) * lons + b, (p * lats + a2) * lons + b2))
     return lax.ppermute(value, AXES, pairs)
+
+
+def swap_pairs(value, axis, first):
+    size = lax.axis_size(axis)
+    pairs = []
+    for i in range(first, size - 1, 2):
+        pairs += [(i, i + 1), (i + 1, i)]
+    return lax.ppermute(value, axis, pairs)
+
+
+def exchange(axis, to_low, to_high):
+    odd = lax.axis_index(axis) % 2 == 1
+    one = swap_pairs(jnp.where(odd, to_low, to_high), axis, 0)
+    two = swap_pairs(jnp.where(odd, to_high, to_low), axis, 1)
+    return jnp.where(odd, one, two), jnp.where(odd, two, one)
+
+
+def two_neighbours(axis, value):
+    odd = lax.axis_index(axis) % 2 == 1
+    one = swap_pairs(value, axis, 0)
+    two = swap_pairs(jnp.concatenate([value, one], axis=0), axis, 1)
+    near, far = jnp.split(two, 2, axis=0)
+    three = swap_pairs(near, axis, 0)
+    left = (jnp.where(odd, three, far), jnp.where(odd, one, near))
+    right = (jnp.where(odd, near, one), jnp.where(odd, far, three))
+    return left, right
 
 
 def lanes_of(shape):
@@ -498,8 +524,7 @@
     values = lax.ppermute(values.reshape(lons, 1, 1152), "patch", [(0, 1), (1, 0)])
     around = lax.all_to_all(values, "lon", 0, 0, tiled=True)
     to_above, to_below = kernel(cut_kernel, ((32, 8, 128),) * 2, [VMEM] * 3)(v, f, mu)
-    below = shifted(to_above, -1, 0)
-    above = shifted(to_below, 1, 0)
+    above, below = exchange("lat", to_above, to_below)
 
     chosen = pl.pallas_call(
         pick_kernel,
@@ -512,8 +537,7 @@
     everything = lax.all_to_all(chosen.reshape(lats, 3 * CELLS, 128), "lat", 0, 0, tiled=True)
     everything = everything.reshape(lats * 3 * CELLS, 1, 128)
     to_right, to_left = kernel(pack_kernel, ((92, 8, 128),) * 2, [VMEM] * 5)(v, f, mu, above, below)
-    left = shifted(to_right, 0, 1)
-    right = shifted(to_left, 0, -1)
+    left, right = exchange("lon", to_left, to_right)
 
     block = jax.ShapeDtypeStruct((3, 16, 8, 128), f32)
     field = (3, 28, 24, 128)
@@ -531,21 +555,16 @@
         name="smooth",
     )(place, ghost_rows, v, f, mu, left, right, above, below, everything)
 
-    tiles = [
-        shifted(message, 0, 2),
-        shifted(message, 0, 1),
-        message,
-        shifted(message, 0, -1),
-        shifted(message, 0, -2),
-    ]
-    band = jnp.concatenate(tiles, axis=1)
+    left, right = two_neighbours("lon", message)
+    band = jnp.concatenate([*left, message, *right], axis=1)
     tile_list = (-1, 8, 128)
     inverse = band[8:10].reshape(tile_list)
     to_above = [band[0:2].reshape(tile_list), band[2:7, 8:32].reshape(tile_list), inverse]
     to_below = [band[7:8], band[6:7]] + [band[r : r + 1, 8:32] for r in (5, 4, 3, 2, 1)]
     to_below = [part.reshape(tile_list) for part in to_below] + [inverse]
-    band_below = shifted(jnp.concatenate(to_above, axis=0), -1, 0)
-    band_above = shifted(jnp.concatenate(to_below, axis=0), 1, 0)
+    band_above, band_below = exchange(
+        "lat", jnp.concatenate(to_above, axis=0), jnp.concatenate(to_below, axis=0)
+    )
     coarse = pltpu.VMEM((22, 40, 128), f32)
     new = pl.pallas_call(
         coarse_kernel,

time: 118 us -> 114 us (0.966)
  the two profiles are of different devices: /device:TPU:88 before, /device:TPU:30 now
where the time goes in v6:
time: 114 us
  starting transfers between devices  57.6 us (51%)
  waiting for transfers between devices  37.8 us (33%)
  Pallas kernels  8.88 us (8%)
  local copies, waits for them, and re-layouts  7.53 us (7%)
    ppermute x9, starting transfers between devices, swap_pairs(): return lax.ppermute(value, axis, pairs)  28.9 us
    ppermute x9, waiting for transfers between devices, swap_pairs(): return lax.ppermute(value, axis, pairs)  24.4 us
    all_to_all x1, starting transfers between devices, per_device(): around = lax.all_to_all(values, 'lon', 0, 0, tiled=True)  13.1 us
    all_to_all x1, waiting for transfers between devices, per_device(): around = lax.all_to_all(values, 'lon', 0, 0, tiled=True)  8.32 us
    ppermute x3, starting transfers between devices, shifted(): return lax.ppermute(value, AXES, pairs)  7.11 us
    all_to_all x1, starting transfers between devices, per_device(): lax.all_to_all(chosen.reshape(lats, 3 * CELLS, 128), 'lat', 0, 0, tiled=T...  6.55 us
    unnamed x26, local copies, waits for them, and re-layouts  6.23 us
    pallas_call x1, Pallas kernels, per_device(): pl.pallas_call(smooth_kernel, out_shape=(block, block, jax.ShapeDtypeStru...  4.71 us
  transfers between devices with their start and end apart: 15, of which 9 were waited for; matrix products, arithmetic and copies ran while one was open for 1% of the time, Pallas kernels for 1%

profile of v6, /device:TPU:30, one launch (start us, length us, event | category | flops | bytes accessed | tf_op | source)
XLA Modules:
  0.0 113.6 jit_solution(17069432469610314243)
XLA Ops:
  0.6 0.0 copy-start
  0.7 0.9 copy-done
  1.6 0.9 copy-done.2
  2.5 0.8 copy-done.4
  3.4 0.0 copy-start.1
  3.4 2.5 %collective-permute-start = (f32[32,8,128]{2,1,0:T(8,128)S(1)}, f32[32,8,128]{2,1,0:T(8,128)S(1)}, u32[]{:S(2)}, u32[]{:S(2)}) collective-permute-start(f32[32,8,128]{2,1,0:T(8,128)S(1)} %get-tuple-element.50), channel_id=1, source_target_pairs={{0,32},{32,0},{64,96},{96,64},{128,160},{160,128},{192,224},{224,1... | collective-permute-start | bytes 393224 | tf_op jit(solution)/shard_map/ppermute | solution.py:35
  5.9 4.9 %collective-permute-start.1 = (f32[32,8,128]{2,1,0:T(8,128)S(1)}, f32[32,8,128]{2,1,0:T(8,128)S(1)}, u32[]{:S(2)}, u32[]{:S(2)}) collective-permute-start(f32[32,8,128]{2,1,0:T(8,128)S(1)} %get-tuple-element.49), channel_id=1, source_target_pairs={{32,64},{64,32},{96,128},{128,96},{160,192},{192,160},{33,65},{65,... | collective-permute-start | bytes 393224 | tf_op jit(solution)/shard_map/ppermute | solution.py:35
  10.9 2.7 %collective-permute-start.4 = (f32[3,16,128]{2,1,0:T(8,128)S(1)}, f32[3,16,128]{2,1,0:T(8,128)S(1)}, u32[]{:S(2)}, u32[]{:S(2)}) collective-permute-start(f32[3,16,128]{2,1,0:T(8,128)S(1)} %get-tuple-element.24), channel_id=1, source_target_pairs={{1,0},{2,1},{3,2},{4,3},{5,4},{6,5},{7,6},{8,7},{9,8},{10,9},{11,1... | collective-permute-start | bytes 73736 | tf_op jit(solution)/shard_map/ppermute | solution.py:27
  13.6 1.9 %collective-permute-start.5 = (f32[3,8,128]{2,1,0:T(8,128)S(1)}, f32[3,8,128]{2,1,0:T(8,128)S(1)}, u32[]{:S(2)}, u32[]{:S(2)}) collective-permute-start(f32[3,8,128]{2,1,0:T(8,128)S(1)} %get-tuple-element.25), channel_id=1, source_target_pairs={{32,0},{33,1},{34,2},{35,3},{36,4},{37,5},{38,6},{39,7},{40,8},{41... | collective-permute-start | bytes 36872 | tf_op jit(solution)/shard_map/ppermute | solution.py:27
  15.5 2.5 %collective-permute-start.6 = (f32[3,128]{1,0:T(4,128)S(1)}, f32[3,128]{1,0:T(4,128)S(1)}, u32[]{:S(2)}, u32[]{:S(2)}) collective-permute-start(f32[3,128]{1,0:T(4,128)S(1)} %get-tuple-element.26), channel_id=1, source_target_pairs={{33,0},{34,1},{35,2},{36,3},{37,4},{38,5},{39,6},{40,7},{41,8},{42... | collective-permute-start | bytes 4616 | tf_op jit(solution)/shard_map/ppermute | solution.py:27
  18.0 0.0 copy-start.9
  18.1 0.6 copy-done.9
  18.8 0.1 fusion.10
  18.9 0.1 clamp_add_fusion
  19.0 0.1 iota_select_fusion
  19.1 0.1 reshape.135
  19.2 0.1 reshape.134
  19.2 0.1 broadcast_in_dim.43
  19.3 0.1 select_n.180
  19.4 0.1 add.115
  19.5 0.1 add.116
  19.6 0.6 copy-done.10
  20.2 0.1 copy.10
  20.3 0.6 copy-done.6
  20.9 0.0 copy-done.7
  20.9 0.6 shard_map.88
  21.5 3.7 %collective-permute-done.6.corner_ref = f32[3,128]{1,0:T(4,128)S(1)} collective-permute-done((f32[3,128]{1,0:T(4,128)S(1)}, f32[3,128]{1,0:T(4,128)S(1)}, u32[]{:S(2)}, u32[]{:S(2)}) %collective-permute-start.6) | collective-permute-done | bytes 1568 | tf_op jit(solution)/shard_map/ppermute | solution.py:27
  25.2 0.0 collective-permute-done.5.below_ref
  25.2 0.0 collective-permute-done.4.edge_ref
  25.2 0.1 shard_map.90
  25.3 1.9 %collective-permute-start.7 = (f32[32,1,1152]{2,1,0:T(1,128)S(1)}, f32[32,1,1152]{2,1,0:T(1,128)}, u32[]{:S(2)}, u32[]{:S(2)}) collective-permute-start(f32[32,1,1152]{2,1,0:T(1,128)S(1)} %bitcast.58), channel_id=1, source_target_pairs={{0,256},{256,0},{1,257},{257,1},{2,258},{258,2},{3,259},{259,3},{4... | collective-permute-start | bytes 442376 | tf_op jit(solution)/shard_map/ppermute | solution.py:524
  27.3 1.4 %collective-permute-done.7 = f32[32,1,1152]{2,1,0:T(1,128)} collective-permute-done((f32[32,1,1152]{2,1,0:T(1,128)S(1)}, f32[32,1,1152]{2,1,0:T(1,128)}, u32[]{:S(2)}, u32[]{:S(2)}) %collective-permute-start.7) | collective-permute-done | bytes 147488 | tf_op jit(solution)/shard_map/ppermute | solution.py:524
  28.7 13.1 %all-to-all-start = ((f32[32,1,1152]{2,1,0:T(1,128)}), f32[32,1,1152]{2,1,0:T(1,128)S(1)}, u32[]{:S(2)}, u32[]{:S(2)}) async-start(f32[32,1,1152]{2,1,0:T(1,128)} %collective-permute-done.7), calls=%async_computation | async-start | bytes 294912 | tf_op jit(solution)/shard_map/all_to_all | solution.py:525
  41.9 0.1 pad_add_fusion.place_ref
  42.0 0.0 collective-permute-done.1
  42.0 0.9 copy-done.3
  42.9 0.0 copy-done.5
  42.9 0.1 shard_map.87
  43.0 8.3 %all-to-all-done = f32[32,1,1152]{2,1,0:T(1,128)S(1)} async-done(((f32[32,1,1152]{2,1,0:T(1,128)}), f32[32,1,1152]{2,1,0:T(1,128)S(1)}, u32[]{:S(2)}, u32[]{:S(2)}) %all-to-all-start) | async-done | bytes 147488 | tf_op jit(solution)/shard_map/all_to_all | solution.py:525
  51.3 1.4 %pick.1 = f32[768,1,128]{2,1,0:T(1,128)} custom-call(s32[4]{0:T(128)S(1)} %pad_add_fusion.place_ref, s32[256]{0:T(256)S(1)} %add_select_fusion.4.cells_ref, s32[768]{0:T(1024)S(1)} %get-tuple-element.53.source_ref, f32[288,1,128]{2,1,0:T(1,128)S(1)} %bitcast.54), custom_call_target="tpu_custom_call" | custom-call | tf_op jit(solution)/shard_map/pick/pallas_call | solution.py:529
  52.7 6.5 %all-to-all-start.1 = ((f32[8,96,128]{2,1,0:T(8,128)}), f32[8,96,128]{2,1,0:T(8,128)S(1)}, u32[]{:S(2)}, u32[]{:S(2)}) async-start(f32[8,96,128]{2,1,0:T(8,128)} %bitcast.10), calls=%async_computation.1 | async-start | bytes 786432 | tf_op jit(solution)/shard_map/all_to_all | solution.py:537
  59.3 0.1 broadcast_select_fusion.2
  59.3 2.4 %collective-permute-start.2 = (f32[92,8,128]{2,1,0:T(8,128)S(1)}, f32[92,8,128]{2,1,0:T(8,128)S(1)}, u32[]{:S(2)}, u32[]{:S(2)}) collective-permute-start(f32[92,8,128]{2,1,0:T(8,128)S(1)} %get-tuple-element.42), channel_id=1, source_target_pairs={{0,1},{1,0},{2,3},{3,2},{4,5},{5,4},{6,7},{7,6},{8,9},{9,8},{10,11... | collective-permute-start | bytes 1130504 | tf_op jit(solution)/shard_map/ppermute | solution.py:35
  61.7 4.2 %collective-permute-start.3 = (f32[92,8,128]{2,1,0:T(8,128)S(1)}, f32[92,8,128]{2,1,0:T(8,128)S(1)}, u32[]{:S(2)}, u32[]{:S(2)}) collective-permute-start(f32[92,8,128]{2,1,0:T(8,128)S(1)} %get-tuple-element.41), channel_id=1, source_target_pairs={{1,2},{2,1},{3,4},{4,3},{5,6},{6,5},{7,8},{8,7},{9,10},{10,9},{11,... | collective-permute-start | bytes 1130504 | tf_op jit(solution)/shard_map/ppermute | solution.py:35
  65.9 3.7 %collective-permute-done.2 = f32[92,8,128]{2,1,0:T(8,128)S(1)} collective-permute-done((f32[92,8,128]{2,1,0:T(8,128)S(1)}, f32[92,8,128]{2,1,0:T(8,128)S(1)}, u32[]{:S(2)}, u32[]{:S(2)}) %collective-permute-start.2) | collective-permute-done | bytes 376864 | tf_op jit(solution)/shard_map/ppermute | solution.py:35
  69.6 4.7 %collective-permute-done.3 = f32[92,8,128]{2,1,0:T(8,128)S(1)} collective-permute-done((f32[92,8,128]{2,1,0:T(8,128)S(1)}, f32[92,8,128]{2,1,0:T(8,128)S(1)}, u32[]{:S(2)}, u32[]{:S(2)}) %collective-permute-start.3) | collective-permute-done | bytes 376864 | tf_op jit(solution)/shard_map/ppermute | solution.py:35
  74.3 0.1 broadcast_select_fusion
  74.4 0.0 all-to-all-done.1
  74.4 4.7 %smooth.1 = (f32[3,16,8,128]{3,2,1,0:T(8,128)}, f32[3,16,8,128]{3,2,1,0:T(8,128)S(1)}, f32[10,8,128]{2,1,0:T(8,128)S(1)}) custom-call(s32[4]{0:T(128)S(1)} %pad_add_fusion.place_ref, s32[768]{0:T(1024)S(1)} %get-tuple-element.54.ghost_ref, f32[3,16,8,128]{3,2,1,0:T(8,128)S(1)} %bitcast.49, f32[3,16,8,128]{3,2,1,0:T(8,128)S(1)} %bitcast.52, ...), custom_call_target="tpu_custom_call" | custom-call | tf_op jit(solution)/shard_map/smooth/pallas_call | solution.py:544
  79.1 1.9 %collective-permute-start.8 = (f32[10,8,128]{2,1,0:T(8,128)S(1)}, f32[10,8,128]{2,1,0:T(8,128)S(1)}, u32[]{:S(2)}, u32[]{:S(2)}) collective-permute-start(f32[10,8,128]{2,1,0:T(8,128)S(1)} %get-tuple-element.27), channel_id=1, source_target_pairs={{0,1},{1,0},{2,3},{3,2},{4,5},{5,4},{6,7},{7,6},{8,9},{9,8},{10,11... | collective-permute-start | bytes 122888 | tf_op jit(solution)/shard_map/ppermute | solution.py:35
  81.0 4.0 %collective-permute-done.8 = f32[10,8,128]{2,1,0:T(8,128)S(1)} collective-permute-done((f32[10,8,128]{2,1,0:T(8,128)S(1)}, f32[10,8,128]{2,1,0:T(8,128)S(1)}, u32[]{:S(2)}, u32[]{:S(2)}) %collective-permute-start.8) | collective-permute-done | bytes 40992 | tf_op jit(solution)/shard_map/ppermute | solution.py:35
  85.0 4.0 %collective-permute-start.9 = (f32[20,8,128]{2,1,0:T(8,128)S(1)}, f32[20,8,128]{2,1,0:T(8,128)S(1)}, u32[]{:S(2)}, u32[]{:S(2)}) collective-permute-start(f32[20,8,128]{2,1,0:T(8,128)S(1)} %pad_maximum_fusion.2), channel_id=1, source_target_pairs={{1,2},{2,1},{3,4},{4,3},{5,6},{6,5},{7,8},{8,7},{9,10},{10,9},{11,... | collective-permute-start | bytes 245768 | tf_op jit(solution)/shard_map/ppermute | solution.py:35
  89.0 4.4 %collective-permute-done.9 = f32[20,8,128]{2,1,0:T(8,128)S(1)} collective-permute-done((f32[20,8,128]{2,1,0:T(8,128)S(1)}, f32[20,8,128]{2,1,0:T(8,128)S(1)}, u32[]{:S(2)}, u32[]{:S(2)}) %collective-permute-start.9) | collective-permute-done | bytes 81952 | tf_op jit(solution)/shard_map/ppermute | solution.py:35
  93.4 1.9 %collective-permute-start.10 = (f32[10,8,128]{2,1,0:T(8,128)S(1)}, f32[10,8,128]{2,1,0:T(8,128)S(1)}, u32[]{:S(2)}, u32[]{:S(2)}) collective-permute-start(f32[10,8,128]{2,1,0:T(8,128)S(1)} %split.8), channel_id=1, source_target_pairs={{0,1},{1,0},{2,3},{3,2},{4,5},{5,4},{6,7},{7,6},{8,9},{9,8},{10,11... | collective-permute-start | bytes 122888 | tf_op jit(solution)/shard_map/ppermute | solution.py:35
  95.3 4.0 %collective-permute-done.10 = f32[10,8,128]{2,1,0:T(8,128)S(1)} collective-permute-done((f32[10,8,128]{2,1,0:T(8,128)S(1)}, f32[10,8,128]{2,1,0:T(8,128)S(1)}, u32[]{:S(2)}, u32[]{:S(2)}) %collective-permute-start.10) | collective-permute-done | bytes 40992 | tf_op jit(solution)/shard_map/ppermute | solution.py:35
  99.4 0.0 copy-start.8
  99.5 0.6 copy-done.8
  100.1 0.0 slice-start
  100.1 0.8 slice-done
  101.0 2.5 %collective-permute-start.11 = (f32[35,8,128]{2,1,0:T(8,128)S(1)}, f32[35,8,128]{2,1,0:T(8,128)S(1)}, u32[]{:S(2)}, u32[]{:S(2)}) collective-permute-start(f32[35,8,128]{2,1,0:T(8,128)S(1)} %get-tuple-element.46), channel_id=1, source_target_pairs={{0,32},{32,0},{64,96},{96,64},{128,160},{160,128},{192,224},{224,1... | collective-permute-start | bytes 430088 | tf_op jit(solution)/shard_map/ppermute | solution.py:35
  103.5 4.6 %collective-permute-start.12 = (f32[35,8,128]{2,1,0:T(8,128)S(1)}, f32[35,8,128]{2,1,0:T(8,128)S(1)}, u32[]{:S(2)}, u32[]{:S(2)}) collective-permute-start(f32[35,8,128]{2,1,0:T(8,128)S(1)} %get-tuple-element.45), channel_id=1, source_target_pairs={{32,64},{64,32},{96,128},{128,96},{160,192},{192,160},{33,65},{65,... | collective-permute-start | bytes 430088 | tf_op jit(solution)/shard_map/ppermute | solution.py:35
  108.0 0.0 collective-permute-done.11
  108.1 3.6 %collective-permute-done.12 = f32[35,8,128]{2,1,0:T(8,128)S(1)} collective-permute-done((f32[35,8,128]{2,1,0:T(8,128)S(1)}, f32[35,8,128]{2,1,0:T(8,128)S(1)}, u32[]{:S(2)}, u32[]{:S(2)}) %collective-permute-start.12) | collective-permute-done | bytes 143392 | tf_op jit(solution)/shard_map/ppermute | solution.py:35
  111.7 1.9 %coarse.1 = f32[3,16,8,128]{3,2,1,0:T(8,128)} custom-call(f32[10,40,128]{2,1,0:T(8,128)S(1)} %select_dynamic-update-slice_fusion.mid_ref, f32[35,8,128]{2,1,0:T(8,128)S(1)} %get-tuple-element.44.above_ref, f32[35,8,128]{2,1,0:T(8,128)S(1)} %get-tuple-element.43.below_ref, f32[3,16,8,128]{3,2,1,0:T(8,128)S(1)} %get-tuple-element.28.smooth_ref), custom_call_target="tpu_custom_call" | custom-call | tf_op jit(solution)/shard_map/coarse/pallas_call | solution.py:569
  (44 shorter events, 0.4 us)
Async XLA Ops:
  0.6 0.9 copy-start
  1.6 0.9 copy-start.2
  2.5 0.8 copy-start.4
  3.4 16.9 %copy-start.1 = (f32[1,3,16,8,128]{4,3,2,1,0:T(8,128)S(1)}, f32[1,3,16,8,128]{4,3,2,1,0:T(8,128)}, u32[]{:S(2)}) copy-start(f32[1,3,16,8,128]{4,3,2,1,0:T(8,128)} %param.7) | copy-start | bytes 589828
  3.4 38.6 %collective-permute-start = (f32[32,8,128]{2,1,0:T(8,128)S(1)}, f32[32,8,128]{2,1,0:T(8,128)S(1)}, u32[]{:S(2)}, u32[]{:S(2)}) collective-permute-start(f32[32,8,128]{2,1,0:T(8,128)S(1)} %get-tuple-element.50), channel_id=1, source_target_pairs={{0,32},{32,0},{64,96},{96,64},{128,160},{160,128},{192,224},{224,1... | collective-permute-start | bytes 393224 | tf_op jit(solution)/shard_map/ppermute | solution.py:35
  5.9 36.1 %collective-permute-start.1 = (f32[32,8,128]{2,1,0:T(8,128)S(1)}, f32[32,8,128]{2,1,0:T(8,128)S(1)}, u32[]{:S(2)}, u32[]{:S(2)}) collective-permute-start(f32[32,8,128]{2,1,0:T(8,128)S(1)} %get-tuple-element.49), channel_id=1, source_target_pairs={{32,64},{64,32},{96,128},{128,96},{160,192},{192,160},{33,65},{65,... | collective-permute-start | bytes 393224 | tf_op jit(solution)/shard_map/ppermute | solution.py:35
  10.9 14.4 %collective-permute-start.4 = (f32[3,16,128]{2,1,0:T(8,128)S(1)}, f32[3,16,128]{2,1,0:T(8,128)S(1)}, u32[]{:S(2)}, u32[]{:S(2)}) collective-permute-start(f32[3,16,128]{2,1,0:T(8,128)S(1)} %get-tuple-element.24), channel_id=1, source_target_pairs={{1,0},{2,1},{3,2},{4,3},{5,4},{6,5},{7,6},{8,7},{9,8},{10,9},{11,1... | collective-permute-start | bytes 73736 | tf_op jit(solution)/shard_map/ppermute | solution.py:27
  13.6 11.6 %collective-permute-start.5 = (f32[3,8,128]{2,1,0:T(8,128)S(1)}, f32[3,8,128]{2,1,0:T(8,128)S(1)}, u32[]{:S(2)}, u32[]{:S(2)}) collective-permute-start(f32[3,8,128]{2,1,0:T(8,128)S(1)} %get-tuple-element.25), channel_id=1, source_target_pairs={{32,0},{33,1},{34,2},{35,3},{36,4},{37,5},{38,6},{39,7},{40,8},{41... | collective-permute-start | bytes 36872 | tf_op jit(solution)/shard_map/ppermute | solution.py:27
  15.5 9.7 %collective-permute-start.6 = (f32[3,128]{1,0:T(4,128)S(1)}, f32[3,128]{1,0:T(4,128)S(1)}, u32[]{:S(2)}, u32[]{:S(2)}) collective-permute-start(f32[3,128]{1,0:T(4,128)S(1)} %get-tuple-element.26), channel_id=1, source_target_pairs={{33,0},{34,1},{35,2},{36,3},{37,4},{38,5},{39,6},{40,7},{41,8},{42... | collective-permute-start | bytes 4616 | tf_op jit(solution)/shard_map/ppermute | solution.py:27
  18.0 0.7 copy-start.9
  19.5 0.7 copy-start.10
  20.2 0.7 copy-start.6
  20.2 0.7 copy-start.7
  25.3 3.4 %collective-permute-start.7 = (f32[32,1,1152]{2,1,0:T(1,128)S(1)}, f32[32,1,1152]{2,1,0:T(1,128)}, u32[]{:S(2)}, u32[]{:S(2)}) collective-permute-start(f32[32,1,1152]{2,1,0:T(1,128)S(1)} %bitcast.58), channel_id=1, source_target_pairs={{0,256},{256,0},{1,257},{257,1},{2,258},{258,2},{3,259},{259,3},{4... | collective-permute-start | bytes 442376 | tf_op jit(solution)/shard_map/ppermute | solution.py:524
  28.7 22.6 %all-to-all-start = ((f32[32,1,1152]{2,1,0:T(1,128)}), f32[32,1,1152]{2,1,0:T(1,128)S(1)}, u32[]{:S(2)}, u32[]{:S(2)}) async-start(f32[32,1,1152]{2,1,0:T(1,128)} %collective-permute-done.7), calls=%async_computation | async-start | bytes 294912 | tf_op jit(solution)/shard_map/all_to_all | solution.py:525
  42.0 0.9 copy-start.3
  42.0 0.9 copy-start.5
  52.7 21.7 %all-to-all-start.1 = ((f32[8,96,128]{2,1,0:T(8,128)}), f32[8,96,128]{2,1,0:T(8,128)S(1)}, u32[]{:S(2)}, u32[]{:S(2)}) async-start(f32[8,96,128]{2,1,0:T(8,128)} %bitcast.10), calls=%async_computation.1 | async-start | bytes 786432 | tf_op jit(solution)/shard_map/all_to_all | solution.py:537
  59.3 10.3 %collective-permute-start.2 = (f32[92,8,128]{2,1,0:T(8,128)S(1)}, f32[92,8,128]{2,1,0:T(8,128)S(1)}, u32[]{:S(2)}, u32[]{:S(2)}) collective-permute-start(f32[92,8,128]{2,1,0:T(8,128)S(1)} %get-tuple-element.42), channel_id=1, source_target_pairs={{0,1},{1,0},{2,3},{3,2},{4,5},{5,4},{6,7},{7,6},{8,9},{9,8},{10,11... | collective-permute-start | bytes 1130504 | tf_op jit(solution)/shard_map/ppermute | solution.py:35
  61.7 12.6 %collective-permute-start.3 = (f32[92,8,128]{2,1,0:T(8,128)S(1)}, f32[92,8,128]{2,1,0:T(8,128)S(1)}, u32[]{:S(2)}, u32[]{:S(2)}) collective-permute-start(f32[92,8,128]{2,1,0:T(8,128)S(1)} %get-tuple-element.41), channel_id=1, source_target_pairs={{1,2},{2,1},{3,4},{4,3},{5,6},{6,5},{7,8},{8,7},{9,10},{10,9},{11,... | collective-permute-start | bytes 1130504 | tf_op jit(solution)/shard_map/ppermute | solution.py:35
  79.1 5.9 %collective-permute-start.8 = (f32[10,8,128]{2,1,0:T(8,128)S(1)}, f32[10,8,128]{2,1,0:T(8,128)S(1)}, u32[]{:S(2)}, u32[]{:S(2)}) collective-permute-start(f32[10,8,128]{2,1,0:T(8,128)S(1)} %get-tuple-element.27), channel_id=1, source_target_pairs={{0,1},{1,0},{2,3},{3,2},{4,5},{5,4},{6,7},{7,6},{8,9},{9,8},{10,11... | collective-permute-start | bytes 122888 | tf_op jit(solution)/shard_map/ppermute | solution.py:35
  85.0 8.4 %collective-permute-start.9 = (f32[20,8,128]{2,1,0:T(8,128)S(1)}, f32[20,8,128]{2,1,0:T(8,128)S(1)}, u32[]{:S(2)}, u32[]{:S(2)}) collective-permute-start(f32[20,8,128]{2,1,0:T(8,128)S(1)} %pad_maximum_fusion.2), channel_id=1, source_target_pairs={{1,2},{2,1},{3,4},{4,3},{5,6},{6,5},{7,8},{8,7},{9,10},{10,9},{11,... | collective-permute-start | bytes 245768 | tf_op jit(solution)/shard_map/ppermute | solution.py:35
  93.4 5.9 %collective-permute-start.10 = (f32[10,8,128]{2,1,0:T(8,128)S(1)}, f32[10,8,128]{2,1,0:T(8,128)S(1)}, u32[]{:S(2)}, u32[]{:S(2)}) collective-permute-start(f32[10,8,128]{2,1,0:T(8,128)S(1)} %split.8), channel_id=1, source_target_pairs={{0,1},{1,0},{2,3},{3,2},{4,5},{5,4},{6,7},{7,6},{8,9},{9,8},{10,11... | collective-permute-start | bytes 122888 | tf_op jit(solution)/shard_map/ppermute | solution.py:35
  99.4 0.7 copy-start.8
  100.1 0.8 slice-start
  101.0 7.1 %collective-permute-start.11 = (f32[35,8,128]{2,1,0:T(8,128)S(1)}, f32[35,8,128]{2,1,0:T(8,128)S(1)}, u32[]{:S(2)}, u32[]{:S(2)}) collective-permute-start(f32[35,8,128]{2,1,0:T(8,128)S(1)} %get-tuple-element.46), channel_id=1, source_target_pairs={{0,32},{32,0},{64,96},{96,64},{128,160},{160,128},{192,224},{224,1... | collective-permute-start | bytes 430088 | tf_op jit(solution)/shard_map/ppermute | solution.py:35
  103.5 8.2 %collective-permute-start.12 = (f32[35,8,128]{2,1,0:T(8,128)S(1)}, f32[35,8,128]{2,1,0:T(8,128)S(1)}, u32[]{:S(2)}, u32[]{:S(2)}) collective-permute-start(f32[35,8,128]{2,1,0:T(8,128)S(1)} %get-tuple-element.45), channel_id=1, source_target_pairs={{32,64},{64,32},{96,128},{128,96},{160,192},{192,160},{33,65},{65,... | collective-permute-start | bytes 430088 | tf_op jit(solution)/shard_map/ppermute | solution.py:35

commit v7 on v5

--- a/solution.py
+++ b/solution.py
@@ -15,7 +15,7 @@
 SMEM = pl.BlockSpec(memory_space=pltpu.SMEM)
 
 
-def shifted(value, by_lat, by_lon):
+def shifted(value, by_lat, by_lon, flip=0):
     patches, lats, lons = (lax.axis_size(axis) for axis in AXES)
     pairs = []
     for p in range(patches):
@@ -23,7 +23,7 @@
             for b in range(lons):
                 a2, b2 = a + by_lat, b + by_lon
                 if 0 <= a2 < lats and 0 <= b2 < lons:
-                    pairs.append(((p * lats + a) * lons + b, (p * lats + a2) * lons + b2))
+                    pairs.append(((p * lats + a) * lons + b, ((p ^ flip) * lats + a2) * lons + b2))
     return lax.ppermute(value, AXES, pairs)
 
 
@@ -76,7 +76,7 @@
                 ref[lat_tile(field, away)] = value
 
 
-def blend_kernel(rows_ref, cols_ref, weights_ref, v_ref, own_ref, edge_ref, below_ref, corner_ref):
+def blend_kernel(rows_ref, cols_ref, weights_ref, v_ref, out_ref):
     tall, flat = rows_of((16, 128)), rows_of((8, 128))
     for slot in range(3):
         row, col = rows_ref[slot], cols_ref[slot]
@@ -89,25 +89,29 @@
         inner = jnp.where(within, lower, 0.0)
         for comp in range(3):
             total = upper * v_ref[comp, row] + inner * v_ref[comp, next_row]
-            own_ref[3 * slot + comp] = jnp.sum(total, axis=0, keepdims=True)
+            at = 3 * slot + comp
+            out_ref[at : at + 1] = jnp.sum(total, axis=0, keepdims=True)
         beside = jnp.where(tall == row, w2, jnp.where(tall == row + 1, w3, 0.0))
-        edge_ref[slot] = jnp.where(col == 7, beside, 0.0)
-        below_ref[slot] = jnp.where(within, 0.0, lower)
+        out_ref[16 + 16 * slot : 32 + 16 * slot] = jnp.where(col == 7, beside, 0.0)
+        out_ref[64 + 8 * slot : 72 + 8 * slot] = jnp.where(within, 0.0, lower)
         both = jnp.where((row == 15) & (col == 7), w3, 0.0)
-        corner_ref[slot] = jnp.full((1, 128), both, jnp.float32)
-
-
-def interp_kernel(
-    own_ref, edge_w, below_w, corner_w, edge_ref, below_ref, corner_ref, out_ref
-):
+        out_ref[9 + slot : 10 + slot] = jnp.full((1, 128), both, jnp.float32)
+    out_ref[12:16] = jnp.zeros((4, 128), jnp.float32)
+
+
+def interp_kernel(blend_ref, edge_ref, below_ref, corner_ref, out_ref):
     for slot in range(3):
+        edge_w = blend_ref[16 + 16 * slot : 32 + 16 * slot]
+        below_w = blend_ref[64 + 8 * slot : 72 + 8 * slot]
+        corner_w = blend_ref[9 + slot : 10 + slot]
         for comp in range(3):
-            beside = edge_w[slot] * edge_ref[comp]
-            total = beside[0:8] + beside[8:16] + below_w[slot] * below_ref[comp]
-            total = jnp.sum(total, axis=0, keepdims=True) + own_ref[3 * slot + comp]
-            total = total + corner_w[slot] * corner_ref[comp : comp + 1]
+            at = 3 * slot + comp
+            beside = edge_w * edge_ref[comp]
+            total = beside[0:8] + beside[8:16] + below_w * below_ref[comp]
+            total = jnp.sum(total, axis=0, keepdims=True) + blend_ref[at : at + 1]
+            total = total + corner_w * corner_ref[comp : comp + 1]
             for dest in range(out_ref.shape[0] // 9):
-                out_ref[9 * dest + 3 * slot + comp] = total
+                out_ref[9 * dest + at] = total
 
 
 def pick_kernel(place_ref, cells_ref, source_ref, row_ref, out_ref):
@@ -486,17 +490,17 @@
     edge, first_row, first_cell = kernel(
         first_kernel, ((3, 16, 128), (3, 8, 128), (3, 128)), [VMEM]
     )(v)
-    edge = shifted(edge, 0, -1)
-    first_cell = shifted(first_cell, -1, -1)
-    first_row = shifted(first_row, -1, 0)
-    blended = kernel(
-        blend_kernel, ((9, 1, 128), (3, 16, 128), (3, 8, 128), (3, 1, 128)), [SMEM] * 3 + [VMEM]
-    )(corner_rows[0, 0], corner_cols[0, 0], corner_weights[0, 0], v)
-    (values,) = kernel(interp_kernel, ((9 * lons, 1, 128),), [VMEM] * 7)(
-        *blended, edge, first_row, first_cell
+    first_cell = shifted(first_cell, -1, -1, 1)
+    first_row = shifted(first_row, -1, 0, 1)
+    edge = shifted(edge, 0, -1, 1)
+    (blended,) = kernel(blend_kernel, ((88, 128),), [SMEM] * 3 + [VMEM])(
+        corner_rows[0, 0], corner_cols[0, 0], corner_weights[0, 0], v
     )
-    values = lax.ppermute(values.reshape(lons, 1, 1152), "patch", [(0, 1), (1, 0)])
-    around = lax.all_to_all(values, "lon", 0, 0, tiled=True)
+    blended = shifted(blended, 0, 0, 1)
+    (values,) = kernel(interp_kernel, ((9 * lons, 1, 128),), [VMEM] * 4)(
+        blended, edge, first_row, first_cell
+    )
+    around = lax.all_to_all(values.reshape(lons, 1, 1152), "lon", 0, 0, tiled=True)
     to_above, to_below = kernel(cut_kernel, ((32, 8, 128),) * 2, [VMEM] * 3)(v, f, mu)
     below = shifted(to_above, -1, 0)
     above = shifted(to_below, 1, 0)

time: 118 us -> 115 us (0.975)
  starting transfers between devices: 67.9 us -> 66 us
  waiting for transfers between devices: 35.8 us -> 34.3 us
    ppermute x1 -> x0, starting transfers between devices: 1.92 us -> none  [per_device(): lax.ppermute(values.reshape(lons, 1, 1152), 'patch', [(0, 1), (1, 0)])]
    ppermute x13 -> x14, starting transfers between devices: 44.9 us -> 46.7 us  [shifted(): return lax.ppermute(value, AXES, pairs)]
    all_to_all x1, starting transfers between devices: 13.4 us -> 11.7 us  [per_device(): lax.all_to_all(values.reshape(lons, 1, 1152), 'lon', 0, 0, tiled=True)]
    ppermute x1 -> x0, waiting for transfers between devices: 1.36 us -> none  [per_device(): lax.ppermute(values.reshape(lons, 1, 1152), 'patch', [(0, 1), (1, 0)])]
    ppermute x13 -> x14, waiting for transfers between devices: 24.3 us -> 24.3 us  [shifted(): return lax.ppermute(value, AXES, pairs)]
  transfers between devices with their start and end apart: 16 -> 16, of which waited for: 10 -> 8; matrix products, arithmetic and copies ran while one was open for 1% -> 1% of each run, Pallas kernels for 1% -> 1%
where the time goes in v7:
time: 115 us; the launch traced here: 114 us
  starting transfers between devices  66 us (57%)
  waiting for transfers between devices  34.3 us (30%)
  Pallas kernels  9.53 us (8%)
  local copies, waits for them, and re-layouts  2.86 us (2%)
    ppermute x14, starting transfers between devices, shifted(): return lax.ppermute(value, AXES, pairs)  46.7 us
    ppermute x14, waiting for transfers between devices, shifted(): return lax.ppermute(value, AXES, pairs)  24.3 us
    all_to_all x1, starting transfers between devices, per_device(): lax.all_to_all(values.reshape(lons, 1, 1152), 'lon', 0, 0, tiled=True)  11.7 us
    all_to_all x1, waiting for transfers between devices, per_device(): lax.all_to_all(values.reshape(lons, 1, 1152), 'lon', 0, 0, tiled=True)  10 us
    all_to_all x1, starting transfers between devices, per_device(): lax.all_to_all(chosen.reshape(lats, 3 * CELLS, 128), 'lat', 0, 0, tiled=T...  7.68 us
    pallas_call x1, Pallas kernels, per_device(): pl.pallas_call(smooth_kernel, out_shape=(block, block, jax.ShapeDtypeStru...  4.71 us
    unnamed x27, local copies, waits for them, and re-layouts  2.35 us
  transfers between devices with their start and end apart: 16, of which 8 were waited for; matrix products, arithmetic and copies ran while one was open for 1% of the time, Pallas kernels for 1%

profile of v7, /device:TPU:88, one launch (start us, length us, event | category | flops | bytes accessed | tf_op | source)
XLA Modules:
  0.0 114.3 jit_solution(11908494817329023025)
XLA Ops:
  0.6 0.0 copy-start
  0.6 0.9 copy-done
  1.6 0.0 copy-start.1
  1.6 0.0 copy-start.7
  1.6 3.2 %collective-permute-start.7 = (f32[3,128]{1,0:T(4,128)S(1)}, f32[3,128]{1,0:T(4,128)S(1)}, u32[]{:S(2)}, u32[]{:S(2)}) collective-permute-start(f32[3,128]{1,0:T(4,128)S(1)} %get-tuple-element.18), channel_id=1, source_target_pairs={{33,256},{34,257},{35,258},{36,259},{37,260},{38,261},{39,262},{40... | collective-permute-start | bytes 4616 | tf_op jit(solution)/shard_map/ppermute | solution.py:27
  4.8 2.6 %collective-permute-start.6 = (f32[3,8,128]{2,1,0:T(8,128)S(1)}, f32[3,8,128]{2,1,0:T(8,128)S(1)}, u32[]{:S(2)}, u32[]{:S(2)}) collective-permute-start(f32[3,8,128]{2,1,0:T(8,128)S(1)} %get-tuple-element.17), channel_id=1, source_target_pairs={{32,256},{33,257},{34,258},{35,259},{36,260},{37,261},{38,262},{39... | collective-permute-start | bytes 36872 | tf_op jit(solution)/shard_map/ppermute | solution.py:27
  7.5 2.3 %collective-permute-start.5 = (f32[3,16,128]{2,1,0:T(8,128)S(1)}, f32[3,16,128]{2,1,0:T(8,128)S(1)}, u32[]{:S(2)}, u32[]{:S(2)}) collective-permute-start(f32[3,16,128]{2,1,0:T(8,128)S(1)} %get-tuple-element.16), channel_id=1, source_target_pairs={{1,256},{2,257},{3,258},{4,259},{5,260},{6,261},{7,262},{8,263},{9... | collective-permute-start | bytes 73736 | tf_op jit(solution)/shard_map/ppermute | solution.py:27
  9.8 0.0 copy-done.7
  9.8 0.1 copy.10
  9.9 0.0 copy-start.4
  9.9 0.0 copy-start.5
  9.9 0.0 copy-done.1
  9.9 0.6 copy-done.4
  10.5 0.0 copy-done.5
  10.5 0.6 shard_map.88
  11.2 2.5 %collective-permute-start.4 = (f32[88,128]{1,0:T(8,128)S(1)}, f32[88,128]{1,0:T(8,128)S(1)}, u32[]{:S(2)}, u32[]{:S(2)}) collective-permute-start(f32[88,128]{1,0:T(8,128)S(1)} %shard_map.88), channel_id=1, source_target_pairs={{0,256},{1,257},{2,258},{3,259},{4,260},{5,261},{6,262},{7,263},{8... | collective-permute-start | bytes 135176 | tf_op jit(solution)/shard_map/ppermute | solution.py:27
  13.7 0.1 fusion.8
  13.8 0.1 reshape.135
  13.9 0.1 iota_select_fusion
  14.0 0.1 select_n.73
  14.0 0.1 clamp_add_fusion
  14.1 0.1 reshape.134
  14.2 0.1 add.104
  14.3 0.1 add.105
  14.3 0.0 copy-start.6
  14.3 0.1 broadcast_in_dim.43
  14.4 0.6 copy-done.6
  15.1 0.0 collective-permute-done.7.corner_ref
  15.2 0.0 collective-permute-done.6.below_ref
  15.2 0.0 collective-permute-done.5.edge_ref
  15.2 0.0 collective-permute-done.4.blend_ref
  15.2 0.8 shard_map.90
  15.9 11.7 %all-to-all-start = ((f32[32,1,1152]{2,1,0:T(1,128)}), f32[32,1,1152]{2,1,0:T(1,128)S(1)}, u32[]{:S(2)}, u32[]{:S(2)}) async-start(f32[32,1,1152]{2,1,0:T(1,128)} %bitcast.8), calls=%async_computation | async-start | bytes 294912 | tf_op jit(solution)/shard_map/all_to_all | solution.py:503
  27.6 0.1 pad_add_fusion.place_ref
  27.7 10.0 %all-to-all-done = f32[32,1,1152]{2,1,0:T(1,128)S(1)} async-done(((f32[32,1,1152]{2,1,0:T(1,128)}), f32[32,1,1152]{2,1,0:T(1,128)S(1)}, u32[]{:S(2)}, u32[]{:S(2)}) %all-to-all-start) | async-done | bytes 147488 | tf_op jit(solution)/shard_map/all_to_all | solution.py:503
  37.7 1.4 %pick.1 = f32[768,1,128]{2,1,0:T(1,128)} custom-call(s32[4]{0:T(128)S(1)} %pad_add_fusion.place_ref, s32[256]{0:T(256)S(1)} %add_select_fusion.4.cells_ref, s32[768]{0:T(1024)S(1)} %get-tuple-element.35.source_ref, f32[288,1,128]{2,1,0:T(1,128)S(1)} %bitcast.54), custom_call_target="tpu_custom_call" | custom-call | tf_op jit(solution)/shard_map/pick/pallas_call | solution.py:508
  39.1 0.0 copy-start.2
  39.1 7.7 %all-to-all-start.1 = ((f32[8,96,128]{2,1,0:T(8,128)}), f32[8,96,128]{2,1,0:T(8,128)S(1)}, u32[]{:S(2)}, u32[]{:S(2)}) async-start(f32[8,96,128]{2,1,0:T(8,128)} %bitcast.10), calls=%async_computation.1 | async-start | bytes 786432 | tf_op jit(solution)/shard_map/all_to_all | solution.py:516
  46.8 0.0 copy-done.2
  46.8 0.0 copy-done.3
  46.8 4.6 %collective-permute-start = (f32[32,8,128]{2,1,0:T(8,128)S(1)}, f32[32,8,128]{2,1,0:T(8,128)S(1)}, u32[]{:S(2)}, u32[]{:S(2)}) collective-permute-start(f32[32,8,128]{2,1,0:T(8,128)S(1)} %get-tuple-element.12), channel_id=1, source_target_pairs={{0,32},{1,33},{2,34},{3,35},{4,36},{5,37},{6,38},{7,39},{8,40},{9,... | collective-permute-start | bytes 393224 | tf_op jit(solution)/shard_map/ppermute | solution.py:27
  51.4 1.9 %collective-permute-start.1 = (f32[32,8,128]{2,1,0:T(8,128)S(1)}, f32[32,8,128]{2,1,0:T(8,128)S(1)}, u32[]{:S(2)}, u32[]{:S(2)}) collective-permute-start(f32[32,8,128]{2,1,0:T(8,128)S(1)} %get-tuple-element.13), channel_id=1, source_target_pairs={{32,0},{33,1},{34,2},{35,3},{36,4},{37,5},{38,6},{39,7},{40,8},{41... | collective-permute-start | bytes 393224 | tf_op jit(solution)/shard_map/ppermute | solution.py:27
  53.3 3.8 %collective-permute-done.above_ref = f32[32,8,128]{2,1,0:T(8,128)S(1)} collective-permute-done((f32[32,8,128]{2,1,0:T(8,128)S(1)}, f32[32,8,128]{2,1,0:T(8,128)S(1)}, u32[]{:S(2)}, u32[]{:S(2)}) %collective-permute-start) | collective-permute-done | bytes 131104 | tf_op jit(solution)/shard_map/ppermute | solution.py:27
  57.2 2.4 %collective-permute-done.1.below_ref = f32[32,8,128]{2,1,0:T(8,128)S(1)} collective-permute-done((f32[32,8,128]{2,1,0:T(8,128)S(1)}, f32[32,8,128]{2,1,0:T(8,128)S(1)}, u32[]{:S(2)}, u32[]{:S(2)}) %collective-permute-start.1) | collective-permute-done | bytes 131104 | tf_op jit(solution)/shard_map/ppermute | solution.py:27
  59.6 0.1 shard_map.87
  59.6 2.6 %collective-permute-start.2 = (f32[92,8,128]{2,1,0:T(8,128)S(1)}, f32[92,8,128]{2,1,0:T(8,128)S(1)}, u32[]{:S(2)}, u32[]{:S(2)}) collective-permute-start(f32[92,8,128]{2,1,0:T(8,128)S(1)} %get-tuple-element.14), channel_id=1, source_target_pairs={{0,1},{1,2},{2,3},{3,4},{4,5},{5,6},{6,7},{7,8},{8,9},{9,10},{10,1... | collective-permute-start | bytes 1130504 | tf_op jit(solution)/shard_map/ppermute | solution.py:27
  62.3 5.3 %collective-permute-start.3 = (f32[92,8,128]{2,1,0:T(8,128)S(1)}, f32[92,8,128]{2,1,0:T(8,128)S(1)}, u32[]{:S(2)}, u32[]{:S(2)}) collective-permute-start(f32[92,8,128]{2,1,0:T(8,128)S(1)} %get-tuple-element.15), channel_id=1, source_target_pairs={{1,0},{2,1},{3,2},{4,3},{5,4},{6,5},{7,6},{8,7},{9,8},{10,9},{11,1... | collective-permute-start | bytes 1130504 | tf_op jit(solution)/shard_map/ppermute | solution.py:27
  67.6 5.0 %collective-permute-done.2.left_ref = f32[92,8,128]{2,1,0:T(8,128)S(1)} collective-permute-done((f32[92,8,128]{2,1,0:T(8,128)S(1)}, f32[92,8,128]{2,1,0:T(8,128)S(1)}, u32[]{:S(2)}, u32[]{:S(2)}) %collective-permute-start.2) | collective-permute-done | bytes 376864 | tf_op jit(solution)/shard_map/ppermute | solution.py:27
  72.6 1.2 %collective-permute-done.3.right_ref = f32[92,8,128]{2,1,0:T(8,128)S(1)} collective-permute-done((f32[92,8,128]{2,1,0:T(8,128)S(1)}, f32[92,8,128]{2,1,0:T(8,128)S(1)}, u32[]{:S(2)}, u32[]{:S(2)}) %collective-permute-start.3) | collective-permute-done | bytes 376864 | tf_op jit(solution)/shard_map/ppermute | solution.py:27
  73.8 0.0 all-to-all-done.1
  73.8 4.7 %smooth.1 = (f32[3,16,8,128]{3,2,1,0:T(8,128)}, f32[3,16,8,128]{3,2,1,0:T(8,128)S(1)}, f32[10,8,128]{2,1,0:T(8,128)S(1)}) custom-call(s32[4]{0:T(128)S(1)} %pad_add_fusion.place_ref, s32[768]{0:T(1024)S(1)} %get-tuple-element.36.ghost_ref, f32[3,16,8,128]{3,2,1,0:T(8,128)S(1)} %bitcast.49, f32[3,16,8,128]{3,2,1,0:T(8,128)S(1)} %bitcast.52, ...), custom_call_target="tpu_custom_call" | custom-call | tf_op jit(solution)/shard_map/smooth/pallas_call | solution.py:524
  78.5 4.2 %collective-permute-start.8 = (f32[10,8,128]{2,1,0:T(8,128)S(1)}, f32[10,8,128]{2,1,0:T(8,128)S(1)}, u32[]{:S(2)}, u32[]{:S(2)}) collective-permute-start(f32[10,8,128]{2,1,0:T(8,128)S(1)} %get-tuple-element.19), channel_id=1, source_target_pairs={{0,2},{1,3},{2,4},{3,5},{4,6},{5,7},{6,8},{7,9},{8,10},{9,11},{10,... | collective-permute-start | bytes 122888 | tf_op jit(solution)/shard_map/ppermute | solution.py:27
  82.7 4.0 %collective-permute-start.11 = (f32[10,8,128]{2,1,0:T(8,128)S(1)}, f32[10,8,128]{2,1,0:T(8,128)S(1)}, u32[]{:S(2)}, u32[]{:S(2)}) collective-permute-start(f32[10,8,128]{2,1,0:T(8,128)S(1)} %get-tuple-element.19), channel_id=1, source_target_pairs={{2,0},{3,1},{4,2},{5,3},{6,4},{7,5},{8,6},{9,7},{10,8},{11,9},{12,... | collective-permute-start | bytes 122888 | tf_op jit(solution)/shard_map/ppermute | solution.py:27
  86.7 5.6 %collective-permute-start.10 = (f32[10,8,128]{2,1,0:T(8,128)S(1)}, f32[10,8,128]{2,1,0:T(8,128)S(1)}, u32[]{:S(2)}, u32[]{:S(2)}) collective-permute-start(f32[10,8,128]{2,1,0:T(8,128)S(1)} %get-tuple-element.19), channel_id=1, source_target_pairs={{1,0},{2,1},{3,2},{4,3},{5,4},{6,5},{7,6},{8,7},{9,8},{10,9},{11,1... | collective-permute-start | bytes 122888 | tf_op jit(solution)/shard_map/ppermute | solution.py:27
  92.3 1.9 %collective-permute-start.9 = (f32[10,8,128]{2,1,0:T(8,128)S(1)}, f32[10,8,128]{2,1,0:T(8,128)S(1)}, u32[]{:S(2)}, u32[]{:S(2)}) collective-permute-start(f32[10,8,128]{2,1,0:T(8,128)S(1)} %get-tuple-element.19), channel_id=1, source_target_pairs={{0,1},{1,2},{2,3},{3,4},{4,5},{5,6},{6,7},{7,8},{8,9},{9,10},{10,1... | collective-permute-start | bytes 122888 | tf_op jit(solution)/shard_map/ppermute | solution.py:27
  94.3 0.0 collective-permute-done.8
  94.3 6.1 %collective-permute-done.9 = f32[10,8,128]{2,1,0:T(8,128)S(1)} collective-permute-done((f32[10,8,128]{2,1,0:T(8,128)S(1)}, f32[10,8,128]{2,1,0:T(8,128)S(1)}, u32[]{:S(2)}, u32[]{:S(2)}) %collective-permute-start.9) | collective-permute-done | bytes 40992 | tf_op jit(solution)/shard_map/ppermute | solution.py:27
  100.3 0.0 collective-permute-done.10
  100.4 0.0 collective-permute-done.11
  100.5 3.6 %collective-permute-start.12 = (f32[35,8,128]{2,1,0:T(8,128)S(1)}, f32[35,8,128]{2,1,0:T(8,128)S(1)}, u32[]{:S(2)}, u32[]{:S(2)}) collective-permute-start(f32[35,8,128]{2,1,0:T(8,128)S(1)} %constant_dynamic-update-slice_fusion.8), channel_id=1, source_target_pairs={{0,32},{1,33},{2,34},{3,35},{4,36},{5,37},{6,38},{7,39},{8,40},{9,... | collective-permute-start | bytes 430088 | tf_op jit(solution)/shard_map/ppermute | solution.py:27
  104.1 2.3 %collective-permute-start.13 = (f32[35,8,128]{2,1,0:T(8,128)S(1)}, f32[35,8,128]{2,1,0:T(8,128)S(1)}, u32[]{:S(2)}, u32[]{:S(2)}) collective-permute-start(f32[35,8,128]{2,1,0:T(8,128)S(1)} %pad_maximum_fusion), channel_id=1, source_target_pairs={{32,0},{33,1},{34,2},{35,3},{36,4},{37,5},{38,6},{39,7},{40,8},{41... | collective-permute-start | bytes 430088 | tf_op jit(solution)/shard_map/ppermute | solution.py:27
  106.4 1.1 collective-permute-done.12.above_ref
  107.5 4.8 %collective-permute-done.13.below_ref = f32[35,8,128]{2,1,0:T(8,128)S(1)} collective-permute-done((f32[35,8,128]{2,1,0:T(8,128)S(1)}, f32[35,8,128]{2,1,0:T(8,128)S(1)}, u32[]{:S(2)}, u32[]{:S(2)}) %collective-permute-start.13) | collective-permute-done | bytes 143392 | tf_op jit(solution)/shard_map/ppermute | solution.py:27
  112.3 1.9 %coarse.1 = f32[3,16,8,128]{3,2,1,0:T(8,128)} custom-call(f32[10,40,128]{2,1,0:T(8,128)S(1)} %constant_dynamic-update-slice_fusion.mid_ref, f32[35,8,128]{2,1,0:T(8,128)S(1)} %collective-permute-done.12.above_ref, f32[35,8,128]{2,1,0:T(8,128)S(1)} %collective-permute-done.13.below_ref, f32[3,16,8,128]{3,2,1,0:T(8,128)S(1)} %get-tuple-element.20.smooth_ref), custom_call_target="tpu_custom_call" | custom-call | tf_op jit(solution)/shard_map/coarse/pallas_call | solution.py:554
  (31 shorter events, 0.3 us)
Async XLA Ops:
  0.6 0.9 copy-start
  1.6 8.3 %copy-start.1 = (f32[1,3,16,8,128]{4,3,2,1,0:T(8,128)S(1)}, f32[1,3,16,8,128]{4,3,2,1,0:T(8,128)}, u32[]{:S(2)}) copy-start(f32[1,3,16,8,128]{4,3,2,1,0:T(8,128)} %param.7) | copy-start | bytes 589828
  1.6 8.2 %copy-start.7 = (f32[1,1,4,3]{2,1,3,0:T(1,128)S(1)}, f32[1,1,4,3]{2,1,3,0:T(1,128)}, u32[]{:S(2)}) copy-start(f32[1,1,4,3]{2,1,3,0:T(1,128)} %param.13) | copy-start | bytes 148
  1.6 13.6 %collective-permute-start.7 = (f32[3,128]{1,0:T(4,128)S(1)}, f32[3,128]{1,0:T(4,128)S(1)}, u32[]{:S(2)}, u32[]{:S(2)}) collective-permute-start(f32[3,128]{1,0:T(4,128)S(1)} %get-tuple-element.18), channel_id=1, source_target_pairs={{33,256},{34,257},{35,258},{36,259},{37,260},{38,261},{39,262},{40... | collective-permute-start | bytes 4616 | tf_op jit(solution)/shard_map/ppermute | solution.py:27
  4.8 10.3 %collective-permute-start.6 = (f32[3,8,128]{2,1,0:T(8,128)S(1)}, f32[3,8,128]{2,1,0:T(8,128)S(1)}, u32[]{:S(2)}, u32[]{:S(2)}) collective-permute-start(f32[3,8,128]{2,1,0:T(8,128)S(1)} %get-tuple-element.17), channel_id=1, source_target_pairs={{32,256},{33,257},{34,258},{35,259},{36,260},{37,261},{38,262},{39... | collective-permute-start | bytes 36872 | tf_op jit(solution)/shard_map/ppermute | solution.py:27
  7.5 7.7 %collective-permute-start.5 = (f32[3,16,128]{2,1,0:T(8,128)S(1)}, f32[3,16,128]{2,1,0:T(8,128)S(1)}, u32[]{:S(2)}, u32[]{:S(2)}) collective-permute-start(f32[3,16,128]{2,1,0:T(8,128)S(1)} %get-tuple-element.16), channel_id=1, source_target_pairs={{1,256},{2,257},{3,258},{4,259},{5,260},{6,261},{7,262},{8,263},{9... | collective-permute-start | bytes 73736 | tf_op jit(solution)/shard_map/ppermute | solution.py:27
  9.9 0.7 copy-start.4
  9.9 0.7 copy-start.5
  11.2 4.0 %collective-permute-start.4 = (f32[88,128]{1,0:T(8,128)S(1)}, f32[88,128]{1,0:T(8,128)S(1)}, u32[]{:S(2)}, u32[]{:S(2)}) collective-permute-start(f32[88,128]{1,0:T(8,128)S(1)} %shard_map.88), channel_id=1, source_target_pairs={{0,256},{1,257},{2,258},{3,259},{4,260},{5,261},{6,262},{7,263},{8... | collective-permute-start | bytes 135176 | tf_op jit(solution)/shard_map/ppermute | solution.py:27
  14.3 0.7 copy-start.6
  15.9 21.8 %all-to-all-start = ((f32[32,1,1152]{2,1,0:T(1,128)}), f32[32,1,1152]{2,1,0:T(1,128)S(1)}, u32[]{:S(2)}, u32[]{:S(2)}) async-start(f32[32,1,1152]{2,1,0:T(1,128)} %bitcast.8), calls=%async_computation | async-start | bytes 294912 | tf_op jit(solution)/shard_map/all_to_all | solution.py:503
  39.1 7.7 %copy-start.2 = (f32[1,3,16,8,128]{4,3,2,1,0:T(8,128)S(1)}, f32[1,3,16,8,128]{4,3,2,1,0:T(8,128)}, u32[]{:S(2)}) copy-start(f32[1,3,16,8,128]{4,3,2,1,0:T(8,128)} %param.8) | copy-start | bytes 589828
  39.1 7.7 %copy-start.3 = (f32[1,16,8,128]{3,2,1,0:T(8,128)S(1)}, f32[1,16,8,128]{3,2,1,0:T(8,128)}, u32[]{:S(2)}) copy-start(f32[1,16,8,128]{3,2,1,0:T(8,128)} %param.9) | copy-start | bytes 196612
  39.1 34.7 %all-to-all-start.1 = ((f32[8,96,128]{2,1,0:T(8,128)}), f32[8,96,128]{2,1,0:T(8,128)S(1)}, u32[]{:S(2)}, u32[]{:S(2)}) async-start(f32[8,96,128]{2,1,0:T(8,128)} %bitcast.10), calls=%async_computation.1 | async-start | bytes 786432 | tf_op jit(solution)/shard_map/all_to_all | solution.py:516
  46.8 10.3 %collective-permute-start = (f32[32,8,128]{2,1,0:T(8,128)S(1)}, f32[32,8,128]{2,1,0:T(8,128)S(1)}, u32[]{:S(2)}, u32[]{:S(2)}) collective-permute-start(f32[32,8,128]{2,1,0:T(8,128)S(1)} %get-tuple-element.12), channel_id=1, source_target_pairs={{0,32},{1,33},{2,34},{3,35},{4,36},{5,37},{6,38},{7,39},{8,40},{9,... | collective-permute-start | bytes 393224 | tf_op jit(solution)/shard_map/ppermute | solution.py:27
  51.4 8.2 %collective-permute-start.1 = (f32[32,8,128]{2,1,0:T(8,128)S(1)}, f32[32,8,128]{2,1,0:T(8,128)S(1)}, u32[]{:S(2)}, u32[]{:S(2)}) collective-permute-start(f32[32,8,128]{2,1,0:T(8,128)S(1)} %get-tuple-element.13), channel_id=1, source_target_pairs={{32,0},{33,1},{34,2},{35,3},{36,4},{37,5},{38,6},{39,7},{40,8},{41... | collective-permute-start | bytes 393224 | tf_op jit(solution)/shard_map/ppermute | solution.py:27
  59.6 12.9 %collective-permute-start.2 = (f32[92,8,128]{2,1,0:T(8,128)S(1)}, f32[92,8,128]{2,1,0:T(8,128)S(1)}, u32[]{:S(2)}, u32[]{:S(2)}) collective-permute-start(f32[92,8,128]{2,1,0:T(8,128)S(1)} %get-tuple-element.14), channel_id=1, source_target_pairs={{0,1},{1,2},{2,3},{3,4},{4,5},{5,6},{6,7},{7,8},{8,9},{9,10},{10,1... | collective-permute-start | bytes 1130504 | tf_op jit(solution)/shard_map/ppermute | solution.py:27
  62.3 11.5 %collective-permute-start.3 = (f32[92,8,128]{2,1,0:T(8,128)S(1)}, f32[92,8,128]{2,1,0:T(8,128)S(1)}, u32[]{:S(2)}, u32[]{:S(2)}) collective-permute-start(f32[92,8,128]{2,1,0:T(8,128)S(1)} %get-tuple-element.15), channel_id=1, source_target_pairs={{1,0},{2,1},{3,2},{4,3},{5,4},{6,5},{7,6},{8,7},{9,8},{10,9},{11,1... | collective-permute-start | bytes 1130504 | tf_op jit(solution)/shard_map/ppermute | solution.py:27
  78.5 15.8 %collective-permute-start.8 = (f32[10,8,128]{2,1,0:T(8,128)S(1)}, f32[10,8,128]{2,1,0:T(8,128)S(1)}, u32[]{:S(2)}, u32[]{:S(2)}) collective-permute-start(f32[10,8,128]{2,1,0:T(8,128)S(1)} %get-tuple-element.19), channel_id=1, source_target_pairs={{0,2},{1,3},{2,4},{3,5},{4,6},{5,7},{6,8},{7,9},{8,10},{9,11},{10,... | collective-permute-start | bytes 122888 | tf_op jit(solution)/shard_map/ppermute | solution.py:27
  82.7 17.7 %collective-permute-start.11 = (f32[10,8,128]{2,1,0:T(8,128)S(1)}, f32[10,8,128]{2,1,0:T(8,128)S(1)}, u32[]{:S(2)}, u32[]{:S(2)}) collective-permute-start(f32[10,8,128]{2,1,0:T(8,128)S(1)} %get-tuple-element.19), channel_id=1, source_target_pairs={{2,0},{3,1},{4,2},{5,3},{6,4},{7,5},{8,6},{9,7},{10,8},{11,9},{12,... | collective-permute-start | bytes 122888 | tf_op jit(solution)/shard_map/ppermute | solution.py:27
  86.7 13.6 %collective-permute-start.10 = (f32[10,8,128]{2,1,0:T(8,128)S(1)}, f32[10,8,128]{2,1,0:T(8,128)S(1)}, u32[]{:S(2)}, u32[]{:S(2)}) collective-permute-start(f32[10,8,128]{2,1,0:T(8,128)S(1)} %get-tuple-element.19), channel_id=1, source_target_pairs={{1,0},{2,1},{3,2},{4,3},{5,4},{6,5},{7,6},{8,7},{9,8},{10,9},{11,1... | collective-permute-start | bytes 122888 | tf_op jit(solution)/shard_map/ppermute | solution.py:27
  92.3 8.0 %collective-permute-start.9 = (f32[10,8,128]{2,1,0:T(8,128)S(1)}, f32[10,8,128]{2,1,0:T(8,128)S(1)}, u32[]{:S(2)}, u32[]{:S(2)}) collective-permute-start(f32[10,8,128]{2,1,0:T(8,128)S(1)} %get-tuple-element.19), channel_id=1, source_target_pairs={{0,1},{1,2},{2,3},{3,4},{4,5},{5,6},{6,7},{7,8},{8,9},{9,10},{10,1... | collective-permute-start | bytes 122888 | tf_op jit(solution)/shard_map/ppermute | solution.py:27
  100.5 7.0 %collective-permute-start.12 = (f32[35,8,128]{2,1,0:T(8,128)S(1)}, f32[35,8,128]{2,1,0:T(8,128)S(1)}, u32[]{:S(2)}, u32[]{:S(2)}) collective-permute-start(f32[35,8,128]{2,1,0:T(8,128)S(1)} %constant_dynamic-update-slice_fusion.8), channel_id=1, source_target_pairs={{0,32},{1,33},{2,34},{3,35},{4,36},{5,37},{6,38},{7,39},{8,40},{9,... | collective-permute-start | bytes 430088 | tf_op jit(solution)/shard_map/ppermute | solution.py:27
  104.1 8.2 %collective-permute-start.13 = (f32[35,8,128]{2,1,0:T(8,128)S(1)}, f32[35,8,128]{2,1,0:T(8,128)S(1)}, u32[]{:S(2)}, u32[]{:S(2)}) collective-permute-start(f32[35,8,128]{2,1,0:T(8,128)S(1)} %pad_maximum_fusion), channel_id=1, source_target_pairs={{32,0},{33,1},{34,2},{35,3},{36,4},{37,5},{38,6},{39,7},{40,8},{41... | collective-permute-start | bytes 430088 | tf_op jit(solution)/shard_map/ppermute | solution.py:27

commit v8 on v7

--- a/solution.py
+++ b/solution.py
@@ -47,8 +47,18 @@
     return jnp.where(odd_row, roll(value, 1, 0), roll(value, -1, 0))
 
 
-def first_kernel(v_ref, edge_ref, below_ref, corner_ref):
+def first_kernel(
+    rows_hbm, cols_hbm, weights_hbm, v_hbm, edge_ref, below_ref, corner_ref, blend_ref,
+    rows_ref, cols_ref, weights_ref, v_ref, done,
+):
     sub = rows_of((8, 128))
+    pairs = (v_hbm, v_ref), (rows_hbm, rows_ref), (cols_hbm, cols_ref), (weights_hbm, weights_ref)
+    copies = [pltpu.make_async_copy(*pair, done.at[n]) for n, pair in enumerate(pairs)]
+    for copy in copies:
+        copy.start()
+    for copy in copies:
+        copy.wait()
+    blend(rows_ref, cols_ref, weights_ref, v_ref, blend_ref)
     for comp in range(3):
         corner_ref[comp : comp + 1] = v_ref[comp, 0, 0:1]
         below_ref[comp] = v_ref[comp, 0]
@@ -76,11 +86,11 @@
                 ref[lat_tile(field, away)] = value
 
 
-def blend_kernel(rows_ref, cols_ref, weights_ref, v_ref, out_ref):
+def blend(rows_ref, cols_ref, weights_ref, v_ref, out_ref):
     tall, flat = rows_of((16, 128)), rows_of((8, 128))
     for slot in range(3):
-        row, col = rows_ref[slot], cols_ref[slot]
-        w0, w1, w2, w3 = (weights_ref[k, slot] for k in range(4))
+        row, col = rows_ref[0, slot], cols_ref[0, slot]
+        w0, w1, w2, w3 = (weights_ref[slot, 0, k] for k in range(4))
         here, next_one = flat == col, flat == col + 1
         upper = jnp.where(here, w0, jnp.where(next_one, w2, 0.0))
         lower = jnp.where(here, w1, jnp.where(next_one, w3, 0.0))
@@ -377,8 +387,11 @@
 
 
 def coarse_kernel(
-    mid_ref, above_ref, below_ref, smooth_ref, out_ref, Q, CV, DV, E, AN, AS, AW, AE, AD, AU
+    mid_ref, above_ref, below_ref, smooth_ref, left_ref, out_ref, res_ref,
+    done, Q, CV, DV, E, AN, AS, AW, AE, AD, AU,
 ):
+    leave = pltpu.make_async_copy(left_ref, res_ref, done)
+    leave.start()
     wide = (40, 128)
     lane, row = lanes_of(wide), rows_of(wide)
     odd_lane, odd_row = (lane & 1) == 1, (row & 1) == 1
@@ -448,6 +461,7 @@
             error = spread(value, comp, odd_lane8, odd_row8)
             for r in (2 * k, 2 * k + 1):
                 out_ref[comp, r] = smooth_ref[comp, r] + error
+    leave.wait()
 
 
 def wanted_cells(lats, lons, lon):
@@ -470,13 +484,6 @@
     lats, lons = lax.axis_size("lat"), lax.axis_size("lon")
     params = pltpu.CompilerParams(vmem_limit_bytes=32 * 2**20)
     f32 = jnp.float32
-    place = jnp.stack(
-        [lax.axis_index("lat"), lax.axis_index("lon"), jnp.int32(lats - 1), jnp.int32(lons - 1)]
-    ).astype(jnp.int32)
-    slots = ghost_slots[0]
-    source_rows = ((slots // 3) % lons) * 9 + (slots % 3) * 3
-    ghost_rows = (slots // (3 * lons)) * (3 * CELLS)
-    cells = wanted_cells(lats, lons, lax.axis_index("lon")).reshape(-1)
 
     def kernel(body, shapes, specs):
         return pl.pallas_call(
@@ -487,21 +494,45 @@
             compiler_params=params,
         )
 
-    edge, first_row, first_cell = kernel(
-        first_kernel, ((3, 16, 128), (3, 8, 128), (3, 128)), [VMEM]
-    )(v)
+    weights = jnp.transpose(corner_weights, (0, 3, 1, 2))[0]
+    shapes = ((3, 16, 128), (3, 8, 128), (3, 128), (88, 128))
+    edge, first_row, first_cell, blended = pl.pallas_call(
+        first_kernel,
+        out_shape=[jax.ShapeDtypeStruct(shape, f32) for shape in shapes],
+        in_specs=[pl.BlockSpec(memory_space=pltpu.HBM)] * 4,
+        out_specs=[VMEM] * 4,
+        scratch_shapes=[
+            pltpu.SMEM((1, 3), jnp.int32),
+            pltpu.SMEM((1, 3), jnp.int32),
+            pltpu.SMEM((3, 1, 4), f32),
+            pltpu.VMEM(v.shape, f32),
+            pltpu.SemaphoreType.DMA((4,)),
+        ],
+        compiler_params=params,
+        name="first",
+    )(
+        *(
+            pltpu.with_memory_space_constraint(operand, pltpu.HBM)
+            for operand in (corner_rows[0], corner_cols[0], weights, v)
+        )
+    )
     first_cell = shifted(first_cell, -1, -1, 1)
     first_row = shifted(first_row, -1, 0, 1)
     edge = shifted(edge, 0, -1, 1)
-    (blended,) = kernel(blend_kernel, ((88, 128),), [SMEM] * 3 + [VMEM])(
-        corner_rows[0, 0], corner_cols[0, 0], corner_weights[0, 0], v
-    )
     blended = shifted(blended, 0, 0, 1)
     (values,) = kernel(interp_kernel, ((9 * lons, 1, 128),), [VMEM] * 4)(
         blended, edge, first_row, first_cell
     )
     around = lax.all_to_all(values.reshape(lons, 1, 1152), "lon", 0, 0, tiled=True)
     to_above, to_below = kernel(cut_kernel, ((32, 8, 128),) * 2, [VMEM] * 3)(v, f, mu)
+    slots, lat_at, lon_at, to_above = lax.optimization_barrier(
+        (ghost_slots, lax.axis_index("lat"), lax.axis_index("lon"), to_above)
+    )
+    slots = slots[0]
+    place = jnp.stack([lat_at, lon_at, jnp.int32(lats - 1), jnp.int32(lons - 1)])
+    source_rows = ((slots // 3) % lons) * 9 + (slots % 3) * 3
+    ghost_rows = (slots // (3 * lons)) * (3 * CELLS)
+    cells = wanted_cells(lats, lons, lon_at).reshape(-1)
     below = shifted(to_above, -1, 0)
     above = shifted(to_below, 1, 0)
 
@@ -551,15 +582,17 @@
     band_below = shifted(jnp.concatenate(to_above, axis=0), -1, 0)
     band_above = shifted(jnp.concatenate(to_below, axis=0), 1, 0)
     coarse = pltpu.VMEM((22, 40, 128), f32)
-    new = pl.pallas_call(
+    new, residual = pl.pallas_call(
         coarse_kernel,
-        out_shape=block,
-        in_specs=[VMEM] * 4,
-        out_specs=VMEM,
-        scratch_shapes=[coarse, coarse, coarse, pltpu.VMEM((2, 22, 40, 128), f32)] + [coarse] * 6,
+        out_shape=(block, block),
+        in_specs=[VMEM] * 5,
+        out_specs=(VMEM, pl.BlockSpec(memory_space=pl.ANY)),
+        scratch_shapes=[pltpu.SemaphoreType.DMA(()), coarse, coarse, coarse]
+        + [pltpu.VMEM((2, 22, 40, 128), f32)]
+        + [coarse] * 6,
         compiler_params=params,
         name="coarse",
-    )(band, band_above, band_below, smoothed)
+    )(band, band_above, band_below, smoothed, residual)
     return new[None], residual[None]
 
 

time: 115 us -> 114 us (level)
    pallas_call x3 -> x2, Pallas kernels: 2.56 us -> 3.04 us  [the longest x1 1.95 us: per_device(): pl.pallas_call(coarse_kernel, out_shape=(block, block), in_specs=[VMEM] *...]
    unnamed x27 -> x22, local copies, waits for them, and re-layouts: 2.35 us -> 2.43 us
  transfers between devices with their start and end apart: 16 -> 16, of which waited for: 8 -> 7; matrix products, arithmetic and copies ran while one was open for 1% -> 1% of each run, Pallas kernels for 1% -> 0%
where the time goes in v8:
time: 114 us
  starting transfers between devices  66.4 us (58%)
  waiting for transfers between devices  33.3 us (29%)
  Pallas kernels  9.41 us (8%)
  local copies, waits for them, and re-layouts  2.94 us (3%)
    ppermute x14, starting transfers between devices, shifted(): return lax.ppermute(value, AXES, pairs)  47.1 us
    ppermute x14, waiting for transfers between devices, shifted(): return lax.ppermute(value, AXES, pairs)  23.3 us
    all_to_all x1, starting transfers between devices, per_device(): lax.all_to_all(values.reshape(lons, 1, 1152), 'lon', 0, 0, tiled=True)  11.7 us
    all_to_all x1, waiting for transfers between devices, per_device(): lax.all_to_all(values.reshape(lons, 1, 1152), 'lon', 0, 0, tiled=True)  10 us
    all_to_all x1, starting transfers between devices, per_device(): lax.all_to_all(chosen.reshape(lats, 3 * CELLS, 128), 'lat', 0, 0, tiled=T...  7.68 us
    pallas_call x1, Pallas kernels, per_device(): pl.pallas_call(smooth_kernel, out_shape=(block, block, jax.ShapeDtypeStru...  4.1 us
    unnamed x22, local copies, waits for them, and re-layouts  2.43 us
  transfers between devices with their start and end apart: 16, of which 7 were waited for; matrix products, arithmetic and copies ran while one was open for 1% of the time, Pallas kernels for 0%

profile of v8, /device:TPU:88, one launch (start us, length us, event | category | flops | bytes accessed | tf_op | source)
XLA Modules:
  0.0 113.6 jit_solution(17398666318774090935)
XLA Ops:
  0.6 0.0 copy-start
  0.6 1.1 first.1
  1.7 3.1 %collective-permute-start.7 = (f32[3,128]{1,0:T(4,128)S(1)}, f32[3,128]{1,0:T(4,128)S(1)}, u32[]{:S(2)}, u32[]{:S(2)}) collective-permute-start(f32[3,128]{1,0:T(4,128)S(1)} %get-tuple-element.30), channel_id=1, source_target_pairs={{33,256},{34,257},{35,258},{36,259},{37,260},{38,261},{39,262},{40... | collective-permute-start | bytes 4616 | tf_op jit(solution)/shard_map/ppermute | solution.py:27
  4.8 2.6 %collective-permute-start.6 = (f32[3,8,128]{2,1,0:T(8,128)S(1)}, f32[3,8,128]{2,1,0:T(8,128)S(1)}, u32[]{:S(2)}, u32[]{:S(2)}) collective-permute-start(f32[3,8,128]{2,1,0:T(8,128)S(1)} %get-tuple-element.29), channel_id=1, source_target_pairs={{32,256},{33,257},{34,258},{35,259},{36,260},{37,261},{38,262},{39... | collective-permute-start | bytes 36872 | tf_op jit(solution)/shard_map/ppermute | solution.py:27
  7.5 2.3 %collective-permute-start.5 = (f32[3,16,128]{2,1,0:T(8,128)S(1)}, f32[3,16,128]{2,1,0:T(8,128)S(1)}, u32[]{:S(2)}, u32[]{:S(2)}) collective-permute-start(f32[3,16,128]{2,1,0:T(8,128)S(1)} %get-tuple-element.28), channel_id=1, source_target_pairs={{1,256},{2,257},{3,258},{4,259},{5,260},{6,261},{7,262},{8,263},{9... | collective-permute-start | bytes 73736 | tf_op jit(solution)/shard_map/ppermute | solution.py:27
  9.8 2.5 %collective-permute-start.4 = (f32[88,128]{1,0:T(8,128)S(1)}, f32[88,128]{1,0:T(8,128)S(1)}, u32[]{:S(2)}, u32[]{:S(2)}) collective-permute-start(f32[88,128]{1,0:T(8,128)S(1)} %get-tuple-element.27), channel_id=1, source_target_pairs={{0,256},{1,257},{2,258},{3,259},{4,260},{5,261},{6,262},{7,263},{8... | collective-permute-start | bytes 135176 | tf_op jit(solution)/shard_map/ppermute | solution.py:27
  12.3 0.1 iota_select_fusion
  12.4 0.1 select_n.73
  12.5 0.1 add.104
  12.5 0.1 add.105
  12.6 0.0 copy-done
  12.6 0.0 copy-start.1
  12.6 0.9 copy-done.1
  13.6 0.0 copy-start.3
  13.6 0.8 copy-done.3
  14.4 0.1 fusion.8
  14.5 0.1 reshape.135
  14.6 0.1 clamp_add_fusion
  14.7 0.1 reshape.134
  14.8 0.0 copy-start.5
  14.8 0.1 broadcast_in_dim.43
  14.9 0.6 copy-done.5
  15.6 0.0 collective-permute-done.7.corner_ref
  15.6 0.0 collective-permute-done.6.below_ref
  15.6 0.0 collective-permute-done.5.edge_ref
  15.6 0.0 collective-permute-done.4.blend_ref
  15.6 0.8 shard_map.88
  16.4 11.7 %all-to-all-start = ((f32[32,1,1152]{2,1,0:T(1,128)}), f32[32,1,1152]{2,1,0:T(1,128)S(1)}, u32[]{:S(2)}, u32[]{:S(2)}) async-start(f32[32,1,1152]{2,1,0:T(1,128)} %bitcast.9), calls=%async_computation | async-start | bytes 294912 | tf_op jit(solution)/shard_map/all_to_all | solution.py:526
  28.0 0.1 pad_add_fusion.place_ref
  28.1 10.0 %all-to-all-done = f32[32,1,1152]{2,1,0:T(1,128)S(1)} async-done(((f32[32,1,1152]{2,1,0:T(1,128)}), f32[32,1,1152]{2,1,0:T(1,128)S(1)}, u32[]{:S(2)}, u32[]{:S(2)}) %all-to-all-start) | async-done | bytes 147488 | tf_op jit(solution)/shard_map/all_to_all | solution.py:526
  38.1 1.4 %pick.1 = f32[768,1,128]{2,1,0:T(1,128)} custom-call(s32[4]{0:T(128)S(1)} %pad_add_fusion.place_ref, s32[256]{0:T(256)S(1)} %add_select_fusion.4.cells_ref, s32[768]{0:T(1024)S(1)} %get-tuple-element.49.source_ref, f32[288,1,128]{2,1,0:T(1,128)S(1)} %bitcast.55), custom_call_target="tpu_custom_call" | custom-call | tf_op jit(solution)/shard_map/pick/pallas_call | solution.py:539
  39.5 0.0 copy-start.2
  39.5 0.0 copy-start.4
  39.5 7.7 %all-to-all-start.1 = ((f32[8,96,128]{2,1,0:T(8,128)}), f32[8,96,128]{2,1,0:T(8,128)S(1)}, u32[]{:S(2)}, u32[]{:S(2)}) async-start(f32[8,96,128]{2,1,0:T(8,128)} %bitcast.11), calls=%async_computation.1 | async-start | bytes 786432 | tf_op jit(solution)/shard_map/all_to_all | solution.py:547
  47.2 2.5 %collective-permute-start.1 = (f32[32,8,128]{2,1,0:T(8,128)S(1)}, f32[32,8,128]{2,1,0:T(8,128)S(1)}, u32[]{:S(2)}, u32[]{:S(2)}) collective-permute-start(f32[32,8,128]{2,1,0:T(8,128)S(1)} %get-tuple-element.24), channel_id=1, source_target_pairs={{32,0},{33,1},{34,2},{35,3},{36,4},{37,5},{38,6},{39,7},{40,8},{41... | collective-permute-start | bytes 393224 | tf_op jit(solution)/shard_map/ppermute | solution.py:27
  49.7 4.6 %collective-permute-start = (f32[32,8,128]{2,1,0:T(8,128)S(1)}, f32[32,8,128]{2,1,0:T(8,128)S(1)}, u32[]{:S(2)}, u32[]{:S(2)}) collective-permute-start(f32[32,8,128]{2,1,0:T(8,128)S(1)} %get-tuple-element.23), channel_id=1, source_target_pairs={{0,32},{1,33},{2,34},{3,35},{4,36},{5,37},{6,38},{7,39},{8,40},{9,... | collective-permute-start | bytes 393224 | tf_op jit(solution)/shard_map/ppermute | solution.py:27
  54.3 5.7 %collective-permute-done.1.below_ref = f32[32,8,128]{2,1,0:T(8,128)S(1)} collective-permute-done((f32[32,8,128]{2,1,0:T(8,128)S(1)}, f32[32,8,128]{2,1,0:T(8,128)S(1)}, u32[]{:S(2)}, u32[]{:S(2)}) %collective-permute-start.1) | collective-permute-done | bytes 131104 | tf_op jit(solution)/shard_map/ppermute | solution.py:27
  60.0 0.0 collective-permute-done.above_ref
  60.0 0.0 copy-done.2
  60.0 0.0 copy-done.4
  60.0 0.1 shard_map.87
  60.1 2.6 %collective-permute-start.2 = (f32[92,8,128]{2,1,0:T(8,128)S(1)}, f32[92,8,128]{2,1,0:T(8,128)S(1)}, u32[]{:S(2)}, u32[]{:S(2)}) collective-permute-start(f32[92,8,128]{2,1,0:T(8,128)S(1)} %get-tuple-element.25), channel_id=1, source_target_pairs={{0,1},{1,2},{2,3},{3,4},{4,5},{5,6},{6,7},{7,8},{8,9},{9,10},{10,1... | collective-permute-start | bytes 1130504 | tf_op jit(solution)/shard_map/ppermute | solution.py:27
  62.7 5.3 %collective-permute-start.3 = (f32[92,8,128]{2,1,0:T(8,128)S(1)}, f32[92,8,128]{2,1,0:T(8,128)S(1)}, u32[]{:S(2)}, u32[]{:S(2)}) collective-permute-start(f32[92,8,128]{2,1,0:T(8,128)S(1)} %get-tuple-element.26), channel_id=1, source_target_pairs={{1,0},{2,1},{3,2},{4,3},{5,4},{6,5},{7,6},{8,7},{9,8},{10,9},{11,1... | collective-permute-start | bytes 1130504 | tf_op jit(solution)/shard_map/ppermute | solution.py:27
  68.1 5.5 %collective-permute-done.2.left_ref = f32[92,8,128]{2,1,0:T(8,128)S(1)} collective-permute-done((f32[92,8,128]{2,1,0:T(8,128)S(1)}, f32[92,8,128]{2,1,0:T(8,128)S(1)}, u32[]{:S(2)}, u32[]{:S(2)}) %collective-permute-start.2) | collective-permute-done | bytes 376864 | tf_op jit(solution)/shard_map/ppermute | solution.py:27
  73.5 1.2 %collective-permute-done.3.right_ref = f32[92,8,128]{2,1,0:T(8,128)S(1)} collective-permute-done((f32[92,8,128]{2,1,0:T(8,128)S(1)}, f32[92,8,128]{2,1,0:T(8,128)S(1)}, u32[]{:S(2)}, u32[]{:S(2)}) %collective-permute-start.3) | collective-permute-done | bytes 376864 | tf_op jit(solution)/shard_map/ppermute | solution.py:27
  74.7 0.0 all-to-all-done.1
  74.7 4.1 %smooth.1 = (f32[3,16,8,128]{3,2,1,0:T(8,128)S(1)}, f32[3,16,8,128]{3,2,1,0:T(8,128)S(1)}, f32[10,8,128]{2,1,0:T(8,128)S(1)}) custom-call(s32[4]{0:T(128)S(1)} %pad_add_fusion.place_ref, s32[768]{0:T(1024)S(1)} %get-tuple-element.50.ghost_ref, f32[3,16,8,128]{3,2,1,0:T(8,128)S(1)} %bitcast.50, f32[3,16,8,128]{3,2,1,0:T(8,128)S(1)} %bitcast.53, ...), custom_call_target="tpu_custom_call" | custom-call | tf_op jit(solution)/shard_map/smooth/pallas_call | solution.py:555
  78.8 3.9 %collective-permute-start.8 = (f32[10,8,128]{2,1,0:T(8,128)S(1)}, f32[10,8,128]{2,1,0:T(8,128)S(1)}, u32[]{:S(2)}, u32[]{:S(2)}) collective-permute-start(f32[10,8,128]{2,1,0:T(8,128)S(1)} %get-tuple-element.31), channel_id=1, source_target_pairs={{0,2},{1,3},{2,4},{3,5},{4,6},{5,7},{6,8},{7,9},{8,10},{9,11},{10,... | collective-permute-start | bytes 122888 | tf_op jit(solution)/shard_map/ppermute | solution.py:27
  82.7 4.4 %collective-permute-start.11 = (f32[10,8,128]{2,1,0:T(8,128)S(1)}, f32[10,8,128]{2,1,0:T(8,128)S(1)}, u32[]{:S(2)}, u32[]{:S(2)}) collective-permute-start(f32[10,8,128]{2,1,0:T(8,128)S(1)} %get-tuple-element.31), channel_id=1, source_target_pairs={{2,0},{3,1},{4,2},{5,3},{6,4},{7,5},{8,6},{9,7},{10,8},{11,9},{12,... | collective-permute-start | bytes 122888 | tf_op jit(solution)/shard_map/ppermute | solution.py:27
  87.1 5.6 %collective-permute-start.10 = (f32[10,8,128]{2,1,0:T(8,128)S(1)}, f32[10,8,128]{2,1,0:T(8,128)S(1)}, u32[]{:S(2)}, u32[]{:S(2)}) collective-permute-start(f32[10,8,128]{2,1,0:T(8,128)S(1)} %get-tuple-element.31), channel_id=1, source_target_pairs={{1,0},{2,1},{3,2},{4,3},{5,4},{6,5},{7,6},{8,7},{9,8},{10,9},{11,1... | collective-permute-start | bytes 122888 | tf_op jit(solution)/shard_map/ppermute | solution.py:27
  92.7 1.9 %collective-permute-start.9 = (f32[10,8,128]{2,1,0:T(8,128)S(1)}, f32[10,8,128]{2,1,0:T(8,128)S(1)}, u32[]{:S(2)}, u32[]{:S(2)}) collective-permute-start(f32[10,8,128]{2,1,0:T(8,128)S(1)} %get-tuple-element.31), channel_id=1, source_target_pairs={{0,1},{1,2},{2,3},{3,4},{4,5},{5,6},{6,7},{7,8},{8,9},{9,10},{10,1... | collective-permute-start | bytes 122888 | tf_op jit(solution)/shard_map/ppermute | solution.py:27
  94.6 0.0 collective-permute-done.8
  94.6 6.1 %collective-permute-done.9 = f32[10,8,128]{2,1,0:T(8,128)S(1)} collective-permute-done((f32[10,8,128]{2,1,0:T(8,128)S(1)}, f32[10,8,128]{2,1,0:T(8,128)S(1)}, u32[]{:S(2)}, u32[]{:S(2)}) %collective-permute-start.9) | collective-permute-done | bytes 40992 | tf_op jit(solution)/shard_map/ppermute | solution.py:27
  100.7 0.0 collective-permute-done.10
  100.7 0.0 collective-permute-done.11
  100.9 2.5 %collective-permute-start.12 = (f32[35,8,128]{2,1,0:T(8,128)S(1)}, f32[35,8,128]{2,1,0:T(8,128)S(1)}, u32[]{:S(2)}, u32[]{:S(2)}) collective-permute-start(f32[35,8,128]{2,1,0:T(8,128)S(1)} %constant_dynamic-update-slice_fusion.8), channel_id=1, source_target_pairs={{0,32},{1,33},{2,34},{3,35},{4,36},{5,37},{6,38},{7,39},{8,40},{9,... | collective-permute-start | bytes 430088 | tf_op jit(solution)/shard_map/ppermute | solution.py:27
  103.4 3.3 %collective-permute-start.13 = (f32[35,8,128]{2,1,0:T(8,128)S(1)}, f32[35,8,128]{2,1,0:T(8,128)S(1)}, u32[]{:S(2)}, u32[]{:S(2)}) collective-permute-start(f32[35,8,128]{2,1,0:T(8,128)S(1)} %pad_maximum_fusion), channel_id=1, source_target_pairs={{32,0},{33,1},{34,2},{35,3},{36,4},{37,5},{38,6},{39,7},{40,8},{41... | collective-permute-start | bytes 430088 | tf_op jit(solution)/shard_map/ppermute | solution.py:27
  106.8 1.1 collective-permute-done.12.above_ref
  107.9 3.8 %collective-permute-done.13.below_ref = f32[35,8,128]{2,1,0:T(8,128)S(1)} collective-permute-done((f32[35,8,128]{2,1,0:T(8,128)S(1)}, f32[35,8,128]{2,1,0:T(8,128)S(1)}, u32[]{:S(2)}, u32[]{:S(2)}) %collective-permute-start.13) | collective-permute-done | bytes 143392 | tf_op jit(solution)/shard_map/ppermute | solution.py:27
  111.6 2.0 %coarse.1 = (f32[3,16,8,128]{3,2,1,0:T(8,128)}, f32[3,16,8,128]{3,2,1,0:T(8,128)}) custom-call(f32[10,40,128]{2,1,0:T(8,128)S(1)} %constant_dynamic-update-slice_fusion.mid_ref, f32[35,8,128]{2,1,0:T(8,128)S(1)} %collective-permute-done.12.above_ref, f32[35,8,128]{2,1,0:T(8,128)S(1)} %collective-permute-done.13.below_ref, ...), custom_call_target="tpu_custom_call" | custom-call | tf_op jit(solution)/shard_map/coarse/pallas_call | solution.py:585
  (29 shorter events, 0.3 us)
Async XLA Ops:
  0.6 12.0 %copy-start = (f32[1,3,16,8,128]{4,3,2,1,0:T(8,128)S(1)}, f32[1,3,16,8,128]{4,3,2,1,0:T(8,128)}, u32[]{:S(2)}) copy-start(f32[1,3,16,8,128]{4,3,2,1,0:T(8,128)} %param.7) | copy-start | bytes 589828
  1.7 13.8 %collective-permute-start.7 = (f32[3,128]{1,0:T(4,128)S(1)}, f32[3,128]{1,0:T(4,128)S(1)}, u32[]{:S(2)}, u32[]{:S(2)}) collective-permute-start(f32[3,128]{1,0:T(4,128)S(1)} %get-tuple-element.30), channel_id=1, source_target_pairs={{33,256},{34,257},{35,258},{36,259},{37,260},{38,261},{39,262},{40... | collective-permute-start | bytes 4616 | tf_op jit(solution)/shard_map/ppermute | solution.py:27
  4.8 10.7 %collective-permute-start.6 = (f32[3,8,128]{2,1,0:T(8,128)S(1)}, f32[3,8,128]{2,1,0:T(8,128)S(1)}, u32[]{:S(2)}, u32[]{:S(2)}) collective-permute-start(f32[3,8,128]{2,1,0:T(8,128)S(1)} %get-tuple-element.29), channel_id=1, source_target_pairs={{32,256},{33,257},{34,258},{35,259},{36,260},{37,261},{38,262},{39... | collective-permute-start | bytes 36872 | tf_op jit(solution)/shard_map/ppermute | solution.py:27
  7.5 8.1 %collective-permute-start.5 = (f32[3,16,128]{2,1,0:T(8,128)S(1)}, f32[3,16,128]{2,1,0:T(8,128)S(1)}, u32[]{:S(2)}, u32[]{:S(2)}) collective-permute-start(f32[3,16,128]{2,1,0:T(8,128)S(1)} %get-tuple-element.28), channel_id=1, source_target_pairs={{1,256},{2,257},{3,258},{4,259},{5,260},{6,261},{7,262},{8,263},{9... | collective-permute-start | bytes 73736 | tf_op jit(solution)/shard_map/ppermute | solution.py:27
  9.8 5.8 %collective-permute-start.4 = (f32[88,128]{1,0:T(8,128)S(1)}, f32[88,128]{1,0:T(8,128)S(1)}, u32[]{:S(2)}, u32[]{:S(2)}) collective-permute-start(f32[88,128]{1,0:T(8,128)S(1)} %get-tuple-element.27), channel_id=1, source_target_pairs={{0,256},{1,257},{2,258},{3,259},{4,260},{5,261},{6,262},{7,263},{8... | collective-permute-start | bytes 135176 | tf_op jit(solution)/shard_map/ppermute | solution.py:27
  12.6 0.9 copy-start.1
  13.6 0.8 copy-start.3
  14.8 0.7 copy-start.5
  16.4 21.8 %all-to-all-start = ((f32[32,1,1152]{2,1,0:T(1,128)}), f32[32,1,1152]{2,1,0:T(1,128)S(1)}, u32[]{:S(2)}, u32[]{:S(2)}) async-start(f32[32,1,1152]{2,1,0:T(1,128)} %bitcast.9), calls=%async_computation | async-start | bytes 294912 | tf_op jit(solution)/shard_map/all_to_all | solution.py:526
  39.5 20.5 %copy-start.2 = (f32[1,3,16,8,128]{4,3,2,1,0:T(8,128)S(1)}, f32[1,3,16,8,128]{4,3,2,1,0:T(8,128)}, u32[]{:S(2)}) copy-start(f32[1,3,16,8,128]{4,3,2,1,0:T(8,128)} %param.8) | copy-start | bytes 589828
  39.5 20.5 %copy-start.4 = (f32[1,16,8,128]{3,2,1,0:T(8,128)S(1)}, f32[1,16,8,128]{3,2,1,0:T(8,128)}, u32[]{:S(2)}) copy-start(f32[1,16,8,128]{3,2,1,0:T(8,128)} %param.9) | copy-start | bytes 196612
  39.5 35.2 %all-to-all-start.1 = ((f32[8,96,128]{2,1,0:T(8,128)}), f32[8,96,128]{2,1,0:T(8,128)S(1)}, u32[]{:S(2)}, u32[]{:S(2)}) async-start(f32[8,96,128]{2,1,0:T(8,128)} %bitcast.11), calls=%async_computation.1 | async-start | bytes 786432 | tf_op jit(solution)/shard_map/all_to_all | solution.py:547
  47.2 12.8 %collective-permute-start.1 = (f32[32,8,128]{2,1,0:T(8,128)S(1)}, f32[32,8,128]{2,1,0:T(8,128)S(1)}, u32[]{:S(2)}, u32[]{:S(2)}) collective-permute-start(f32[32,8,128]{2,1,0:T(8,128)S(1)} %get-tuple-element.24), channel_id=1, source_target_pairs={{32,0},{33,1},{34,2},{35,3},{36,4},{37,5},{38,6},{39,7},{40,8},{41... | collective-permute-start | bytes 393224 | tf_op jit(solution)/shard_map/ppermute | solution.py:27
  49.7 10.3 %collective-permute-start = (f32[32,8,128]{2,1,0:T(8,128)S(1)}, f32[32,8,128]{2,1,0:T(8,128)S(1)}, u32[]{:S(2)}, u32[]{:S(2)}) collective-permute-start(f32[32,8,128]{2,1,0:T(8,128)S(1)} %get-tuple-element.23), channel_id=1, source_target_pairs={{0,32},{1,33},{2,34},{3,35},{4,36},{5,37},{6,38},{7,39},{8,40},{9,... | collective-permute-start | bytes 393224 | tf_op jit(solution)/shard_map/ppermute | solution.py:27
  60.1 13.4 %collective-permute-start.2 = (f32[92,8,128]{2,1,0:T(8,128)S(1)}, f32[92,8,128]{2,1,0:T(8,128)S(1)}, u32[]{:S(2)}, u32[]{:S(2)}) collective-permute-start(f32[92,8,128]{2,1,0:T(8,128)S(1)} %get-tuple-element.25), channel_id=1, source_target_pairs={{0,1},{1,2},{2,3},{3,4},{4,5},{5,6},{6,7},{7,8},{8,9},{9,10},{10,1... | collective-permute-start | bytes 1130504 | tf_op jit(solution)/shard_map/ppermute | solution.py:27
  62.7 12.0 %collective-permute-start.3 = (f32[92,8,128]{2,1,0:T(8,128)S(1)}, f32[92,8,128]{2,1,0:T(8,128)S(1)}, u32[]{:S(2)}, u32[]{:S(2)}) collective-permute-start(f32[92,8,128]{2,1,0:T(8,128)S(1)} %get-tuple-element.26), channel_id=1, source_target_pairs={{1,0},{2,1},{3,2},{4,3},{5,4},{6,5},{7,6},{8,7},{9,8},{10,9},{11,1... | collective-permute-start | bytes 1130504 | tf_op jit(solution)/shard_map/ppermute | solution.py:27
  78.8 15.8 %collective-permute-start.8 = (f32[10,8,128]{2,1,0:T(8,128)S(1)}, f32[10,8,128]{2,1,0:T(8,128)S(1)}, u32[]{:S(2)}, u32[]{:S(2)}) collective-permute-start(f32[10,8,128]{2,1,0:T(8,128)S(1)} %get-tuple-element.31), channel_id=1, source_target_pairs={{0,2},{1,3},{2,4},{3,5},{4,6},{5,7},{6,8},{7,9},{8,10},{9,11},{10,... | collective-permute-start | bytes 122888 | tf_op jit(solution)/shard_map/ppermute | solution.py:27
  82.7 18.1 %collective-permute-start.11 = (f32[10,8,128]{2,1,0:T(8,128)S(1)}, f32[10,8,128]{2,1,0:T(8,128)S(1)}, u32[]{:S(2)}, u32[]{:S(2)}) collective-permute-start(f32[10,8,128]{2,1,0:T(8,128)S(1)} %get-tuple-element.31), channel_id=1, source_target_pairs={{2,0},{3,1},{4,2},{5,3},{6,4},{7,5},{8,6},{9,7},{10,8},{11,9},{12,... | collective-permute-start | bytes 122888 | tf_op jit(solution)/shard_map/ppermute | solution.py:27
  87.1 13.6 %collective-permute-start.10 = (f32[10,8,128]{2,1,0:T(8,128)S(1)}, f32[10,8,128]{2,1,0:T(8,128)S(1)}, u32[]{:S(2)}, u32[]{:S(2)}) collective-permute-start(f32[10,8,128]{2,1,0:T(8,128)S(1)} %get-tuple-element.31), channel_id=1, source_target_pairs={{1,0},{2,1},{3,2},{4,3},{5,4},{6,5},{7,6},{8,7},{9,8},{10,9},{11,1... | collective-permute-start | bytes 122888 | tf_op jit(solution)/shard_map/ppermute | solution.py:27
  92.7 8.0 %collective-permute-start.9 = (f32[10,8,128]{2,1,0:T(8,128)S(1)}, f32[10,8,128]{2,1,0:T(8,128)S(1)}, u32[]{:S(2)}, u32[]{:S(2)}) collective-permute-start(f32[10,8,128]{2,1,0:T(8,128)S(1)} %get-tuple-element.31), channel_id=1, source_target_pairs={{0,1},{1,2},{2,3},{3,4},{4,5},{5,6},{6,7},{7,8},{8,9},{9,10},{10,1... | collective-permute-start | bytes 122888 | tf_op jit(solution)/shard_map/ppermute | solution.py:27
  100.9 7.0 %collective-permute-start.12 = (f32[35,8,128]{2,1,0:T(8,128)S(1)}, f32[35,8,128]{2,1,0:T(8,128)S(1)}, u32[]{:S(2)}, u32[]{:S(2)}) collective-permute-start(f32[35,8,128]{2,1,0:T(8,128)S(1)} %constant_dynamic-update-slice_fusion.8), channel_id=1, source_target_pairs={{0,32},{1,33},{2,34},{3,35},{4,36},{5,37},{6,38},{7,39},{8,40},{9,... | collective-permute-start | bytes 430088 | tf_op jit(solution)/shard_map/ppermute | solution.py:27
  103.4 8.2 %collective-permute-start.13 = (f32[35,8,128]{2,1,0:T(8,128)S(1)}, f32[35,8,128]{2,1,0:T(8,128)S(1)}, u32[]{:S(2)}, u32[]{:S(2)}) collective-permute-start(f32[35,8,128]{2,1,0:T(8,128)S(1)} %pad_maximum_fusion), channel_id=1, source_target_pairs={{32,0},{33,1},{34,2},{35,3},{36,4},{37,5},{38,6},{39,7},{40,8},{41... | collective-permute-start | bytes 430088 | tf_op jit(solution)/shard_map/ppermute | solution.py:27

commit v9 on v8

--- a/solution.py
+++ b/solution.py
@@ -11,6 +11,7 @@
 COARSE = 8
 PAD = 6
 CELLS = 32
+OUTER = (-3, -4, 18, 19)
 VMEM = pl.BlockSpec(memory_space=pltpu.VMEM)
 SMEM = pl.BlockSpec(memory_space=pltpu.SMEM)
 
@@ -48,16 +49,22 @@
 
 
 def first_kernel(
-    rows_hbm, cols_hbm, weights_hbm, v_hbm, edge_ref, below_ref, corner_ref, blend_ref,
-    rows_ref, cols_ref, weights_ref, v_ref, done,
+    rows_hbm, cols_hbm, weights_hbm, v_hbm, slot_hbm,
+    edge_ref, below_ref, corner_ref, blend_ref, source_ref, ghost_ref,
+    rows_ref, cols_ref, weights_ref, v_ref, slot_ref, done,
 ):
     sub = rows_of((8, 128))
     pairs = (v_hbm, v_ref), (rows_hbm, rows_ref), (cols_hbm, cols_ref), (weights_hbm, weights_ref)
+    pairs = pairs + ((slot_hbm, slot_ref),)
     copies = [pltpu.make_async_copy(*pair, done.at[n]) for n, pair in enumerate(pairs)]
     for copy in copies:
         copy.start()
     for copy in copies:
         copy.wait()
+    slots = slot_ref[...]
+    third = (slots * 21846) >> 16
+    source_ref[...] = (third & 31) * 9 + (slots - 3 * third) * 3
+    ghost_ref[...] = (third >> 5) * (3 * CELLS)
     blend(rows_ref, cols_ref, weights_ref, v_ref, blend_ref)
     for comp in range(3):
         corner_ref[comp : comp + 1] = v_ref[comp, 0, 0:1]
@@ -75,7 +82,10 @@
     return 5 * min(field, 3) + away - 1
 
 
-def cut_kernel(v_ref, f_ref, mu_ref, up_ref, down_ref):
+def cut_kernel(
+    place_ref, v_ref, f_ref, mu_ref, up_ref, down_ref, cells_ref
+):
+    cells_ref[...] = wanted_cells(place_ref)
     for field in range(7):
         for away in range(1, 5 if 3 <= field < 6 else 6):
             for ref, r in ((up_ref, away - 1), (down_ref, 16 - away)):
@@ -129,7 +139,7 @@
     edge = (lon == 0) | (lon == last_lon)
 
     def copy(dest, position):
-        base = source_ref[cells_ref[dest * CELLS + position]]
+        base = source_ref[0, cells_ref[dest, position]]
         for comp in range(3):
             out_ref[dest * 3 * CELLS + position * 3 + comp] = row_ref[base + comp]
 
@@ -150,13 +160,16 @@
 
 
 def side_tile(ref, field, r, col, sub):
-    value = ref[12 * field + (r + 4) // 2]
+    if r in OUTER:
+        by = 2 * OUTER.index(r)
+        return roll(ref[70 + field], by if col == 3 else -by, 0)
+    value = ref[10 * field + (r + 2) // 2]
     if r % 2:
         value = roll(value, 4, 0)
     extra = {0: 0, 1: 1, 2: 2, 6: 3}.get(field)
     if extra is None or not 0 <= r < 16:
         return value
-    fifth = roll(ref[84 + 2 * extra + r // 8], col - r % 8, 0)
+    fifth = roll(ref[77 + 2 * extra + r // 8], col - r % 8, 0)
     return jnp.where(sub == col, fifth, value)
 
 
@@ -173,10 +186,17 @@
         return v_ref[field, r] if field < 3 else f_ref[field - 3, r]
 
     for field in range(7):
-        for t in range(12):
-            even, odd = row(field, 2 * t - 4), roll(row(field, 2 * t - 3), 4, 0)
-            right_ref[12 * field + t] = jnp.where(sub < 4, odd, even)
-            left_ref[12 * field + t] = jnp.where(sub < 4, even, odd)
+        for t in range(10):
+            even, odd = row(field, 2 * t - 2), roll(row(field, 2 * t - 1), 4, 0)
+            right_ref[10 * field + t] = jnp.where(sub < 4, odd, even)
+            left_ref[10 * field + t] = jnp.where(sub < 4, even, odd)
+        high = low = row(field, OUTER[0])
+        for k in range(1, 4):
+            value = row(field, OUTER[k])
+            high = jnp.where((sub >> 1) == 3 - k, roll(value, -2 * k, 0), high)
+            low = jnp.where((sub >> 1) == k, roll(value, 2 * k, 0), low)
+        right_ref[70 + field] = high
+        left_ref[70 + field] = low
     for n, field in enumerate((0, 1, 2, 6)):
         for j in range(2):
             third = fourth = row(field, 8 * j)
@@ -184,8 +204,8 @@
                 value = row(field, 8 * j + r)
                 third = jnp.where(sub == r, roll(value, r - 3, 0), third)
                 fourth = jnp.where(sub == r, roll(value, r - 4, 0), fourth)
-            right_ref[84 + 2 * n + j] = third
-            left_ref[84 + 2 * n + j] = fourth
+            right_ref[77 + 2 * n + j] = third
+            left_ref[77 + 2 * n + j] = fourth
 
 
 def prepare(
@@ -309,13 +329,13 @@
             packed_at = jnp.where((lat == 0) & (along < 4), along, along + 20)
             position = jnp.clip(jnp.where(edge, packed_at, col + 4), 0, CELLS - 1)
             cell = start + jnp.clip(lon * 8 + col, 0, all_cols - 1)
-            base = ghost_ref[cell] + 3 * position
+            base = ghost_ref[0, cell] + 3 * position
             for comp in range(3):
                 A[comp, i, 8 + col : 9 + col] = slot_ref[base + comp]
 
     def fill_side(col, start):
         for r in range(-4, 20):
-            base = ghost_ref[start + jnp.clip(lat * 16 + r, 0, all_rows - 1)] + 3 * (r + 4)
+            base = ghost_ref[0, start + jnp.clip(lat * 16 + r, 0, all_rows - 1)] + 3 * (r + 4)
             for comp in range(3):
                 A[comp, r + PAD, 8 + col : 9 + col] = slot_ref[base + comp]
 
@@ -464,17 +484,19 @@
     leave.wait()
 
 
-def wanted_cells(lats, lons, lon):
-    dest = jnp.arange(lats, dtype=jnp.int32)[:, None]
-    position = jnp.arange(CELLS, dtype=jnp.int32)[None, :]
-    rows, cols = lats * 16, lons * 8
-    edge = (lon == 0) | (lon == lons - 1)
+def wanted_cells(place_ref):
+    lon, last_lat, last_lon = place_ref[1], place_ref[2], place_ref[3]
+    dest = lax.broadcasted_iota(jnp.int32, (8, CELLS), 0)
+    position = lax.broadcasted_iota(jnp.int32, (8, CELLS), 1)
+    rows, cols = (last_lat + 1) * 16, (last_lon + 1) * 8
+    first = jnp.where(lon == 0, 1, 0)
+    edge = jnp.where((lon == 0) | (lon == last_lon), 1, 0)
     side_row = dest * 16 + position - 4
-    on_side = edge & (position < 24) & (side_row >= 0) & (side_row < rows)
-    side = 2 * cols + jnp.where(lon == 0, 0, rows) + jnp.clip(side_row, 0, rows - 1)
+    on_side = (edge > 0) & (position < 24) & (side_row >= 0) & (side_row < rows)
+    side = 2 * cols + (1 - first) * rows + jnp.clip(side_row, 0, rows - 1)
     along = jnp.where((dest == 0) & (position < 4), position, position - 20)
-    corner_col = jnp.where(lon == 0, along, lon * 8 + along - 4)
-    col = jnp.where(edge, corner_col, lon * 8 + position - 4)
+    corner_col = along + (1 - first) * (lon * 8 - 4)
+    col = edge * corner_col + (1 - edge) * (lon * 8 + position - 4)
     row_cell = jnp.where(dest == 0, 0, cols) + jnp.clip(col, 0, cols - 1)
     return jnp.where(on_side, side, row_cell)
 
@@ -496,24 +518,26 @@
 
     weights = jnp.transpose(corner_weights, (0, 3, 1, 2))[0]
     shapes = ((3, 16, 128), (3, 8, 128), (3, 128), (88, 128))
-    edge, first_row, first_cell, blended = pl.pallas_call(
+    edge, first_row, first_cell, blended, source_rows, ghost_rows = pl.pallas_call(
         first_kernel,
-        out_shape=[jax.ShapeDtypeStruct(shape, f32) for shape in shapes],
-        in_specs=[pl.BlockSpec(memory_space=pltpu.HBM)] * 4,
-        out_specs=[VMEM] * 4,
+        out_shape=[jax.ShapeDtypeStruct(shape, f32) for shape in shapes]
+        + [jax.ShapeDtypeStruct(ghost_slots.shape, jnp.int32)] * 2,
+        in_specs=[pl.BlockSpec(memory_space=pltpu.HBM)] * 5,
+        out_specs=[VMEM] * 6,
         scratch_shapes=[
             pltpu.SMEM((1, 3), jnp.int32),
             pltpu.SMEM((1, 3), jnp.int32),
             pltpu.SMEM((3, 1, 4), f32),
             pltpu.VMEM(v.shape, f32),
-            pltpu.SemaphoreType.DMA((4,)),
+            pltpu.VMEM(ghost_slots.shape, jnp.int32),
+            pltpu.SemaphoreType.DMA((5,)),
         ],
         compiler_params=params,
         name="first",
     )(
         *(
             pltpu.with_memory_space_constraint(operand, pltpu.HBM)
-            for operand in (corner_rows[0], corner_cols[0], weights, v)
+            for operand in (corner_rows[0], corner_cols[0], weights, v, ghost_slots)
         )
     )
     first_cell = shifted(first_cell, -1, -1, 1)
@@ -524,15 +548,18 @@
         blended, edge, first_row, first_cell
     )
     around = lax.all_to_all(values.reshape(lons, 1, 1152), "lon", 0, 0, tiled=True)
-    to_above, to_below = kernel(cut_kernel, ((32, 8, 128),) * 2, [VMEM] * 3)(v, f, mu)
-    slots, lat_at, lon_at, to_above = lax.optimization_barrier(
-        (ghost_slots, lax.axis_index("lat"), lax.axis_index("lon"), to_above)
+    place = jnp.stack(
+        [lax.axis_index("lat"), lax.axis_index("lon"), jnp.int32(lats - 1), jnp.int32(lons - 1)]
     )
-    slots = slots[0]
-    place = jnp.stack([lat_at, lon_at, jnp.int32(lats - 1), jnp.int32(lons - 1)])
-    source_rows = ((slots // 3) % lons) * 9 + (slots % 3) * 3
-    ghost_rows = (slots // (3 * lons)) * (3 * CELLS)
-    cells = wanted_cells(lats, lons, lon_at).reshape(-1)
+    to_above, to_below, cells = pl.pallas_call(
+        cut_kernel,
+        out_shape=[jax.ShapeDtypeStruct((32, 8, 128), f32)] * 2
+        + [jax.ShapeDtypeStruct((lats, CELLS), jnp.int32)],
+        in_specs=[SMEM] + [VMEM] * 3,
+        out_specs=[VMEM] * 3,
+        compiler_params=params,
+        name="cut",
+    )(place, v, f, mu)
     below = shifted(to_above, -1, 0)
     above = shifted(to_below, 1, 0)
 
@@ -546,7 +573,7 @@
     )(place, cells, source_rows, around.reshape(lons * 9, 1, 128))
     everything = lax.all_to_all(chosen.reshape(lats, 3 * CELLS, 128), "lat", 0, 0, tiled=True)
     everything = everything.reshape(lats * 3 * CELLS, 1, 128)
-    to_right, to_left = kernel(pack_kernel, ((92, 8, 128),) * 2, [VMEM] * 5)(v, f, mu, above, below)
+    to_right, to_left = kernel(pack_kernel, ((85, 8, 128),) * 2, [VMEM] * 5)(v, f, mu, above, below)
     left = shifted(to_right, 0, 1)
     right = shifted(to_left, 0, -1)
 

time: 114 us -> 116 us (1.018)
  waiting for transfers between devices: 33.3 us -> 38.5 us
  local copies, waits for them, and re-layouts: 2.94 us -> 0.09 us
    ppermute x14, waiting for transfers between devices: 23.3 us -> 28.6 us  [shifted(): return lax.ppermute(value, AXES, pairs)]
    unnamed x22 -> x16, local copies, waits for them, and re-layouts: 2.43 us -> 0.06 us
    all_to_all x1, starting transfers between devices: 11.7 us -> 13.5 us  [per_device(): lax.all_to_all(values.reshape(lons, 1, 1152), 'lon', 0, 0, tiled=True)]
    all_to_all x1, starting transfers between devices: 7.68 us -> 6.22 us  [per_device(): lax.all_to_all(chosen.reshape(lats, 3 * CELLS, 128), 'lat', 0, 0, tiled=T...]
  transfers between devices with their start and end apart: 16 -> 16, of which waited for: 7 -> 9; matrix products, arithmetic and copies ran while one was open for 1% -> 0% of each run, Pallas kernels for 0% -> 1%
where the time goes in v9:
time: 116 us
  starting transfers between devices  66.3 us (57%)
  waiting for transfers between devices  38.5 us (33%)
  Pallas kernels  9.98 us (9%)
    ppermute x14, starting transfers between devices, shifted(): return lax.ppermute(value, AXES, pairs)  46.5 us
    ppermute x14, waiting for transfers between devices, shifted(): return lax.ppermute(value, AXES, pairs)  28.6 us
    all_to_all x1, starting transfers between devices, per_device(): lax.all_to_all(values.reshape(lons, 1, 1152), 'lon', 0, 0, tiled=True)  13.5 us
    all_to_all x1, waiting for transfers between devices, per_device(): lax.all_to_all(values.reshape(lons, 1, 1152), 'lon', 0, 0, tiled=True)  9.91 us
    all_to_all x1, starting transfers between devices, per_device(): lax.all_to_all(chosen.reshape(lats, 3 * CELLS, 128), 'lat', 0, 0, tiled=T...  6.22 us
    pallas_call x1, Pallas kernels, per_device(): pl.pallas_call(smooth_kernel, out_shape=(block, block, jax.ShapeDtypeStru...  4.12 us
  transfers between devices with their start and end apart: 16, of which 9 were waited for; matrix products, arithmetic and copies ran while one was open for 0% of the time, Pallas kernels for 1%

profile of v9, /device:TPU:88, one launch (start us, length us, event | category | flops | bytes accessed | tf_op | source)
XLA Modules:
  0.0 115.9 jit_solution(2143940448001356765)
XLA Ops:
  0.6 1.0 first.1
  1.7 1.9 %collective-permute-start.4 = (f32[88,128]{1,0:T(8,128)S(1)}, f32[88,128]{1,0:T(8,128)S(1)}, u32[]{:S(2)}, u32[]{:S(2)}) collective-permute-start(f32[88,128]{1,0:T(8,128)S(1)} %get-tuple-element.25), channel_id=1, source_target_pairs={{0,256},{1,257},{2,258},{3,259},{4,260},{5,261},{6,262},{7,263},{8... | collective-permute-start | bytes 135176 | tf_op jit(solution)/shard_map/ppermute | solution.py:28
  3.6 3.9 %collective-permute-start.5 = (f32[3,16,128]{2,1,0:T(8,128)S(1)}, f32[3,16,128]{2,1,0:T(8,128)S(1)}, u32[]{:S(2)}, u32[]{:S(2)}) collective-permute-start(f32[3,16,128]{2,1,0:T(8,128)S(1)} %get-tuple-element.26), channel_id=1, source_target_pairs={{1,256},{2,257},{3,258},{4,259},{5,260},{6,261},{7,262},{8,263},{9... | collective-permute-start | bytes 73736 | tf_op jit(solution)/shard_map/ppermute | solution.py:28
  7.5 2.0 %collective-permute-start.6 = (f32[3,8,128]{2,1,0:T(8,128)S(1)}, f32[3,8,128]{2,1,0:T(8,128)S(1)}, u32[]{:S(2)}, u32[]{:S(2)}) collective-permute-start(f32[3,8,128]{2,1,0:T(8,128)S(1)} %get-tuple-element.27), channel_id=1, source_target_pairs={{32,256},{33,257},{34,258},{35,259},{36,260},{37,261},{38,262},{39... | collective-permute-start | bytes 36872 | tf_op jit(solution)/shard_map/ppermute | solution.py:28
  9.5 2.7 %collective-permute-start.7 = (f32[3,128]{1,0:T(4,128)S(1)}, f32[3,128]{1,0:T(4,128)S(1)}, u32[]{:S(2)}, u32[]{:S(2)}) collective-permute-start(f32[3,128]{1,0:T(4,128)S(1)} %get-tuple-element.28), channel_id=1, source_target_pairs={{33,256},{34,257},{35,258},{36,259},{37,260},{38,261},{39,262},{40... | collective-permute-start | bytes 4616 | tf_op jit(solution)/shard_map/ppermute | solution.py:28
  12.2 4.3 %collective-permute-done.7.corner_ref = f32[3,128]{1,0:T(4,128)S(1)} collective-permute-done((f32[3,128]{1,0:T(4,128)S(1)}, f32[3,128]{1,0:T(4,128)S(1)}, u32[]{:S(2)}, u32[]{:S(2)}) %collective-permute-start.7) | collective-permute-done | bytes 1568 | tf_op jit(solution)/shard_map/ppermute | solution.py:28
  16.5 0.0 collective-permute-done.6.below_ref
  16.5 0.0 collective-permute-done.5.edge_ref
  16.5 0.0 collective-permute-done.4.blend_ref
  16.5 0.0 copy-start.1
  16.5 0.8 shard_map.87
  17.3 0.0 copy-start
  17.3 0.0 copy-start.2
  17.3 13.5 %all-to-all-start = ((f32[32,1,1152]{2,1,0:T(1,128)}), f32[32,1,1152]{2,1,0:T(1,128)S(1)}, u32[]{:S(2)}, u32[]{:S(2)}) async-start(f32[32,1,1152]{2,1,0:T(1,128)} %bitcast.9), calls=%async_computation | async-start | bytes 294912 | tf_op jit(solution)/shard_map/all_to_all | solution.py:550
  30.8 0.1 pad_add_fusion.place_ref
  30.9 0.0 copy-done.1
  30.9 0.0 copy-done
  30.9 0.0 copy-done.2
  30.9 0.6 cut.1
  31.5 9.9 %all-to-all-done = f32[32,1,1152]{2,1,0:T(1,128)S(1)} async-done(((f32[32,1,1152]{2,1,0:T(1,128)}), f32[32,1,1152]{2,1,0:T(1,128)S(1)}, u32[]{:S(2)}, u32[]{:S(2)}) %all-to-all-start) | async-done | bytes 147488 | tf_op jit(solution)/shard_map/all_to_all | solution.py:550
  41.4 1.5 %pick.1 = f32[768,1,128]{2,1,0:T(1,128)} custom-call(s32[4]{0:T(128)S(1)} %pad_add_fusion.place_ref, s32[8,32]{1,0:T(8,128)S(1)} %get-tuple-element.23.cells_ref, s32[1,768]{1,0:T(1,128)S(1)} %get-tuple-element.24.source_ref, f32[288,1,128]{2,1,0:T(1,128)S(1)} %bitcast.55), custom_call_target="tpu_custom_call" | custom-call | tf_op jit(solution)/shard_map/pick/pallas_call | solution.py:566
  42.8 6.2 %all-to-all-start.1 = ((f32[8,96,128]{2,1,0:T(8,128)}), f32[8,96,128]{2,1,0:T(8,128)S(1)}, u32[]{:S(2)}, u32[]{:S(2)}) async-start(f32[8,96,128]{2,1,0:T(8,128)} %bitcast.11), calls=%async_computation.1 | async-start | bytes 786432 | tf_op jit(solution)/shard_map/all_to_all | solution.py:574
  49.1 4.6 %collective-permute-start = (f32[32,8,128]{2,1,0:T(8,128)S(1)}, f32[32,8,128]{2,1,0:T(8,128)S(1)}, u32[]{:S(2)}, u32[]{:S(2)}) collective-permute-start(f32[32,8,128]{2,1,0:T(8,128)S(1)} %get-tuple-element.19), channel_id=1, source_target_pairs={{0,32},{1,33},{2,34},{3,35},{4,36},{5,37},{6,38},{7,39},{8,40},{9,... | collective-permute-start | bytes 393224 | tf_op jit(solution)/shard_map/ppermute | solution.py:28
  53.6 1.9 %collective-permute-start.1 = (f32[32,8,128]{2,1,0:T(8,128)S(1)}, f32[32,8,128]{2,1,0:T(8,128)S(1)}, u32[]{:S(2)}, u32[]{:S(2)}) collective-permute-start(f32[32,8,128]{2,1,0:T(8,128)S(1)} %get-tuple-element.20), channel_id=1, source_target_pairs={{32,0},{33,1},{34,2},{35,3},{36,4},{37,5},{38,6},{39,7},{40,8},{41... | collective-permute-start | bytes 393224 | tf_op jit(solution)/shard_map/ppermute | solution.py:28
  55.6 4.2 %collective-permute-done.above_ref = f32[32,8,128]{2,1,0:T(8,128)S(1)} collective-permute-done((f32[32,8,128]{2,1,0:T(8,128)S(1)}, f32[32,8,128]{2,1,0:T(8,128)S(1)}, u32[]{:S(2)}, u32[]{:S(2)}) %collective-permute-start) | collective-permute-done | bytes 131104 | tf_op jit(solution)/shard_map/ppermute | solution.py:28
  59.8 2.4 %collective-permute-done.1.below_ref = f32[32,8,128]{2,1,0:T(8,128)S(1)} collective-permute-done((f32[32,8,128]{2,1,0:T(8,128)S(1)}, f32[32,8,128]{2,1,0:T(8,128)S(1)}, u32[]{:S(2)}, u32[]{:S(2)}) %collective-permute-start.1) | collective-permute-done | bytes 131104 | tf_op jit(solution)/shard_map/ppermute | solution.py:28
  62.2 0.1 shard_map.86
  62.3 2.7 %collective-permute-start.2 = (f32[85,8,128]{2,1,0:T(8,128)S(1)}, f32[85,8,128]{2,1,0:T(8,128)S(1)}, u32[]{:S(2)}, u32[]{:S(2)}) collective-permute-start(f32[85,8,128]{2,1,0:T(8,128)S(1)} %get-tuple-element.21), channel_id=1, source_target_pairs={{0,1},{1,2},{2,3},{3,4},{4,5},{5,6},{6,7},{7,8},{8,9},{9,10},{10,1... | collective-permute-start | bytes 1044488 | tf_op jit(solution)/shard_map/ppermute | solution.py:28
  65.0 5.2 %collective-permute-start.3 = (f32[85,8,128]{2,1,0:T(8,128)S(1)}, f32[85,8,128]{2,1,0:T(8,128)S(1)}, u32[]{:S(2)}, u32[]{:S(2)}) collective-permute-start(f32[85,8,128]{2,1,0:T(8,128)S(1)} %get-tuple-element.22), channel_id=1, source_target_pairs={{1,0},{2,1},{3,2},{4,3},{5,4},{6,5},{7,6},{8,7},{9,8},{10,9},{11,1... | collective-permute-start | bytes 1044488 | tf_op jit(solution)/shard_map/ppermute | solution.py:28
  70.3 5.0 %collective-permute-done.2.left_ref = f32[85,8,128]{2,1,0:T(8,128)S(1)} collective-permute-done((f32[85,8,128]{2,1,0:T(8,128)S(1)}, f32[85,8,128]{2,1,0:T(8,128)S(1)}, u32[]{:S(2)}, u32[]{:S(2)}) %collective-permute-start.2) | collective-permute-done | bytes 348192 | tf_op jit(solution)/shard_map/ppermute | solution.py:28
  75.3 1.2 %collective-permute-done.3.right_ref = f32[85,8,128]{2,1,0:T(8,128)S(1)} collective-permute-done((f32[85,8,128]{2,1,0:T(8,128)S(1)}, f32[85,8,128]{2,1,0:T(8,128)S(1)}, u32[]{:S(2)}, u32[]{:S(2)}) %collective-permute-start.3) | collective-permute-done | bytes 348192 | tf_op jit(solution)/shard_map/ppermute | solution.py:28
  76.4 0.0 all-to-all-done.1
  76.4 4.1 %smooth.1 = (f32[3,16,8,128]{3,2,1,0:T(8,128)S(1)}, f32[3,16,8,128]{3,2,1,0:T(8,128)S(1)}, f32[10,8,128]{2,1,0:T(8,128)S(1)}) custom-call(s32[4]{0:T(128)S(1)} %pad_add_fusion.place_ref, s32[1,768]{1,0:T(1,128)S(1)} %get-tuple-element.18.ghost_ref, f32[3,16,8,128]{3,2,1,0:T(8,128)S(1)} %bitcast.50, f32[3,16,8,128]{3,2,1,0:T(8,128)S(1)} %bitcast.53, ...), custom_call_target="tpu_custom_call" | custom-call | tf_op jit(solution)/shard_map/smooth/pallas_call | solution.py:582
  80.6 3.8 %collective-permute-start.8 = (f32[10,8,128]{2,1,0:T(8,128)S(1)}, f32[10,8,128]{2,1,0:T(8,128)S(1)}, u32[]{:S(2)}, u32[]{:S(2)}) collective-permute-start(f32[10,8,128]{2,1,0:T(8,128)S(1)} %get-tuple-element.29), channel_id=1, source_target_pairs={{0,2},{1,3},{2,4},{3,5},{4,6},{5,7},{6,8},{7,9},{8,10},{9,11},{10,... | collective-permute-start | bytes 122888 | tf_op jit(solution)/shard_map/ppermute | solution.py:28
  84.4 4.4 %collective-permute-start.11 = (f32[10,8,128]{2,1,0:T(8,128)S(1)}, f32[10,8,128]{2,1,0:T(8,128)S(1)}, u32[]{:S(2)}, u32[]{:S(2)}) collective-permute-start(f32[10,8,128]{2,1,0:T(8,128)S(1)} %get-tuple-element.29), channel_id=1, source_target_pairs={{2,0},{3,1},{4,2},{5,3},{6,4},{7,5},{8,6},{9,7},{10,8},{11,9},{12,... | collective-permute-start | bytes 122888 | tf_op jit(solution)/shard_map/ppermute | solution.py:28
  88.8 5.6 %collective-permute-start.10 = (f32[10,8,128]{2,1,0:T(8,128)S(1)}, f32[10,8,128]{2,1,0:T(8,128)S(1)}, u32[]{:S(2)}, u32[]{:S(2)}) collective-permute-start(f32[10,8,128]{2,1,0:T(8,128)S(1)} %get-tuple-element.29), channel_id=1, source_target_pairs={{1,0},{2,1},{3,2},{4,3},{5,4},{6,5},{7,6},{8,7},{9,8},{10,9},{11,1... | collective-permute-start | bytes 122888 | tf_op jit(solution)/shard_map/ppermute | solution.py:28
  94.4 1.9 %collective-permute-start.9 = (f32[10,8,128]{2,1,0:T(8,128)S(1)}, f32[10,8,128]{2,1,0:T(8,128)S(1)}, u32[]{:S(2)}, u32[]{:S(2)}) collective-permute-start(f32[10,8,128]{2,1,0:T(8,128)S(1)} %get-tuple-element.29), channel_id=1, source_target_pairs={{0,1},{1,2},{2,3},{3,4},{4,5},{5,6},{6,7},{7,8},{8,9},{9,10},{10,1... | collective-permute-start | bytes 122888 | tf_op jit(solution)/shard_map/ppermute | solution.py:28
  96.4 0.0 collective-permute-done.8
  96.4 6.1 %collective-permute-done.9 = f32[10,8,128]{2,1,0:T(8,128)S(1)} collective-permute-done((f32[10,8,128]{2,1,0:T(8,128)S(1)}, f32[10,8,128]{2,1,0:T(8,128)S(1)}, u32[]{:S(2)}, u32[]{:S(2)}) %collective-permute-start.9) | collective-permute-done | bytes 40992 | tf_op jit(solution)/shard_map/ppermute | solution.py:28
  102.5 0.0 collective-permute-done.10
  102.5 0.0 collective-permute-done.11
  102.6 3.0 %collective-permute-start.12 = (f32[35,8,128]{2,1,0:T(8,128)S(1)}, f32[35,8,128]{2,1,0:T(8,128)S(1)}, u32[]{:S(2)}, u32[]{:S(2)}) collective-permute-start(f32[35,8,128]{2,1,0:T(8,128)S(1)} %constant_dynamic-update-slice_fusion.8), channel_id=1, source_target_pairs={{0,32},{1,33},{2,34},{3,35},{4,36},{5,37},{6,38},{7,39},{8,40},{9,... | collective-permute-start | bytes 430088 | tf_op jit(solution)/shard_map/ppermute | solution.py:28
  105.7 2.8 %collective-permute-start.13 = (f32[35,8,128]{2,1,0:T(8,128)S(1)}, f32[35,8,128]{2,1,0:T(8,128)S(1)}, u32[]{:S(2)}, u32[]{:S(2)}) collective-permute-start(f32[35,8,128]{2,1,0:T(8,128)S(1)} %pad_maximum_fusion), channel_id=1, source_target_pairs={{32,0},{33,1},{34,2},{35,3},{36,4},{37,5},{38,6},{39,7},{40,8},{41... | collective-permute-start | bytes 430088 | tf_op jit(solution)/shard_map/ppermute | solution.py:28
  108.5 1.1 collective-permute-done.12.above_ref
  109.6 4.3 %collective-permute-done.13.below_ref = f32[35,8,128]{2,1,0:T(8,128)S(1)} collective-permute-done((f32[35,8,128]{2,1,0:T(8,128)S(1)}, f32[35,8,128]{2,1,0:T(8,128)S(1)}, u32[]{:S(2)}, u32[]{:S(2)}) %collective-permute-start.13) | collective-permute-done | bytes 143392 | tf_op jit(solution)/shard_map/ppermute | solution.py:28
  113.9 2.0 %coarse.1 = (f32[3,16,8,128]{3,2,1,0:T(8,128)}, f32[3,16,8,128]{3,2,1,0:T(8,128)}) custom-call(f32[10,40,128]{2,1,0:T(8,128)S(1)} %constant_dynamic-update-slice_fusion.mid_ref, f32[35,8,128]{2,1,0:T(8,128)S(1)} %collective-permute-done.12.above_ref, f32[35,8,128]{2,1,0:T(8,128)S(1)} %collective-permute-done.13.below_ref, ...), custom_call_target="tpu_custom_call" | custom-call | tf_op jit(solution)/shard_map/coarse/pallas_call | solution.py:612
  (16 shorter events, 0.1 us)
Async XLA Ops:
  1.7 14.8 %collective-permute-start.4 = (f32[88,128]{1,0:T(8,128)S(1)}, f32[88,128]{1,0:T(8,128)S(1)}, u32[]{:S(2)}, u32[]{:S(2)}) collective-permute-start(f32[88,128]{1,0:T(8,128)S(1)} %get-tuple-element.25), channel_id=1, source_target_pairs={{0,256},{1,257},{2,258},{3,259},{4,260},{5,261},{6,262},{7,263},{8... | collective-permute-start | bytes 135176 | tf_op jit(solution)/shard_map/ppermute | solution.py:28
  3.6 12.9 %collective-permute-start.5 = (f32[3,16,128]{2,1,0:T(8,128)S(1)}, f32[3,16,128]{2,1,0:T(8,128)S(1)}, u32[]{:S(2)}, u32[]{:S(2)}) collective-permute-start(f32[3,16,128]{2,1,0:T(8,128)S(1)} %get-tuple-element.26), channel_id=1, source_target_pairs={{1,256},{2,257},{3,258},{4,259},{5,260},{6,261},{7,262},{8,263},{9... | collective-permute-start | bytes 73736 | tf_op jit(solution)/shard_map/ppermute | solution.py:28
  7.5 9.0 %collective-permute-start.6 = (f32[3,8,128]{2,1,0:T(8,128)S(1)}, f32[3,8,128]{2,1,0:T(8,128)S(1)}, u32[]{:S(2)}, u32[]{:S(2)}) collective-permute-start(f32[3,8,128]{2,1,0:T(8,128)S(1)} %get-tuple-element.27), channel_id=1, source_target_pairs={{32,256},{33,257},{34,258},{35,259},{36,260},{37,261},{38,262},{39... | collective-permute-start | bytes 36872 | tf_op jit(solution)/shard_map/ppermute | solution.py:28
  9.5 7.0 %collective-permute-start.7 = (f32[3,128]{1,0:T(4,128)S(1)}, f32[3,128]{1,0:T(4,128)S(1)}, u32[]{:S(2)}, u32[]{:S(2)}) collective-permute-start(f32[3,128]{1,0:T(4,128)S(1)} %get-tuple-element.28), channel_id=1, source_target_pairs={{33,256},{34,257},{35,258},{36,259},{37,260},{38,261},{39,262},{40... | collective-permute-start | bytes 4616 | tf_op jit(solution)/shard_map/ppermute | solution.py:28
  16.5 14.4 %copy-start.1 = (f32[1,3,16,8,128]{4,3,2,1,0:T(8,128)S(1)}, f32[1,3,16,8,128]{4,3,2,1,0:T(8,128)}, u32[]{:S(2)}) copy-start(f32[1,3,16,8,128]{4,3,2,1,0:T(8,128)} %param.8) | copy-start | bytes 589828
  17.3 13.6 %copy-start = (f32[1,3,16,8,128]{4,3,2,1,0:T(8,128)S(1)}, f32[1,3,16,8,128]{4,3,2,1,0:T(8,128)}, u32[]{:S(2)}) copy-start(f32[1,3,16,8,128]{4,3,2,1,0:T(8,128)} %param.7) | copy-start | bytes 589828
  17.3 13.6 %copy-start.2 = (f32[1,16,8,128]{3,2,1,0:T(8,128)S(1)}, f32[1,16,8,128]{3,2,1,0:T(8,128)}, u32[]{:S(2)}) copy-start(f32[1,16,8,128]{3,2,1,0:T(8,128)} %param.9) | copy-start | bytes 196612
  17.3 24.1 %all-to-all-start = ((f32[32,1,1152]{2,1,0:T(1,128)}), f32[32,1,1152]{2,1,0:T(1,128)S(1)}, u32[]{:S(2)}, u32[]{:S(2)}) async-start(f32[32,1,1152]{2,1,0:T(1,128)} %bitcast.9), calls=%async_computation | async-start | bytes 294912 | tf_op jit(solution)/shard_map/all_to_all | solution.py:550
  42.8 33.6 %all-to-all-start.1 = ((f32[8,96,128]{2,1,0:T(8,128)}), f32[8,96,128]{2,1,0:T(8,128)S(1)}, u32[]{:S(2)}, u32[]{:S(2)}) async-start(f32[8,96,128]{2,1,0:T(8,128)} %bitcast.11), calls=%async_computation.1 | async-start | bytes 786432 | tf_op jit(solution)/shard_map/all_to_all | solution.py:574
  49.1 10.8 %collective-permute-start = (f32[32,8,128]{2,1,0:T(8,128)S(1)}, f32[32,8,128]{2,1,0:T(8,128)S(1)}, u32[]{:S(2)}, u32[]{:S(2)}) collective-permute-start(f32[32,8,128]{2,1,0:T(8,128)S(1)} %get-tuple-element.19), channel_id=1, source_target_pairs={{0,32},{1,33},{2,34},{3,35},{4,36},{5,37},{6,38},{7,39},{8,40},{9,... | collective-permute-start | bytes 393224 | tf_op jit(solution)/shard_map/ppermute | solution.py:28
  53.6 8.6 %collective-permute-start.1 = (f32[32,8,128]{2,1,0:T(8,128)S(1)}, f32[32,8,128]{2,1,0:T(8,128)S(1)}, u32[]{:S(2)}, u32[]{:S(2)}) collective-permute-start(f32[32,8,128]{2,1,0:T(8,128)S(1)} %get-tuple-element.20), channel_id=1, source_target_pairs={{32,0},{33,1},{34,2},{35,3},{36,4},{37,5},{38,6},{39,7},{40,8},{41... | collective-permute-start | bytes 393224 | tf_op jit(solution)/shard_map/ppermute | solution.py:28
  62.3 13.0 %collective-permute-start.2 = (f32[85,8,128]{2,1,0:T(8,128)S(1)}, f32[85,8,128]{2,1,0:T(8,128)S(1)}, u32[]{:S(2)}, u32[]{:S(2)}) collective-permute-start(f32[85,8,128]{2,1,0:T(8,128)S(1)} %get-tuple-element.21), channel_id=1, source_target_pairs={{0,1},{1,2},{2,3},{3,4},{4,5},{5,6},{6,7},{7,8},{8,9},{9,10},{10,1... | collective-permute-start | bytes 1044488 | tf_op jit(solution)/shard_map/ppermute | solution.py:28
  65.0 11.4 %collective-permute-start.3 = (f32[85,8,128]{2,1,0:T(8,128)S(1)}, f32[85,8,128]{2,1,0:T(8,128)S(1)}, u32[]{:S(2)}, u32[]{:S(2)}) collective-permute-start(f32[85,8,128]{2,1,0:T(8,128)S(1)} %get-tuple-element.22), channel_id=1, source_target_pairs={{1,0},{2,1},{3,2},{4,3},{5,4},{6,5},{7,6},{8,7},{9,8},{10,9},{11,1... | collective-permute-start | bytes 1044488 | tf_op jit(solution)/shard_map/ppermute | solution.py:28
  80.6 15.8 %collective-permute-start.8 = (f32[10,8,128]{2,1,0:T(8,128)S(1)}, f32[10,8,128]{2,1,0:T(8,128)S(1)}, u32[]{:S(2)}, u32[]{:S(2)}) collective-permute-start(f32[10,8,128]{2,1,0:T(8,128)S(1)} %get-tuple-element.29), channel_id=1, source_target_pairs={{0,2},{1,3},{2,4},{3,5},{4,6},{5,7},{6,8},{7,9},{8,10},{9,11},{10,... | collective-permute-start | bytes 122888 | tf_op jit(solution)/shard_map/ppermute | solution.py:28
  84.4 18.1 %collective-permute-start.11 = (f32[10,8,128]{2,1,0:T(8,128)S(1)}, f32[10,8,128]{2,1,0:T(8,128)S(1)}, u32[]{:S(2)}, u32[]{:S(2)}) collective-permute-start(f32[10,8,128]{2,1,0:T(8,128)S(1)} %get-tuple-element.29), channel_id=1, source_target_pairs={{2,0},{3,1},{4,2},{5,3},{6,4},{7,5},{8,6},{9,7},{10,8},{11,9},{12,... | collective-permute-start | bytes 122888 | tf_op jit(solution)/shard_map/ppermute | solution.py:28
  88.8 13.6 %collective-permute-start.10 = (f32[10,8,128]{2,1,0:T(8,128)S(1)}, f32[10,8,128]{2,1,0:T(8,128)S(1)}, u32[]{:S(2)}, u32[]{:S(2)}) collective-permute-start(f32[10,8,128]{2,1,0:T(8,128)S(1)} %get-tuple-element.29), channel_id=1, source_target_pairs={{1,0},{2,1},{3,2},{4,3},{5,4},{6,5},{7,6},{8,7},{9,8},{10,9},{11,1... | collective-permute-start | bytes 122888 | tf_op jit(solution)/shard_map/ppermute | solution.py:28
  94.4 8.0 %collective-permute-start.9 = (f32[10,8,128]{2,1,0:T(8,128)S(1)}, f32[10,8,128]{2,1,0:T(8,128)S(1)}, u32[]{:S(2)}, u32[]{:S(2)}) collective-permute-start(f32[10,8,128]{2,1,0:T(8,128)S(1)} %get-tuple-element.29), channel_id=1, source_target_pairs={{0,1},{1,2},{2,3},{3,4},{4,5},{5,6},{6,7},{7,8},{8,9},{9,10},{10,1... | collective-permute-start | bytes 122888 | tf_op jit(solution)/shard_map/ppermute | solution.py:28
  102.6 7.0 %collective-permute-start.12 = (f32[35,8,128]{2,1,0:T(8,128)S(1)}, f32[35,8,128]{2,1,0:T(8,128)S(1)}, u32[]{:S(2)}, u32[]{:S(2)}) collective-permute-start(f32[35,8,128]{2,1,0:T(8,128)S(1)} %constant_dynamic-update-slice_fusion.8), channel_id=1, source_target_pairs={{0,32},{1,33},{2,34},{3,35},{4,36},{5,37},{6,38},{7,39},{8,40},{9,... | collective-permute-start | bytes 430088 | tf_op jit(solution)/shard_map/ppermute | solution.py:28
  105.7 8.2 %collective-permute-start.13 = (f32[35,8,128]{2,1,0:T(8,128)S(1)}, f32[35,8,128]{2,1,0:T(8,128)S(1)}, u32[]{:S(2)}, u32[]{:S(2)}) collective-permute-start(f32[35,8,128]{2,1,0:T(8,128)S(1)} %pad_maximum_fusion), channel_id=1, source_target_pairs={{32,0},{33,1},{34,2},{35,3},{36,4},{37,5},{38,6},{39,7},{40,8},{41... | collective-permute-start | bytes 430088 | tf_op jit(solution)/shard_map/ppermute | solution.py:28

commit v10 on v9

--- a/solution.py
+++ b/solution.py
@@ -82,10 +82,8 @@
     return 5 * min(field, 3) + away - 1
 
 
-def cut_kernel(
-    place_ref, v_ref, f_ref, mu_ref, up_ref, down_ref, cells_ref
-):
-    cells_ref[...] = wanted_cells(place_ref)
+def cut_kernel(v_ref, f_ref, mu_ref, up_ref, down_ref, cells_ref):
+    cells_ref[...] = wanted_cells()
     for field in range(7):
         for away in range(1, 5 if 3 <= field < 6 else 6):
             for ref, r in ((up_ref, away - 1), (down_ref, 16 - away)):
@@ -134,29 +132,35 @@
                 out_ref[9 * dest + at] = total
 
 
-def pick_kernel(place_ref, cells_ref, source_ref, row_ref, out_ref):
-    lon, last_lat, last_lon = place_ref[1], place_ref[2], place_ref[3]
+def pick_kernel(cells_ref, source_ref, row_ref, out_ref, held, done):
+    _, lon, last_lat, last_lon = place()
     edge = (lon == 0) | (lon == last_lon)
 
-    def copy(dest, position):
-        base = source_ref[0, cells_ref[dest, position]]
-        for comp in range(3):
-            out_ref[dest * 3 * CELLS + position * 3 + comp] = row_ref[base + comp]
+    def fill(dest, count):
+        for position in range(count):
+            base = source_ref[0, cells_ref[dest, position]]
+            for comp in range(3):
+                held[dest, position * 3 + comp] = row_ref[base + comp]
+        return leave(dest, count)
+
+    def leave(dest, count):
+        rows = pl.ds(0, 3 * count)
+        return pltpu.make_async_copy(held.at[dest, rows], out_ref.at[dest, rows], done.at[dest])
 
     @pl.when(edge)
     def _():
-        def step(dest, carry):
-            for position in range(CELLS):
-                copy(dest, position)
-            return carry
-
-        lax.fori_loop(0, last_lat + 1, step, 0)
+        for dest in range(last_lat + 1):
+            fill(dest, CELLS).start()
+        for dest in range(last_lat + 1):
+            leave(dest, CELLS).wait()
 
     @pl.when(~edge)
     def _():
-        for position in range(16):
-            copy(0, position)
-            copy(last_lat, position)
+        copies = [fill(dest, 16) for dest in (0, last_lat)]
+        for copy in copies:
+            copy.start()
+        for copy in copies:
+            copy.wait()
 
 
 def side_tile(ref, field, r, col, sub):
@@ -209,11 +213,10 @@
 
 
 def prepare(
-    place_ref, f_ref, mu_ref, left_ref, right_ref, above_ref, below_ref,
+    f_ref, mu_ref, left_ref, right_ref, above_ref, below_ref,
     F, C, DG, over_ref, visc_ref, MU,
 ):
-    lat, lon = place_ref[0], place_ref[1]
-    last_lat, last_lon = place_ref[2], place_ref[3]
+    lat, lon, last_lat, last_lon = place()
     wide = (24, 128)
     lane, row = lanes_of(wide), rows_of(wide)
     odd_lane, odd_row = (lane & 1) == 1, (row & 1) == 1
@@ -298,11 +301,10 @@
 
 
 def smooth_kernel(
-    place_ref, ghost_ref, v_ref, f_ref, mu_ref, left_ref, right_ref, above_ref, below_ref, slot_ref,
+    ghost_ref, v_ref, f_ref, mu_ref, left_ref, right_ref, above_ref, below_ref, slot_ref,
     res_ref, smooth_ref, message_ref, A, B, F, C, DG, over_ref, visc_ref, MU,
 ):
-    lat, lon = place_ref[0], place_ref[1]
-    last_lat, last_lon = place_ref[2], place_ref[3]
+    lat, lon, last_lat, last_lon = place()
     wide = (24, 128)
     lane, row = lanes_of(wide), rows_of(wide)
     sub = rows_of((8, 128))
@@ -340,7 +342,7 @@
                 A[comp, r + PAD, 8 + col : 9 + col] = slot_ref[base + comp]
 
     prepare(
-        place_ref, f_ref, mu_ref, left_ref, right_ref, above_ref, below_ref,
+        f_ref, mu_ref, left_ref, right_ref, above_ref, below_ref,
         F, C, DG, over_ref, visc_ref, MU,
     )
     pl.when(lat == 0)(lambda: fill_row(5, 0))
@@ -484,8 +486,13 @@
     leave.wait()
 
 
-def wanted_cells(place_ref):
-    lon, last_lat, last_lon = place_ref[1], place_ref[2], place_ref[3]
+def place():
+    last_lat, last_lon = lax.axis_size("lat") - 1, lax.axis_size("lon") - 1
+    return lax.axis_index("lat"), lax.axis_index("lon"), last_lat, last_lon
+
+
+def wanted_cells():
+    _, lon, last_lat, last_lon = place()
     dest = lax.broadcasted_iota(jnp.int32, (8, CELLS), 0)
     position = lax.broadcasted_iota(jnp.int32, (8, CELLS), 1)
     rows, cols = (last_lat + 1) * 16, (last_lon + 1) * 8
@@ -548,32 +555,35 @@
         blended, edge, first_row, first_cell
     )
     around = lax.all_to_all(values.reshape(lons, 1, 1152), "lon", 0, 0, tiled=True)
-    place = jnp.stack(
-        [lax.axis_index("lat"), lax.axis_index("lon"), jnp.int32(lats - 1), jnp.int32(lons - 1)]
-    )
     to_above, to_below, cells = pl.pallas_call(
         cut_kernel,
         out_shape=[jax.ShapeDtypeStruct((32, 8, 128), f32)] * 2
         + [jax.ShapeDtypeStruct((lats, CELLS), jnp.int32)],
-        in_specs=[SMEM] + [VMEM] * 3,
+        in_specs=[VMEM] * 3,
         out_specs=[VMEM] * 3,
         compiler_params=params,
         name="cut",
-    )(place, v, f, mu)
+    )(v, f, mu)
     below = shifted(to_above, -1, 0)
     above = shifted(to_below, 1, 0)
 
     chosen = pl.pallas_call(
         pick_kernel,
-        out_shape=jax.ShapeDtypeStruct((lats * 3 * CELLS, 1, 128), f32),
-        in_specs=[SMEM, SMEM, SMEM, VMEM],
-        out_specs=VMEM,
+        out_shape=jax.ShapeDtypeStruct((lats, 3 * CELLS, 1, 128), f32),
+        in_specs=[SMEM, SMEM, VMEM],
+        out_specs=pl.BlockSpec(memory_space=pltpu.HBM),
+        scratch_shapes=[
+            pltpu.VMEM((lats, 3 * CELLS, 1, 128), f32),
+            pltpu.SemaphoreType.DMA((lats,)),
+        ],
         compiler_params=params,
         name="pick",
-    )(place, cells, source_rows, around.reshape(lons * 9, 1, 128))
+    )(cells, source_rows, around.reshape(lons * 9, 1, 128))
     everything = lax.all_to_all(chosen.reshape(lats, 3 * CELLS, 128), "lat", 0, 0, tiled=True)
     everything = everything.reshape(lats * 3 * CELLS, 1, 128)
-    to_right, to_left = kernel(pack_kernel, ((85, 8, 128),) * 2, [VMEM] * 5)(v, f, mu, above, below)
+    to_right, to_left = kernel(pack_kernel, ((85, 8, 128),) * 2, [VMEM] * 5)(
+        v, f, mu, above, below
+    )
     left = shifted(to_right, 0, 1)
     right = shifted(to_left, 0, -1)
 
@@ -582,16 +592,18 @@
     residual, smoothed, message = pl.pallas_call(
         smooth_kernel,
         out_shape=(block, block, jax.ShapeDtypeStruct((10, 8, 128), f32)),
-        in_specs=[SMEM, SMEM] + [VMEM] * 8,
+        in_specs=[SMEM] + [VMEM] * 8,
         out_specs=(VMEM, VMEM, VMEM),
         scratch_shapes=[pltpu.VMEM(field, f32)] * 3
         + [
             pltpu.VMEM(shape, f32)
-            for shape in ((6, 28, 24, 128), (16, 8, 128), (8, 8, 128), (8, 8, 128), (28, 24, 128))
+            for shape in (
+                (6, 28, 24, 128), (16, 8, 128), (8, 8, 128), (8, 8, 128), (28, 24, 128)
+            )
         ],
         compiler_params=params,
         name="smooth",
-    )(place, ghost_rows, v, f, mu, left, right, above, below, everything)
+    )(ghost_rows, v, f, mu, left, right, above, below, everything)
 
     tiles = [
         shifted(message, 0, 2),

time: 116 us -> 116 us (level)
  transfers between devices with their start and end apart: 16 -> 16, of which waited for: 9 -> 9; matrix products, arithmetic and copies ran while one was open for 0% -> 0% of each run, Pallas kernels for 1% -> 0%
where the time goes in v10:
time: 116 us
  starting transfers between devices  66.3 us (57%)
  waiting for transfers between devices  39.1 us (34%)
  Pallas kernels  9.37 us (8%)
    ppermute x14, starting transfers between devices, shifted(): return lax.ppermute(value, AXES, pairs)  46.5 us
    ppermute x14, waiting for transfers between devices, shifted(): return lax.ppermute(value, AXES, pairs)  28.6 us
    all_to_all x1, starting transfers between devices, per_device(): lax.all_to_all(values.reshape(lons, 1, 1152), 'lon', 0, 0, tiled=True)  13.5 us
    all_to_all x1, waiting for transfers between devices, per_device(): lax.all_to_all(values.reshape(lons, 1, 1152), 'lon', 0, 0, tiled=True)  10.5 us
    all_to_all x1, starting transfers between devices, per_device(): lax.all_to_all(chosen.reshape(lats, 3 * CELLS, 128), 'lat', 0, 0, tiled=T...  6.24 us
    pallas_call x1, Pallas kernels, per_device(): pl.pallas_call(smooth_kernel, out_shape=(block, block, jax.ShapeDtypeStru...  4.11 us
  transfers between devices with their start and end apart: 16, of which 9 were waited for; matrix products, arithmetic and copies ran while one was open for 0% of the time, Pallas kernels for 0%

profile of v10, /device:TPU:88, one launch (start us, length us, event | category | flops | bytes accessed | tf_op | source)
XLA Modules:
  0.0 115.8 jit_solution(4898117691426505797)
XLA Ops:
  0.6 1.0 first.1
  1.7 1.9 %collective-permute-start.4 = (f32[88,128]{1,0:T(8,128)S(1)}, f32[88,128]{1,0:T(8,128)S(1)}, u32[]{:S(2)}, u32[]{:S(2)}) collective-permute-start(f32[88,128]{1,0:T(8,128)S(1)} %get-tuple-element.25), channel_id=1, source_target_pairs={{0,256},{1,257},{2,258},{3,259},{4,260},{5,261},{6,262},{7,263},{8... | collective-permute-start | bytes 135176 | tf_op jit(solution)/shard_map/ppermute | solution.py:28
  3.6 3.9 %collective-permute-start.5 = (f32[3,16,128]{2,1,0:T(8,128)S(1)}, f32[3,16,128]{2,1,0:T(8,128)S(1)}, u32[]{:S(2)}, u32[]{:S(2)}) collective-permute-start(f32[3,16,128]{2,1,0:T(8,128)S(1)} %get-tuple-element.26), channel_id=1, source_target_pairs={{1,256},{2,257},{3,258},{4,259},{5,260},{6,261},{7,262},{8,263},{9... | collective-permute-start | bytes 73736 | tf_op jit(solution)/shard_map/ppermute | solution.py:28
  7.5 2.0 %collective-permute-start.6 = (f32[3,8,128]{2,1,0:T(8,128)S(1)}, f32[3,8,128]{2,1,0:T(8,128)S(1)}, u32[]{:S(2)}, u32[]{:S(2)}) collective-permute-start(f32[3,8,128]{2,1,0:T(8,128)S(1)} %get-tuple-element.27), channel_id=1, source_target_pairs={{32,256},{33,257},{34,258},{35,259},{36,260},{37,261},{38,262},{39... | collective-permute-start | bytes 36872 | tf_op jit(solution)/shard_map/ppermute | solution.py:28
  9.5 2.7 %collective-permute-start.7 = (f32[3,128]{1,0:T(4,128)S(1)}, f32[3,128]{1,0:T(4,128)S(1)}, u32[]{:S(2)}, u32[]{:S(2)}) collective-permute-start(f32[3,128]{1,0:T(4,128)S(1)} %get-tuple-element.28), channel_id=1, source_target_pairs={{33,256},{34,257},{35,258},{36,259},{37,260},{38,261},{39,262},{40... | collective-permute-start | bytes 4616 | tf_op jit(solution)/shard_map/ppermute | solution.py:28
  12.2 4.3 %collective-permute-done.7.corner_ref = f32[3,128]{1,0:T(4,128)S(1)} collective-permute-done((f32[3,128]{1,0:T(4,128)S(1)}, f32[3,128]{1,0:T(4,128)S(1)}, u32[]{:S(2)}, u32[]{:S(2)}) %collective-permute-start.7) | collective-permute-done | bytes 1568 | tf_op jit(solution)/shard_map/ppermute | solution.py:28
  16.5 0.0 collective-permute-done.6.below_ref
  16.5 0.0 collective-permute-done.5.edge_ref
  16.5 0.0 collective-permute-done.4.blend_ref
  16.5 0.0 copy-start.1
  16.5 0.8 shard_map.87
  17.3 0.0 copy-start
  17.3 0.0 copy-start.2
  17.3 13.5 %all-to-all-start = ((f32[32,1,1152]{2,1,0:T(1,128)}), f32[32,1,1152]{2,1,0:T(1,128)S(1)}, u32[]{:S(2)}, u32[]{:S(2)}) async-start(f32[32,1,1152]{2,1,0:T(1,128)} %bitcast.7), calls=%async_computation | async-start | bytes 294912 | tf_op jit(solution)/shard_map/all_to_all | solution.py:557
  30.8 0.0 copy-done.1
  30.8 0.0 copy-done
  30.8 0.0 copy-done.2
  30.9 10.5 %all-to-all-done = f32[32,1,1152]{2,1,0:T(1,128)S(1)} async-done(((f32[32,1,1152]{2,1,0:T(1,128)}), f32[32,1,1152]{2,1,0:T(1,128)S(1)}, u32[]{:S(2)}, u32[]{:S(2)}) %all-to-all-start) | async-done | bytes 147488 | tf_op jit(solution)/shard_map/all_to_all | solution.py:557
  41.4 1.4 %pick.1 = f32[8,96,1,128]{3,2,1,0:T(1,128)} custom-call(s32[8,32]{1,0:T(8,128)S(1)} %get-tuple-element.23.cells_ref, s32[1,768]{1,0:T(1,128)S(1)} %get-tuple-element.24.source_ref, f32[288,1,128]{2,1,0:T(1,128)S(1)} %bitcast.53), custom_call_target="tpu_custom_call" | custom-call | tf_op jit(solution)/shard_map/pick/pallas_call | solution.py:570
  42.8 6.2 %all-to-all-start.1 = ((f32[8,96,128]{2,1,0:T(8,128)}), f32[8,96,128]{2,1,0:T(8,128)S(1)}, u32[]{:S(2)}, u32[]{:S(2)}) async-start(f32[8,96,128]{2,1,0:T(8,128)} %bitcast.9), calls=%async_computation.1 | async-start | bytes 786432 | tf_op jit(solution)/shard_map/all_to_all | solution.py:582
  49.0 4.6 %collective-permute-start = (f32[32,8,128]{2,1,0:T(8,128)S(1)}, f32[32,8,128]{2,1,0:T(8,128)S(1)}, u32[]{:S(2)}, u32[]{:S(2)}) collective-permute-start(f32[32,8,128]{2,1,0:T(8,128)S(1)} %get-tuple-element.19), channel_id=1, source_target_pairs={{0,32},{1,33},{2,34},{3,35},{4,36},{5,37},{6,38},{7,39},{8,40},{9,... | collective-permute-start | bytes 393224 | tf_op jit(solution)/shard_map/ppermute | solution.py:28
  53.6 1.9 %collective-permute-start.1 = (f32[32,8,128]{2,1,0:T(8,128)S(1)}, f32[32,8,128]{2,1,0:T(8,128)S(1)}, u32[]{:S(2)}, u32[]{:S(2)}) collective-permute-start(f32[32,8,128]{2,1,0:T(8,128)S(1)} %get-tuple-element.20), channel_id=1, source_target_pairs={{32,0},{33,1},{34,2},{35,3},{36,4},{37,5},{38,6},{39,7},{40,8},{41... | collective-permute-start | bytes 393224 | tf_op jit(solution)/shard_map/ppermute | solution.py:28
  55.5 4.2 %collective-permute-done.above_ref = f32[32,8,128]{2,1,0:T(8,128)S(1)} collective-permute-done((f32[32,8,128]{2,1,0:T(8,128)S(1)}, f32[32,8,128]{2,1,0:T(8,128)S(1)}, u32[]{:S(2)}, u32[]{:S(2)}) %collective-permute-start) | collective-permute-done | bytes 131104 | tf_op jit(solution)/shard_map/ppermute | solution.py:28
  59.8 2.4 %collective-permute-done.1.below_ref = f32[32,8,128]{2,1,0:T(8,128)S(1)} collective-permute-done((f32[32,8,128]{2,1,0:T(8,128)S(1)}, f32[32,8,128]{2,1,0:T(8,128)S(1)}, u32[]{:S(2)}, u32[]{:S(2)}) %collective-permute-start.1) | collective-permute-done | bytes 131104 | tf_op jit(solution)/shard_map/ppermute | solution.py:28
  62.2 0.1 shard_map.86
  62.2 2.7 %collective-permute-start.2 = (f32[85,8,128]{2,1,0:T(8,128)S(1)}, f32[85,8,128]{2,1,0:T(8,128)S(1)}, u32[]{:S(2)}, u32[]{:S(2)}) collective-permute-start(f32[85,8,128]{2,1,0:T(8,128)S(1)} %get-tuple-element.21), channel_id=1, source_target_pairs={{0,1},{1,2},{2,3},{3,4},{4,5},{5,6},{6,7},{7,8},{8,9},{9,10},{10,1... | collective-permute-start | bytes 1044488 | tf_op jit(solution)/shard_map/ppermute | solution.py:28
  65.0 5.2 %collective-permute-start.3 = (f32[85,8,128]{2,1,0:T(8,128)S(1)}, f32[85,8,128]{2,1,0:T(8,128)S(1)}, u32[]{:S(2)}, u32[]{:S(2)}) collective-permute-start(f32[85,8,128]{2,1,0:T(8,128)S(1)} %get-tuple-element.22), channel_id=1, source_target_pairs={{1,0},{2,1},{3,2},{4,3},{5,4},{6,5},{7,6},{8,7},{9,8},{10,9},{11,1... | collective-permute-start | bytes 1044488 | tf_op jit(solution)/shard_map/ppermute | solution.py:28
  70.2 5.0 %collective-permute-done.2.left_ref = f32[85,8,128]{2,1,0:T(8,128)S(1)} collective-permute-done((f32[85,8,128]{2,1,0:T(8,128)S(1)}, f32[85,8,128]{2,1,0:T(8,128)S(1)}, u32[]{:S(2)}, u32[]{:S(2)}) %collective-permute-start.2) | collective-permute-done | bytes 348192 | tf_op jit(solution)/shard_map/ppermute | solution.py:28
  75.2 1.2 %collective-permute-done.3.right_ref = f32[85,8,128]{2,1,0:T(8,128)S(1)} collective-permute-done((f32[85,8,128]{2,1,0:T(8,128)S(1)}, f32[85,8,128]{2,1,0:T(8,128)S(1)}, u32[]{:S(2)}, u32[]{:S(2)}) %collective-permute-start.3) | collective-permute-done | bytes 348192 | tf_op jit(solution)/shard_map/ppermute | solution.py:28
  76.4 0.0 all-to-all-done.1
  76.4 4.1 %smooth.1 = (f32[3,16,8,128]{3,2,1,0:T(8,128)S(1)}, f32[3,16,8,128]{3,2,1,0:T(8,128)S(1)}, f32[10,8,128]{2,1,0:T(8,128)S(1)}) custom-call(s32[1,768]{1,0:T(1,128)S(1)} %get-tuple-element.18.ghost_ref, f32[3,16,8,128]{3,2,1,0:T(8,128)S(1)} %bitcast.48, f32[3,16,8,128]{3,2,1,0:T(8,128)S(1)} %bitcast.51, f32[16,8,128]{2,1,0:T(8,128)S(1)} %bitcast.56, ...), custom_call_target="tpu_custom_call" | custom-call | tf_op jit(solution)/shard_map/smooth/pallas_call | solution.py:592
  80.5 3.8 %collective-permute-start.8 = (f32[10,8,128]{2,1,0:T(8,128)S(1)}, f32[10,8,128]{2,1,0:T(8,128)S(1)}, u32[]{:S(2)}, u32[]{:S(2)}) collective-permute-start(f32[10,8,128]{2,1,0:T(8,128)S(1)} %get-tuple-element.29), channel_id=1, source_target_pairs={{0,2},{1,3},{2,4},{3,5},{4,6},{5,7},{6,8},{7,9},{8,10},{9,11},{10,... | collective-permute-start | bytes 122888 | tf_op jit(solution)/shard_map/ppermute | solution.py:28
  84.3 4.4 %collective-permute-start.11 = (f32[10,8,128]{2,1,0:T(8,128)S(1)}, f32[10,8,128]{2,1,0:T(8,128)S(1)}, u32[]{:S(2)}, u32[]{:S(2)}) collective-permute-start(f32[10,8,128]{2,1,0:T(8,128)S(1)} %get-tuple-element.29), channel_id=1, source_target_pairs={{2,0},{3,1},{4,2},{5,3},{6,4},{7,5},{8,6},{9,7},{10,8},{11,9},{12,... | collective-permute-start | bytes 122888 | tf_op jit(solution)/shard_map/ppermute | solution.py:28
  88.8 5.6 %collective-permute-start.10 = (f32[10,8,128]{2,1,0:T(8,128)S(1)}, f32[10,8,128]{2,1,0:T(8,128)S(1)}, u32[]{:S(2)}, u32[]{:S(2)}) collective-permute-start(f32[10,8,128]{2,1,0:T(8,128)S(1)} %get-tuple-element.29), channel_id=1, source_target_pairs={{1,0},{2,1},{3,2},{4,3},{5,4},{6,5},{7,6},{8,7},{9,8},{10,9},{11,1... | collective-permute-start | bytes 122888 | tf_op jit(solution)/shard_map/ppermute | solution.py:28
  94.4 1.9 %collective-permute-start.9 = (f32[10,8,128]{2,1,0:T(8,128)S(1)}, f32[10,8,128]{2,1,0:T(8,128)S(1)}, u32[]{:S(2)}, u32[]{:S(2)}) collective-permute-start(f32[10,8,128]{2,1,0:T(8,128)S(1)} %get-tuple-element.29), channel_id=1, source_target_pairs={{0,1},{1,2},{2,3},{3,4},{4,5},{5,6},{6,7},{7,8},{8,9},{9,10},{10,1... | collective-permute-start | bytes 122888 | tf_op jit(solution)/shard_map/ppermute | solution.py:28
  96.3 0.0 collective-permute-done.8
  96.3 6.1 %collective-permute-done.9 = f32[10,8,128]{2,1,0:T(8,128)S(1)} collective-permute-done((f32[10,8,128]{2,1,0:T(8,128)S(1)}, f32[10,8,128]{2,1,0:T(8,128)S(1)}, u32[]{:S(2)}, u32[]{:S(2)}) %collective-permute-start.9) | collective-permute-done | bytes 40992 | tf_op jit(solution)/shard_map/ppermute | solution.py:28
  102.4 0.0 collective-permute-done.10
  102.4 0.0 collective-permute-done.11
  102.6 3.0 %collective-permute-start.12 = (f32[35,8,128]{2,1,0:T(8,128)S(1)}, f32[35,8,128]{2,1,0:T(8,128)S(1)}, u32[]{:S(2)}, u32[]{:S(2)}) collective-permute-start(f32[35,8,128]{2,1,0:T(8,128)S(1)} %constant_dynamic-update-slice_fusion.8), channel_id=1, source_target_pairs={{0,32},{1,33},{2,34},{3,35},{4,36},{5,37},{6,38},{7,39},{8,40},{9,... | collective-permute-start | bytes 430088 | tf_op jit(solution)/shard_map/ppermute | solution.py:28
  105.7 2.8 %collective-permute-start.13 = (f32[35,8,128]{2,1,0:T(8,128)S(1)}, f32[35,8,128]{2,1,0:T(8,128)S(1)}, u32[]{:S(2)}, u32[]{:S(2)}) collective-permute-start(f32[35,8,128]{2,1,0:T(8,128)S(1)} %pad_maximum_fusion), channel_id=1, source_target_pairs={{32,0},{33,1},{34,2},{35,3},{36,4},{37,5},{38,6},{39,7},{40,8},{41... | collective-permute-start | bytes 430088 | tf_op jit(solution)/shard_map/ppermute | solution.py:28
  108.5 1.1 collective-permute-done.12.above_ref
  109.6 4.3 %collective-permute-done.13.below_ref = f32[35,8,128]{2,1,0:T(8,128)S(1)} collective-permute-done((f32[35,8,128]{2,1,0:T(8,128)S(1)}, f32[35,8,128]{2,1,0:T(8,128)S(1)}, u32[]{:S(2)}, u32[]{:S(2)}) %collective-permute-start.13) | collective-permute-done | bytes 143392 | tf_op jit(solution)/shard_map/ppermute | solution.py:28
  113.9 1.9 %coarse.1 = (f32[3,16,8,128]{3,2,1,0:T(8,128)}, f32[3,16,8,128]{3,2,1,0:T(8,128)}) custom-call(f32[10,40,128]{2,1,0:T(8,128)S(1)} %constant_dynamic-update-slice_fusion.mid_ref, f32[35,8,128]{2,1,0:T(8,128)S(1)} %collective-permute-done.12.above_ref, f32[35,8,128]{2,1,0:T(8,128)S(1)} %collective-permute-done.13.below_ref, ...), custom_call_target="tpu_custom_call" | custom-call | tf_op jit(solution)/shard_map/coarse/pallas_call | solution.py:624
  (17 shorter events, 0.1 us)
Async XLA Ops:
  1.7 14.8 %collective-permute-start.4 = (f32[88,128]{1,0:T(8,128)S(1)}, f32[88,128]{1,0:T(8,128)S(1)}, u32[]{:S(2)}, u32[]{:S(2)}) collective-permute-start(f32[88,128]{1,0:T(8,128)S(1)} %get-tuple-element.25), channel_id=1, source_target_pairs={{0,256},{1,257},{2,258},{3,259},{4,260},{5,261},{6,262},{7,263},{8... | collective-permute-start | bytes 135176 | tf_op jit(solution)/shard_map/ppermute | solution.py:28
  3.6 12.9 %collective-permute-start.5 = (f32[3,16,128]{2,1,0:T(8,128)S(1)}, f32[3,16,128]{2,1,0:T(8,128)S(1)}, u32[]{:S(2)}, u32[]{:S(2)}) collective-permute-start(f32[3,16,128]{2,1,0:T(8,128)S(1)} %get-tuple-element.26), channel_id=1, source_target_pairs={{1,256},{2,257},{3,258},{4,259},{5,260},{6,261},{7,262},{8,263},{9... | collective-permute-start | bytes 73736 | tf_op jit(solution)/shard_map/ppermute | solution.py:28
  7.5 9.0 %collective-permute-start.6 = (f32[3,8,128]{2,1,0:T(8,128)S(1)}, f32[3,8,128]{2,1,0:T(8,128)S(1)}, u32[]{:S(2)}, u32[]{:S(2)}) collective-permute-start(f32[3,8,128]{2,1,0:T(8,128)S(1)} %get-tuple-element.27), channel_id=1, source_target_pairs={{32,256},{33,257},{34,258},{35,259},{36,260},{37,261},{38,262},{39... | collective-permute-start | bytes 36872 | tf_op jit(solution)/shard_map/ppermute | solution.py:28
  9.5 7.0 %collective-permute-start.7 = (f32[3,128]{1,0:T(4,128)S(1)}, f32[3,128]{1,0:T(4,128)S(1)}, u32[]{:S(2)}, u32[]{:S(2)}) collective-permute-start(f32[3,128]{1,0:T(4,128)S(1)} %get-tuple-element.28), channel_id=1, source_target_pairs={{33,256},{34,257},{35,258},{36,259},{37,260},{38,261},{39,262},{40... | collective-permute-start | bytes 4616 | tf_op jit(solution)/shard_map/ppermute | solution.py:28
  16.5 14.3 %copy-start.1 = (f32[1,3,16,8,128]{4,3,2,1,0:T(8,128)S(1)}, f32[1,3,16,8,128]{4,3,2,1,0:T(8,128)}, u32[]{:S(2)}) copy-start(f32[1,3,16,8,128]{4,3,2,1,0:T(8,128)} %param.8) | copy-start | bytes 589828
  17.3 13.6 %copy-start = (f32[1,3,16,8,128]{4,3,2,1,0:T(8,128)S(1)}, f32[1,3,16,8,128]{4,3,2,1,0:T(8,128)}, u32[]{:S(2)}) copy-start(f32[1,3,16,8,128]{4,3,2,1,0:T(8,128)} %param.7) | copy-start | bytes 589828
  17.3 13.6 %copy-start.2 = (f32[1,16,8,128]{3,2,1,0:T(8,128)S(1)}, f32[1,16,8,128]{3,2,1,0:T(8,128)}, u32[]{:S(2)}) copy-start(f32[1,16,8,128]{3,2,1,0:T(8,128)} %param.9) | copy-start | bytes 196612
  17.3 24.1 %all-to-all-start = ((f32[32,1,1152]{2,1,0:T(1,128)}), f32[32,1,1152]{2,1,0:T(1,128)S(1)}, u32[]{:S(2)}, u32[]{:S(2)}) async-start(f32[32,1,1152]{2,1,0:T(1,128)} %bitcast.7), calls=%async_computation | async-start | bytes 294912 | tf_op jit(solution)/shard_map/all_to_all | solution.py:557
  42.8 33.6 %all-to-all-start.1 = ((f32[8,96,128]{2,1,0:T(8,128)}), f32[8,96,128]{2,1,0:T(8,128)S(1)}, u32[]{:S(2)}, u32[]{:S(2)}) async-start(f32[8,96,128]{2,1,0:T(8,128)} %bitcast.9), calls=%async_computation.1 | async-start | bytes 786432 | tf_op jit(solution)/shard_map/all_to_all | solution.py:582
  49.0 10.8 %collective-permute-start = (f32[32,8,128]{2,1,0:T(8,128)S(1)}, f32[32,8,128]{2,1,0:T(8,128)S(1)}, u32[]{:S(2)}, u32[]{:S(2)}) collective-permute-start(f32[32,8,128]{2,1,0:T(8,128)S(1)} %get-tuple-element.19), channel_id=1, source_target_pairs={{0,32},{1,33},{2,34},{3,35},{4,36},{5,37},{6,38},{7,39},{8,40},{9,... | collective-permute-start | bytes 393224 | tf_op jit(solution)/shard_map/ppermute | solution.py:28
  53.6 8.6 %collective-permute-start.1 = (f32[32,8,128]{2,1,0:T(8,128)S(1)}, f32[32,8,128]{2,1,0:T(8,128)S(1)}, u32[]{:S(2)}, u32[]{:S(2)}) collective-permute-start(f32[32,8,128]{2,1,0:T(8,128)S(1)} %get-tuple-element.20), channel_id=1, source_target_pairs={{32,0},{33,1},{34,2},{35,3},{36,4},{37,5},{38,6},{39,7},{40,8},{41... | collective-permute-start | bytes 393224 | tf_op jit(solution)/shard_map/ppermute | solution.py:28
  62.2 13.0 %collective-permute-start.2 = (f32[85,8,128]{2,1,0:T(8,128)S(1)}, f32[85,8,128]{2,1,0:T(8,128)S(1)}, u32[]{:S(2)}, u32[]{:S(2)}) collective-permute-start(f32[85,8,128]{2,1,0:T(8,128)S(1)} %get-tuple-element.21), channel_id=1, source_target_pairs={{0,1},{1,2},{2,3},{3,4},{4,5},{5,6},{6,7},{7,8},{8,9},{9,10},{10,1... | collective-permute-start | bytes 1044488 | tf_op jit(solution)/shard_map/ppermute | solution.py:28
  65.0 11.4 %collective-permute-start.3 = (f32[85,8,128]{2,1,0:T(8,128)S(1)}, f32[85,8,128]{2,1,0:T(8,128)S(1)}, u32[]{:S(2)}, u32[]{:S(2)}) collective-permute-start(f32[85,8,128]{2,1,0:T(8,128)S(1)} %get-tuple-element.22), channel_id=1, source_target_pairs={{1,0},{2,1},{3,2},{4,3},{5,4},{6,5},{7,6},{8,7},{9,8},{10,9},{11,1... | collective-permute-start | bytes 1044488 | tf_op jit(solution)/shard_map/ppermute | solution.py:28
  80.5 15.8 %collective-permute-start.8 = (f32[10,8,128]{2,1,0:T(8,128)S(1)}, f32[10,8,128]{2,1,0:T(8,128)S(1)}, u32[]{:S(2)}, u32[]{:S(2)}) collective-permute-start(f32[10,8,128]{2,1,0:T(8,128)S(1)} %get-tuple-element.29), channel_id=1, source_target_pairs={{0,2},{1,3},{2,4},{3,5},{4,6},{5,7},{6,8},{7,9},{8,10},{9,11},{10,... | collective-permute-start | bytes 122888 | tf_op jit(solution)/shard_map/ppermute | solution.py:28
  84.3 18.1 %collective-permute-start.11 = (f32[10,8,128]{2,1,0:T(8,128)S(1)}, f32[10,8,128]{2,1,0:T(8,128)S(1)}, u32[]{:S(2)}, u32[]{:S(2)}) collective-permute-start(f32[10,8,128]{2,1,0:T(8,128)S(1)} %get-tuple-element.29), channel_id=1, source_target_pairs={{2,0},{3,1},{4,2},{5,3},{6,4},{7,5},{8,6},{9,7},{10,8},{11,9},{12,... | collective-permute-start | bytes 122888 | tf_op jit(solution)/shard_map/ppermute | solution.py:28
  88.8 13.6 %collective-permute-start.10 = (f32[10,8,128]{2,1,0:T(8,128)S(1)}, f32[10,8,128]{2,1,0:T(8,128)S(1)}, u32[]{:S(2)}, u32[]{:S(2)}) collective-permute-start(f32[10,8,128]{2,1,0:T(8,128)S(1)} %get-tuple-element.29), channel_id=1, source_target_pairs={{1,0},{2,1},{3,2},{4,3},{5,4},{6,5},{7,6},{8,7},{9,8},{10,9},{11,1... | collective-permute-start | bytes 122888 | tf_op jit(solution)/shard_map/ppermute | solution.py:28
  94.4 8.0 %collective-permute-start.9 = (f32[10,8,128]{2,1,0:T(8,128)S(1)}, f32[10,8,128]{2,1,0:T(8,128)S(1)}, u32[]{:S(2)}, u32[]{:S(2)}) collective-permute-start(f32[10,8,128]{2,1,0:T(8,128)S(1)} %get-tuple-element.29), channel_id=1, source_target_pairs={{0,1},{1,2},{2,3},{3,4},{4,5},{5,6},{6,7},{7,8},{8,9},{9,10},{10,1... | collective-permute-start | bytes 122888 | tf_op jit(solution)/shard_map/ppermute | solution.py:28
  102.6 7.0 %collective-permute-start.12 = (f32[35,8,128]{2,1,0:T(8,128)S(1)}, f32[35,8,128]{2,1,0:T(8,128)S(1)}, u32[]{:S(2)}, u32[]{:S(2)}) collective-permute-start(f32[35,8,128]{2,1,0:T(8,128)S(1)} %constant_dynamic-update-slice_fusion.8), channel_id=1, source_target_pairs={{0,32},{1,33},{2,34},{3,35},{4,36},{5,37},{6,38},{7,39},{8,40},{9,... | collective-permute-start | bytes 430088 | tf_op jit(solution)/shard_map/ppermute | solution.py:28
  105.7 8.2 %collective-permute-start.13 = (f32[35,8,128]{2,1,0:T(8,128)S(1)}, f32[35,8,128]{2,1,0:T(8,128)S(1)}, u32[]{:S(2)}, u32[]{:S(2)}) collective-permute-start(f32[35,8,128]{2,1,0:T(8,128)S(1)} %pad_maximum_fusion), channel_id=1, source_target_pairs={{32,0},{33,1},{34,2},{35,3},{36,4},{37,5},{38,6},{39,7},{40,8},{41... | collective-permute-start | bytes 430088 | tf_op jit(solution)/shard_map/ppermute | solution.py:28

commit v11 on v10

--- a/solution.py
+++ b/solution.py
@@ -581,9 +581,7 @@
     )(cells, source_rows, around.reshape(lons * 9, 1, 128))
     everything = lax.all_to_all(chosen.reshape(lats, 3 * CELLS, 128), "lat", 0, 0, tiled=True)
     everything = everything.reshape(lats * 3 * CELLS, 1, 128)
-    to_right, to_left = kernel(pack_kernel, ((85, 8, 128),) * 2, [VMEM] * 5)(
-        v, f, mu, above, below
-    )
+    to_right, to_left = kernel(pack_kernel, ((85, 8, 128),) * 2, [VMEM] * 5)(v, f, mu, above, below)
     left = shifted(to_right, 0, 1)
     right = shifted(to_left, 0, -1)
 
@@ -597,21 +595,15 @@
         scratch_shapes=[pltpu.VMEM(field, f32)] * 3
         + [
             pltpu.VMEM(shape, f32)
-            for shape in (
-                (6, 28, 24, 128), (16, 8, 128), (8, 8, 128), (8, 8, 128), (28, 24, 128)
-            )
+            for shape in ((6, 28, 24, 128), (16, 8, 128), (8, 8, 128), (8, 8, 128), (28, 24, 128))
         ],
         compiler_params=params,
         name="smooth",
     )(ghost_rows, v, f, mu, left, right, above, below, everything)
 
-    tiles = [
-        shifted(message, 0, 2),
-        shifted(message, 0, 1),
-        message,
-        shifted(message, 0, -1),
-        shifted(message, 0, -2),
-    ]
+    near = shifted(message, 0, 1), shifted(message, 0, -1)
+    distant = shifted(message, 0, 2), shifted(message, 0, -2)
+    tiles = [distant[0], near[0], message, near[1], distant[1]]
     band = jnp.concatenate(tiles, axis=1)
     tile_list = (-1, 8, 128)
     inverse = band[8:10].reshape(tile_list)

time: 116 us -> 116 us (level)
  no operation moved by 1% of the time
where the time goes in v11:
time: 116 us
  starting transfers between devices  66.3 us (57%)
  waiting for transfers between devices  39.1 us (34%)
  Pallas kernels  9.37 us (8%)
    ppermute x14, starting transfers between devices, shifted(): return lax.ppermute(value, AXES, pairs)  46.5 us
    ppermute x14, waiting for transfers between devices, shifted(): return lax.ppermute(value, AXES, pairs)  28.6 us
    all_to_all x1, starting transfers between devices, per_device(): lax.all_to_all(values.reshape(lons, 1, 1152), 'lon', 0, 0, tiled=True)  13.5 us
    all_to_all x1, waiting for transfers between devices, per_device(): lax.all_to_all(values.reshape(lons, 1, 1152), 'lon', 0, 0, tiled=True)  10.5 us
    all_to_all x1, starting transfers between devices, per_device(): lax.all_to_all(chosen.reshape(lats, 3 * CELLS, 128), 'lat', 0, 0, tiled=T...  6.24 us
    pallas_call x1, Pallas kernels, per_device(): pl.pallas_call(smooth_kernel, out_shape=(block, block, jax.ShapeDtypeStru...  4.11 us
  transfers between devices with their start and end apart: 16, of which 9 were waited for; matrix products, arithmetic and copies ran while one was open for 0% of the time, Pallas kernels for 0%

profile of v11, /device:TPU:88, one launch (start us, length us, event | category | flops | bytes accessed | tf_op | source)
XLA Modules:
  0.0 115.8 jit_solution(4898117691426505797)
XLA Ops:
  0.6 1.0 first.1
  1.7 1.9 %collective-permute-start.4 = (f32[88,128]{1,0:T(8,128)S(1)}, f32[88,128]{1,0:T(8,128)S(1)}, u32[]{:S(2)}, u32[]{:S(2)}) collective-permute-start(f32[88,128]{1,0:T(8,128)S(1)} %get-tuple-element.25), channel_id=1, source_target_pairs={{0,256},{1,257},{2,258},{3,259},{4,260},{5,261},{6,262},{7,263},{8... | collective-permute-start | bytes 135176 | tf_op jit(solution)/shard_map/ppermute | solution.py:28
  3.6 3.9 %collective-permute-start.5 = (f32[3,16,128]{2,1,0:T(8,128)S(1)}, f32[3,16,128]{2,1,0:T(8,128)S(1)}, u32[]{:S(2)}, u32[]{:S(2)}) collective-permute-start(f32[3,16,128]{2,1,0:T(8,128)S(1)} %get-tuple-element.26), channel_id=1, source_target_pairs={{1,256},{2,257},{3,258},{4,259},{5,260},{6,261},{7,262},{8,263},{9... | collective-permute-start | bytes 73736 | tf_op jit(solution)/shard_map/ppermute | solution.py:28
  7.5 2.0 %collective-permute-start.6 = (f32[3,8,128]{2,1,0:T(8,128)S(1)}, f32[3,8,128]{2,1,0:T(8,128)S(1)}, u32[]{:S(2)}, u32[]{:S(2)}) collective-permute-start(f32[3,8,128]{2,1,0:T(8,128)S(1)} %get-tuple-element.27), channel_id=1, source_target_pairs={{32,256},{33,257},{34,258},{35,259},{36,260},{37,261},{38,262},{39... | collective-permute-start | bytes 36872 | tf_op jit(solution)/shard_map/ppermute | solution.py:28
  9.5 2.7 %collective-permute-start.7 = (f32[3,128]{1,0:T(4,128)S(1)}, f32[3,128]{1,0:T(4,128)S(1)}, u32[]{:S(2)}, u32[]{:S(2)}) collective-permute-start(f32[3,128]{1,0:T(4,128)S(1)} %get-tuple-element.28), channel_id=1, source_target_pairs={{33,256},{34,257},{35,258},{36,259},{37,260},{38,261},{39,262},{40... | collective-permute-start | bytes 4616 | tf_op jit(solution)/shard_map/ppermute | solution.py:28
  12.2 4.3 %collective-permute-done.7.corner_ref = f32[3,128]{1,0:T(4,128)S(1)} collective-permute-done((f32[3,128]{1,0:T(4,128)S(1)}, f32[3,128]{1,0:T(4,128)S(1)}, u32[]{:S(2)}, u32[]{:S(2)}) %collective-permute-start.7) | collective-permute-done | bytes 1568 | tf_op jit(solution)/shard_map/ppermute | solution.py:28
  16.5 0.0 collective-permute-done.6.below_ref
  16.5 0.0 collective-permute-done.5.edge_ref
  16.5 0.0 collective-permute-done.4.blend_ref
  16.5 0.0 copy-start.1
  16.5 0.8 shard_map.87
  17.3 0.0 copy-start
  17.3 0.0 copy-start.2
  17.3 13.5 %all-to-all-start = ((f32[32,1,1152]{2,1,0:T(1,128)}), f32[32,1,1152]{2,1,0:T(1,128)S(1)}, u32[]{:S(2)}, u32[]{:S(2)}) async-start(f32[32,1,1152]{2,1,0:T(1,128)} %bitcast.7), calls=%async_computation | async-start | bytes 294912 | tf_op jit(solution)/shard_map/all_to_all | solution.py:557
  30.8 0.0 copy-done.1
  30.8 0.0 copy-done
  30.8 0.0 copy-done.2
  30.9 10.5 %all-to-all-done = f32[32,1,1152]{2,1,0:T(1,128)S(1)} async-done(((f32[32,1,1152]{2,1,0:T(1,128)}), f32[32,1,1152]{2,1,0:T(1,128)S(1)}, u32[]{:S(2)}, u32[]{:S(2)}) %all-to-all-start) | async-done | bytes 147488 | tf_op jit(solution)/shard_map/all_to_all | solution.py:557
  41.4 1.4 %pick.1 = f32[8,96,1,128]{3,2,1,0:T(1,128)} custom-call(s32[8,32]{1,0:T(8,128)S(1)} %get-tuple-element.23.cells_ref, s32[1,768]{1,0:T(1,128)S(1)} %get-tuple-element.24.source_ref, f32[288,1,128]{2,1,0:T(1,128)S(1)} %bitcast.53), custom_call_target="tpu_custom_call" | custom-call | tf_op jit(solution)/shard_map/pick/pallas_call | solution.py:570
  42.8 6.2 %all-to-all-start.1 = ((f32[8,96,128]{2,1,0:T(8,128)}), f32[8,96,128]{2,1,0:T(8,128)S(1)}, u32[]{:S(2)}, u32[]{:S(2)}) async-start(f32[8,96,128]{2,1,0:T(8,128)} %bitcast.9), calls=%async_computation.1 | async-start | bytes 786432 | tf_op jit(solution)/shard_map/all_to_all | solution.py:582
  49.0 4.6 %collective-permute-start = (f32[32,8,128]{2,1,0:T(8,128)S(1)}, f32[32,8,128]{2,1,0:T(8,128)S(1)}, u32[]{:S(2)}, u32[]{:S(2)}) collective-permute-start(f32[32,8,128]{2,1,0:T(8,128)S(1)} %get-tuple-element.19), channel_id=1, source_target_pairs={{0,32},{1,33},{2,34},{3,35},{4,36},{5,37},{6,38},{7,39},{8,40},{9,... | collective-permute-start | bytes 393224 | tf_op jit(solution)/shard_map/ppermute | solution.py:28
  53.6 1.9 %collective-permute-start.1 = (f32[32,8,128]{2,1,0:T(8,128)S(1)}, f32[32,8,128]{2,1,0:T(8,128)S(1)}, u32[]{:S(2)}, u32[]{:S(2)}) collective-permute-start(f32[32,8,128]{2,1,0:T(8,128)S(1)} %get-tuple-element.20), channel_id=1, source_target_pairs={{32,0},{33,1},{34,2},{35,3},{36,4},{37,5},{38,6},{39,7},{40,8},{41... | collective-permute-start | bytes 393224 | tf_op jit(solution)/shard_map/ppermute | solution.py:28
  55.5 4.2 %collective-permute-done.above_ref = f32[32,8,128]{2,1,0:T(8,128)S(1)} collective-permute-done((f32[32,8,128]{2,1,0:T(8,128)S(1)}, f32[32,8,128]{2,1,0:T(8,128)S(1)}, u32[]{:S(2)}, u32[]{:S(2)}) %collective-permute-start) | collective-permute-done | bytes 131104 | tf_op jit(solution)/shard_map/ppermute | solution.py:28
  59.8 2.4 %collective-permute-done.1.below_ref = f32[32,8,128]{2,1,0:T(8,128)S(1)} collective-permute-done((f32[32,8,128]{2,1,0:T(8,128)S(1)}, f32[32,8,128]{2,1,0:T(8,128)S(1)}, u32[]{:S(2)}, u32[]{:S(2)}) %collective-permute-start.1) | collective-permute-done | bytes 131104 | tf_op jit(solution)/shard_map/ppermute | solution.py:28
  62.2 0.1 shard_map.86
  62.2 2.7 %collective-permute-start.2 = (f32[85,8,128]{2,1,0:T(8,128)S(1)}, f32[85,8,128]{2,1,0:T(8,128)S(1)}, u32[]{:S(2)}, u32[]{:S(2)}) collective-permute-start(f32[85,8,128]{2,1,0:T(8,128)S(1)} %get-tuple-element.21), channel_id=1, source_target_pairs={{0,1},{1,2},{2,3},{3,4},{4,5},{5,6},{6,7},{7,8},{8,9},{9,10},{10,1... | collective-permute-start | bytes 1044488 | tf_op jit(solution)/shard_map/ppermute | solution.py:28
  65.0 5.2 %collective-permute-start.3 = (f32[85,8,128]{2,1,0:T(8,128)S(1)}, f32[85,8,128]{2,1,0:T(8,128)S(1)}, u32[]{:S(2)}, u32[]{:S(2)}) collective-permute-start(f32[85,8,128]{2,1,0:T(8,128)S(1)} %get-tuple-element.22), channel_id=1, source_target_pairs={{1,0},{2,1},{3,2},{4,3},{5,4},{6,5},{7,6},{8,7},{9,8},{10,9},{11,1... | collective-permute-start | bytes 1044488 | tf_op jit(solution)/shard_map/ppermute | solution.py:28
  70.2 5.0 %collective-permute-done.2.left_ref = f32[85,8,128]{2,1,0:T(8,128)S(1)} collective-permute-done((f32[85,8,128]{2,1,0:T(8,128)S(1)}, f32[85,8,128]{2,1,0:T(8,128)S(1)}, u32[]{:S(2)}, u32[]{:S(2)}) %collective-permute-start.2) | collective-permute-done | bytes 348192 | tf_op jit(solution)/shard_map/ppermute | solution.py:28
  75.2 1.2 %collective-permute-done.3.right_ref = f32[85,8,128]{2,1,0:T(8,128)S(1)} collective-permute-done((f32[85,8,128]{2,1,0:T(8,128)S(1)}, f32[85,8,128]{2,1,0:T(8,128)S(1)}, u32[]{:S(2)}, u32[]{:S(2)}) %collective-permute-start.3) | collective-permute-done | bytes 348192 | tf_op jit(solution)/shard_map/ppermute | solution.py:28
  76.4 0.0 all-to-all-done.1
  76.4 4.1 %smooth.1 = (f32[3,16,8,128]{3,2,1,0:T(8,128)S(1)}, f32[3,16,8,128]{3,2,1,0:T(8,128)S(1)}, f32[10,8,128]{2,1,0:T(8,128)S(1)}) custom-call(s32[1,768]{1,0:T(1,128)S(1)} %get-tuple-element.18.ghost_ref, f32[3,16,8,128]{3,2,1,0:T(8,128)S(1)} %bitcast.48, f32[3,16,8,128]{3,2,1,0:T(8,128)S(1)} %bitcast.51, f32[16,8,128]{2,1,0:T(8,128)S(1)} %bitcast.56, ...), custom_call_target="tpu_custom_call" | custom-call | tf_op jit(solution)/shard_map/smooth/pallas_call | solution.py:590
  80.5 3.8 %collective-permute-start.8 = (f32[10,8,128]{2,1,0:T(8,128)S(1)}, f32[10,8,128]{2,1,0:T(8,128)S(1)}, u32[]{:S(2)}, u32[]{:S(2)}) collective-permute-start(f32[10,8,128]{2,1,0:T(8,128)S(1)} %get-tuple-element.29), channel_id=1, source_target_pairs={{0,2},{1,3},{2,4},{3,5},{4,6},{5,7},{6,8},{7,9},{8,10},{9,11},{10,... | collective-permute-start | bytes 122888 | tf_op jit(solution)/shard_map/ppermute | solution.py:28
  84.3 4.4 %collective-permute-start.11 = (f32[10,8,128]{2,1,0:T(8,128)S(1)}, f32[10,8,128]{2,1,0:T(8,128)S(1)}, u32[]{:S(2)}, u32[]{:S(2)}) collective-permute-start(f32[10,8,128]{2,1,0:T(8,128)S(1)} %get-tuple-element.29), channel_id=1, source_target_pairs={{2,0},{3,1},{4,2},{5,3},{6,4},{7,5},{8,6},{9,7},{10,8},{11,9},{12,... | collective-permute-start | bytes 122888 | tf_op jit(solution)/shard_map/ppermute | solution.py:28
  88.8 5.6 %collective-permute-start.10 = (f32[10,8,128]{2,1,0:T(8,128)S(1)}, f32[10,8,128]{2,1,0:T(8,128)S(1)}, u32[]{:S(2)}, u32[]{:S(2)}) collective-permute-start(f32[10,8,128]{2,1,0:T(8,128)S(1)} %get-tuple-element.29), channel_id=1, source_target_pairs={{1,0},{2,1},{3,2},{4,3},{5,4},{6,5},{7,6},{8,7},{9,8},{10,9},{11,1... | collective-permute-start | bytes 122888 | tf_op jit(solution)/shard_map/ppermute | solution.py:28
  94.4 1.9 %collective-permute-start.9 = (f32[10,8,128]{2,1,0:T(8,128)S(1)}, f32[10,8,128]{2,1,0:T(8,128)S(1)}, u32[]{:S(2)}, u32[]{:S(2)}) collective-permute-start(f32[10,8,128]{2,1,0:T(8,128)S(1)} %get-tuple-element.29), channel_id=1, source_target_pairs={{0,1},{1,2},{2,3},{3,4},{4,5},{5,6},{6,7},{7,8},{8,9},{9,10},{10,1... | collective-permute-start | bytes 122888 | tf_op jit(solution)/shard_map/ppermute | solution.py:28
  96.3 0.0 collective-permute-done.8
  96.3 6.1 %collective-permute-done.9 = f32[10,8,128]{2,1,0:T(8,128)S(1)} collective-permute-done((f32[10,8,128]{2,1,0:T(8,128)S(1)}, f32[10,8,128]{2,1,0:T(8,128)S(1)}, u32[]{:S(2)}, u32[]{:S(2)}) %collective-permute-start.9) | collective-permute-done | bytes 40992 | tf_op jit(solution)/shard_map/ppermute | solution.py:28
  102.4 0.0 collective-permute-done.10
  102.4 0.0 collective-permute-done.11
  102.6 3.0 %collective-permute-start.12 = (f32[35,8,128]{2,1,0:T(8,128)S(1)}, f32[35,8,128]{2,1,0:T(8,128)S(1)}, u32[]{:S(2)}, u32[]{:S(2)}) collective-permute-start(f32[35,8,128]{2,1,0:T(8,128)S(1)} %constant_dynamic-update-slice_fusion.8), channel_id=1, source_target_pairs={{0,32},{1,33},{2,34},{3,35},{4,36},{5,37},{6,38},{7,39},{8,40},{9,... | collective-permute-start | bytes 430088 | tf_op jit(solution)/shard_map/ppermute | solution.py:28
  105.7 2.8 %collective-permute-start.13 = (f32[35,8,128]{2,1,0:T(8,128)S(1)}, f32[35,8,128]{2,1,0:T(8,128)S(1)}, u32[]{:S(2)}, u32[]{:S(2)}) collective-permute-start(f32[35,8,128]{2,1,0:T(8,128)S(1)} %pad_maximum_fusion), channel_id=1, source_target_pairs={{32,0},{33,1},{34,2},{35,3},{36,4},{37,5},{38,6},{39,7},{40,8},{41... | collective-permute-start | bytes 430088 | tf_op jit(solution)/shard_map/ppermute | solution.py:28
  108.5 1.1 collective-permute-done.12.above_ref
  109.6 4.3 %collective-permute-done.13.below_ref = f32[35,8,128]{2,1,0:T(8,128)S(1)} collective-permute-done((f32[35,8,128]{2,1,0:T(8,128)S(1)}, f32[35,8,128]{2,1,0:T(8,128)S(1)}, u32[]{:S(2)}, u32[]{:S(2)}) %collective-permute-start.13) | collective-permute-done | bytes 143392 | tf_op jit(solution)/shard_map/ppermute | solution.py:28
  113.9 1.9 %coarse.1 = (f32[3,16,8,128]{3,2,1,0:T(8,128)}, f32[3,16,8,128]{3,2,1,0:T(8,128)}) custom-call(f32[10,40,128]{2,1,0:T(8,128)S(1)} %constant_dynamic-update-slice_fusion.mid_ref, f32[35,8,128]{2,1,0:T(8,128)S(1)} %collective-permute-done.12.above_ref, f32[35,8,128]{2,1,0:T(8,128)S(1)} %collective-permute-done.13.below_ref, ...), custom_call_target="tpu_custom_call" | custom-call | tf_op jit(solution)/shard_map/coarse/pallas_call | solution.py:616
  (17 shorter events, 0.1 us)
Async XLA Ops:
  1.7 14.8 %collective-permute-start.4 = (f32[88,128]{1,0:T(8,128)S(1)}, f32[88,128]{1,0:T(8,128)S(1)}, u32[]{:S(2)}, u32[]{:S(2)}) collective-permute-start(f32[88,128]{1,0:T(8,128)S(1)} %get-tuple-element.25), channel_id=1, source_target_pairs={{0,256},{1,257},{2,258},{3,259},{4,260},{5,261},{6,262},{7,263},{8... | collective-permute-start | bytes 135176 | tf_op jit(solution)/shard_map/ppermute | solution.py:28
  3.6 12.9 %collective-permute-start.5 = (f32[3,16,128]{2,1,0:T(8,128)S(1)}, f32[3,16,128]{2,1,0:T(8,128)S(1)}, u32[]{:S(2)}, u32[]{:S(2)}) collective-permute-start(f32[3,16,128]{2,1,0:T(8,128)S(1)} %get-tuple-element.26), channel_id=1, source_target_pairs={{1,256},{2,257},{3,258},{4,259},{5,260},{6,261},{7,262},{8,263},{9... | collective-permute-start | bytes 73736 | tf_op jit(solution)/shard_map/ppermute | solution.py:28
  7.5 9.0 %collective-permute-start.6 = (f32[3,8,128]{2,1,0:T(8,128)S(1)}, f32[3,8,128]{2,1,0:T(8,128)S(1)}, u32[]{:S(2)}, u32[]{:S(2)}) collective-permute-start(f32[3,8,128]{2,1,0:T(8,128)S(1)} %get-tuple-element.27), channel_id=1, source_target_pairs={{32,256},{33,257},{34,258},{35,259},{36,260},{37,261},{38,262},{39... | collective-permute-start | bytes 36872 | tf_op jit(solution)/shard_map/ppermute | solution.py:28
  9.5 7.0 %collective-permute-start.7 = (f32[3,128]{1,0:T(4,128)S(1)}, f32[3,128]{1,0:T(4,128)S(1)}, u32[]{:S(2)}, u32[]{:S(2)}) collective-permute-start(f32[3,128]{1,0:T(4,128)S(1)} %get-tuple-element.28), channel_id=1, source_target_pairs={{33,256},{34,257},{35,258},{36,259},{37,260},{38,261},{39,262},{40... | collective-permute-start | bytes 4616 | tf_op jit(solution)/shard_map/ppermute | solution.py:28
  16.5 14.3 %copy-start.1 = (f32[1,3,16,8,128]{4,3,2,1,0:T(8,128)S(1)}, f32[1,3,16,8,128]{4,3,2,1,0:T(8,128)}, u32[]{:S(2)}) copy-start(f32[1,3,16,8,128]{4,3,2,1,0:T(8,128)} %param.8) | copy-start | bytes 589828
  17.3 13.6 %copy-start = (f32[1,3,16,8,128]{4,3,2,1,0:T(8,128)S(1)}, f32[1,3,16,8,128]{4,3,2,1,0:T(8,128)}, u32[]{:S(2)}) copy-start(f32[1,3,16,8,128]{4,3,2,1,0:T(8,128)} %param.7) | copy-start | bytes 589828
  17.3 13.6 %copy-start.2 = (f32[1,16,8,128]{3,2,1,0:T(8,128)S(1)}, f32[1,16,8,128]{3,2,1,0:T(8,128)}, u32[]{:S(2)}) copy-start(f32[1,16,8,128]{3,2,1,0:T(8,128)} %param.9) | copy-start | bytes 196612
  17.3 24.1 %all-to-all-start = ((f32[32,1,1152]{2,1,0:T(1,128)}), f32[32,1,1152]{2,1,0:T(1,128)S(1)}, u32[]{:S(2)}, u32[]{:S(2)}) async-start(f32[32,1,1152]{2,1,0:T(1,128)} %bitcast.7), calls=%async_computation | async-start | bytes 294912 | tf_op jit(solution)/shard_map/all_to_all | solution.py:557
  42.8 33.6 %all-to-all-start.1 = ((f32[8,96,128]{2,1,0:T(8,128)}), f32[8,96,128]{2,1,0:T(8,128)S(1)}, u32[]{:S(2)}, u32[]{:S(2)}) async-start(f32[8,96,128]{2,1,0:T(8,128)} %bitcast.9), calls=%async_computation.1 | async-start | bytes 786432 | tf_op jit(solution)/shard_map/all_to_all | solution.py:582
  49.0 10.8 %collective-permute-start = (f32[32,8,128]{2,1,0:T(8,128)S(1)}, f32[32,8,128]{2,1,0:T(8,128)S(1)}, u32[]{:S(2)}, u32[]{:S(2)}) collective-permute-start(f32[32,8,128]{2,1,0:T(8,128)S(1)} %get-tuple-element.19), channel_id=1, source_target_pairs={{0,32},{1,33},{2,34},{3,35},{4,36},{5,37},{6,38},{7,39},{8,40},{9,... | collective-permute-start | bytes 393224 | tf_op jit(solution)/shard_map/ppermute | solution.py:28
  53.6 8.6 %collective-permute-start.1 = (f32[32,8,128]{2,1,0:T(8,128)S(1)}, f32[32,8,128]{2,1,0:T(8,128)S(1)}, u32[]{:S(2)}, u32[]{:S(2)}) collective-permute-start(f32[32,8,128]{2,1,0:T(8,128)S(1)} %get-tuple-element.20), channel_id=1, source_target_pairs={{32,0},{33,1},{34,2},{35,3},{36,4},{37,5},{38,6},{39,7},{40,8},{41... | collective-permute-start | bytes 393224 | tf_op jit(solution)/shard_map/ppermute | solution.py:28
  62.2 13.0 %collective-permute-start.2 = (f32[85,8,128]{2,1,0:T(8,128)S(1)}, f32[85,8,128]{2,1,0:T(8,128)S(1)}, u32[]{:S(2)}, u32[]{:S(2)}) collective-permute-start(f32[85,8,128]{2,1,0:T(8,128)S(1)} %get-tuple-element.21), channel_id=1, source_target_pairs={{0,1},{1,2},{2,3},{3,4},{4,5},{5,6},{6,7},{7,8},{8,9},{9,10},{10,1... | collective-permute-start | bytes 1044488 | tf_op jit(solution)/shard_map/ppermute | solution.py:28
  65.0 11.4 %collective-permute-start.3 = (f32[85,8,128]{2,1,0:T(8,128)S(1)}, f32[85,8,128]{2,1,0:T(8,128)S(1)}, u32[]{:S(2)}, u32[]{:S(2)}) collective-permute-start(f32[85,8,128]{2,1,0:T(8,128)S(1)} %get-tuple-element.22), channel_id=1, source_target_pairs={{1,0},{2,1},{3,2},{4,3},{5,4},{6,5},{7,6},{8,7},{9,8},{10,9},{11,1... | collective-permute-start | bytes 1044488 | tf_op jit(solution)/shard_map/ppermute | solution.py:28
  80.5 15.8 %collective-permute-start.8 = (f32[10,8,128]{2,1,0:T(8,128)S(1)}, f32[10,8,128]{2,1,0:T(8,128)S(1)}, u32[]{:S(2)}, u32[]{:S(2)}) collective-permute-start(f32[10,8,128]{2,1,0:T(8,128)S(1)} %get-tuple-element.29), channel_id=1, source_target_pairs={{0,2},{1,3},{2,4},{3,5},{4,6},{5,7},{6,8},{7,9},{8,10},{9,11},{10,... | collective-permute-start | bytes 122888 | tf_op jit(solution)/shard_map/ppermute | solution.py:28
  84.3 18.1 %collective-permute-start.11 = (f32[10,8,128]{2,1,0:T(8,128)S(1)}, f32[10,8,128]{2,1,0:T(8,128)S(1)}, u32[]{:S(2)}, u32[]{:S(2)}) collective-permute-start(f32[10,8,128]{2,1,0:T(8,128)S(1)} %get-tuple-element.29), channel_id=1, source_target_pairs={{2,0},{3,1},{4,2},{5,3},{6,4},{7,5},{8,6},{9,7},{10,8},{11,9},{12,... | collective-permute-start | bytes 122888 | tf_op jit(solution)/shard_map/ppermute | solution.py:28
  88.8 13.6 %collective-permute-start.10 = (f32[10,8,128]{2,1,0:T(8,128)S(1)}, f32[10,8,128]{2,1,0:T(8,128)S(1)}, u32[]{:S(2)}, u32[]{:S(2)}) collective-permute-start(f32[10,8,128]{2,1,0:T(8,128)S(1)} %get-tuple-element.29), channel_id=1, source_target_pairs={{1,0},{2,1},{3,2},{4,3},{5,4},{6,5},{7,6},{8,7},{9,8},{10,9},{11,1... | collective-permute-start | bytes 122888 | tf_op jit(solution)/shard_map/ppermute | solution.py:28
  94.4 8.0 %collective-permute-start.9 = (f32[10,8,128]{2,1,0:T(8,128)S(1)}, f32[10,8,128]{2,1,0:T(8,128)S(1)}, u32[]{:S(2)}, u32[]{:S(2)}) collective-permute-start(f32[10,8,128]{2,1,0:T(8,128)S(1)} %get-tuple-element.29), channel_id=1, source_target_pairs={{0,1},{1,2},{2,3},{3,4},{4,5},{5,6},{6,7},{7,8},{8,9},{9,10},{10,1... | collective-permute-start | bytes 122888 | tf_op jit(solution)/shard_map/ppermute | solution.py:28
  102.6 7.0 %collective-permute-start.12 = (f32[35,8,128]{2,1,0:T(8,128)S(1)}, f32[35,8,128]{2,1,0:T(8,128)S(1)}, u32[]{:S(2)}, u32[]{:S(2)}) collective-permute-start(f32[35,8,128]{2,1,0:T(8,128)S(1)} %constant_dynamic-update-slice_fusion.8), channel_id=1, source_target_pairs={{0,32},{1,33},{2,34},{3,35},{4,36},{5,37},{6,38},{7,39},{8,40},{9,... | collective-permute-start | bytes 430088 | tf_op jit(solution)/shard_map/ppermute | solution.py:28
  105.7 8.2 %collective-permute-start.13 = (f32[35,8,128]{2,1,0:T(8,128)S(1)}, f32[35,8,128]{2,1,0:T(8,128)S(1)}, u32[]{:S(2)}, u32[]{:S(2)}) collective-permute-start(f32[35,8,128]{2,1,0:T(8,128)S(1)} %pad_maximum_fusion), channel_id=1, source_target_pairs={{32,0},{33,1},{34,2},{35,3},{36,4},{37,5},{38,6},{39,7},{40,8},{41... | collective-permute-start | bytes 430088 | tf_op jit(solution)/shard_map/ppermute | solution.py:28
